TPU v7x, 32 devices: a whole 2x2x4 slice. The times are simulated.
32 devices in a mesh: clus: 4 (over y, x), dir: 8 (over z, core).
Axes of the slice: x: 2, y: 2, z: 4, core: 2. Of those that a mesh axis runs over, the one named last changes fastest.
Arguments:
- child_patterns: float32 [192, 2, 256, 128], P('clus', None, 'dir'), may hold values from -6 to 6
- trans_table: bfloat16 [316, 2, 73728], P(None, None, 'dir'), may hold values from -0.875 to 0.875
- child_parent: int32 [4, 48], P('clus'), may hold values from 0 to 7, never falling along the last dimension, each value on 1 to 8 neighbouring positions
- child_octant: int32 [192], P('clus'), may hold values from 0 to 7
- partner_src: int32 [32, 31], replicated, may hold values from 0 to 31, as said below
- partner_off: int32 [32, 31], replicated, may hold values from 0 to 315
- partner_count: int32 [32], replicated, may hold values from 8 to 31, as said below
Outputs:
- child_incoming: float32 [192, 2, 256, 128], P('clus', None, 'dir')
Inputs may be any that keep to these rules, and one draw needn't show every extreme that they name: `partner_src`: each row lists 31 distinct parent clusters, none equal to the row's own index. `partner_count`: the number of live slots at the head of each row of partner_src and partner_off. On one index of clus, all of its 8 parents have 31 live slots. `child_parent`: Non-decreasing along each row; every one of the 8 parents of the row has 1 to 8 children.
All inputs are finite; a program needn't handle non-finite values.
Results may differ from a plain program's by a relative error of at most 0.0003.
Values sent between devices are 32-bit elements; how exact they have to be, the bound alone decides.
No kernel may reach another device: no remote copies, remote signals or barrier semaphores. Data moves between devices by JAX's collectives and lax.ppermute only.
A program may use at most 128 MiB of HBM per device.

v0:
```python
import functools
import math

import jax
import jax.numpy as jnp
import numpy as np
from jax import lax
from jax.experimental import pallas as pl
from jax.experimental.pallas import tpu as pltpu
from jax.sharding import PartitionSpec as P


NTHETA_C = 128
NPHI_C = 256
NTHETA_P = 192
NPHI_P = 384

LANES = 128
PERIOD_P = 6
PERIOD_C = 4
ROWS_PER_PERIOD = PERIOD_P * NTHETA_P // LANES
GROUP = 8
UNROLL = 8
PAIR = 2

phase_scale = 8.0 * math.pi
highest = lax.Precision.HIGHEST
f32 = jnp.float32
bf16 = jnp.bfloat16


def lagrange(offset):
    weights = []
    for anchor in range(5):
        factor = 1.0
        for neighbour in range(5):
            if neighbour != anchor:
                factor = factor * (offset - neighbour) / (anchor - neighbour)
        weights.append(factor)
    return weights


TAPS_A = [float(w) for w in lagrange(5.0 / 3.0)]
TAPS_B = [float(w) for w in lagrange(7.0 / 3.0)]


def polar_matrix_np():
    target = (np.arange(NTHETA_P, dtype=np.float32) + np.float32(0.5)) * NTHETA_C / NTHETA_P - np.float32(0.5)
    start = np.clip(np.floor(target + 0.5).astype(np.int32) - 2, 0, NTHETA_C - 5)
    weights = lagrange((target - start).astype(np.float64))
    matrix = np.zeros((NTHETA_P, NTHETA_C), np.float64)
    for anchor in range(5):
        matrix[np.arange(NTHETA_P), start + anchor] += weights[anchor]
    return matrix.astype(np.float32)


def polar_blocks():
    matrix = polar_matrix_np().T
    even = np.zeros((NTHETA_C, 2 * LANES), np.float32)
    odd = np.zeros((NTHETA_C, 2 * LANES), np.float32)
    half = NTHETA_P - LANES
    even[:, :NTHETA_P] = matrix
    odd[:, :LANES] = matrix[:, half:]
    odd[:, 2 * LANES - half :] = matrix[:, :half]
    return even, odd


def split_np(matrix):
    high = matrix.astype(bf16)
    low = (matrix - high.astype(np.float32)).astype(bf16)
    return high, low


def split(values):
    high = values.astype(bf16)
    low = (values - high.astype(f32)).astype(bf16)
    return high, low


def dot3(values, high_matrix, low_matrix):
    high, low = split(values)
    dot = functools.partial(jnp.dot, preferred_element_type=f32)
    return dot(high, high_matrix) + dot(low, high_matrix) + dot(high, low_matrix)


SIN_COEFFS = [(-1) ** k * math.pi ** (2 * k + 1) / math.factorial(2 * k + 1) for k in range(7)]
COS_COEFFS = [(-1) ** k * math.pi ** (2 * k) / math.factorial(2 * k) for k in range(7)]


def sincos_turns(turns):
    rest = turns - jnp.round(turns)
    square = rest * rest
    sine = jnp.full_like(square, SIN_COEFFS[-1])
    for coeff in SIN_COEFFS[-2::-1]:
        sine = sine * square + coeff
    sine = sine * rest
    cosine = jnp.full_like(square, COS_COEFFS[-1])
    for coeff in COS_COEFFS[-2::-1]:
        cosine = cosine * square + coeff
    return 2.0 * sine * cosine, 1.0 - 2.0 * sine * sine


def fill_phases(direction, out_ref):
    periods = out_ref.shape[3]
    lane = lax.broadcasted_iota(jnp.int32, (periods, LANES), 1)
    period = lax.broadcasted_iota(jnp.int32, (periods, LANES), 0)
    first = direction * (PERIOD_P * periods)
    for w in range(ROWS_PER_PERIOD):
        position = lane + w * LANES
        row = w * LANES // NTHETA_P
        row = jnp.where(position >= (row + 1) * NTHETA_P, row + 1, row)
        polar_index = position - row * NTHETA_P
        azimuth_index = first + period * PERIOD_P + row
        sin_polar, cos_polar = sincos_turns((polar_index.astype(f32) + 0.5) / (2 * NTHETA_P))
        sin_azimuth, cos_azimuth = sincos_turns(azimuth_index.astype(f32) / NPHI_P)
        along_x = 4.0 * sin_polar * cos_azimuth
        along_y = 4.0 * sin_polar * sin_azimuth
        along_z = 4.0 * cos_polar
        for octant in (0, 2, 4, 6):
            turns = along_x + along_y if octant % 4 == 0 else along_x - along_y
            turns = turns + along_z if octant < 4 else turns - along_z
            sine, cosine = sincos_turns(turns)
            out_ref[octant, 0, w] = cosine
            out_ref[octant, 1, w] = sine
            out_ref[7 - octant, 0, w] = cosine
            out_ref[7 - octant, 1, w] = -sine


def edge_rows(periods):
    return [(w, 0) for w in (1, 2, 3, 4)] + [(w, periods - 1) for w in (6, 7, 8)]


def rows_kernel(octants_ref, x_ref, held_ref, last_ref, first_ref, phase_ref, edge_phase_ref, sem):
    pairs, azimuth_in, _ = x_ref.shape
    periods = phase_ref.shape[3]
    copy = pltpu.make_async_copy(x_ref, held_ref, sem)
    copy.start()
    fill_phases(lax.axis_index("dir"), phase_ref)

    def edges_of(step, carry):
        for j in range(GROUP):
            k = step * GROUP + j
            octant = octants_ref[k]
            for e, (w, m) in enumerate(edge_rows(periods)):
                for i in range(2):
                    edge_phase_ref[e, i, pl.ds(k, 1), :] = phase_ref[octant, i, w, m : m + 1, :]
        return carry

    lax.fori_loop(0, pairs // 2 // GROUP, edges_of, 0)
    copy.wait()
    for part in range(2):
        source = pl.ds(part, pairs // 2, stride=2)
        target = slice(part * (pairs // 2), (part + 1) * (pairs // 2))
        last_ref[target] = held_ref[source, azimuth_in - 1, :]
        for i in range(2):
            first_ref[i, target] = held_ref[source, i, :]


def taps(weights, rows):
    total = weights[0] * rows[0]
    for weight, row in zip(weights[1:], rows[1:]):
        total = total + weight * row
    return total


def main_kernel(peers, parents_ref, octants_ref, x_ref, table_ref, phase_ref, spread_ref, *rest):
    flat_ref, slice_ref, az_e, az_o, res_e, res_o, acc, flat, table_sem = rest
    children = octants_ref.shape[0]
    periods = phase_ref.shape[3]
    azimuth_in = periods * PERIOD_C
    own = acc.shape[0]
    me = lax.axis_index("clus")
    share = ROWS_PER_PERIOD * periods // peers
    first_tile = me * (2 * share) // 8
    table_rows = pl.ds(pl.multiple_of(first_tile * 8, 8), slice_ref.shape[1])
    table_copy = pltpu.make_async_copy(table_ref.at[:, table_rows, :], slice_ref, table_sem)
    table_copy.start()
    acc[...] = jnp.zeros_like(acc)
    sublane = lax.broadcasted_iota(jnp.int32, (periods, LANES), 0)

    def azimuth(step, h):
        for kp in range(2 * GROUP):
            start = pl.multiple_of((step * (2 * GROUP) + kp) * azimuth_in, 8)
            x = [x_ref[pl.ds(start + u, periods, stride=PERIOD_C), :] for u in range(PERIOD_C)]
            left = jnp.where(sublane == 0, 0.0, pltpu.roll(x[3], 1, 0))
            right = [jnp.where(sublane == periods - 1, 0.0, pltpu.roll(x[i], periods - 1, 0)) for i in range(2)]
            lower = [left, x[0], x[1], x[2], x[3]]
            upper = [x[1], x[2], x[3], right[0], right[1]]
            rows = [x[0], taps(TAPS_A, lower), taps(TAPS_B, lower), x[2], taps(TAPS_A, upper), taps(TAPS_B, upper)]
            for r in range(3):
                base = (kp * 3 + r) * periods
                az_e[h, base : base + periods, :] = rows[2 * r]
                az_o[h, base : base + periods, :] = rows[2 * r + 1]

    def polar(h):
        res_e[h] = dot3(az_e[h], spread_ref[0], spread_ref[1])
        res_o[h] = dot3(az_o[h], spread_ref[2], spread_ref[3])

    def shift(step, h):
        for k in range(GROUP):
            octant = octants_ref[step * GROUP + k]
            parent = parents_ref[step * GROUP + k]
            for r in range(3):
                parts = []
                for part in range(2):
                    rows = pl.ds(((2 * k + part) * 3 + r) * periods, periods)
                    middle = res_e[h, rows, LANES:] + res_o[h, rows, LANES:]
                    parts.append((res_e[h, rows, :LANES], middle, res_o[h, rows, :LANES]))
                for i in range(3):
                    w = 3 * r + i
                    real, imaginary = parts[0][i], parts[1][i]
                    cosine, sine = phase_ref[octant, 0, w], phase_ref[octant, 1, w]
                    acc[parent, 0, w] += real * cosine - imaginary * sine
                    acc[parent, 1, w] += real * sine + imaginary * cosine

    def some_groups(i, carry):
        for h in range(PAIR):
            azimuth(i * PAIR + h, h)
            polar(h)
        for h in range(PAIR):
            shift(i * PAIR + h, h)
        return carry

    lax.fori_loop(0, children // (PAIR * GROUP), some_groups, 0)
    for gp in range(2 * own):
        for w in range(ROWS_PER_PERIOD):
            flat[pl.ds(gp * ROWS_PER_PERIOD * periods + w, periods, stride=ROWS_PER_PERIOD), :] = acc[gp // 2, gp % 2, w]
        for q in range(peers):
            source = gp * ROWS_PER_PERIOD * periods + q * share
            target = (q * 2 * own + gp) * share
            flat_ref[target : target + share, :] = flat[source : source + share, :]
    table_copy.wait()


def one_hot(parents, own):
    index = lax.broadcasted_iota(jnp.int32, (own, parents.shape[1]), 0)
    return (index == parents).astype(f32)


def dot2(exact, values):
    exact = exact.astype(bf16)
    high, low = split(values)
    dot = functools.partial(jnp.dot, preferred_element_type=f32)
    return dot(exact, high) + dot(exact, low)


def fix_kernel(
    peers, own, parents_ref, before_ref, after_ref, flat_ref, edge_phase_ref, spread_ref, *rest
):
    outs, (fixed,) = rest[:peers], rest[peers:]
    pairs = before_ref.shape[0]
    children = pairs // 2
    chunk_rows = outs[0].shape[0]
    share = chunk_rows // (2 * own)
    periods = share * peers // ROWS_PER_PERIOD
    fixed[...] = flat_ref[...]
    left, right = before_ref[...], [after_ref[0], after_ref[1]]
    a, b = TAPS_A, TAPS_B
    even = jnp.concatenate([b[0] * left, a[3] * right[0] + a[4] * right[1]], axis=0)
    odd = jnp.concatenate([a[0] * left, b[3] * right[0] + b[4] * right[1]], axis=0)
    even = dot3(even, spread_ref[0], spread_ref[1])
    odd = dot3(odd, spread_ref[2], spread_ref[3])
    first, last = slice(0, pairs), slice(pairs, 2 * pairs)
    low, high = slice(0, LANES), slice(LANES, 2 * LANES)
    refined = [
        odd[first, high],
        odd[first, low],
        even[first, low],
        even[first, high],
        even[last, low],
        even[last, high] + odd[last, high],
        odd[last, low],
    ]
    shifted_rows = []
    for e, rows in enumerate(refined):
        real, imaginary = rows[:children], rows[children:]
        cosine, sine = edge_phase_ref[e, 0], edge_phase_ref[e, 1]
        shifted_rows.append(real * cosine - imaginary * sine)
        shifted_rows.append(real * sine + imaginary * cosine)
    summed = dot2(one_hot(parents_ref[...], own), jnp.concatenate(shifted_rows, axis=1))
    for e, (w, m) in enumerate(edge_rows(periods)):
        q, row = divmod(ROWS_PER_PERIOD * m + w, share)
        for part in range(2):
            rows = pl.ds(q * chunk_rows + part * share + row, own, stride=2 * share)
            column = (2 * e + part) * LANES
            fixed[rows, :] = fixed[rows, :] + summed[:, column : column + LANES]
    me = lax.axis_index("clus")
    for d in range(peers):
        start = pl.multiple_of((me ^ d) * chunk_rows, 8)
        outs[d][...] = fixed[pl.ds(start, chunk_rows), :]


def widen_kernel(source_ref, offset_ref, count_ref, table_ref, wide_ref, sources_ref, offsets_ref):
    targets, partners = source_ref.shape
    frame = table_ref.shape[1]
    slots = sources_ref.shape[0] // targets

    def some_offsets(i, carry):
        for j in range(4):
            wide_ref[pl.ds(pl.multiple_of((i * 4 + j) * frame, 8), frame), :] = table_ref[i * 4 + j].astype(f32)
        return carry

    whole_steps = table_ref.shape[0] // 4
    lax.fori_loop(0, whole_steps, some_offsets, 0)
    for offset in range(whole_steps * 4, table_ref.shape[0]):
        wide_ref[offset * frame : (offset + 1) * frame, :] = table_ref[offset].astype(f32)

    def one_target(t, carry):
        count = count_ref[t]
        for p in range(slots):
            index = min(p, partners - 1)
            source = jnp.where(p < count, source_ref[t, index], targets)
            sources_ref[t * slots + p] = source * frame
            offsets_ref[t * slots + p] = offset_ref[t, index] * frame
        return carry

    lax.fori_loop(0, targets, one_target, 0)


def translate_kernel(peers, targets, prepare, frame, sources_ref, offsets_ref, count_ref, *rest):
    table = rest[0]
    if prepare:
        chunks, real_twice, imag_twice = rest[1 : peers + 1], rest[peers + 1], rest[peers + 2]
        outs, (sum_real, sum_imag) = rest[peers + 3 : -2], rest[-2:]
    else:
        real_twice, imag_twice = rest[1:3]
        outs, (sum_real, sum_imag) = rest[3:-2], rest[-2:]
    me = lax.axis_index("clus")
    parents = count_ref.shape[0]
    slots = sources_ref.shape[0] // parents
    own = parents // peers
    share = outs[0].shape[0] // (2 * own)
    skip = lax.rem(me * (2 * share), 8)
    if prepare:
        zeros = jnp.zeros((frame, LANES), f32)
        real_twice[parents * frame :, :] = zeros
        imag_twice[parents * frame :, :] = zeros
        for d in range(peers):
            base = (me ^ d) * (own * frame) + skip
            for g in range(own):
                for part, twice in enumerate((real_twice, imag_twice)):
                    rows = chunks[d][(2 * g + part) * share : (2 * g + part + 1) * share, :]
                    twice[pl.ds(base + g * frame, share, stride=2), :] = rows
                    twice[pl.ds(base + g * frame + 1, share, stride=2), :] = rows
    for out, d in zip(outs, targets):
        first = (me ^ d) * own

        def one_target(g, carry):
            target = first + g

            def some_slots(i, sums):
                by_real, by_imag = sums
                for j in range(UNROLL):
                    slot = target * slots + i * UNROLL + j
                    source = pl.ds(pl.multiple_of(sources_ref[slot], 8), frame)
                    operator = table[pl.ds(pl.multiple_of(offsets_ref[slot], 8), frame), :]
                    by_real = by_real + operator * real_twice[source, :]
                    by_imag = by_imag + operator * imag_twice[source, :]
                return by_real, by_imag

            zero = jnp.zeros((frame, LANES), f32)
            steps = (count_ref[target] + (UNROLL - 1)) // UNROLL
            by_real, by_imag = lax.fori_loop(0, steps, some_slots, (zero, zero))
            sum_real[...] = by_real
            sum_imag[...] = by_imag
            even, odd = pl.ds(skip, share, stride=2), pl.ds(skip + 1, share, stride=2)
            row = g * (2 * share)
            out[pl.ds(row, share), :] = sum_real[even, :] - sum_imag[odd, :]
            out[pl.ds(row + share, share), :] = sum_real[odd, :] + sum_imag[even, :]
            return carry

        lax.fori_loop(0, own, one_target, 0)


def edge_kernel(peers, parents_ref, edge_phase_ref, gather_ref, *rest):
    chunks = rest[:peers]
    incoming_ref, next_ref, prev_ref, flat = rest[peers:]
    own2, _, periods, _ = incoming_ref.shape
    own = own2 // 2
    pairs = prev_ref.shape[0]
    flat_rows = ROWS_PER_PERIOD * periods
    share = flat_rows // peers
    me = lax.axis_index("clus")
    for gp in range(own2):
        for d in range(peers):
            flat[pl.ds(gp * flat_rows + (me ^ d) * share, share), :] = chunks[d][gp * share : (gp + 1) * share, :]
    edges = []
    for w, m in edge_rows(periods):
        for part in range(2):
            edges.append(flat[pl.ds(part * flat_rows + ROWS_PER_PERIOD * m + w, own, stride=2 * flat_rows), :])
    per_child = dot2(one_hot(parents_ref[...], own).T, jnp.concatenate(edges, axis=1))
    returned = []
    for e in range(len(edges) // 2):
        real = per_child[:, 2 * e * LANES : (2 * e + 1) * LANES]
        imaginary = per_child[:, (2 * e + 1) * LANES : (2 * e + 2) * LANES]
        cosine, sine = edge_phase_ref[e, 0], edge_phase_ref[e, 1]
        returned.append(
            jnp.concatenate([real * cosine + imaginary * sine, imaginary * cosine - real * sine], axis=0)
        )
    join = functools.partial(jnp.concatenate, axis=1)
    even = jnp.concatenate([join([returned[2], returned[3]]), join([returned[4], returned[5]])], axis=0)
    odd = jnp.concatenate([join([returned[1], returned[0]]), join([returned[6], returned[5]])], axis=0)
    even = dot3(even, gather_ref[0], gather_ref[1])
    odd = dot3(odd, gather_ref[2], gather_ref[3])
    a, b = TAPS_A, TAPS_B
    prev_ref[...] = a[0] * odd[:pairs] + b[0] * even[:pairs]
    next_ref[0] = a[3] * even[pairs:] + b[3] * odd[pairs:]
    next_ref[1] = a[4] * even[pairs:] + b[4] * odd[pairs:]
    for gp in range(own2):
        for w in range(ROWS_PER_PERIOD):
            incoming_ref[gp, w] = flat[pl.ds(gp * flat_rows + w, periods, stride=ROWS_PER_PERIOD), :]


def disaggregate(groups, parents_ref, octants_ref, incoming_ref, phase_ref, gather_ref, out_ref, lhs_e, lhs_o, coarse_e, coarse_o):
    periods = incoming_ref.shape[2]
    azimuth_in = periods * PERIOD_C
    sublane = lax.broadcasted_iota(jnp.int32, (periods, LANES), 0)

    def shift(step, h):
        for k in range(GROUP):
            octant = octants_ref[step * GROUP + k]
            parent = parents_ref[step * GROUP + k]
            for r in range(3):
                parts = ([], [])
                for i in range(3):
                    w = 3 * r + i
                    real, imaginary = incoming_ref[2 * parent, w], incoming_ref[2 * parent + 1, w]
                    cosine, sine = phase_ref[octant, 0, w], phase_ref[octant, 1, w]
                    parts[0].append(real * cosine + imaginary * sine)
                    parts[1].append(imaginary * cosine - real * sine)
                for part in range(2):
                    base = ((2 * k + part) * 3 + r) * periods
                    low, middle, high = parts[part]
                    lhs_e[h, base : base + periods, :LANES] = low
                    lhs_e[h, base : base + periods, LANES:] = middle
                    lhs_o[h, base : base + periods, :LANES] = high
                    lhs_o[h, base : base + periods, LANES:] = middle

    def polar(h):
        coarse_e[h] = dot3(lhs_e[h], gather_ref[0], gather_ref[1])
        coarse_o[h] = dot3(lhs_o[h], gather_ref[2], gather_ref[3])

    def azimuth(step, h):
        for kp in range(2 * GROUP):
            c = []
            for r in range(3):
                base = (kp * 3 + r) * periods
                c.append(coarse_e[h, base : base + periods, :])
                c.append(coarse_o[h, base : base + periods, :])
            a, b = TAPS_A, TAPS_B
            to_left = a[0] * c[1] + b[0] * c[2]
            to_right = [a[3] * c[4] + b[3] * c[5], a[4] * c[4] + b[4] * c[5]]
            down = [jnp.where(sublane == 0, 0.0, pltpu.roll(v, 1, 0)) for v in to_right]
            up = jnp.where(sublane == periods - 1, 0.0, pltpu.roll(to_left, periods - 1, 0))
            rows = [
                c[0] + a[1] * c[1] + b[1] * c[2] + down[0],
                a[2] * c[1] + b[2] * c[2] + a[0] * c[4] + b[0] * c[5] + down[1],
                c[3] + a[3] * c[1] + b[3] * c[2] + a[1] * c[4] + b[1] * c[5],
                a[4] * c[1] + b[4] * c[2] + a[2] * c[4] + b[2] * c[5] + up,
            ]
            start = pl.multiple_of((step * (2 * GROUP) + kp) * azimuth_in, 8)
            for u in range(PERIOD_C):
                out_ref[pl.ds(start + u, periods, stride=PERIOD_C), :] = rows[u]

    def some_groups(i, carry):
        for h in range(PAIR):
            shift(i * PAIR + h, h)
            polar(h)
        for h in range(PAIR):
            azimuth(i * PAIR + h, h)
        return carry

    lax.fori_loop(groups[0] // PAIR, groups[1] // PAIR, some_groups, 0)


def add_edges(children, pairs, azimuth_in, before_ref, after_ref, out_ref):
    for part in range(2):
        for k in range(*children, 8):
            source = slice(part * (pairs // 2) + k, part * (pairs // 2) + k + 8)
            for row, values in ((0, before_ref[0, source]), (1, before_ref[1, source]), (azimuth_in - 1, after_ref[source])):
                target = pl.ds((2 * k + part) * azimuth_in + row, 8, stride=2 * azimuth_in)
                out_ref[target, :] = out_ref[target, :] + values


def finish_kernel(groups, parents_ref, octants_ref, incoming_ref, phase_ref, gather_ref, *rest):
    part_ref, before_ref, after_ref, out_ref, whole_out, lhs_e, lhs_o, coarse_e, coarse_o, sems = rest
    pairs = after_ref.shape[0]
    azimuth_in = out_ref.shape[0] // pairs
    done = part_ref.shape[0]
    whole_out[:done, :] = part_ref[...]
    add_edges((0, groups[0] * GROUP), pairs, azimuth_in, before_ref, after_ref, whole_out)
    first = pltpu.make_async_copy(whole_out.at[pl.ds(0, done)], out_ref.at[pl.ds(0, done)], sems.at[0])
    first.start()
    disaggregate(
        groups, parents_ref, octants_ref, incoming_ref, phase_ref, gather_ref, whole_out, lhs_e, lhs_o, coarse_e, coarse_o
    )
    add_edges((groups[0] * GROUP, pairs // 2), pairs, azimuth_in, before_ref, after_ref, whole_out)
    rest_rows = pl.ds(done, out_ref.shape[0] - done)
    second = pltpu.make_async_copy(whole_out.at[rest_rows], out_ref.at[rest_rows], sems.at[1])
    second.start()
    first.wait()
    second.wait()


def shifted(values, axis, by):
    size = lax.axis_size(axis)
    return lax.ppermute(values, axis, [(i, (i + by) % size) for i in range(size)])


def exchanged(values, axis, mask):
    size = lax.axis_size(axis)
    return lax.ppermute(values, axis, [(i, i ^ mask) for i in range(size)])


ROWS_GRANT = 50
MAIN_GRANT = 46

SMEM = pl.BlockSpec(memory_space=pltpu.SMEM)
VMEM = pl.BlockSpec(memory_space=pltpu.VMEM)
HBM = pl.BlockSpec(memory_space=pltpu.HBM)


def local_call(kernel, out_shape, in_specs, scratch, grant, flops=1_000_000, bytes_accessed=1_000_000, out_specs=None):
    return pl.pallas_call(
        kernel,
        out_shape=out_shape,
        in_specs=in_specs,
        out_specs=jax.tree.map(lambda _: VMEM, out_shape) if out_specs is None else out_specs,
        scratch_shapes=scratch,
        compiler_params=pltpu.CompilerParams(vmem_limit_bytes=grant << 20),
        cost_estimate=pl.CostEstimate(flops=flops, bytes_accessed=bytes_accessed, transcendentals=0),
    )


def on_device_exchange(
    child_patterns, trans_table, child_parent, child_octant, partner_src, partner_off, partner_count
):
    children, _, azimuth_in, polar_in = child_patterns.shape
    pairs = 2 * children
    peers = lax.axis_size("clus")
    parent_total, _ = partner_src.shape
    own = parent_total // peers
    periods = azimuth_in // PERIOD_C
    flat_rows = ROWS_PER_PERIOD * periods
    share = flat_rows // peers
    offsets = trans_table.shape[0]
    array = lambda *shape: jax.ShapeDtypeStruct(shape, f32)
    buffer = lambda *shape: pltpu.VMEM(shape, f32)
    parents = child_parent[0]

    edges = len(edge_rows(periods))
    held, last, first, phases, edge_phases = local_call(
        rows_kernel,
        [
            array(pairs, azimuth_in, polar_in),
            array(pairs, polar_in),
            array(2, pairs, polar_in),
            array(8, 2, ROWS_PER_PERIOD, periods, LANES),
            array(edges, 2, children, LANES),
        ],
        [SMEM, HBM],
        [pltpu.SemaphoreType.DMA],
        ROWS_GRANT,
    )(child_octant, child_patterns.reshape(pairs, azimuth_in, polar_in))
    before = shifted(last, "dir", 1)
    after = shifted(first, "dir", -1)

    even, odd = polar_blocks()
    spread = np.stack([*split_np(even), *split_np(odd)])
    gather = np.stack([*split_np(even.T), *split_np(odd.T)])

    frame = max(-(-((q * 2 * share) % 8 + 2 * share) // 8) * 8 for q in range(peers))
    view = trans_table.reshape(offsets, 2, flat_rows, LANES).transpose(0, 2, 1, 3).reshape(offsets, 2 * flat_rows, LANES)
    rows = 2 * GROUP * 3 * periods
    flat, table = local_call(
        functools.partial(main_kernel, peers),
        [array(2 * own * flat_rows, LANES), jax.ShapeDtypeStruct((offsets, frame, LANES), bf16)],
        [SMEM] * 2 + [VMEM, HBM, VMEM, VMEM],
        [
            buffer(PAIR, rows, LANES),
            buffer(PAIR, rows, LANES),
            buffer(PAIR, rows, 2 * LANES),
            buffer(PAIR, rows, 2 * LANES),
            buffer(own, 2, ROWS_PER_PERIOD, periods, LANES),
            buffer(2 * own * flat_rows, LANES),
            pltpu.SemaphoreType.DMA,
        ],
        MAIN_GRANT,
        flops=4_000_000_000,
        bytes_accessed=12_000_000,
    )(parents, child_octant, held.reshape(pairs * azimuth_in, polar_in), view, phases, spread)

    chunk = array(2 * own * share, LANES)
    sent = local_call(
        functools.partial(fix_kernel, peers, own), [chunk] * peers, [VMEM] * 6, [buffer(2 * own * flat_rows, LANES)], 8
    )(child_parent, before, after, flat, edge_phases, spread)

    masks = sorted(range(1, peers), key=lambda d: -bin(d).count("1"))
    received = {0: sent[0]}
    for d in masks:
        received[d] = exchanged(sent[d], "clus", d)

    slots = -(-partner_src.shape[1] // UNROLL) * UNROLL
    listed = jax.ShapeDtypeStruct((parent_total * slots,), jnp.int32)
    wide, sources, slot_offsets = local_call(
        widen_kernel,
        [array(offsets * frame, LANES), listed, listed],
        [SMEM] * 3 + [VMEM],
        [],
        20,
        flops=50_000_000,
        bytes_accessed=8_000_000,
        out_specs=[VMEM, SMEM, SMEM],
    )(partner_src, partner_off, partner_count, table)

    twice = array((parent_total + 1) * frame, LANES)
    sums = [buffer(frame, LANES)] * 2
    lists = (sources, slot_offsets, partner_count)
    back = {}
    real_twice = imag_twice = None
    for targets in (masks[:1], masks[1:], [0]):
        prepare = real_twice is None
        call = local_call(
            functools.partial(translate_kernel, peers, tuple(targets), prepare, frame),
            ([twice] * 2 if prepare else []) + [chunk] * len(targets),
            [SMEM] * 3 + [VMEM] * (1 + peers if prepare else 3),
            sums,
            20,
            flops=20_000_000 * len(targets),
            bytes_accessed=4_000_000 * len(targets),
        )
        if prepare:
            real_twice, imag_twice, *results = call(*lists, wide, *[received[d] for d in range(peers)])
        else:
            results = call(*lists, wide, real_twice, imag_twice)
        for d, result in zip(targets, results):
            back[d] = exchanged(result, "clus", d) if d else result

    incoming, to_next, to_prev = local_call(
        functools.partial(edge_kernel, peers),
        [array(2 * own, ROWS_PER_PERIOD, periods, LANES), array(2, pairs, polar_in), array(pairs, polar_in)],
        [VMEM] * (3 + peers),
        [buffer(2 * own * flat_rows, LANES)],
        8,
    )(child_parent, edge_phases, gather, *[back[d] for d in range(peers)])

    from_before = shifted(to_next, "dir", 1)
    from_after = shifted(to_prev, "dir", -1)

    split_at = children // GROUP - PAIR
    work = [
        buffer(PAIR, rows, 2 * LANES),
        buffer(PAIR, rows, 2 * LANES),
        buffer(PAIR, rows, LANES),
        buffer(PAIR, rows, LANES),
    ]
    operands = (parents, child_octant, incoming, phases, gather)
    partial_out = local_call(
        functools.partial(disaggregate, (0, split_at)),
        array(split_at * 2 * GROUP * azimuth_in, polar_in),
        [SMEM] * 2 + [VMEM] * 3,
        work,
        12,
        flops=4_000_000_000,
        bytes_accessed=12_000_000,
    )(*operands)

    out = local_call(
        functools.partial(finish_kernel, (split_at, children // GROUP)),
        array(pairs * azimuth_in, polar_in),
        [SMEM] * 2 + [VMEM] * 6,
        [buffer(pairs * azimuth_in, polar_in)] + work + [pltpu.SemaphoreType.DMA((2,))],
        16,
        out_specs=HBM,
    )(*operands, partial_out, from_before, from_after)
    return out.reshape(child_patterns.shape)


def with_halo(shard, sides, width):
    for axis, dim in sides:
        size, length = (lax.axis_size(axis), shard.shape[dim])
        up = [(i, (i + 1) % size) for i in range(size)]
        down = [(j, i) for i, j in up]
        last = lax.slice_in_dim(shard, length - width, length, axis=dim)
        initial = lax.slice_in_dim(shard, 0, width, axis=dim)
        before = lax.ppermute(last, axis, up)
        after = lax.ppermute(initial, axis, down)
        shard = jnp.concatenate([before, shard, after], axis=dim)
    return shard


def lagrange_rows(offset):
    weights = []
    for anchor in range(5):
        factor = jnp.ones_like(offset)
        for neighbour in range(5):
            if neighbour != anchor:
                factor = factor * (offset - neighbour) / (anchor - neighbour)
        weights.append(factor)
    return weights


def polar_matrix_of(rows_out, rows_in):
    target = (jnp.arange(rows_out, dtype=jnp.float32) + 0.5) * rows_in / rows_out - 0.5
    start_row = jnp.clip(jnp.floor(target + 0.5).astype(jnp.int32) - 2, 0, rows_in - 5)
    weights = lagrange_rows(target - start_row.astype(jnp.float32))
    columns = jnp.arange(rows_in, dtype=jnp.int32)
    matrix = jnp.zeros((rows_out, rows_in), jnp.float32)
    for anchor in range(5):
        matrix = matrix + jnp.where(
            columns[None, :] == (start_row + anchor)[:, None], weights[anchor][:, None], 0.0
        )
    return matrix


def azimuth_matrix_of(out_index, in_index, total_out, total_in):
    target = (out_index * total_in).astype(jnp.float32) / total_out
    nearest = jnp.floor(target + 0.5).astype(jnp.int32)
    weights = lagrange_rows(target - nearest.astype(jnp.float32) + 2.0)
    matrix = jnp.zeros((out_index.shape[0], in_index.shape[0]), jnp.float32)
    for anchor in range(5):
        columns = nearest + anchor - 2
        matrix = matrix + jnp.where(
            in_index[None, :] == columns[:, None], weights[anchor][:, None], 0.0
        )
    return matrix


def shift_phases(octant, azimuth_index, azimuth_total, polar_total):
    azimuth = 2.0 * math.pi * azimuth_index.astype(jnp.float32) / azimuth_total
    polar = math.pi * (jnp.arange(polar_total, dtype=jnp.float32) + 0.5) / polar_total
    first_axis = jnp.sin(polar)[None, :] * jnp.cos(azimuth)[:, None]
    second_axis = jnp.sin(polar)[None, :] * jnp.sin(azimuth)[:, None]
    third_axis = jnp.cos(polar)[None, :] * jnp.ones_like(azimuth)[:, None]
    first_sign = (1 - 2 * (octant % 2)).astype(jnp.float32)
    second_sign = (1 - 2 * (octant // 2 % 2)).astype(jnp.float32)
    third_sign = (1 - 2 * (octant // 4)).astype(jnp.float32)
    phase_angle = phase_scale * (
        first_sign[:, None, None] * first_axis[None]
        + second_sign[:, None, None] * second_axis[None]
        + third_sign[:, None, None] * third_axis[None]
    )
    return (jnp.cos(phase_angle), jnp.sin(phase_angle))


def translate(sources, table, partner_src, partner_off, partner_count):
    live_mask = (
        jnp.arange(partner_src.shape[1], dtype=jnp.int32)[None, :] < partner_count[:, None]
    ).astype(jnp.float32)
    picked = sources[partner_src]
    operator = table[partner_off].astype(jnp.float32) * live_mask[:, :, None, None]
    real_part = jnp.sum(
        operator[:, :, 0] * picked[:, :, 0] - operator[:, :, 1] * picked[:, :, 1], axis=1
    )
    imaginary = jnp.sum(
        operator[:, :, 0] * picked[:, :, 1] + operator[:, :, 1] * picked[:, :, 0], axis=1
    )
    return jnp.stack([real_part, imaginary], axis=1)


def forward_shift(patterns, cosine, sine_part):
    real_part = patterns[:, 0] * cosine - patterns[:, 1] * sine_part
    imaginary = patterns[:, 0] * sine_part + patterns[:, 1] * cosine
    return jnp.stack([real_part, imaginary], axis=1)


def conjugate_shift(patterns, cosine, sine_part):
    real_part = patterns[:, 0] * cosine + patterns[:, 1] * sine_part
    imaginary = patterns[:, 1] * cosine - patterns[:, 0] * sine_part
    return jnp.stack([real_part, imaginary], axis=1)


def on_device_gather(
    child_patterns, trans_table, child_parent, child_octant, partner_src, partner_off, partner_count
):
    _, _, azimuth_in, _ = child_patterns.shape
    polar_out = NTHETA_P
    azimuth_out = trans_table.shape[2] // polar_out
    parent_slots = partner_src.shape[0] // lax.axis_size("clus")
    cluster_index = lax.axis_index("clus")
    direction_index = lax.axis_index("dir")
    parents = child_parent[0]
    polar_matrix = polar_matrix_of(NTHETA_P, NTHETA_C)
    onehot = (parents[None, :] == jnp.arange(parent_slots, dtype=jnp.int32)[:, None]).astype(
        jnp.float32
    )
    own_rows = jnp.mod(
        direction_index * azimuth_out + jnp.arange(azimuth_out, dtype=jnp.int32), NPHI_P
    )
    cosine, sine_part = shift_phases(child_octant, own_rows, NPHI_P, polar_out)
    extended = with_halo(child_patterns, (("dir", 2),), 2)
    gather_matrix = azimuth_matrix_of(
        jnp.arange(azimuth_out, dtype=jnp.int32),
        jnp.arange(azimuth_in + 4, dtype=jnp.int32) - 2,
        NPHI_P,
        NPHI_C,
    )
    along_azimuth = jnp.einsum("pc,kacz->kapz", gather_matrix, extended, precision=highest)
    refined = jnp.einsum("kapz,tz->kapt", along_azimuth, polar_matrix, precision=highest)
    shifted = forward_shift(refined, cosine, sine_part)
    radiation = jnp.einsum("gk,kapt->gapt", onehot, shifted, precision=highest)
    flattened = radiation.reshape(parent_slots, 2, azimuth_out * polar_out)
    sources = lax.all_gather(flattened, "clus", axis=0, tiled=True)
    first_row = cluster_index * parent_slots
    own_src = lax.dynamic_slice_in_dim(partner_src, first_row, parent_slots, 0)
    own_off = lax.dynamic_slice_in_dim(partner_off, first_row, parent_slots, 0)
    own_count = lax.dynamic_slice_in_dim(partner_count, first_row, parent_slots, 0)
    incoming = translate(sources, trans_table, own_src, own_off, own_count)
    incoming = incoming.reshape(parent_slots, 2, azimuth_out, polar_out)
    return_matrix = azimuth_matrix_of(
        jnp.arange(azimuth_out + 6, dtype=jnp.int32) - 3,
        jnp.arange(azimuth_in, dtype=jnp.int32),
        NPHI_P,
        NPHI_C,
    )
    per_child = jnp.einsum("gk,gapt->kapt", onehot, incoming, precision=highest)
    returned = conjugate_shift(per_child, cosine, sine_part)
    coarse_own = jnp.einsum("kapt,tz->kapz", returned, polar_matrix, precision=highest)
    coarse = with_halo(coarse_own, (("dir", 2),), 3)
    return jnp.einsum("pc,kapz->kacz", return_matrix, coarse, precision=highest)


def solution(mesh):
    def on_device(child_patterns, trans_table, *rest):
        peers = lax.axis_size("clus")
        children, _, azimuth_in, polar_in = child_patterns.shape
        flat_rows = trans_table.shape[2] // LANES
        fits = (
            azimuth_in % (8 * PERIOD_C) == 0
            and polar_in == LANES
            and flat_rows * PERIOD_C == ROWS_PER_PERIOD * azimuth_in
            and flat_rows % peers == 0
            and peers & (peers - 1) == 0
            and children % (PAIR * GROUP) == 0
            and children > PAIR * GROUP
        )
        plan = on_device_exchange if fits else on_device_gather
        return plan(child_patterns, trans_table, *rest)

    return jax.shard_map(
        on_device,
        mesh=mesh,
        in_specs=(
            P("clus", None, "dir", None),
            P(None, None, "dir"),
            P("clus", None),
            P("clus"),
            P(),
            P(),
            P(),
        ),
        out_specs=P("clus", None, "dir", None),
        check_vma=False,
    )
```

profile of v0, /device:TPU:0, one launch (start us, length us, event | category | flops | bytes accessed | tf_op | source)
XLA Modules:
  0.0 46.3 jit_solution(8692128045891764562)
XLA Ops:
  0.0 0.7 %copy-done.6 = s32[48]{0:T(128)S(1)} copy-done((s32[48]{0:T(128)S(1)}, s32[48]{0:T(128)}, u32[]{:S(2)}) %copy-start.6) | copy-done | bytes 216
  0.7 2.1 %shard_map.91 = (f32[96,32,128]{2,1,0:T(8,128)S(1)}, f32[96,128]{1,0:T(8,128)S(1)}, f32[2,96,128]{2,1,0:T(8,128)S(1)}, f32[8,2,9,8,128]{4,3,2,1,0:T(8,128)S(1)}, f32[7,2,48,128]{3,2,1,0:T(8,128)S(1)}) custom-call(s32[48]{0:T(128)S(1)} %copy-done.6, f32[96,32,128]{2,1,0:T(8,128)} %bitcast.13), custom_call_target="tpu_custom_call" | custom-call | flops 1000000 | bytes 1000000 | tf_op jit(solution)/shard_map/pallas_call | solution.py:552
  2.7 0.5 %collective-permute-start = (f32[96,128]{1,0:T(8,128)S(1)}, f32[96,128]{1,0:T(8,128)S(1)}, u32[]{:S(2)}, u32[]{:S(2)}) collective-permute-start(f32[96,128]{1,0:T(8,128)S(1)} %get-tuple-element.34), channel_id=1, source_target_pairs={{0,1},{1,2},{2,3},{3,4},{4,5},{5,6},{6,7},{7,0},{8,9},{9,10},{10,1... | collective-permute-start | bytes 147464 | tf_op jit(solution)/shard_map/ppermute | solution.py:507
  3.3 4.1 %collective-permute-start.1 = (f32[2,96,128]{2,1,0:T(8,128)S(1)}, f32[2,96,128]{2,1,0:T(8,128)S(1)}, u32[]{:S(2)}, u32[]{:S(2)}) collective-permute-start(f32[2,96,128]{2,1,0:T(8,128)S(1)} %get-tuple-element.35), channel_id=1, source_target_pairs={{0,7},{1,0},{2,1},{3,2},{4,3},{5,4},{6,5},{7,6},{8,15},{9,8},{10,9... | collective-permute-start | bytes 294920 | tf_op jit(solution)/shard_map/ppermute | solution.py:507
  7.4 0.9 %copy-done.1 = bf16[4,128,256]{2,1,0:T(8,128)(2,1)S(1)} copy-done((bf16[4,128,256]{2,1,0:T(8,128)(2,1)S(1)}, bf16[4,128,256]{2,1,0:T(8,128)(2,1)}, u32[]{:S(2)}) %copy-start.1) | copy-done | bytes 262168
  8.3 0.7 %copy-done.5 = s32[1,48]{1,0:T(1,128)S(1)} copy-done((s32[1,48]{1,0:T(1,128)S(1)}, s32[1,48]{1,0:T(1,128)}, u32[]{:S(2)}) %copy-start.5) | copy-done | bytes 216
  9.0 0.7 %copy-done.7 = s32[48]{0:T(128)S(1)} copy-done((s32[48]{0:T(128)S(1)}, s32[48]{0:T(128)}, u32[]{:S(2)}) %copy-start.7) | copy-done | bytes 216
  9.6 3.3 %shard_map.92 = (f32[1152,128]{1,0:T(8,128)S(1)}, bf16[316,40,128]{2,1,0:T(8,128)(2,1)S(1)}) custom-call(s32[48]{0:T(128)S(1)} %bitcast.9, s32[48]{0:T(128)S(1)} %copy-done.7, f32[3072,128]{1,0:T(8,128)S(1)} %bitcast.12, bf16[316,144,128]{2,1,0:T(8,128)(2,1)} %bitcast.14, f32[8,2,9,8,128]{4,3,2,1,0:T(8,128)S(1)} %get-tuple-element.29.phase_ref, ...), custom_call_target="tpu_custom_call" | custom-call | flops 4000000000 | bytes 12000000 | tf_op jit(solution)/shard_map/pallas_call | solution.py:575
  12.9 0.0 collective-permute-done.before_ref
  12.9 0.5 %shard_map.94 = (f32[288,128]{1,0:T(8,128)S(1)}, f32[288,128]{1,0:T(8,128)S(1)}, f32[288,128]{1,0:T(8,128)S(1)}, f32[288,128]{1,0:T(8,128)S(1)}) custom-call(s32[1,48]{1,0:T(1,128)S(1)} %copy-done.5, f32[96,128]{1,0:T(8,128)S(1)} %collective-permute-done.before_ref, f32[2,96,128]{2,1,0:T(8,128)S(1)} %collective-permute-done.1.after_ref, ...), custom_call_target="tpu_custom_call" | custom-call | flops 1000000 | bytes 1000000 | tf_op jit(solution)/shard_map/pallas_call | solution.py:594
  13.5 2.0 %collective-permute-start.2 = (f32[288,128]{1,0:T(8,128)S(1)}, f32[288,128]{1,0:T(8,128)S(1)}, u32[]{:S(2)}, u32[]{:S(2)}) collective-permute-start(f32[288,128]{1,0:T(8,128)S(1)} %get-tuple-element.38), channel_id=1, source_target_pairs={{0,8},{8,0},{16,24},{24,16},{1,9},{9,1},{17,25},{25,17},{2,10},{10... | collective-permute-start | bytes 442376 | tf_op jit(solution)/shard_map/ppermute | solution.py:512
  15.4 1.5 %collective-permute-start.3 = (f32[288,128]{1,0:T(8,128)S(1)}, f32[288,128]{1,0:T(8,128)S(1)}, u32[]{:S(2)}, u32[]{:S(2)}) collective-permute-start(f32[288,128]{1,0:T(8,128)S(1)} %get-tuple-element.39), channel_id=1, source_target_pairs={{0,16},{8,24},{16,0},{24,8},{1,17},{9,25},{17,1},{25,9},{2,18},{10... | collective-permute-start | bytes 442376 | tf_op jit(solution)/shard_map/ppermute | solution.py:512
  17.0 0.0 collective-permute-start.4
  17.0 5.6 %shard_map.93 = (f32[12640,128]{1,0:T(8,128)S(1)}, s32[1024]{0:T(1024)S(1)}, s32[1024]{0:T(1024)S(1)}) custom-call(s32[32,31]{1,0:T(8,128)S(1)} %copy-done.2, s32[32,31]{1,0:T(8,128)S(1)} %copy-done.3, s32[32]{0:T(128)S(1)} %copy-done.4, bf16[316,40,128]{2,1,0:T(8,128)(2,1)S(1)} %get-tuple-element.30.table_ref), custom_call_target="tpu_custom_call" | custom-call | flops 50000000 | bytes 8000000 | tf_op jit(solution)/shard_map/pallas_call | solution.py:605
  22.6 0.0 collective-permute-done.3.rest_3_
  22.6 0.4 collective-permute-done.4.rest_4_
  23.1 1.8 %shard_map.95 = (f32[1320,128]{1,0:T(8,128)S(1)}, f32[1320,128]{1,0:T(8,128)S(1)}, f32[288,128]{1,0:T(8,128)S(1)}) custom-call(s32[1024]{0:T(1024)S(1)} %get-tuple-element.31.sources_ref, s32[1024]{0:T(1024)S(1)} %get-tuple-element.32.offsets_ref, s32[32]{0:T(128)S(1)} %copy-done.4, f32[12640,128]{1,0:T(8,128)S(1)} %get-tuple-element.33.rest_0_, ...), custom_call_target="tpu_custom_call" | custom-call | flops 20000000 | bytes 4000000 | tf_op jit(solution)/shard_map/pallas_call | solution.py:633
  24.9 3.1 %shard_map.97 = (f32[288,128]{1,0:T(8,128)S(1)}, f32[288,128]{1,0:T(8,128)S(1)}) custom-call(s32[1024]{0:T(1024)S(1)} %get-tuple-element.31.sources_ref, s32[1024]{0:T(1024)S(1)} %get-tuple-element.32.offsets_ref, s32[32]{0:T(128)S(1)} %copy-done.4, f32[12640,128]{1,0:T(8,128)S(1)} %get-tuple-element.33.rest_0_, f32[1320,128]{1,0:T(8,128)S(1)} %get-tuple-element.41.rest_1_, ...), custom_call_target="tpu_custom_call" | custom-call | flops 40000000 | bytes 8000000 | tf_op jit(solution)/shard_map/pallas_call | solution.py:635
  28.0 1.7 %collective-permute-start.5 = (f32[288,128]{1,0:T(8,128)S(1)}, f32[288,128]{1,0:T(8,128)S(1)}, u32[]{:S(2)}, u32[]{:S(2)}) collective-permute-start(f32[288,128]{1,0:T(8,128)S(1)} %get-tuple-element.43), channel_id=1, source_target_pairs={{0,8},{8,0},{16,24},{24,16},{1,9},{9,1},{17,25},{25,17},{2,10},{10... | collective-permute-start | bytes 442376 | tf_op jit(solution)/shard_map/ppermute | solution.py:512
  29.7 1.5 %collective-permute-start.6 = (f32[288,128]{1,0:T(8,128)S(1)}, f32[288,128]{1,0:T(8,128)S(1)}, u32[]{:S(2)}, u32[]{:S(2)}) collective-permute-start(f32[288,128]{1,0:T(8,128)S(1)} %get-tuple-element.44), channel_id=1, source_target_pairs={{0,16},{8,24},{16,0},{24,8},{1,17},{9,25},{17,1},{25,9},{2,18},{10... | collective-permute-start | bytes 442376 | tf_op jit(solution)/shard_map/ppermute | solution.py:512
  31.2 0.4 collective-permute-start.7
  31.5 1.8 %shard_map.96.rest_0_ = f32[288,128]{1,0:T(8,128)S(1)} custom-call(s32[1024]{0:T(1024)S(1)} %get-tuple-element.31.sources_ref, s32[1024]{0:T(1024)S(1)} %get-tuple-element.32.offsets_ref, s32[32]{0:T(128)S(1)} %copy-done.4, f32[12640,128]{1,0:T(8,128)S(1)} %get-tuple-element.33.rest_0_, f32[1320,128]{1,0:T(8,128)S(1)} %get-tuple-element.41.rest_1_, ...), custom_call_target="tpu_custom_call" | custom-call | flops 20000000 | bytes 4000000 | tf_op jit(solution)/shard_map/pallas_call | solution.py:635
  33.3 0.3 collective-permute-done.5.rest_1_
  33.7 1.3 %collective-permute-done.6.rest_2_ = f32[288,128]{1,0:T(8,128)S(1)} collective-permute-done((f32[288,128]{1,0:T(8,128)S(1)}, f32[288,128]{1,0:T(8,128)S(1)}, u32[]{:S(2)}, u32[]{:S(2)}) %collective-permute-start.6) | collective-permute-done | bytes 147488 | tf_op jit(solution)/shard_map/ppermute | solution.py:512
  35.0 2.2 %collective-permute-done.7.rest_3_ = f32[288,128]{1,0:T(8,128)S(1)} collective-permute-done((f32[288,128]{1,0:T(8,128)S(1)}, f32[288,128]{1,0:T(8,128)S(1)}, u32[]{:S(2)}, u32[]{:S(2)}) %collective-permute-start.7) | collective-permute-done | bytes 147488 | tf_op jit(solution)/shard_map/ppermute | solution.py:512
  37.2 0.6 %shard_map.98 = (f32[16,9,8,128]{3,2,1,0:T(8,128)S(1)}, f32[2,96,128]{2,1,0:T(8,128)S(1)}, f32[96,128]{1,0:T(8,128)S(1)}) custom-call(s32[1,48]{1,0:T(1,128)S(1)} %copy-done.5, f32[7,2,48,128]{3,2,1,0:T(8,128)S(1)} %get-tuple-element.27.edge_phase_ref, bf16[4,256,128]{2,1,0:T(8,128)(2,1)S(1)} %copy-done, f32[288,128]{1,0:T(8,128)S(1)} %shard_map.96.rest_0_, ...), custom_call_target="tpu_custom_call" | custom-call | flops 1000000 | bytes 1000000 | tf_op jit(solution)/shard_map/pallas_call | solution.py:639
  37.9 0.1 collective-permute-start.9
  37.9 0.5 %collective-permute-start.8 = (f32[2,96,128]{2,1,0:T(8,128)S(1)}, f32[2,96,128]{2,1,0:T(8,128)S(1)}, u32[]{:S(2)}, u32[]{:S(2)}) collective-permute-start(f32[2,96,128]{2,1,0:T(8,128)S(1)} %get-tuple-element.47), channel_id=1, source_target_pairs={{0,1},{1,2},{2,3},{3,4},{4,5},{5,6},{6,7},{7,0},{8,9},{9,10},{10,1... | collective-permute-start | bytes 294920 | tf_op jit(solution)/shard_map/ppermute | solution.py:507
  38.4 2.3 %shard_map.99.rest_0_ = f32[2048,128]{1,0:T(8,128)S(1)} custom-call(s32[48]{0:T(128)S(1)} %bitcast.10, s32[48]{0:T(128)S(1)} %copy-done.7, f32[16,9,8,128]{3,2,1,0:T(8,128)S(1)} %get-tuple-element.46.incoming_ref, f32[8,2,9,8,128]{4,3,2,1,0:T(8,128)S(1)} %get-tuple-element.29.phase_ref, bf16[4,256,128]{2,1,0:T(8,128)(2,1)S(1)} %copy-done), custom_call_target="tpu_custom_call" | custom-call | flops 4000000000 | bytes 12000000 | tf_op jit(solution)/shard_map/pallas_call | solution.py:658
  40.8 0.0 collective-permute-done.9.rest_2_
  40.8 3.0 %collective-permute-done.8.rest_1_ = f32[2,96,128]{2,1,0:T(8,128)S(1)} collective-permute-done((f32[2,96,128]{2,1,0:T(8,128)S(1)}, f32[2,96,128]{2,1,0:T(8,128)S(1)}, u32[]{:S(2)}, u32[]{:S(2)}) %collective-permute-start.8) | collective-permute-done | bytes 98336 | tf_op jit(solution)/shard_map/ppermute | solution.py:507
  43.8 2.5 %shard_map.100 = f32[3072,128]{1,0:T(8,128)} custom-call(s32[48]{0:T(128)S(1)} %bitcast.11, s32[48]{0:T(128)S(1)} %copy-done.7, f32[16,9,8,128]{3,2,1,0:T(8,128)S(1)} %get-tuple-element.46.incoming_ref, f32[8,2,9,8,128]{4,3,2,1,0:T(8,128)S(1)} %get-tuple-element.29.phase_ref, bf16[4,256,128]{2,1,0:T(8,128)(2,1)S(1)} %copy-done, ...), custom_call_target="tpu_custom_call" | custom-call | flops 1000000 | bytes 1000000 | tf_op jit(solution)/shard_map/pallas_call | solution.py:668
  (14 shorter events, 0.0 us)
Async XLA Ops:
  0.0 0.7 %copy-start.6 = (s32[48]{0:T(128)S(1)}, s32[48]{0:T(128)}, u32[]{:S(2)}) copy-start(s32[48]{0:T(128)} %octants_ref.7) | copy-start | bytes 580
  2.7 10.2 %collective-permute-start = (f32[96,128]{1,0:T(8,128)S(1)}, f32[96,128]{1,0:T(8,128)S(1)}, u32[]{:S(2)}, u32[]{:S(2)}) collective-permute-start(f32[96,128]{1,0:T(8,128)S(1)} %get-tuple-element.34), channel_id=1, source_target_pairs={{0,1},{1,2},{2,3},{3,4},{4,5},{5,6},{6,7},{7,0},{8,9},{9,10},{10,1... | collective-permute-start | bytes 147464 | tf_op jit(solution)/shard_map/ppermute | solution.py:507
  3.3 9.6 %collective-permute-start.1 = (f32[2,96,128]{2,1,0:T(8,128)S(1)}, f32[2,96,128]{2,1,0:T(8,128)S(1)}, u32[]{:S(2)}, u32[]{:S(2)}) collective-permute-start(f32[2,96,128]{2,1,0:T(8,128)S(1)} %get-tuple-element.35), channel_id=1, source_target_pairs={{0,7},{1,0},{2,1},{3,2},{4,3},{5,4},{6,5},{7,6},{8,15},{9,8},{10,9... | collective-permute-start | bytes 294920 | tf_op jit(solution)/shard_map/ppermute | solution.py:507
  7.4 0.9 %copy-start.1 = (bf16[4,128,256]{2,1,0:T(8,128)(2,1)S(1)}, bf16[4,128,256]{2,1,0:T(8,128)(2,1)}, u32[]{:S(2)}) copy-start(bf16[4,128,256]{2,1,0:T(8,128)(2,1)} %constant.4.clone.spread_ref) | copy-start | bytes 786436
  8.3 0.7 %copy-start.5 = (s32[1,48]{1,0:T(1,128)S(1)}, s32[1,48]{1,0:T(1,128)}, u32[]{:S(2)}) copy-start(s32[1,48]{1,0:T(1,128)} %parents_ref.3) | copy-start | bytes 580
  9.0 0.7 %copy-start.7 = (s32[48]{0:T(128)S(1)}, s32[48]{0:T(128)}, u32[]{:S(2)}) copy-start(s32[48]{0:T(128)} %octants_ref.7) | copy-start | bytes 580
  9.6 7.4 %copy-start.2 = (s32[32,31]{1,0:T(8,128)S(1)}, s32[32,31]{1,0:T(8,128)}, u32[]{:S(2)}) copy-start(s32[32,31]{1,0:T(8,128)} %source_ref.1) | copy-start | bytes 11908
  9.6 7.4 %copy-start.3 = (s32[32,31]{1,0:T(8,128)S(1)}, s32[32,31]{1,0:T(8,128)}, u32[]{:S(2)}) copy-start(s32[32,31]{1,0:T(8,128)} %offset_ref.1) | copy-start | bytes 11908
  9.6 7.4 %copy-start.4 = (s32[32]{0:T(128)S(1)}, s32[32]{0:T(128)}, u32[]{:S(2)}) copy-start(s32[32]{0:T(128)} %count_ref.7) | copy-start | bytes 388
  13.5 9.2 %collective-permute-start.2 = (f32[288,128]{1,0:T(8,128)S(1)}, f32[288,128]{1,0:T(8,128)S(1)}, u32[]{:S(2)}, u32[]{:S(2)}) collective-permute-start(f32[288,128]{1,0:T(8,128)S(1)} %get-tuple-element.38), channel_id=1, source_target_pairs={{0,8},{8,0},{16,24},{24,16},{1,9},{9,1},{17,25},{25,17},{2,10},{10... | collective-permute-start | bytes 442376 | tf_op jit(solution)/shard_map/ppermute | solution.py:512
  15.4 7.2 %collective-permute-start.3 = (f32[288,128]{1,0:T(8,128)S(1)}, f32[288,128]{1,0:T(8,128)S(1)}, u32[]{:S(2)}, u32[]{:S(2)}) collective-permute-start(f32[288,128]{1,0:T(8,128)S(1)} %get-tuple-element.39), channel_id=1, source_target_pairs={{0,16},{8,24},{16,0},{24,8},{1,17},{9,25},{17,1},{25,9},{2,18},{10... | collective-permute-start | bytes 442376 | tf_op jit(solution)/shard_map/ppermute | solution.py:512
  17.0 6.1 %collective-permute-start.4 = (f32[288,128]{1,0:T(8,128)S(1)}, f32[288,128]{1,0:T(8,128)S(1)}, u32[]{:S(2)}, u32[]{:S(2)}) collective-permute-start(f32[288,128]{1,0:T(8,128)S(1)} %get-tuple-element.40), channel_id=1, source_target_pairs={{0,24},{8,16},{16,8},{24,0},{1,25},{9,17},{17,9},{25,1},{2,26},{10... | collective-permute-start | bytes 442376 | tf_op jit(solution)/shard_map/ppermute | solution.py:512
  28.0 5.7 %collective-permute-start.5 = (f32[288,128]{1,0:T(8,128)S(1)}, f32[288,128]{1,0:T(8,128)S(1)}, u32[]{:S(2)}, u32[]{:S(2)}) collective-permute-start(f32[288,128]{1,0:T(8,128)S(1)} %get-tuple-element.43), channel_id=1, source_target_pairs={{0,8},{8,0},{16,24},{24,16},{1,9},{9,1},{17,25},{25,17},{2,10},{10... | collective-permute-start | bytes 442376 | tf_op jit(solution)/shard_map/ppermute | solution.py:512
  29.7 5.4 %collective-permute-start.6 = (f32[288,128]{1,0:T(8,128)S(1)}, f32[288,128]{1,0:T(8,128)S(1)}, u32[]{:S(2)}, u32[]{:S(2)}) collective-permute-start(f32[288,128]{1,0:T(8,128)S(1)} %get-tuple-element.44), channel_id=1, source_target_pairs={{0,16},{8,24},{16,0},{24,8},{1,17},{9,25},{17,1},{25,9},{2,18},{10... | collective-permute-start | bytes 442376 | tf_op jit(solution)/shard_map/ppermute | solution.py:512
  31.2 6.0 %copy-start = (bf16[4,256,128]{2,1,0:T(8,128)(2,1)S(1)}, bf16[4,256,128]{2,1,0:T(8,128)(2,1)}, u32[]{:S(2)}) copy-start(bf16[4,256,128]{2,1,0:T(8,128)(2,1)} %constant.5.clone.gather_ref) | copy-start | bytes 786436
  31.2 6.0 %collective-permute-start.7 = (f32[288,128]{1,0:T(8,128)S(1)}, f32[288,128]{1,0:T(8,128)S(1)}, u32[]{:S(2)}, u32[]{:S(2)}) collective-permute-start(f32[288,128]{1,0:T(8,128)S(1)} %get-tuple-element.45), channel_id=1, source_target_pairs={{0,24},{8,16},{16,8},{24,0},{1,25},{9,17},{17,9},{25,1},{2,26},{10... | collective-permute-start | bytes 442376 | tf_op jit(solution)/shard_map/ppermute | solution.py:512
  37.9 2.9 %collective-permute-start.9 = (f32[96,128]{1,0:T(8,128)S(1)}, f32[96,128]{1,0:T(8,128)S(1)}, u32[]{:S(2)}, u32[]{:S(2)}) collective-permute-start(f32[96,128]{1,0:T(8,128)S(1)} %get-tuple-element.48), channel_id=1, source_target_pairs={{0,7},{1,0},{2,1},{3,2},{4,3},{5,4},{6,5},{7,6},{8,15},{9,8},{10,9... | collective-permute-start | bytes 147464 | tf_op jit(solution)/shard_map/ppermute | solution.py:507
  37.9 5.9 %collective-permute-start.8 = (f32[2,96,128]{2,1,0:T(8,128)S(1)}, f32[2,96,128]{2,1,0:T(8,128)S(1)}, u32[]{:S(2)}, u32[]{:S(2)}) collective-permute-start(f32[2,96,128]{2,1,0:T(8,128)S(1)} %get-tuple-element.47), channel_id=1, source_target_pairs={{0,1},{1,2},{2,3},{3,4},{4,5},{5,6},{6,7},{7,0},{8,9},{9,10},{10,1... | collective-permute-start | bytes 294920 | tf_op jit(solution)/shard_map/ppermute | solution.py:507
where the time goes:
time: 46.5 us; the launch traced here: 46.3 us
  Pallas kernels  23.6 us (51%)
  starting transfers between devices  12.3 us (26%)
  waiting for transfers between devices  7.33 us (16%)
  local copies, waits for them, and re-layouts  2.93 us (6%)
    ppermute x6, starting transfers between devices, exchanged(): return lax.ppermute(values, axis, [(i, i ^ mask) for i in range(size)])  7.11 us
    pallas_call x1, Pallas kernels, on_device_exchange(): local_call(widen_kernel, [array(offsets * frame, LANES), listed, listed],...  5.6 us
    ppermute x4, starting transfers between devices, shifted(): lax.ppermute(values, axis, [(i, (i + by) % size) for i in range(size)])  5.19 us
    pallas_call x2, Pallas kernels, on_device_exchange(): results = call(*lists, wide, real_twice, imag_twice)  4.89 us
    ppermute x6, waiting for transfers between devices, exchanged(): return lax.ppermute(values, axis, [(i, i ^ mask) for i in range(size)])  4.28 us
    pallas_call x1, Pallas kernels, on_device_exchange(): local_call(functools.partial(main_kernel, peers), [array(2 * own * flat_r...  3.26 us
    ppermute x4, waiting for transfers between devices, shifted(): lax.ppermute(values, axis, [(i, (i + by) % size) for i in range(size)])  3.05 us
    unnamed x16, local copies, waits for them, and re-layouts  2.93 us
  transfers between devices with their start and end apart: 10, of which 5 were waited for; matrix products, arithmetic and copies ran while one was open for 0% of the time, Pallas kernels for 28%

commit v1 on v0

--- a/solution.py
+++ b/solution.py
@@ -20,8 +20,9 @@
 PERIOD_C = 4
 ROWS_PER_PERIOD = PERIOD_P * NTHETA_P // LANES
 GROUP = 8
+TILE = 8
 UNROLL = 8
-PAIR = 2
+BLOCK = 2 * GROUP
 
 phase_scale = 8.0 * math.pi
 highest = lax.Precision.HIGHEST
@@ -42,6 +43,11 @@
 
 TAPS_A = [float(w) for w in lagrange(5.0 / 3.0)]
 TAPS_B = [float(w) for w in lagrange(7.0 / 3.0)]
+
+
+SUMS = [(TAPS_A[i] + TAPS_A[4 - i]) / 2 for i in range(2)]
+DIFFS = [(TAPS_A[i] - TAPS_A[4 - i]) / 2 for i in range(2)]
+CENTRE = TAPS_A[2]
 
 
 def polar_matrix_np():
@@ -130,11 +136,13 @@
     return [(w, 0) for w in (1, 2, 3, 4)] + [(w, periods - 1) for w in (6, 7, 8)]
 
 
-def rows_kernel(octants_ref, x_ref, held_ref, last_ref, first_ref, phase_ref, edge_phase_ref, sem):
+def rows_kernel(octants_ref, x_ref, blocks_ref, held_ref, last_ref, first_ref, phase_ref, edge_phase_ref, blocks_out, sem, blocks_sem):
     pairs, azimuth_in, _ = x_ref.shape
     periods = phase_ref.shape[3]
     copy = pltpu.make_async_copy(x_ref, held_ref, sem)
     copy.start()
+    blocks_copy = pltpu.make_async_copy(blocks_ref, blocks_out, blocks_sem)
+    blocks_copy.start()
     fill_phases(lax.axis_index("dir"), phase_ref)
 
     def edges_of(step, carry):
@@ -154,18 +162,33 @@
         last_ref[target] = held_ref[source, azimuth_in - 1, :]
         for i in range(2):
             first_ref[i, target] = held_ref[source, i, :]
-
-
-def taps(weights, rows):
-    total = weights[0] * rows[0]
-    for weight, row in zip(weights[1:], rows[1:]):
-        total = total + weight * row
-    return total
+    blocks_copy.wait()
+
+
+def both_taps(rows):
+    even = SUMS[0] * (rows[0] + rows[4]) + SUMS[1] * (rows[1] + rows[3]) + CENTRE * rows[2]
+    odd = DIFFS[0] * (rows[0] - rows[4]) + DIFFS[1] * (rows[1] - rows[3])
+    return even + odd, even - odd
+
+
+def both_taps_transposed(first, second):
+    total, difference = first + second, first - second
+    outer = [SUMS[i] * total for i in range(2)]
+    inner = [DIFFS[i] * difference for i in range(2)]
+    return [outer[0] + inner[0], outer[1] + inner[1], CENTRE * total, outer[1] - inner[1], outer[0] - inner[0]]
+
+
+def in_stages(blocks, before, product, after):
+    for i in range(blocks + 1):
+        if i < blocks:
+            before(i)
+            product(i)
+        if i > 0:
+            after(i - 1)
 
 
 def main_kernel(peers, parents_ref, octants_ref, x_ref, table_ref, phase_ref, spread_ref, *rest):
     flat_ref, slice_ref, az_e, az_o, res_e, res_o, acc, flat, table_sem = rest
-    children = octants_ref.shape[0]
     periods = phase_ref.shape[3]
     azimuth_in = periods * PERIOD_C
     own = acc.shape[0]
@@ -178,34 +201,34 @@
     acc[...] = jnp.zeros_like(acc)
     sublane = lax.broadcasted_iota(jnp.int32, (periods, LANES), 0)
 
-    def azimuth(step, h):
-        for kp in range(2 * GROUP):
-            start = pl.multiple_of((step * (2 * GROUP) + kp) * azimuth_in, 8)
+    def azimuth(block):
+        for kp in range(2 * BLOCK):
+            start = (block * (2 * BLOCK) + kp) * azimuth_in
             x = [x_ref[pl.ds(start + u, periods, stride=PERIOD_C), :] for u in range(PERIOD_C)]
             left = jnp.where(sublane == 0, 0.0, pltpu.roll(x[3], 1, 0))
             right = [jnp.where(sublane == periods - 1, 0.0, pltpu.roll(x[i], periods - 1, 0)) for i in range(2)]
             lower = [left, x[0], x[1], x[2], x[3]]
             upper = [x[1], x[2], x[3], right[0], right[1]]
-            rows = [x[0], taps(TAPS_A, lower), taps(TAPS_B, lower), x[2], taps(TAPS_A, upper), taps(TAPS_B, upper)]
+            rows = [x[0], *both_taps(lower), x[2], *both_taps(upper)]
             for r in range(3):
                 base = (kp * 3 + r) * periods
-                az_e[h, base : base + periods, :] = rows[2 * r]
-                az_o[h, base : base + periods, :] = rows[2 * r + 1]
-
-    def polar(h):
-        res_e[h] = dot3(az_e[h], spread_ref[0], spread_ref[1])
-        res_o[h] = dot3(az_o[h], spread_ref[2], spread_ref[3])
-
-    def shift(step, h):
-        for k in range(GROUP):
-            octant = octants_ref[step * GROUP + k]
-            parent = parents_ref[step * GROUP + k]
+                az_e[block, base : base + periods, :] = rows[2 * r]
+                az_o[block, base : base + periods, :] = rows[2 * r + 1]
+
+    def polar(block):
+        res_e[block] = dot3(az_e[block], spread_ref[0], spread_ref[1])
+        res_o[block] = dot3(az_o[block], spread_ref[2], spread_ref[3])
+
+    def shift(block):
+        for k in range(BLOCK):
+            octant = octants_ref[block * BLOCK + k]
+            parent = parents_ref[block * BLOCK + k]
             for r in range(3):
                 parts = []
                 for part in range(2):
                     rows = pl.ds(((2 * k + part) * 3 + r) * periods, periods)
-                    middle = res_e[h, rows, LANES:] + res_o[h, rows, LANES:]
-                    parts.append((res_e[h, rows, :LANES], middle, res_o[h, rows, :LANES]))
+                    middle = res_e[block, rows, LANES:] + res_o[block, rows, LANES:]
+                    parts.append((res_e[block, rows, :LANES], middle, res_o[block, rows, :LANES]))
                 for i in range(3):
                     w = 3 * r + i
                     real, imaginary = parts[0][i], parts[1][i]
@@ -213,15 +236,7 @@
                     acc[parent, 0, w] += real * cosine - imaginary * sine
                     acc[parent, 1, w] += real * sine + imaginary * cosine
 
-    def some_groups(i, carry):
-        for h in range(PAIR):
-            azimuth(i * PAIR + h, h)
-            polar(h)
-        for h in range(PAIR):
-            shift(i * PAIR + h, h)
-        return carry
-
-    lax.fori_loop(0, children // (PAIR * GROUP), some_groups, 0)
+    in_stages(az_e.shape[0], azimuth, polar, shift)
     for gp in range(2 * own):
         for w in range(ROWS_PER_PERIOD):
             flat[pl.ds(gp * ROWS_PER_PERIOD * periods + w, periods, stride=ROWS_PER_PERIOD), :] = acc[gp // 2, gp % 2, w]
@@ -399,7 +414,7 @@
         )
     join = functools.partial(jnp.concatenate, axis=1)
     even = jnp.concatenate([join([returned[2], returned[3]]), join([returned[4], returned[5]])], axis=0)
-    odd = jnp.concatenate([join([returned[1], returned[0]]), join([returned[6], returned[5]])], axis=0)
+    odd = jnp.concatenate([join([returned[0], returned[1]]), join([returned[5], returned[6]])], axis=0)
     even = dot3(even, gather_ref[0], gather_ref[1])
     odd = dot3(odd, gather_ref[2], gather_ref[3])
     a, b = TAPS_A, TAPS_B
@@ -411,95 +426,83 @@
             incoming_ref[gp, w] = flat[pl.ds(gp * flat_rows + w, periods, stride=ROWS_PER_PERIOD), :]
 
 
-def disaggregate(groups, parents_ref, octants_ref, incoming_ref, phase_ref, gather_ref, out_ref, lhs_e, lhs_o, coarse_e, coarse_o):
+def disaggregate_kernel(parents_ref, octants_ref, incoming_ref, phase_ref, gather_ref, out_ref, edge_ref, lhs, coarse_e, coarse_o, whole_out, sems):
     periods = incoming_ref.shape[2]
     azimuth_in = periods * PERIOD_C
     sublane = lax.broadcasted_iota(jnp.int32, (periods, LANES), 0)
-
-    def shift(step, h):
-        for k in range(GROUP):
-            octant = octants_ref[step * GROUP + k]
-            parent = parents_ref[step * GROUP + k]
+    inner = pl.ds(TILE, azimuth_in - 2 * TILE)
+    copies = []
+
+    def shift(block):
+        for k in range(BLOCK):
+            octant = octants_ref[block * BLOCK + k]
+            parent = parents_ref[block * BLOCK + k]
             for r in range(3):
-                parts = ([], [])
                 for i in range(3):
                     w = 3 * r + i
                     real, imaginary = incoming_ref[2 * parent, w], incoming_ref[2 * parent + 1, w]
                     cosine, sine = phase_ref[octant, 0, w], phase_ref[octant, 1, w]
-                    parts[0].append(real * cosine + imaginary * sine)
-                    parts[1].append(imaginary * cosine - real * sine)
-                for part in range(2):
-                    base = ((2 * k + part) * 3 + r) * periods
-                    low, middle, high = parts[part]
-                    lhs_e[h, base : base + periods, :LANES] = low
-                    lhs_e[h, base : base + periods, LANES:] = middle
-                    lhs_o[h, base : base + periods, :LANES] = high
-                    lhs_o[h, base : base + periods, LANES:] = middle
-
-    def polar(h):
-        coarse_e[h] = dot3(lhs_e[h], gather_ref[0], gather_ref[1])
-        coarse_o[h] = dot3(lhs_o[h], gather_ref[2], gather_ref[3])
-
-    def azimuth(step, h):
-        for kp in range(2 * GROUP):
+                    returned = (real * cosine + imaginary * sine, imaginary * cosine - real * sine)
+                    for part in range(2):
+                        base = ((2 * k + part) * 3 + r) * periods
+                        lhs[block, base : base + periods, i * LANES : (i + 1) * LANES] = returned[part]
+
+    def polar(block):
+        high, low = split(lhs[block])
+        dot = functools.partial(jnp.dot, preferred_element_type=f32)
+        for coarse, columns, i in ((coarse_e, slice(0, 2 * LANES), 0), (coarse_o, slice(LANES, 3 * LANES), 2)):
+            coarse[block] = (
+                dot(high[:, columns], gather_ref[i])
+                + dot(low[:, columns], gather_ref[i])
+                + dot(high[:, columns], gather_ref[i + 1])
+            )
+
+    def azimuth(block):
+        for j in range(2 * BLOCK):
             c = []
             for r in range(3):
-                base = (kp * 3 + r) * periods
-                c.append(coarse_e[h, base : base + periods, :])
-                c.append(coarse_o[h, base : base + periods, :])
-            a, b = TAPS_A, TAPS_B
-            to_left = a[0] * c[1] + b[0] * c[2]
-            to_right = [a[3] * c[4] + b[3] * c[5], a[4] * c[4] + b[4] * c[5]]
-            down = [jnp.where(sublane == 0, 0.0, pltpu.roll(v, 1, 0)) for v in to_right]
-            up = jnp.where(sublane == periods - 1, 0.0, pltpu.roll(to_left, periods - 1, 0))
-            rows = [
-                c[0] + a[1] * c[1] + b[1] * c[2] + down[0],
-                a[2] * c[1] + b[2] * c[2] + a[0] * c[4] + b[0] * c[5] + down[1],
-                c[3] + a[3] * c[1] + b[3] * c[2] + a[1] * c[4] + b[1] * c[5],
-                a[4] * c[1] + b[4] * c[2] + a[2] * c[4] + b[2] * c[5] + up,
-            ]
-            start = pl.multiple_of((step * (2 * GROUP) + kp) * azimuth_in, 8)
+                base = (j * 3 + r) * periods
+                c.append(coarse_e[block, base : base + periods, :])
+                c.append(coarse_o[block, base : base + periods, :])
+            lower = both_taps_transposed(c[1], c[2])
+            upper = both_taps_transposed(c[4], c[5])
+            down = [jnp.where(sublane == 0, 0.0, pltpu.roll(upper[i], 1, 0)) for i in (3, 4)]
+            up = jnp.where(sublane == periods - 1, 0.0, pltpu.roll(lower[0], periods - 1, 0))
+            rows = [c[0] + lower[1] + down[0], lower[2] + upper[0] + down[1], c[3] + lower[3] + upper[1], lower[4] + upper[2] + up]
+            kp = block * (2 * BLOCK) + j
             for u in range(PERIOD_C):
-                out_ref[pl.ds(start + u, periods, stride=PERIOD_C), :] = rows[u]
-
-    def some_groups(i, carry):
-        for h in range(PAIR):
-            shift(i * PAIR + h, h)
-            polar(h)
-        for h in range(PAIR):
-            azimuth(i * PAIR + h, h)
-        return carry
-
-    lax.fori_loop(groups[0] // PAIR, groups[1] // PAIR, some_groups, 0)
-
-
-def add_edges(children, pairs, azimuth_in, before_ref, after_ref, out_ref):
-    for part in range(2):
-        for k in range(*children, 8):
-            source = slice(part * (pairs // 2) + k, part * (pairs // 2) + k + 8)
-            for row, values in ((0, before_ref[0, source]), (1, before_ref[1, source]), (azimuth_in - 1, after_ref[source])):
-                target = pl.ds((2 * k + part) * azimuth_in + row, 8, stride=2 * azimuth_in)
-                out_ref[target, :] = out_ref[target, :] + values
-
-
-def finish_kernel(groups, parents_ref, octants_ref, incoming_ref, phase_ref, gather_ref, *rest):
-    part_ref, before_ref, after_ref, out_ref, whole_out, lhs_e, lhs_o, coarse_e, coarse_o, sems = rest
-    pairs = after_ref.shape[0]
-    azimuth_in = out_ref.shape[0] // pairs
-    done = part_ref.shape[0]
-    whole_out[:done, :] = part_ref[...]
-    add_edges((0, groups[0] * GROUP), pairs, azimuth_in, before_ref, after_ref, whole_out)
-    first = pltpu.make_async_copy(whole_out.at[pl.ds(0, done)], out_ref.at[pl.ds(0, done)], sems.at[0])
-    first.start()
-    disaggregate(
-        groups, parents_ref, octants_ref, incoming_ref, phase_ref, gather_ref, whole_out, lhs_e, lhs_o, coarse_e, coarse_o
-    )
-    add_edges((groups[0] * GROUP, pairs // 2), pairs, azimuth_in, before_ref, after_ref, whole_out)
-    rest_rows = pl.ds(done, out_ref.shape[0] - done)
-    second = pltpu.make_async_copy(whole_out.at[rest_rows], out_ref.at[rest_rows], sems.at[1])
-    second.start()
-    first.wait()
-    second.wait()
+                whole_out[kp, pl.ds(u, periods, stride=PERIOD_C), :] = rows[u]
+            edge_ref[0, kp] = whole_out[kp, :TILE, :]
+            edge_ref[1, kp] = whole_out[kp, azimuth_in - TILE :, :]
+        some = pl.ds(block * (2 * BLOCK), 2 * BLOCK)
+        copy = pltpu.make_async_copy(whole_out.at[some, inner, :], out_ref.at[some, inner, :], sems.at[block])
+        copy.start()
+        copies.append(copy)
+
+    in_stages(lhs.shape[0], shift, polar, azimuth)
+    for copy in copies:
+        copy.wait()
+
+
+def finish_kernel(edge_ref, before_ref, after_ref, part_ref, out_ref, tiles, sems):
+    pairs, azimuth_in, _ = out_ref.shape
+    tiles[...] = edge_ref[...]
+    flat = tiles.reshape(2 * pairs * TILE, LANES)
+    ends = ((0, 0, before_ref.at[0]), (0, 1, before_ref.at[1]), (1, TILE - 1, after_ref))
+    copies = []
+    for i, start in enumerate((0, azimuth_in - TILE)):
+        for end, row, values_ref in ends:
+            if end == i:
+                for part in range(2):
+                    for k in range(0, pairs // 2, 8):
+                        source = slice(part * (pairs // 2) + k, part * (pairs // 2) + k + 8)
+                        rows = pl.ds((i * pairs + 2 * k + part) * TILE + row, 8, stride=2 * TILE)
+                        flat[rows, :] = flat[rows, :] + values_ref[source, :]
+        copy = pltpu.make_async_copy(tiles.at[i], out_ref.at[:, pl.ds(start, TILE), :], sems.at[i])
+        copy.start()
+        copies.append(copy)
+    for copy in copies:
+        copy.wait()
 
 
 def shifted(values, axis, by):
@@ -512,21 +515,23 @@
     return lax.ppermute(values, axis, [(i, i ^ mask) for i in range(size)])
 
 
-ROWS_GRANT = 50
-MAIN_GRANT = 46
-
 SMEM = pl.BlockSpec(memory_space=pltpu.SMEM)
 VMEM = pl.BlockSpec(memory_space=pltpu.VMEM)
 HBM = pl.BlockSpec(memory_space=pltpu.HBM)
 
 
-def local_call(kernel, out_shape, in_specs, scratch, grant, flops=1_000_000, bytes_accessed=1_000_000, out_specs=None):
+def in_hbm(values):
+    return pltpu.with_memory_space_constraint(values, pltpu.HBM)
+
+
+def local_call(kernel, out_shape, in_specs, scratch, grant, flops=1_000_000, bytes_accessed=1_000_000, out_specs=None, aliases={}):
     return pl.pallas_call(
         kernel,
         out_shape=out_shape,
         in_specs=in_specs,
         out_specs=jax.tree.map(lambda _: VMEM, out_shape) if out_specs is None else out_specs,
         scratch_shapes=scratch,
+        input_output_aliases=aliases,
         compiler_params=pltpu.CompilerParams(vmem_limit_bytes=grant << 20),
         cost_estimate=pl.CostEstimate(flops=flops, bytes_accessed=bytes_accessed, transcendentals=0),
     )
@@ -546,10 +551,13 @@
     offsets = trans_table.shape[0]
     array = lambda *shape: jax.ShapeDtypeStruct(shape, f32)
     buffer = lambda *shape: pltpu.VMEM(shape, f32)
-    parents = child_parent[0]
+    parents = in_hbm(child_parent[0])
 
     edges = len(edge_rows(periods))
-    held, last, first, phases, edge_phases = local_call(
+    even, odd = polar_blocks()
+    blocks_np = np.stack([*split_np(even), *split_np(odd)])
+    octants = in_hbm(child_octant)
+    held, last, first, phases, edge_phases, spread = local_call(
         rows_kernel,
         [
             array(pairs, azimuth_in, polar_in),
@@ -557,38 +565,39 @@
             array(2, pairs, polar_in),
             array(8, 2, ROWS_PER_PERIOD, periods, LANES),
             array(edges, 2, children, LANES),
+            jax.ShapeDtypeStruct(blocks_np.shape, bf16),
         ],
-        [SMEM, HBM],
-        [pltpu.SemaphoreType.DMA],
-        ROWS_GRANT,
-    )(child_octant, child_patterns.reshape(pairs, azimuth_in, polar_in))
+        [SMEM, HBM, HBM],
+        [pltpu.SemaphoreType.DMA] * 2,
+        12,
+    )(octants, in_hbm(child_patterns.reshape(pairs, azimuth_in, polar_in)), in_hbm(jnp.asarray(blocks_np)))
     before = shifted(last, "dir", 1)
     after = shifted(first, "dir", -1)
 
-    even, odd = polar_blocks()
-    spread = np.stack([*split_np(even), *split_np(odd)])
-    gather = np.stack([*split_np(even.T), *split_np(odd.T)])
+    odd_gather = np.concatenate([odd.T[LANES:], odd.T[:LANES]])
+    gather = np.stack([*split_np(even.T), *split_np(odd_gather)])
 
     frame = max(-(-((q * 2 * share) % 8 + 2 * share) // 8) * 8 for q in range(peers))
     view = trans_table.reshape(offsets, 2, flat_rows, LANES).transpose(0, 2, 1, 3).reshape(offsets, 2 * flat_rows, LANES)
-    rows = 2 * GROUP * 3 * periods
+    blocks = children // BLOCK
+    rows = 2 * BLOCK * 3 * periods
     flat, table = local_call(
         functools.partial(main_kernel, peers),
         [array(2 * own * flat_rows, LANES), jax.ShapeDtypeStruct((offsets, frame, LANES), bf16)],
         [SMEM] * 2 + [VMEM, HBM, VMEM, VMEM],
         [
-            buffer(PAIR, rows, LANES),
-            buffer(PAIR, rows, LANES),
-            buffer(PAIR, rows, 2 * LANES),
-            buffer(PAIR, rows, 2 * LANES),
+            buffer(blocks, rows, LANES),
+            buffer(blocks, rows, LANES),
+            buffer(blocks, rows, 2 * LANES),
+            buffer(blocks, rows, 2 * LANES),
             buffer(own, 2, ROWS_PER_PERIOD, periods, LANES),
             buffer(2 * own * flat_rows, LANES),
             pltpu.SemaphoreType.DMA,
         ],
-        MAIN_GRANT,
+        24,
         flops=4_000_000_000,
         bytes_accessed=12_000_000,
-    )(parents, child_octant, held.reshape(pairs * azimuth_in, polar_in), view, phases, spread)
+    )(parents, octants, held.reshape(pairs * azimuth_in, polar_in), in_hbm(view), phases, spread)
 
     chunk = array(2 * own * share, LANES)
     sent = local_call(
@@ -647,32 +656,32 @@
     from_before = shifted(to_next, "dir", 1)
     from_after = shifted(to_prev, "dir", -1)
 
-    split_at = children // GROUP - PAIR
-    work = [
-        buffer(PAIR, rows, 2 * LANES),
-        buffer(PAIR, rows, 2 * LANES),
-        buffer(PAIR, rows, LANES),
-        buffer(PAIR, rows, LANES),
-    ]
-    operands = (parents, child_octant, incoming, phases, gather)
-    partial_out = local_call(
-        functools.partial(disaggregate, (0, split_at)),
-        array(split_at * 2 * GROUP * azimuth_in, polar_in),
+    inner, edge_tiles = local_call(
+        disaggregate_kernel,
+        [array(pairs, azimuth_in, polar_in), array(2, pairs, TILE, polar_in)],
         [SMEM] * 2 + [VMEM] * 3,
-        work,
-        12,
+        [
+            buffer(blocks, rows, 3 * LANES),
+            buffer(blocks, rows, LANES),
+            buffer(blocks, rows, LANES),
+            buffer(pairs, azimuth_in, polar_in),
+            pltpu.SemaphoreType.DMA((blocks,)),
+        ],
+        24,
         flops=4_000_000_000,
         bytes_accessed=12_000_000,
-    )(*operands)
+        out_specs=[HBM, VMEM],
+    )(parents, child_octant, incoming, phases, gather)
 
     out = local_call(
-        functools.partial(finish_kernel, (split_at, children // GROUP)),
-        array(pairs * azimuth_in, polar_in),
-        [SMEM] * 2 + [VMEM] * 6,
-        [buffer(pairs * azimuth_in, polar_in)] + work + [pltpu.SemaphoreType.DMA((2,))],
-        16,
+        finish_kernel,
+        array(pairs, azimuth_in, polar_in),
+        [VMEM] * 3 + [HBM],
+        [buffer(2, pairs, TILE, polar_in), pltpu.SemaphoreType.DMA((2,))],
+        8,
         out_specs=HBM,
-    )(*operands, partial_out, from_before, from_after)
+        aliases={3: 0},
+    )(edge_tiles, from_before, from_after, in_hbm(inner))
     return out.reshape(child_patterns.shape)
 
 
@@ -831,8 +840,7 @@
             and flat_rows * PERIOD_C == ROWS_PER_PERIOD * azimuth_in
             and flat_rows % peers == 0
             and peers & (peers - 1) == 0
-            and children % (PAIR * GROUP) == 0
-            and children > PAIR * GROUP
+            and children % BLOCK == 0
         )
         plan = on_device_exchange if fits else on_device_gather
         return plan(child_patterns, trans_table, *rest)

time: 46.5 us -> 44.1 us (0.948)
  local copies, waits for them, and re-layouts: 2.93 us -> 0.02 us
  Pallas kernels: 23.6 us -> 25.7 us
  waiting for transfers between devices: 7.33 us -> 5.79 us
    unnamed x16 -> x12, local copies, waits for them, and re-layouts: 2.93 us -> 0.02 us
    pallas_call x1, Pallas kernels: 3.26 us -> 5.07 us  [on_device_exchange(): local_call(functools.partial(main_kernel, peers), [array(2 * own * flat_r...]
    ppermute x4, waiting for transfers between devices: 3.05 us -> 1.48 us  [shifted(): lax.ppermute(values, axis, [(i, (i + by) % size) for i in range(size)])]
  transfers between devices with their start and end apart: 10 -> 10, of which waited for: 5 -> 5; matrix products, arithmetic and copies ran while one was open for 0% -> 0% of each run, Pallas kernels for 28% -> 37%
where the time goes in v1:
time: 44.1 us; the launch traced here: 43.9 us
  Pallas kernels  25.7 us (58%)
  starting transfers between devices  12.3 us (28%)
  waiting for transfers between devices  5.79 us (13%)
    ppermute x6, starting transfers between devices, exchanged(): return lax.ppermute(values, axis, [(i, i ^ mask) for i in range(size)])  7.11 us
    pallas_call x1, Pallas kernels, on_device_exchange(): local_call(widen_kernel, [array(offsets * frame, LANES), listed, listed],...  5.6 us
    ppermute x4, starting transfers between devices, shifted(): lax.ppermute(values, axis, [(i, (i + by) % size) for i in range(size)])  5.19 us
    pallas_call x1, Pallas kernels, on_device_exchange(): local_call(functools.partial(main_kernel, peers), [array(2 * own * flat_r...  5.07 us
    pallas_call x2, Pallas kernels, on_device_exchange(): results = call(*lists, wide, real_twice, imag_twice)  4.89 us
    ppermute x6, waiting for transfers between devices, exchanged(): return lax.ppermute(values, axis, [(i, i ^ mask) for i in range(size)])  4.31 us
    pallas_call x1, Pallas kernels, on_device_exchange(): local_call(disaggregate_kernel, [array(pairs, azimuth_in, polar_in), arra...  3.9 us
    pallas_call x1, Pallas kernels, on_device_exchange(): local_call(rows_kernel, [array(pairs, azimuth_in, polar_in), array(pairs,...  2.18 us
  transfers between devices with their start and end apart: 10, of which 5 were waited for; matrix products, arithmetic and copies ran while one was open for 0% of the time, Pallas kernels for 37%

profile of v1, /device:TPU:0, one launch (start us, length us, event | category | flops | bytes accessed | tf_op | source)
XLA Modules:
  0.0 43.9 jit_solution(1440452704780328174)
XLA Ops:
  0.0 2.2 %shard_map.91 = (f32[96,32,128]{2,1,0:T(8,128)S(1)}, f32[96,128]{1,0:T(8,128)S(1)}, f32[2,96,128]{2,1,0:T(8,128)S(1)}, f32[8,2,9,8,128]{4,3,2,1,0:T(8,128)S(1)},...) custom-call(s32[48]{0:T(128)} %octants_ref.5, f32[96,32,128]{2,1,0:T(8,128)} %bitcast.12, ...), custom_call_target="tpu_custom_call" | custom-call | flops 1000000 | bytes 1000000 | tf_op jit(solution)/shard_map/pallas_call | solution.py:560
  2.2 0.5 %collective-permute-start = (f32[96,128]{1,0:T(8,128)S(1)}, f32[96,128]{1,0:T(8,128)S(1)}, u32[]{:S(2)}, u32[]{:S(2)}) collective-permute-start(f32[96,128]{1,0:T(8,128)S(1)} %get-tuple-element.38), channel_id=1, source_target_pairs={{0,1},{1,2},{2,3},{3,4},{4,5},{5,6},{6,7},{7,0},{8,9},{9,10},{10,1... | collective-permute-start | bytes 147464 | tf_op jit(solution)/shard_map/ppermute | solution.py:510
  2.7 4.1 %collective-permute-start.1 = (f32[2,96,128]{2,1,0:T(8,128)S(1)}, f32[2,96,128]{2,1,0:T(8,128)S(1)}, u32[]{:S(2)}, u32[]{:S(2)}) collective-permute-start(f32[2,96,128]{2,1,0:T(8,128)S(1)} %get-tuple-element.39), channel_id=1, source_target_pairs={{0,7},{1,0},{2,1},{3,2},{4,3},{5,4},{6,5},{7,6},{8,15},{9,8},{10,9... | collective-permute-start | bytes 294920 | tf_op jit(solution)/shard_map/ppermute | solution.py:510
  6.8 5.1 %shard_map.92 = (f32[1152,128]{1,0:T(8,128)S(1)}, bf16[316,40,128]{2,1,0:T(8,128)(2,1)S(1)}) custom-call(s32[48]{0:T(128)} %bitcast.9, s32[48]{0:T(128)} %octants_ref.5, f32[3072,128]{1,0:T(8,128)S(1)} %bitcast.11, bf16[316,144,128]{2,1,0:T(8,128)(2,1)} %bitcast.13, f32[8,2,9,8,128]{4,3,2,1,0:T(8,128)S(1)} %get-tuple-element.32.phase_ref, ...), custom_call_target="tpu_custom_call" | custom-call | flops 4000000000 | bytes 12000000 | tf_op jit(solution)/shard_map/pallas_call | solution.py:584
  11.9 0.0 collective-permute-done.before_ref
  11.9 0.0 collective-permute-done.1.after_ref
  11.9 0.0 copy-done.4
  12.0 0.5 %shard_map.94 = (f32[288,128]{1,0:T(8,128)S(1)}, f32[288,128]{1,0:T(8,128)S(1)}, f32[288,128]{1,0:T(8,128)S(1)}, f32[288,128]{1,0:T(8,128)S(1)}) custom-call(s32[1,48]{1,0:T(1,128)S(1)} %copy-done.4, f32[96,128]{1,0:T(8,128)S(1)} %collective-permute-done.before_ref, f32[2,96,128]{2,1,0:T(8,128)S(1)} %collective-permute-done.1.after_ref, ...), custom_call_target="tpu_custom_call" | custom-call | flops 1000000 | bytes 1000000 | tf_op jit(solution)/shard_map/pallas_call | solution.py:603
  12.5 2.0 %collective-permute-start.2 = (f32[288,128]{1,0:T(8,128)S(1)}, f32[288,128]{1,0:T(8,128)S(1)}, u32[]{:S(2)}, u32[]{:S(2)}) collective-permute-start(f32[288,128]{1,0:T(8,128)S(1)} %get-tuple-element.42), channel_id=1, source_target_pairs={{0,8},{8,0},{16,24},{24,16},{1,9},{9,1},{17,25},{25,17},{2,10},{10... | collective-permute-start | bytes 442376 | tf_op jit(solution)/shard_map/ppermute | solution.py:515
  14.5 1.5 %collective-permute-start.3 = (f32[288,128]{1,0:T(8,128)S(1)}, f32[288,128]{1,0:T(8,128)S(1)}, u32[]{:S(2)}, u32[]{:S(2)}) collective-permute-start(f32[288,128]{1,0:T(8,128)S(1)} %get-tuple-element.43), channel_id=1, source_target_pairs={{0,16},{8,24},{16,0},{24,8},{1,17},{9,25},{17,1},{25,9},{2,18},{10... | collective-permute-start | bytes 442376 | tf_op jit(solution)/shard_map/ppermute | solution.py:515
  16.0 0.0 collective-permute-start.4
  16.1 0.0 copy-done.3
  16.1 5.6 %shard_map.93 = (f32[12640,128]{1,0:T(8,128)S(1)}, s32[1024]{0:T(1024)S(1)}, s32[1024]{0:T(1024)S(1)}) custom-call(s32[32,31]{1,0:T(8,128)S(1)} %copy-done.1, s32[32,31]{1,0:T(8,128)S(1)} %copy-done.2, s32[32]{0:T(128)S(1)} %copy-done.3, bf16[316,40,128]{2,1,0:T(8,128)(2,1)S(1)} %get-tuple-element.34.table_ref), custom_call_target="tpu_custom_call" | custom-call | flops 50000000 | bytes 8000000 | tf_op jit(solution)/shard_map/pallas_call | solution.py:614
  21.7 0.0 collective-permute-done.2.rest_2_
  21.7 0.0 collective-permute-done.3.rest_3_
  21.7 0.4 %collective-permute-done.4.rest_4_ = f32[288,128]{1,0:T(8,128)S(1)} collective-permute-done((f32[288,128]{1,0:T(8,128)S(1)}, f32[288,128]{1,0:T(8,128)S(1)}, u32[]{:S(2)}, u32[]{:S(2)}) %collective-permute-start.4) | collective-permute-done | bytes 147488 | tf_op jit(solution)/shard_map/ppermute | solution.py:515
  22.1 1.8 %shard_map.95 = (f32[1320,128]{1,0:T(8,128)S(1)}, f32[1320,128]{1,0:T(8,128)S(1)}, f32[288,128]{1,0:T(8,128)S(1)}) custom-call(s32[1024]{0:T(1024)S(1)} %get-tuple-element.35.sources_ref, s32[1024]{0:T(1024)S(1)} %get-tuple-element.36.offsets_ref, s32[32]{0:T(128)S(1)} %copy-done.3, f32[12640,128]{1,0:T(8,128)S(1)} %get-tuple-element.37.rest_0_, ...), custom_call_target="tpu_custom_call" | custom-call | flops 20000000 | bytes 4000000 | tf_op jit(solution)/shard_map/pallas_call | solution.py:642
  24.0 3.1 %shard_map.97 = (f32[288,128]{1,0:T(8,128)S(1)}, f32[288,128]{1,0:T(8,128)S(1)}) custom-call(s32[1024]{0:T(1024)S(1)} %get-tuple-element.35.sources_ref, s32[1024]{0:T(1024)S(1)} %get-tuple-element.36.offsets_ref, s32[32]{0:T(128)S(1)} %copy-done.3, f32[12640,128]{1,0:T(8,128)S(1)} %get-tuple-element.37.rest_0_, f32[1320,128]{1,0:T(8,128)S(1)} %get-tuple-element.45.rest_1_, ...), custom_call_target="tpu_custom_call" | custom-call | flops 40000000 | bytes 8000000 | tf_op jit(solution)/shard_map/pallas_call | solution.py:644
  27.0 1.7 %collective-permute-start.5 = (f32[288,128]{1,0:T(8,128)S(1)}, f32[288,128]{1,0:T(8,128)S(1)}, u32[]{:S(2)}, u32[]{:S(2)}) collective-permute-start(f32[288,128]{1,0:T(8,128)S(1)} %get-tuple-element.47), channel_id=1, source_target_pairs={{0,8},{8,0},{16,24},{24,16},{1,9},{9,1},{17,25},{25,17},{2,10},{10... | collective-permute-start | bytes 442376 | tf_op jit(solution)/shard_map/ppermute | solution.py:515
  28.7 1.5 %collective-permute-start.6 = (f32[288,128]{1,0:T(8,128)S(1)}, f32[288,128]{1,0:T(8,128)S(1)}, u32[]{:S(2)}, u32[]{:S(2)}) collective-permute-start(f32[288,128]{1,0:T(8,128)S(1)} %get-tuple-element.48), channel_id=1, source_target_pairs={{0,16},{8,24},{16,0},{24,8},{1,17},{9,25},{17,1},{25,9},{2,18},{10... | collective-permute-start | bytes 442376 | tf_op jit(solution)/shard_map/ppermute | solution.py:515
  30.2 0.4 collective-permute-start.7
  30.6 1.8 %shard_map.96.rest_0_ = f32[288,128]{1,0:T(8,128)S(1)} custom-call(s32[1024]{0:T(1024)S(1)} %get-tuple-element.35.sources_ref, s32[1024]{0:T(1024)S(1)} %get-tuple-element.36.offsets_ref, s32[32]{0:T(128)S(1)} %copy-done.3, f32[12640,128]{1,0:T(8,128)S(1)} %get-tuple-element.37.rest_0_, f32[1320,128]{1,0:T(8,128)S(1)} %get-tuple-element.45.rest_1_, ...), custom_call_target="tpu_custom_call" | custom-call | flops 20000000 | bytes 4000000 | tf_op jit(solution)/shard_map/pallas_call | solution.py:644
  32.4 0.3 collective-permute-done.5.rest_1_
  32.7 1.3 %collective-permute-done.6.rest_2_ = f32[288,128]{1,0:T(8,128)S(1)} collective-permute-done((f32[288,128]{1,0:T(8,128)S(1)}, f32[288,128]{1,0:T(8,128)S(1)}, u32[]{:S(2)}, u32[]{:S(2)}) %collective-permute-start.6) | collective-permute-done | bytes 147488 | tf_op jit(solution)/shard_map/ppermute | solution.py:515
  34.1 2.2 %collective-permute-done.7.rest_3_ = f32[288,128]{1,0:T(8,128)S(1)} collective-permute-done((f32[288,128]{1,0:T(8,128)S(1)}, f32[288,128]{1,0:T(8,128)S(1)}, u32[]{:S(2)}, u32[]{:S(2)}) %collective-permute-start.7) | collective-permute-done | bytes 147488 | tf_op jit(solution)/shard_map/ppermute | solution.py:515
  36.3 0.6 %shard_map.98 = (f32[16,9,8,128]{3,2,1,0:T(8,128)S(1)}, f32[2,96,128]{2,1,0:T(8,128)S(1)}, f32[96,128]{1,0:T(8,128)S(1)}) custom-call(s32[1,48]{1,0:T(1,128)S(1)} %copy-done.4, f32[7,2,48,128]{3,2,1,0:T(8,128)S(1)} %get-tuple-element.30.edge_phase_ref, bf16[4,256,128]{2,1,0:T(8,128)(2,1)S(1)} %copy-done, f32[288,128]{1,0:T(8,128)S(1)} %shard_map.96.rest_0_, ...), custom_call_target="tpu_custom_call" | custom-call | flops 1000000 | bytes 1000000 | tf_op jit(solution)/shard_map/pallas_call | solution.py:648
  36.9 0.1 collective-permute-start.9
  37.0 0.5 %collective-permute-start.8 = (f32[2,96,128]{2,1,0:T(8,128)S(1)}, f32[2,96,128]{2,1,0:T(8,128)S(1)}, u32[]{:S(2)}, u32[]{:S(2)}) collective-permute-start(f32[2,96,128]{2,1,0:T(8,128)S(1)} %get-tuple-element.52), channel_id=1, source_target_pairs={{0,1},{1,2},{2,3},{3,4},{4,5},{5,6},{6,7},{7,0},{8,9},{9,10},{10,1... | collective-permute-start | bytes 294920 | tf_op jit(solution)/shard_map/ppermute | solution.py:510
  37.5 3.9 %shard_map.99 = (f32[96,32,128]{2,1,0:T(8,128)}, f32[2,96,8,128]{3,2,1,0:T(8,128)S(1)}) custom-call(s32[48]{0:T(128)} %bitcast.10, s32[48]{0:T(128)S(1)} %copy-done.5, f32[16,9,8,128]{3,2,1,0:T(8,128)S(1)} %get-tuple-element.50.incoming_ref, f32[8,2,9,8,128]{4,3,2,1,0:T(8,128)S(1)} %get-tuple-element.32.phase_ref, bf16[4,256,128]{2,1,0:T(8,128)(2,1)S(1)} %copy-done), custom_call_target="tpu_custom_call" | custom-call | flops 4000000000 | bytes 12000000 | tf_op jit(solution)/shard_map/pallas_call | solution.py:659
  41.4 0.0 collective-permute-done.9.after_ref
  41.4 1.5 %collective-permute-done.8.before_ref = f32[2,96,128]{2,1,0:T(8,128)S(1)} collective-permute-done((f32[2,96,128]{2,1,0:T(8,128)S(1)}, f32[2,96,128]{2,1,0:T(8,128)S(1)}, u32[]{:S(2)}, u32[]{:S(2)}) %collective-permute-start.8) | collective-permute-done | bytes 98336 | tf_op jit(solution)/shard_map/ppermute | solution.py:510
  42.9 1.0 %shard_map.100 = f32[96,32,128]{2,1,0:T(8,128)} custom-call(f32[2,96,8,128]{3,2,1,0:T(8,128)S(1)} %get-tuple-element.51.edge_ref, f32[2,96,128]{2,1,0:T(8,128)S(1)} %collective-permute-done.8.before_ref, f32[96,128]{1,0:T(8,128)S(1)} %collective-permute-done.9.after_ref, f32[96,32,128]{2,1,0:T(8,128)} %get-tuple-element.54.part_ref), custom_call_target="tpu_custom_call", output_to_operand_aliasing={{}: (3, {})} | custom-call | flops 1000000 | bytes 1000000 | tf_op jit(solution)/shard_map/pallas_call | solution.py:676
  (10 shorter events, 0.0 us)
Async XLA Ops:
  2.2 9.7 %collective-permute-start = (f32[96,128]{1,0:T(8,128)S(1)}, f32[96,128]{1,0:T(8,128)S(1)}, u32[]{:S(2)}, u32[]{:S(2)}) collective-permute-start(f32[96,128]{1,0:T(8,128)S(1)} %get-tuple-element.38), channel_id=1, source_target_pairs={{0,1},{1,2},{2,3},{3,4},{4,5},{5,6},{6,7},{7,0},{8,9},{9,10},{10,1... | collective-permute-start | bytes 147464 | tf_op jit(solution)/shard_map/ppermute | solution.py:510
  2.7 9.2 %collective-permute-start.1 = (f32[2,96,128]{2,1,0:T(8,128)S(1)}, f32[2,96,128]{2,1,0:T(8,128)S(1)}, u32[]{:S(2)}, u32[]{:S(2)}) collective-permute-start(f32[2,96,128]{2,1,0:T(8,128)S(1)} %get-tuple-element.39), channel_id=1, source_target_pairs={{0,7},{1,0},{2,1},{3,2},{4,3},{5,4},{6,5},{7,6},{8,15},{9,8},{10,9... | collective-permute-start | bytes 294920 | tf_op jit(solution)/shard_map/ppermute | solution.py:510
  6.8 5.1 %copy-start.4 = (s32[1,48]{1,0:T(1,128)S(1)}, s32[1,48]{1,0:T(1,128)}, u32[]{:S(2)}) copy-start(s32[1,48]{1,0:T(1,128)} %parents_ref.3) | copy-start | bytes 580
  6.8 9.2 %copy-start.1 = (s32[32,31]{1,0:T(8,128)S(1)}, s32[32,31]{1,0:T(8,128)}, u32[]{:S(2)}) copy-start(s32[32,31]{1,0:T(8,128)} %source_ref.1) | copy-start | bytes 11908
  6.8 9.2 %copy-start.2 = (s32[32,31]{1,0:T(8,128)S(1)}, s32[32,31]{1,0:T(8,128)}, u32[]{:S(2)}) copy-start(s32[32,31]{1,0:T(8,128)} %offset_ref.1) | copy-start | bytes 11908
  6.8 9.2 %copy-start.3 = (s32[32]{0:T(128)S(1)}, s32[32]{0:T(128)}, u32[]{:S(2)}) copy-start(s32[32]{0:T(128)} %count_ref.7) | copy-start | bytes 388
  12.5 9.2 %collective-permute-start.2 = (f32[288,128]{1,0:T(8,128)S(1)}, f32[288,128]{1,0:T(8,128)S(1)}, u32[]{:S(2)}, u32[]{:S(2)}) collective-permute-start(f32[288,128]{1,0:T(8,128)S(1)} %get-tuple-element.42), channel_id=1, source_target_pairs={{0,8},{8,0},{16,24},{24,16},{1,9},{9,1},{17,25},{25,17},{2,10},{10... | collective-permute-start | bytes 442376 | tf_op jit(solution)/shard_map/ppermute | solution.py:515
  14.5 7.2 %collective-permute-start.3 = (f32[288,128]{1,0:T(8,128)S(1)}, f32[288,128]{1,0:T(8,128)S(1)}, u32[]{:S(2)}, u32[]{:S(2)}) collective-permute-start(f32[288,128]{1,0:T(8,128)S(1)} %get-tuple-element.43), channel_id=1, source_target_pairs={{0,16},{8,24},{16,0},{24,8},{1,17},{9,25},{17,1},{25,9},{2,18},{10... | collective-permute-start | bytes 442376 | tf_op jit(solution)/shard_map/ppermute | solution.py:515
  16.0 6.1 %collective-permute-start.4 = (f32[288,128]{1,0:T(8,128)S(1)}, f32[288,128]{1,0:T(8,128)S(1)}, u32[]{:S(2)}, u32[]{:S(2)}) collective-permute-start(f32[288,128]{1,0:T(8,128)S(1)} %get-tuple-element.44), channel_id=1, source_target_pairs={{0,24},{8,16},{16,8},{24,0},{1,25},{9,17},{17,9},{25,1},{2,26},{10... | collective-permute-start | bytes 442376 | tf_op jit(solution)/shard_map/ppermute | solution.py:515
  27.0 5.7 %collective-permute-start.5 = (f32[288,128]{1,0:T(8,128)S(1)}, f32[288,128]{1,0:T(8,128)S(1)}, u32[]{:S(2)}, u32[]{:S(2)}) collective-permute-start(f32[288,128]{1,0:T(8,128)S(1)} %get-tuple-element.47), channel_id=1, source_target_pairs={{0,8},{8,0},{16,24},{24,16},{1,9},{9,1},{17,25},{25,17},{2,10},{10... | collective-permute-start | bytes 442376 | tf_op jit(solution)/shard_map/ppermute | solution.py:515
  28.7 5.4 %collective-permute-start.6 = (f32[288,128]{1,0:T(8,128)S(1)}, f32[288,128]{1,0:T(8,128)S(1)}, u32[]{:S(2)}, u32[]{:S(2)}) collective-permute-start(f32[288,128]{1,0:T(8,128)S(1)} %get-tuple-element.48), channel_id=1, source_target_pairs={{0,16},{8,24},{16,0},{24,8},{1,17},{9,25},{17,1},{25,9},{2,18},{10... | collective-permute-start | bytes 442376 | tf_op jit(solution)/shard_map/ppermute | solution.py:515
  30.2 6.0 %copy-start = (bf16[4,256,128]{2,1,0:T(8,128)(2,1)S(1)}, bf16[4,256,128]{2,1,0:T(8,128)(2,1)}, u32[]{:S(2)}) copy-start(bf16[4,256,128]{2,1,0:T(8,128)(2,1)} %constant.5.clone.gather_ref) | copy-start | bytes 786436
  30.2 7.3 %copy-start.5 = (s32[48]{0:T(128)S(1)}, s32[48]{0:T(128)}, u32[]{:S(2)}) copy-start(s32[48]{0:T(128)} %octants_ref.5) | copy-start | bytes 580
  30.2 6.0 %collective-permute-start.7 = (f32[288,128]{1,0:T(8,128)S(1)}, f32[288,128]{1,0:T(8,128)S(1)}, u32[]{:S(2)}, u32[]{:S(2)}) collective-permute-start(f32[288,128]{1,0:T(8,128)S(1)} %get-tuple-element.49), channel_id=1, source_target_pairs={{0,24},{8,16},{16,8},{24,0},{1,25},{9,17},{17,9},{25,1},{2,26},{10... | collective-permute-start | bytes 442376 | tf_op jit(solution)/shard_map/ppermute | solution.py:515
  36.9 4.5 %collective-permute-start.9 = (f32[96,128]{1,0:T(8,128)S(1)}, f32[96,128]{1,0:T(8,128)S(1)}, u32[]{:S(2)}, u32[]{:S(2)}) collective-permute-start(f32[96,128]{1,0:T(8,128)S(1)} %get-tuple-element.53), channel_id=1, source_target_pairs={{0,7},{1,0},{2,1},{3,2},{4,3},{5,4},{6,5},{7,6},{8,15},{9,8},{10,9... | collective-permute-start | bytes 147464 | tf_op jit(solution)/shard_map/ppermute | solution.py:510
  37.0 5.9 %collective-permute-start.8 = (f32[2,96,128]{2,1,0:T(8,128)S(1)}, f32[2,96,128]{2,1,0:T(8,128)S(1)}, u32[]{:S(2)}, u32[]{:S(2)}) collective-permute-start(f32[2,96,128]{2,1,0:T(8,128)S(1)} %get-tuple-element.52), channel_id=1, source_target_pairs={{0,1},{1,2},{2,3},{3,4},{4,5},{5,6},{6,7},{7,0},{8,9},{9,10},{10,1... | collective-permute-start | bytes 294920 | tf_op jit(solution)/shard_map/ppermute | solution.py:510

commit v2 on v1

--- a/solution.py
+++ b/solution.py
@@ -21,7 +21,7 @@
 ROWS_PER_PERIOD = PERIOD_P * NTHETA_P // LANES
 GROUP = 8
 TILE = 8
-UNROLL = 8
+TOGETHER = 2
 BLOCK = 2 * GROUP
 
 phase_scale = 8.0 * math.pi
@@ -111,39 +111,50 @@
     lane = lax.broadcasted_iota(jnp.int32, (periods, LANES), 1)
     period = lax.broadcasted_iota(jnp.int32, (periods, LANES), 0)
     first = direction * (PERIOD_P * periods)
-    for w in range(ROWS_PER_PERIOD):
-        position = lane + w * LANES
-        row = w * LANES // NTHETA_P
-        row = jnp.where(position >= (row + 1) * NTHETA_P, row + 1, row)
-        polar_index = position - row * NTHETA_P
-        azimuth_index = first + period * PERIOD_P + row
-        sin_polar, cos_polar = sincos_turns((polar_index.astype(f32) + 0.5) / (2 * NTHETA_P))
-        sin_azimuth, cos_azimuth = sincos_turns(azimuth_index.astype(f32) / NPHI_P)
-        along_x = 4.0 * sin_polar * cos_azimuth
-        along_y = 4.0 * sin_polar * sin_azimuth
-        along_z = 4.0 * cos_polar
-        for octant in (0, 2, 4, 6):
-            turns = along_x + along_y if octant % 4 == 0 else along_x - along_y
-            turns = turns + along_z if octant < 4 else turns - along_z
-            sine, cosine = sincos_turns(turns)
-            out_ref[octant, 0, w] = cosine
-            out_ref[octant, 1, w] = sine
-            out_ref[7 - octant, 0, w] = cosine
-            out_ref[7 - octant, 1, w] = -sine
+
+    def two_rows(r, carry):
+        for i in range(3):
+            position = lane + i * LANES
+            second = (position >= NTHETA_P).astype(jnp.int32)
+            polar_index = position - second * NTHETA_P
+            azimuth_index = first + period * PERIOD_P + 2 * r + second
+            sin_polar, cos_polar = sincos_turns((polar_index.astype(f32) + 0.5) / (2 * NTHETA_P))
+            sin_azimuth, cos_azimuth = sincos_turns(azimuth_index.astype(f32) / NPHI_P)
+            along_x = 4.0 * sin_polar * cos_azimuth
+            along_y = 4.0 * sin_polar * sin_azimuth
+            along_z = 4.0 * cos_polar
+            w = 3 * r + i
+            for octant in (0, 2, 4, 6):
+                turns = along_x + along_y if octant % 4 == 0 else along_x - along_y
+                turns = turns + along_z if octant < 4 else turns - along_z
+                sine, cosine = sincos_turns(turns)
+                out_ref[octant, 0, w] = cosine
+                out_ref[octant, 1, w] = sine
+                out_ref[7 - octant, 0, w] = cosine
+                out_ref[7 - octant, 1, w] = -sine
+        return carry
+
+    lax.fori_loop(0, PERIOD_P // 2, two_rows, 0)
 
 
 def edge_rows(periods):
     return [(w, 0) for w in (1, 2, 3, 4)] + [(w, periods - 1) for w in (6, 7, 8)]
 
 
-def rows_kernel(octants_ref, x_ref, blocks_ref, held_ref, last_ref, first_ref, phase_ref, edge_phase_ref, blocks_out, sem, blocks_sem):
+def rows_kernel(
+    octants_hbm, x_ref, blocks_ref, held_ref, last_ref, first_ref, phase_ref, edge_phase_ref, blocks_out, octants_ref, sem, blocks_sem, octants_sem
+):
     pairs, azimuth_in, _ = x_ref.shape
     periods = phase_ref.shape[3]
     copy = pltpu.make_async_copy(x_ref, held_ref, sem)
     copy.start()
     blocks_copy = pltpu.make_async_copy(blocks_ref, blocks_out, blocks_sem)
     blocks_copy.start()
+    octants_copy = pltpu.make_async_copy(octants_hbm, octants_ref, octants_sem)
+    octants_copy.start()
     fill_phases(lax.axis_index("dir"), phase_ref)
+
+    octants_copy.wait()
 
     def edges_of(step, carry):
         for j in range(GROUP):
@@ -178,17 +189,9 @@
     return [outer[0] + inner[0], outer[1] + inner[1], CENTRE * total, outer[1] - inner[1], outer[0] - inner[0]]
 
 
-def in_stages(blocks, before, product, after):
-    for i in range(blocks + 1):
-        if i < blocks:
-            before(i)
-            product(i)
-        if i > 0:
-            after(i - 1)
-
-
 def main_kernel(peers, parents_ref, octants_ref, x_ref, table_ref, phase_ref, spread_ref, *rest):
     flat_ref, slice_ref, az_e, az_o, res_e, res_o, acc, flat, table_sem = rest
+    children = octants_ref.shape[0]
     periods = phase_ref.shape[3]
     azimuth_in = periods * PERIOD_C
     own = acc.shape[0]
@@ -203,7 +206,7 @@
 
     def azimuth(block):
         for kp in range(2 * BLOCK):
-            start = (block * (2 * BLOCK) + kp) * azimuth_in
+            start = pl.multiple_of((block * (2 * BLOCK) + kp) * azimuth_in, 8)
             x = [x_ref[pl.ds(start + u, periods, stride=PERIOD_C), :] for u in range(PERIOD_C)]
             left = jnp.where(sublane == 0, 0.0, pltpu.roll(x[3], 1, 0))
             right = [jnp.where(sublane == periods - 1, 0.0, pltpu.roll(x[i], periods - 1, 0)) for i in range(2)]
@@ -212,12 +215,12 @@
             rows = [x[0], *both_taps(lower), x[2], *both_taps(upper)]
             for r in range(3):
                 base = (kp * 3 + r) * periods
-                az_e[block, base : base + periods, :] = rows[2 * r]
-                az_o[block, base : base + periods, :] = rows[2 * r + 1]
-
-    def polar(block):
-        res_e[block] = dot3(az_e[block], spread_ref[0], spread_ref[1])
-        res_o[block] = dot3(az_o[block], spread_ref[2], spread_ref[3])
+                az_e[base : base + periods, :] = rows[2 * r]
+                az_o[base : base + periods, :] = rows[2 * r + 1]
+
+    def polar():
+        res_e[...] = dot3(az_e[...], spread_ref[0], spread_ref[1])
+        res_o[...] = dot3(az_o[...], spread_ref[2], spread_ref[3])
 
     def shift(block):
         for k in range(BLOCK):
@@ -227,8 +230,8 @@
                 parts = []
                 for part in range(2):
                     rows = pl.ds(((2 * k + part) * 3 + r) * periods, periods)
-                    middle = res_e[block, rows, LANES:] + res_o[block, rows, LANES:]
-                    parts.append((res_e[block, rows, :LANES], middle, res_o[block, rows, :LANES]))
+                    middle = res_e[rows, LANES:] + res_o[rows, LANES:]
+                    parts.append((res_e[rows, :LANES], middle, res_o[rows, :LANES]))
                 for i in range(3):
                     w = 3 * r + i
                     real, imaginary = parts[0][i], parts[1][i]
@@ -236,7 +239,13 @@
                     acc[parent, 0, w] += real * cosine - imaginary * sine
                     acc[parent, 1, w] += real * sine + imaginary * cosine
 
-    in_stages(az_e.shape[0], azimuth, polar, shift)
+    def one_block(block, carry):
+        azimuth(block)
+        polar()
+        shift(block)
+        return carry
+
+    lax.fori_loop(0, children // BLOCK, one_block, 0)
     for gp in range(2 * own):
         for w in range(ROWS_PER_PERIOD):
             flat[pl.ds(gp * ROWS_PER_PERIOD * periods + w, periods, stride=ROWS_PER_PERIOD), :] = acc[gp // 2, gp % 2, w]
@@ -305,86 +314,112 @@
         outs[d][...] = fixed[pl.ds(start, chunk_rows), :]
 
 
-def widen_kernel(source_ref, offset_ref, count_ref, table_ref, wide_ref, sources_ref, offsets_ref):
+def widen_kernel(source_ref, offset_ref, count_ref, table_ref, wide_ref, operator_ref):
     targets, partners = source_ref.shape
-    frame = table_ref.shape[1]
-    slots = sources_ref.shape[0] // targets
+    offsets, frame, _ = table_ref.shape
 
     def some_offsets(i, carry):
         for j in range(4):
             wide_ref[pl.ds(pl.multiple_of((i * 4 + j) * frame, 8), frame), :] = table_ref[i * 4 + j].astype(f32)
         return carry
 
-    whole_steps = table_ref.shape[0] // 4
+    whole_steps = offsets // 4
     lax.fori_loop(0, whole_steps, some_offsets, 0)
-    for offset in range(whole_steps * 4, table_ref.shape[0]):
+    for offset in range(whole_steps * 4, offsets):
         wide_ref[offset * frame : (offset + 1) * frame, :] = table_ref[offset].astype(f32)
-
-    def one_target(t, carry):
-        count = count_ref[t]
-        for p in range(slots):
-            index = min(p, partners - 1)
-            source = jnp.where(p < count, source_ref[t, index], targets)
-            sources_ref[t * slots + p] = source * frame
-            offsets_ref[t * slots + p] = offset_ref[t, index] * frame
+    wide_ref[offsets * frame :, :] = jnp.zeros((frame, LANES), f32)
+
+    shape = (targets, targets)
+    row, lane = (lax.broadcasted_iota(jnp.int32, shape, d) for d in range(2))
+    count = jnp.sum(jnp.where(row == lane, count_ref[...], 0), axis=1, keepdims=True)
+    operator = jnp.full(shape, offsets, jnp.int32)
+    for p in range(partners):
+        here = (lane == source_ref[:, p : p + 1]) & (p < count)
+        operator = jnp.where(here, offset_ref[:, p : p + 1], operator)
+    operator_ref[...] = operator * frame
+
+
+def doubled(chunk, real_twice, imag_twice, first, own, share, frame, skip):
+    for g in range(own):
+        for part, twice in enumerate((real_twice, imag_twice)):
+            rows = chunk[(2 * g + part) * share : (2 * g + part + 1) * share, :]
+            base = (first + g) * frame + skip
+            twice[pl.ds(base, share, stride=2), :] = rows
+            twice[pl.ds(base + 1, share, stride=2), :] = rows
+
+
+def add_sources(sums, targets, devices, own, frame, operator_ref, wide_ref, real_twice, imag_twice):
+    for number, device in enumerate(devices):
+        for g in range(own):
+            source = slice((number * own + g) * frame, (number * own + g + 1) * frame)
+            real, imaginary = real_twice[source, :], imag_twice[source, :]
+            for i, target in enumerate(targets):
+                first = pl.multiple_of(operator_ref[target, device * own + g], 8)
+                operator = wide_ref[pl.ds(first, frame), :]
+                sums[i] = (sums[i][0] + operator * real, sums[i][1] + operator * imaginary)
+    return sums
+
+
+def gather_kernel(peers, frame, masks, operator_ref, wide_ref, *rest):
+    chunks, rest = rest[: len(masks)], rest[len(masks) :]
+    before, (real_sum, imag_sum, real_twice, imag_twice) = rest[:-4], rest[-4:]
+    me = lax.axis_index("clus")
+    targets = operator_ref.shape[0]
+    own = targets // peers
+    share = chunks[0].shape[0] // (2 * own)
+    skip = lax.rem(me * (2 * share), 8)
+    for number, chunk in enumerate(chunks):
+        doubled(chunk, real_twice, imag_twice, number * own, own, share, frame, skip)
+
+    def some_targets(i, carry):
+        some = [i * TOGETHER + j for j in range(TOGETHER)]
+        places = [pl.ds(pl.multiple_of(target * frame, 8), frame) for target in some]
+        if before:
+            sums = [tuple(ref[place, :] for ref in before) for place in places]
+        else:
+            sums = [(jnp.zeros((frame, LANES), f32),) * 2 for _ in some]
+        sums = add_sources(sums, some, [me ^ d for d in masks], own, frame, operator_ref, wide_ref, real_twice, imag_twice)
+        for place, (by_real, by_imag) in zip(places, sums):
+            real_sum[place, :] = by_real
+            imag_sum[place, :] = by_imag
         return carry
 
-    lax.fori_loop(0, targets, one_target, 0)
-
-
-def translate_kernel(peers, targets, prepare, frame, sources_ref, offsets_ref, count_ref, *rest):
-    table = rest[0]
-    if prepare:
-        chunks, real_twice, imag_twice = rest[1 : peers + 1], rest[peers + 1], rest[peers + 2]
-        outs, (sum_real, sum_imag) = rest[peers + 3 : -2], rest[-2:]
+    lax.fori_loop(0, targets // TOGETHER, some_targets, 0)
+
+
+def translate_kernel(peers, frame, mask, targets, operator_ref, wide_ref, real_sum, imag_sum, *rest):
+    if len(rest) == 5 + len(targets):
+        chunk, real_twice, imag_twice = rest[:3]
+        prepare = True
     else:
-        real_twice, imag_twice = rest[1:3]
-        outs, (sum_real, sum_imag) = rest[3:-2], rest[-2:]
+        real_twice, imag_twice = rest[:2]
+        prepare = False
+    outs, (total_real, total_imag) = rest[-2 - len(targets) : -2], rest[-2:]
     me = lax.axis_index("clus")
-    parents = count_ref.shape[0]
-    slots = sources_ref.shape[0] // parents
-    own = parents // peers
+    own = operator_ref.shape[0] // peers
     share = outs[0].shape[0] // (2 * own)
     skip = lax.rem(me * (2 * share), 8)
     if prepare:
-        zeros = jnp.zeros((frame, LANES), f32)
-        real_twice[parents * frame :, :] = zeros
-        imag_twice[parents * frame :, :] = zeros
-        for d in range(peers):
-            base = (me ^ d) * (own * frame) + skip
-            for g in range(own):
-                for part, twice in enumerate((real_twice, imag_twice)):
-                    rows = chunks[d][(2 * g + part) * share : (2 * g + part + 1) * share, :]
-                    twice[pl.ds(base + g * frame, share, stride=2), :] = rows
-                    twice[pl.ds(base + g * frame + 1, share, stride=2), :] = rows
+        doubled(chunk, real_twice, imag_twice, 0, own, share, frame, skip)
+    even, odd = pl.ds(skip, share, stride=2), pl.ds(skip + 1, share, stride=2)
     for out, d in zip(outs, targets):
         first = (me ^ d) * own
 
-        def one_target(g, carry):
-            target = first + g
-
-            def some_slots(i, sums):
-                by_real, by_imag = sums
-                for j in range(UNROLL):
-                    slot = target * slots + i * UNROLL + j
-                    source = pl.ds(pl.multiple_of(sources_ref[slot], 8), frame)
-                    operator = table[pl.ds(pl.multiple_of(offsets_ref[slot], 8), frame), :]
-                    by_real = by_real + operator * real_twice[source, :]
-                    by_imag = by_imag + operator * imag_twice[source, :]
-                return by_real, by_imag
-
-            zero = jnp.zeros((frame, LANES), f32)
-            steps = (count_ref[target] + (UNROLL - 1)) // UNROLL
-            by_real, by_imag = lax.fori_loop(0, steps, some_slots, (zero, zero))
-            sum_real[...] = by_real
-            sum_imag[...] = by_imag
-            even, odd = pl.ds(skip, share, stride=2), pl.ds(skip + 1, share, stride=2)
-            row = g * (2 * share)
-            out[pl.ds(row, share), :] = sum_real[even, :] - sum_imag[odd, :]
-            out[pl.ds(row + share, share), :] = sum_real[odd, :] + sum_imag[even, :]
+        def some_targets(i, carry):
+            places = [i * TOGETHER + j for j in range(TOGETHER)]
+            some = [first + g for g in places]
+            rows = [pl.ds(pl.multiple_of(target * frame, 8), frame) for target in some]
+            sums = [(real_sum[r, :], imag_sum[r, :]) for r in rows]
+            sums = add_sources(sums, some, [me ^ mask], own, frame, operator_ref, wide_ref, real_twice, imag_twice)
+            for j, (g, (by_real, by_imag)) in enumerate(zip(places, sums)):
+                total_real[j] = by_real
+                total_imag[j] = by_imag
+                row = g * (2 * share)
+                out[pl.ds(row, share), :] = total_real[j, even, :] - total_imag[j, odd, :]
+                out[pl.ds(row + share, share), :] = total_real[j, odd, :] + total_imag[j, even, :]
             return carry
 
-        lax.fori_loop(0, own, one_target, 0)
+        lax.fori_loop(0, own // TOGETHER, some_targets, 0)
 
 
 def edge_kernel(peers, parents_ref, edge_phase_ref, gather_ref, *rest):
@@ -431,7 +466,6 @@
     azimuth_in = periods * PERIOD_C
     sublane = lax.broadcasted_iota(jnp.int32, (periods, LANES), 0)
     inner = pl.ds(TILE, azimuth_in - 2 * TILE)
-    copies = []
 
     def shift(block):
         for k in range(BLOCK):
@@ -445,13 +479,13 @@
                     returned = (real * cosine + imaginary * sine, imaginary * cosine - real * sine)
                     for part in range(2):
                         base = ((2 * k + part) * 3 + r) * periods
-                        lhs[block, base : base + periods, i * LANES : (i + 1) * LANES] = returned[part]
-
-    def polar(block):
-        high, low = split(lhs[block])
+                        lhs[base : base + periods, i * LANES : (i + 1) * LANES] = returned[part]
+
+    def polar():
+        high, low = split(lhs[...])
         dot = functools.partial(jnp.dot, preferred_element_type=f32)
         for coarse, columns, i in ((coarse_e, slice(0, 2 * LANES), 0), (coarse_o, slice(LANES, 3 * LANES), 2)):
-            coarse[block] = (
+            coarse[...] = (
                 dot(high[:, columns], gather_ref[i])
                 + dot(low[:, columns], gather_ref[i])
                 + dot(high[:, columns], gather_ref[i + 1])
@@ -462,8 +496,8 @@
             c = []
             for r in range(3):
                 base = (j * 3 + r) * periods
-                c.append(coarse_e[block, base : base + periods, :])
-                c.append(coarse_o[block, base : base + periods, :])
+                c.append(coarse_e[base : base + periods, :])
+                c.append(coarse_o[base : base + periods, :])
             lower = both_taps_transposed(c[1], c[2])
             upper = both_taps_transposed(c[4], c[5])
             down = [jnp.where(sublane == 0, 0.0, pltpu.roll(upper[i], 1, 0)) for i in (3, 4)]
@@ -474,14 +508,22 @@
                 whole_out[kp, pl.ds(u, periods, stride=PERIOD_C), :] = rows[u]
             edge_ref[0, kp] = whole_out[kp, :TILE, :]
             edge_ref[1, kp] = whole_out[kp, azimuth_in - TILE :, :]
+
+    def written(block):
         some = pl.ds(block * (2 * BLOCK), 2 * BLOCK)
-        copy = pltpu.make_async_copy(whole_out.at[some, inner, :], out_ref.at[some, inner, :], sems.at[block])
-        copy.start()
-        copies.append(copy)
-
-    in_stages(lhs.shape[0], shift, polar, azimuth)
-    for copy in copies:
-        copy.wait()
+        return pltpu.make_async_copy(whole_out.at[some, inner, :], out_ref.at[some, inner, :], sems.at[block])
+
+    def one_block(block, carry):
+        shift(block)
+        polar()
+        azimuth(block)
+        written(block).start()
+        return carry
+
+    blocks = octants_ref.shape[0] // BLOCK
+    lax.fori_loop(0, blocks, one_block, 0)
+    for block in range(blocks):
+        written(block).wait()
 
 
 def finish_kernel(edge_ref, before_ref, after_ref, part_ref, out_ref, tiles, sems):
@@ -551,12 +593,11 @@
     offsets = trans_table.shape[0]
     array = lambda *shape: jax.ShapeDtypeStruct(shape, f32)
     buffer = lambda *shape: pltpu.VMEM(shape, f32)
-    parents = in_hbm(child_parent[0])
+    parents = child_parent[0]
 
     edges = len(edge_rows(periods))
     even, odd = polar_blocks()
     blocks_np = np.stack([*split_np(even), *split_np(odd)])
-    octants = in_hbm(child_octant)
     held, last, first, phases, edge_phases, spread = local_call(
         rows_kernel,
         [
@@ -567,10 +608,10 @@
             array(edges, 2, children, LANES),
             jax.ShapeDtypeStruct(blocks_np.shape, bf16),
         ],
-        [SMEM, HBM, HBM],
-        [pltpu.SemaphoreType.DMA] * 2,
+        [HBM, HBM, HBM],
+        [pltpu.SMEM((children,), jnp.int32)] + [pltpu.SemaphoreType.DMA] * 3,
         12,
-    )(octants, in_hbm(child_patterns.reshape(pairs, azimuth_in, polar_in)), in_hbm(jnp.asarray(blocks_np)))
+    )(in_hbm(child_octant), in_hbm(child_patterns.reshape(pairs, azimuth_in, polar_in)), in_hbm(jnp.asarray(blocks_np)))
     before = shifted(last, "dir", 1)
     after = shifted(first, "dir", -1)
 
@@ -586,10 +627,10 @@
         [array(2 * own * flat_rows, LANES), jax.ShapeDtypeStruct((offsets, frame, LANES), bf16)],
         [SMEM] * 2 + [VMEM, HBM, VMEM, VMEM],
         [
-            buffer(blocks, rows, LANES),
-            buffer(blocks, rows, LANES),
-            buffer(blocks, rows, 2 * LANES),
-            buffer(blocks, rows, 2 * LANES),
+            buffer(rows, LANES),
+            buffer(rows, LANES),
+            buffer(rows, 2 * LANES),
+            buffer(rows, 2 * LANES),
             buffer(own, 2, ROWS_PER_PERIOD, periods, LANES),
             buffer(2 * own * flat_rows, LANES),
             pltpu.SemaphoreType.DMA,
@@ -597,51 +638,57 @@
         24,
         flops=4_000_000_000,
         bytes_accessed=12_000_000,
-    )(parents, octants, held.reshape(pairs * azimuth_in, polar_in), in_hbm(view), phases, spread)
+    )(parents, child_octant, held.reshape(pairs * azimuth_in, polar_in), in_hbm(view), phases, spread)
 
     chunk = array(2 * own * share, LANES)
     sent = local_call(
         functools.partial(fix_kernel, peers, own), [chunk] * peers, [VMEM] * 6, [buffer(2 * own * flat_rows, LANES)], 8
     )(child_parent, before, after, flat, edge_phases, spread)
 
-    masks = sorted(range(1, peers), key=lambda d: -bin(d).count("1"))
+    masks = sorted(range(1, peers), key=lambda d: bin(d).count("1"))
+    middle, late = masks[:-1], masks[-1]
     received = {0: sent[0]}
-    for d in masks:
+    for d in middle:
         received[d] = exchanged(sent[d], "clus", d)
-
-    slots = -(-partner_src.shape[1] // UNROLL) * UNROLL
-    listed = jax.ShapeDtypeStruct((parent_total * slots,), jnp.int32)
-    wide, sources, slot_offsets = local_call(
+    received[late] = exchanged(sent[late], "clus", late)
+
+    wide, operator = local_call(
         widen_kernel,
-        [array(offsets * frame, LANES), listed, listed],
-        [SMEM] * 3 + [VMEM],
+        [array((offsets + 1) * frame, LANES), jax.ShapeDtypeStruct((parent_total, parent_total), jnp.int32)],
+        [VMEM] * 4,
         [],
         20,
         flops=50_000_000,
         bytes_accessed=8_000_000,
-        out_specs=[VMEM, SMEM, SMEM],
-    )(partner_src, partner_off, partner_count, table)
-
-    twice = array((parent_total + 1) * frame, LANES)
-    sums = [buffer(frame, LANES)] * 2
-    lists = (sources, slot_offsets, partner_count)
+    )(partner_src, partner_off, partner_count.reshape(1, parent_total), table)
+
+    sums = []
+    for group in ([0], middle):
+        sums = local_call(
+            functools.partial(gather_kernel, peers, frame, tuple(group)),
+            [array(parent_total * frame, LANES)] * 2,
+            [SMEM] + [VMEM] * (1 + len(group) + len(sums)),
+            [buffer(len(group) * own * frame, LANES)] * 2,
+            20,
+            flops=40_000_000 * len(group),
+            bytes_accessed=4_000_000 * len(group),
+        )(operator, wide, *[received[d] for d in group], *sums)
+
     back = {}
-    real_twice = imag_twice = None
-    for targets in (masks[:1], masks[1:], [0]):
-        prepare = real_twice is None
-        call = local_call(
-            functools.partial(translate_kernel, peers, tuple(targets), prepare, frame),
-            ([twice] * 2 if prepare else []) + [chunk] * len(targets),
-            [SMEM] * 3 + [VMEM] * (1 + peers if prepare else 3),
-            sums,
+    last_sources = [received[late]]
+    for targets in ([late], middle, [0]):
+        prepare = len(last_sources) == 1
+        results = local_call(
+            functools.partial(translate_kernel, peers, frame, late, tuple(targets)),
+            ([array(own * frame, LANES)] * 2 if prepare else []) + [chunk] * len(targets),
+            [SMEM] + [VMEM] * (3 + len(last_sources)),
+            [buffer(TOGETHER, frame, LANES)] * 2,
             20,
-            flops=20_000_000 * len(targets),
-            bytes_accessed=4_000_000 * len(targets),
-        )
+            flops=10_000_000 * len(targets),
+            bytes_accessed=2_000_000 * len(targets),
+        )(operator, wide, *sums, *last_sources)
         if prepare:
-            real_twice, imag_twice, *results = call(*lists, wide, *[received[d] for d in range(peers)])
-        else:
-            results = call(*lists, wide, real_twice, imag_twice)
+            last_sources, results = results[:2], results[2:]
         for d, result in zip(targets, results):
             back[d] = exchanged(result, "clus", d) if d else result
 
@@ -661,9 +708,9 @@
         [array(pairs, azimuth_in, polar_in), array(2, pairs, TILE, polar_in)],
         [SMEM] * 2 + [VMEM] * 3,
         [
-            buffer(blocks, rows, 3 * LANES),
-            buffer(blocks, rows, LANES),
-            buffer(blocks, rows, LANES),
+            buffer(rows, 3 * LANES),
+            buffer(rows, LANES),
+            buffer(rows, LANES),
             buffer(pairs, azimuth_in, polar_in),
             pltpu.SemaphoreType.DMA((blocks,)),
         ],
@@ -840,6 +887,7 @@
             and flat_rows * PERIOD_C == ROWS_PER_PERIOD * azimuth_in
             and flat_rows % peers == 0
             and peers & (peers - 1) == 0
+            and peers > 2
             and children % BLOCK == 0
         )
         plan = on_device_exchange if fits else on_device_gather

time: 44.1 us -> 45.8 us (1.039)
  Pallas kernels: 25.7 us -> 20.3 us
  starting transfers between devices: 12.3 us -> 16.1 us
  waiting for transfers between devices: 5.79 us -> 9.09 us
    ppermute x4, starting transfers between devices: 5.19 us -> 8.97 us  [shifted(): lax.ppermute(values, axis, [(i, (i + by) % size) for i in range(size)])]
    ppermute x6, waiting for transfers between devices: 4.31 us -> 7.18 us  [exchanged(): return lax.ppermute(values, axis, [(i, i ^ mask) for i in range(size)])]
    pallas_call x4 -> x6, Pallas kernels: 12.3 us -> 9.58 us  [the longest x2 4.9 us: on_device_exchange(): local_call(functools.partial(gather_kernel, peers, frame, tuple(group)),...]
    pallas_call x1, Pallas kernels: 5.07 us -> 3.09 us  [on_device_exchange(): local_call(functools.partial(main_kernel, peers), [array(2 * own * flat_r...]
    pallas_call x1, Pallas kernels: 2.18 us -> 1.56 us  [on_device_exchange(): local_call(rows_kernel, [array(pairs, azimuth_in, polar_in), array(pairs,...]
  transfers between devices with their start and end apart: 10 -> 10, of which waited for: 5 -> 5; matrix products, arithmetic and copies ran while one was open for 0% -> 0% of each run, Pallas kernels for 37% -> 31%
where the time goes in v2:
time: 45.8 us; the launch traced here: 45.6 us
  Pallas kernels  20.3 us (44%)
  starting transfers between devices  16.1 us (35%)
  waiting for transfers between devices  9.09 us (20%)
    ppermute x4, starting transfers between devices, shifted(): lax.ppermute(values, axis, [(i, (i + by) % size) for i in range(size)])  8.97 us
    ppermute x6, waiting for transfers between devices, exchanged(): return lax.ppermute(values, axis, [(i, i ^ mask) for i in range(size)])  7.18 us
    ppermute x6, starting transfers between devices, exchanged(): return lax.ppermute(values, axis, [(i, i ^ mask) for i in range(size)])  7.1 us
    pallas_call x2, Pallas kernels, on_device_exchange(): local_call(functools.partial(gather_kernel, peers, frame, tuple(group)),...  4.9 us
    pallas_call x1, Pallas kernels, on_device_exchange(): local_call(disaggregate_kernel, [array(pairs, azimuth_in, polar_in), arra...  3.91 us
    pallas_call x3, Pallas kernels, on_device_exchange(): local_call(functools.partial(translate_kernel, peers, frame, late, tuple(...  3.61 us
    pallas_call x1, Pallas kernels, on_device_exchange(): local_call(functools.partial(main_kernel, peers), [array(2 * own * flat_r...  3.09 us
    ppermute x4, waiting for transfers between devices, shifted(): lax.ppermute(values, axis, [(i, (i + by) % size) for i in range(size)])  1.91 us
  transfers between devices with their start and end apart: 10, of which 5 were waited for; matrix products, arithmetic and copies ran while one was open for 0% of the time, Pallas kernels for 31%

profile of v2, /device:TPU:0, one launch (start us, length us, event | category | flops | bytes accessed | tf_op | source)
XLA Modules:
  0.0 45.6 jit_solution(6851683785494286997)
XLA Ops:
  0.0 1.6 %shard_map.91 = (f32[96,32,128]{2,1,0:T(8,128)S(1)}, f32[96,128]{1,0:T(8,128)S(1)}, f32[2,96,128]{2,1,0:T(8,128)S(1)}, f32[8,2,9,8,128]{4,3,2,1,0:T(8,128)S(1)},...) custom-call(s32[48]{0:T(128)} %octants_ref.3, f32[96,32,128]{2,1,0:T(8,128)} %bitcast.14, ...), custom_call_target="tpu_custom_call" | custom-call | flops 1000000 | bytes 1000000 | tf_op jit(solution)/shard_map/pallas_call | solution.py:601
  1.6 0.5 %collective-permute-start = (f32[96,128]{1,0:T(8,128)S(1)}, f32[96,128]{1,0:T(8,128)S(1)}, u32[]{:S(2)}, u32[]{:S(2)}) collective-permute-start(f32[96,128]{1,0:T(8,128)S(1)} %get-tuple-element.40), channel_id=1, source_target_pairs={{0,1},{1,2},{2,3},{3,4},{4,5},{5,6},{6,7},{7,0},{8,9},{9,10},{10,1... | collective-permute-start | bytes 147464 | tf_op jit(solution)/shard_map/ppermute | solution.py:552
  2.1 4.1 %collective-permute-start.1 = (f32[2,96,128]{2,1,0:T(8,128)S(1)}, f32[2,96,128]{2,1,0:T(8,128)S(1)}, u32[]{:S(2)}, u32[]{:S(2)}) collective-permute-start(f32[2,96,128]{2,1,0:T(8,128)S(1)} %get-tuple-element.41), channel_id=1, source_target_pairs={{0,7},{1,0},{2,1},{3,2},{4,3},{5,4},{6,5},{7,6},{8,15},{9,8},{10,9... | collective-permute-start | bytes 294920 | tf_op jit(solution)/shard_map/ppermute | solution.py:552
  6.2 0.0 copy-start.4
  6.2 3.1 %shard_map.92 = (f32[1152,128]{1,0:T(8,128)S(1)}, bf16[316,40,128]{2,1,0:T(8,128)(2,1)S(1)}) custom-call(s32[48]{0:T(128)S(1)} %bitcast.10, s32[48]{0:T(128)S(1)} %copy-done.5, f32[3072,128]{1,0:T(8,128)S(1)} %bitcast.13, bf16[316,144,128]{2,1,0:T(8,128)(2,1)} %bitcast.15, f32[8,2,9,8,128]{4,3,2,1,0:T(8,128)S(1)} %get-tuple-element.35.phase_ref, ...), custom_call_target="tpu_custom_call" | custom-call | flops 4000000000 | bytes 12000000 | tf_op jit(solution)/shard_map/pallas_call | solution.py:625
  9.3 0.0 collective-permute-done.before_ref
  9.3 0.0 collective-permute-done.1.after_ref
  9.4 0.5 %shard_map.94 = (f32[288,128]{1,0:T(8,128)S(1)}, f32[288,128]{1,0:T(8,128)S(1)}, f32[288,128]{1,0:T(8,128)S(1)}, f32[288,128]{1,0:T(8,128)S(1)}) custom-call(s32[1,48]{1,0:T(1,128)S(1)} %copy-done.3, f32[96,128]{1,0:T(8,128)S(1)} %collective-permute-done.before_ref, f32[2,96,128]{2,1,0:T(8,128)S(1)} %collective-permute-done.1.after_ref, ...), custom_call_target="tpu_custom_call" | custom-call | flops 1000000 | bytes 1000000 | tf_op jit(solution)/shard_map/pallas_call | solution.py:644
  9.9 2.0 %collective-permute-start.2 = (f32[288,128]{1,0:T(8,128)S(1)}, f32[288,128]{1,0:T(8,128)S(1)}, u32[]{:S(2)}, u32[]{:S(2)}) collective-permute-start(f32[288,128]{1,0:T(8,128)S(1)} %get-tuple-element.43), channel_id=1, source_target_pairs={{0,8},{8,0},{16,24},{24,16},{1,9},{9,1},{17,25},{25,17},{2,10},{10... | collective-permute-start | bytes 442376 | tf_op jit(solution)/shard_map/ppermute | solution.py:557
  11.9 1.5 %collective-permute-start.3 = (f32[288,128]{1,0:T(8,128)S(1)}, f32[288,128]{1,0:T(8,128)S(1)}, u32[]{:S(2)}, u32[]{:S(2)}) collective-permute-start(f32[288,128]{1,0:T(8,128)S(1)} %get-tuple-element.44), channel_id=1, source_target_pairs={{0,16},{8,24},{16,0},{24,8},{1,17},{9,25},{17,1},{25,9},{2,18},{10... | collective-permute-start | bytes 442376 | tf_op jit(solution)/shard_map/ppermute | solution.py:557
  13.4 0.0 collective-permute-start.4
  13.5 1.1 %shard_map.93 = (f32[12680,128]{1,0:T(8,128)S(1)}, s32[32,32]{1,0:T(8,128)S(1)}) custom-call(s32[32,31]{1,0:T(8,128)S(1)} %copy-done.1, s32[32,31]{1,0:T(8,128)S(1)} %copy-done.2, s32[1,32]{1,0:T(1,128)S(1)} %bitcast.12, bf16[316,40,128]{2,1,0:T(8,128)(2,1)S(1)} %get-tuple-element.37.table_ref), custom_call_target="tpu_custom_call" | custom-call | flops 50000000 | bytes 8000000 | tf_op jit(solution)/shard_map/pallas_call | solution.py:655
  14.5 1.8 %shard_map.95 = (f32[1280,128]{1,0:T(8,128)S(1)}, f32[1280,128]{1,0:T(8,128)S(1)}) custom-call(s32[32,32]{1,0:T(8,128)S(1)} %get-tuple-element.38.operator_ref, f32[12680,128]{1,0:T(8,128)S(1)} %get-tuple-element.39.wide_ref, f32[288,128]{1,0:T(8,128)S(1)} %get-tuple-element.45.rest_0_), custom_call_target="tpu_custom_call" | custom-call | flops 40000000 | bytes 4000000 | tf_op jit(solution)/shard_map/pallas_call | solution.py:667
  16.4 0.0 collective-permute-done.2.rest_0_
  16.4 3.8 %collective-permute-done.3.rest_1_ = f32[288,128]{1,0:T(8,128)S(1)} collective-permute-done((f32[288,128]{1,0:T(8,128)S(1)}, f32[288,128]{1,0:T(8,128)S(1)}, u32[]{:S(2)}, u32[]{:S(2)}) %collective-permute-start.3) | collective-permute-done | bytes 147488 | tf_op jit(solution)/shard_map/ppermute | solution.py:557
  20.2 3.1 %shard_map.96 = (f32[1280,128]{1,0:T(8,128)S(1)}, f32[1280,128]{1,0:T(8,128)S(1)}) custom-call(s32[32,32]{1,0:T(8,128)S(1)} %get-tuple-element.38.operator_ref, f32[12680,128]{1,0:T(8,128)S(1)} %get-tuple-element.39.wide_ref, f32[288,128]{1,0:T(8,128)S(1)} %collective-permute-done.2.rest_0_, f32[288,128]{1,0:T(8,128)S(1)} %collective-permute-done.3.rest_1_, ...), custom_call_target="tpu_custom_call" | custom-call | flops 80000000 | bytes 8000000 | tf_op jit(solution)/shard_map/pallas_call | solution.py:667
  23.3 0.0 collective-permute-done.4.rest_0_
  23.3 1.1 %shard_map.97 = (f32[320,128]{1,0:T(8,128)S(1)}, f32[320,128]{1,0:T(8,128)S(1)}, f32[288,128]{1,0:T(8,128)S(1)}) custom-call(s32[32,32]{1,0:T(8,128)S(1)} %get-tuple-element.38.operator_ref, f32[12680,128]{1,0:T(8,128)S(1)} %get-tuple-element.39.wide_ref, f32[1280,128]{1,0:T(8,128)S(1)} %get-tuple-element.48.real_sum, ...), custom_call_target="tpu_custom_call" | custom-call | flops 10000000 | bytes 2000000 | tf_op jit(solution)/shard_map/pallas_call | solution.py:681
  24.4 1.4 %shard_map.99 = (f32[288,128]{1,0:T(8,128)S(1)}, f32[288,128]{1,0:T(8,128)S(1)}) custom-call(s32[32,32]{1,0:T(8,128)S(1)} %get-tuple-element.38.operator_ref, f32[12680,128]{1,0:T(8,128)S(1)} %get-tuple-element.39.wide_ref, f32[1280,128]{1,0:T(8,128)S(1)} %get-tuple-element.48.real_sum, f32[1280,128]{1,0:T(8,128)S(1)} %get-tuple-element.49.imag_sum, ...), custom_call_target="tpu_custom_call" | custom-call | flops 20000000 | bytes 4000000 | tf_op jit(solution)/shard_map/pallas_call | solution.py:681
  25.8 0.1 collective-permute-start.5
  25.9 1.9 %collective-permute-start.6 = (f32[288,128]{1,0:T(8,128)S(1)}, f32[288,128]{1,0:T(8,128)S(1)}, u32[]{:S(2)}, u32[]{:S(2)}) collective-permute-start(f32[288,128]{1,0:T(8,128)S(1)} %get-tuple-element.54), channel_id=1, source_target_pairs={{0,16},{8,24},{16,0},{24,8},{1,17},{9,25},{17,1},{25,9},{2,18},{10... | collective-permute-start | bytes 442376 | tf_op jit(solution)/shard_map/ppermute | solution.py:557
  27.8 1.6 %collective-permute-start.7 = (f32[288,128]{1,0:T(8,128)S(1)}, f32[288,128]{1,0:T(8,128)S(1)}, u32[]{:S(2)}, u32[]{:S(2)}) collective-permute-start(f32[288,128]{1,0:T(8,128)S(1)} %get-tuple-element.55), channel_id=1, source_target_pairs={{0,24},{8,16},{16,8},{24,0},{1,25},{9,17},{17,9},{25,1},{2,26},{10... | collective-permute-start | bytes 442376 | tf_op jit(solution)/shard_map/ppermute | solution.py:557
  29.4 1.1 %shard_map.98.rest_0_ = f32[288,128]{1,0:T(8,128)S(1)} custom-call(s32[32,32]{1,0:T(8,128)S(1)} %get-tuple-element.38.operator_ref, f32[12680,128]{1,0:T(8,128)S(1)} %get-tuple-element.39.wide_ref, f32[1280,128]{1,0:T(8,128)S(1)} %get-tuple-element.48.real_sum, f32[1280,128]{1,0:T(8,128)S(1)} %get-tuple-element.49.imag_sum, ...), custom_call_target="tpu_custom_call" | custom-call | flops 10000000 | bytes 2000000 | tf_op jit(solution)/shard_map/pallas_call | solution.py:681
  30.5 0.5 %collective-permute-done.5.rest_1_ = f32[288,128]{1,0:T(8,128)S(1)} collective-permute-done((f32[288,128]{1,0:T(8,128)S(1)}, f32[288,128]{1,0:T(8,128)S(1)}, u32[]{:S(2)}, u32[]{:S(2)}) %collective-permute-start.5) | collective-permute-done | bytes 147488 | tf_op jit(solution)/shard_map/ppermute | solution.py:557
  31.0 1.0 %collective-permute-done.6.rest_2_ = f32[288,128]{1,0:T(8,128)S(1)} collective-permute-done((f32[288,128]{1,0:T(8,128)S(1)}, f32[288,128]{1,0:T(8,128)S(1)}, u32[]{:S(2)}, u32[]{:S(2)}) %collective-permute-start.6) | collective-permute-done | bytes 147488 | tf_op jit(solution)/shard_map/ppermute | solution.py:557
  32.1 1.8 %collective-permute-done.7.rest_3_ = f32[288,128]{1,0:T(8,128)S(1)} collective-permute-done((f32[288,128]{1,0:T(8,128)S(1)}, f32[288,128]{1,0:T(8,128)S(1)}, u32[]{:S(2)}, u32[]{:S(2)}) %collective-permute-start.7) | collective-permute-done | bytes 147488 | tf_op jit(solution)/shard_map/ppermute | solution.py:557
  33.8 0.6 %shard_map.100 = (f32[16,9,8,128]{3,2,1,0:T(8,128)S(1)}, f32[2,96,128]{2,1,0:T(8,128)S(1)}, f32[96,128]{1,0:T(8,128)S(1)}) custom-call(s32[1,48]{1,0:T(1,128)S(1)} %copy-done.3, f32[7,2,48,128]{3,2,1,0:T(8,128)S(1)} %get-tuple-element.33.edge_phase_ref, bf16[4,256,128]{2,1,0:T(8,128)(2,1)S(1)} %copy-done, f32[288,128]{1,0:T(8,128)S(1)} %shard_map.98.rest_0_, ...), custom_call_target="tpu_custom_call" | custom-call | flops 1000000 | bytes 1000000 | tf_op jit(solution)/shard_map/pallas_call | solution.py:695
  34.5 4.3 %collective-permute-start.9 = (f32[96,128]{1,0:T(8,128)S(1)}, f32[96,128]{1,0:T(8,128)S(1)}, u32[]{:S(2)}, u32[]{:S(2)}) collective-permute-start(f32[96,128]{1,0:T(8,128)S(1)} %get-tuple-element.59), channel_id=1, source_target_pairs={{0,7},{1,0},{2,1},{3,2},{4,3},{5,4},{6,5},{7,6},{8,15},{9,8},{10,9... | collective-permute-start | bytes 147464 | tf_op jit(solution)/shard_map/ppermute | solution.py:552
  38.8 3.9 %shard_map.101 = (f32[96,32,128]{2,1,0:T(8,128)}, f32[2,96,8,128]{3,2,1,0:T(8,128)S(1)}) custom-call(s32[48]{0:T(128)S(1)} %bitcast.11, s32[48]{0:T(128)S(1)} %copy-done.5, f32[16,9,8,128]{3,2,1,0:T(8,128)S(1)} %get-tuple-element.56.incoming_ref, f32[8,2,9,8,128]{4,3,2,1,0:T(8,128)S(1)} %get-tuple-element.35.phase_ref, bf16[4,256,128]{2,1,0:T(8,128)(2,1)S(1)} %copy-done), custom_call_target="tpu_custom_call" | custom-call | flops 4000000000 | bytes 12000000 | tf_op jit(solution)/shard_map/pallas_call | solution.py:706
  42.7 0.0 collective-permute-done.9.after_ref
  42.7 1.9 %collective-permute-done.8.before_ref = f32[2,96,128]{2,1,0:T(8,128)S(1)} collective-permute-done((f32[2,96,128]{2,1,0:T(8,128)S(1)}, f32[2,96,128]{2,1,0:T(8,128)S(1)}, u32[]{:S(2)}, u32[]{:S(2)}) %collective-permute-start.8) | collective-permute-done | bytes 98336 | tf_op jit(solution)/shard_map/ppermute | solution.py:552
  44.6 1.0 %shard_map.102 = f32[96,32,128]{2,1,0:T(8,128)} custom-call(f32[2,96,8,128]{3,2,1,0:T(8,128)S(1)} %get-tuple-element.57.edge_ref, f32[2,96,128]{2,1,0:T(8,128)S(1)} %collective-permute-done.8.before_ref, f32[96,128]{1,0:T(8,128)S(1)} %collective-permute-done.9.after_ref, f32[96,32,128]{2,1,0:T(8,128)} %get-tuple-element.60.part_ref), custom_call_target="tpu_custom_call", output_to_operand_aliasing={{}: (3, {})} | custom-call | flops 1000000 | bytes 1000000 | tf_op jit(solution)/shard_map/pallas_call | solution.py:723
  (12 shorter events, 0.0 us)
Async XLA Ops:
  0.0 6.2 %copy-start.5 = (s32[48]{0:T(128)S(1)}, s32[48]{0:T(128)}, u32[]{:S(2)}) copy-start(s32[48]{0:T(128)} %octants_ref.3) | copy-start | bytes 580
  0.0 6.2 %copy-start.3 = (s32[1,48]{1,0:T(1,128)S(1)}, s32[1,48]{1,0:T(1,128)}, u32[]{:S(2)}) copy-start(s32[1,48]{1,0:T(1,128)} %parents_ref.3) | copy-start | bytes 580
  1.6 7.8 %collective-permute-start = (f32[96,128]{1,0:T(8,128)S(1)}, f32[96,128]{1,0:T(8,128)S(1)}, u32[]{:S(2)}, u32[]{:S(2)}) collective-permute-start(f32[96,128]{1,0:T(8,128)S(1)} %get-tuple-element.40), channel_id=1, source_target_pairs={{0,1},{1,2},{2,3},{3,4},{4,5},{5,6},{6,7},{7,0},{8,9},{9,10},{10,1... | collective-permute-start | bytes 147464 | tf_op jit(solution)/shard_map/ppermute | solution.py:552
  2.1 7.2 %collective-permute-start.1 = (f32[2,96,128]{2,1,0:T(8,128)S(1)}, f32[2,96,128]{2,1,0:T(8,128)S(1)}, u32[]{:S(2)}, u32[]{:S(2)}) collective-permute-start(f32[2,96,128]{2,1,0:T(8,128)S(1)} %get-tuple-element.41), channel_id=1, source_target_pairs={{0,7},{1,0},{2,1},{3,2},{4,3},{5,4},{6,5},{7,6},{8,15},{9,8},{10,9... | collective-permute-start | bytes 294920 | tf_op jit(solution)/shard_map/ppermute | solution.py:552
  6.2 7.2 %copy-start.1 = (s32[32,31]{1,0:T(8,128)S(1)}, s32[32,31]{1,0:T(8,128)}, u32[]{:S(2)}) copy-start(s32[32,31]{1,0:T(8,128)} %source_ref.1) | copy-start | bytes 11908
  6.2 7.3 %copy-start.2 = (s32[32,31]{1,0:T(8,128)S(1)}, s32[32,31]{1,0:T(8,128)}, u32[]{:S(2)}) copy-start(s32[32,31]{1,0:T(8,128)} %offset_ref.1) | copy-start | bytes 11908
  6.2 7.2 %copy-start.4 = (s32[32]{0:T(128)S(1)}, s32[32]{0:T(128)}, u32[]{:S(2)}) copy-start(s32[32]{0:T(128)} %param.15) | copy-start | bytes 388
  9.9 6.5 %collective-permute-start.2 = (f32[288,128]{1,0:T(8,128)S(1)}, f32[288,128]{1,0:T(8,128)S(1)}, u32[]{:S(2)}, u32[]{:S(2)}) collective-permute-start(f32[288,128]{1,0:T(8,128)S(1)} %get-tuple-element.43), channel_id=1, source_target_pairs={{0,8},{8,0},{16,24},{24,16},{1,9},{9,1},{17,25},{25,17},{2,10},{10... | collective-permute-start | bytes 442376 | tf_op jit(solution)/shard_map/ppermute | solution.py:557
  11.9 8.3 %collective-permute-start.3 = (f32[288,128]{1,0:T(8,128)S(1)}, f32[288,128]{1,0:T(8,128)S(1)}, u32[]{:S(2)}, u32[]{:S(2)}) collective-permute-start(f32[288,128]{1,0:T(8,128)S(1)} %get-tuple-element.44), channel_id=1, source_target_pairs={{0,16},{8,24},{16,0},{24,8},{1,17},{9,25},{17,1},{25,9},{2,18},{10... | collective-permute-start | bytes 442376 | tf_op jit(solution)/shard_map/ppermute | solution.py:557
  13.4 9.9 %collective-permute-start.4 = (f32[288,128]{1,0:T(8,128)S(1)}, f32[288,128]{1,0:T(8,128)S(1)}, u32[]{:S(2)}, u32[]{:S(2)}) collective-permute-start(f32[288,128]{1,0:T(8,128)S(1)} %get-tuple-element.50), channel_id=1, source_target_pairs={{0,24},{8,16},{16,8},{24,0},{1,25},{9,17},{17,9},{25,1},{2,26},{10... | collective-permute-start | bytes 442376 | tf_op jit(solution)/shard_map/ppermute | solution.py:557
  25.8 5.2 %collective-permute-start.5 = (f32[288,128]{1,0:T(8,128)S(1)}, f32[288,128]{1,0:T(8,128)S(1)}, u32[]{:S(2)}, u32[]{:S(2)}) collective-permute-start(f32[288,128]{1,0:T(8,128)S(1)} %get-tuple-element.53), channel_id=1, source_target_pairs={{0,8},{8,0},{16,24},{24,16},{1,9},{9,1},{17,25},{25,17},{2,10},{10... | collective-permute-start | bytes 442376 | tf_op jit(solution)/shard_map/ppermute | solution.py:557
  25.9 6.2 %collective-permute-start.6 = (f32[288,128]{1,0:T(8,128)S(1)}, f32[288,128]{1,0:T(8,128)S(1)}, u32[]{:S(2)}, u32[]{:S(2)}) collective-permute-start(f32[288,128]{1,0:T(8,128)S(1)} %get-tuple-element.54), channel_id=1, source_target_pairs={{0,16},{8,24},{16,0},{24,8},{1,17},{9,25},{17,1},{25,9},{2,18},{10... | collective-permute-start | bytes 442376 | tf_op jit(solution)/shard_map/ppermute | solution.py:557
  27.8 6.0 %copy-start = (bf16[4,256,128]{2,1,0:T(8,128)(2,1)S(1)}, bf16[4,256,128]{2,1,0:T(8,128)(2,1)}, u32[]{:S(2)}) copy-start(bf16[4,256,128]{2,1,0:T(8,128)(2,1)} %constant.5.clone.gather_ref) | copy-start | bytes 786436
  27.8 6.0 %collective-permute-start.7 = (f32[288,128]{1,0:T(8,128)S(1)}, f32[288,128]{1,0:T(8,128)S(1)}, u32[]{:S(2)}, u32[]{:S(2)}) collective-permute-start(f32[288,128]{1,0:T(8,128)S(1)} %get-tuple-element.55), channel_id=1, source_target_pairs={{0,24},{8,16},{16,8},{24,0},{1,25},{9,17},{17,9},{25,1},{2,26},{10... | collective-permute-start | bytes 442376 | tf_op jit(solution)/shard_map/ppermute | solution.py:557
  34.5 8.3 %collective-permute-start.9 = (f32[96,128]{1,0:T(8,128)S(1)}, f32[96,128]{1,0:T(8,128)S(1)}, u32[]{:S(2)}, u32[]{:S(2)}) collective-permute-start(f32[96,128]{1,0:T(8,128)S(1)} %get-tuple-element.59), channel_id=1, source_target_pairs={{0,7},{1,0},{2,1},{3,2},{4,3},{5,4},{6,5},{7,6},{8,15},{9,8},{10,9... | collective-permute-start | bytes 147464 | tf_op jit(solution)/shard_map/ppermute | solution.py:552
  38.8 5.8 %collective-permute-start.8 = (f32[2,96,128]{2,1,0:T(8,128)S(1)}, f32[2,96,128]{2,1,0:T(8,128)S(1)}, u32[]{:S(2)}, u32[]{:S(2)}) collective-permute-start(f32[2,96,128]{2,1,0:T(8,128)S(1)} %get-tuple-element.58), channel_id=1, source_target_pairs={{0,1},{1,2},{2,3},{3,4},{4,5},{5,6},{6,7},{7,0},{8,9},{9,10},{10,1... | collective-permute-start | bytes 294920 | tf_op jit(solution)/shard_map/ppermute | solution.py:552

commit v3 on v2

--- a/solution.py
+++ b/solution.py
@@ -83,10 +83,20 @@
     return high, low
 
 
-def dot3(values, high_matrix, low_matrix):
+def dot(left, right):
+    return jnp.dot(left, right, preferred_element_type=f32)
+
+
+def spread_dot(values, matrix_ref, i):
     high, low = split(values)
-    dot = functools.partial(jnp.dot, preferred_element_type=f32)
-    return dot(high, high_matrix) + dot(low, high_matrix) + dot(high, low_matrix)
+    depth = values.shape[1]
+    return dot(jnp.concatenate([high, low], axis=1), matrix_ref[i, : 2 * depth]) + dot(high, matrix_ref[i, 2 * depth :])
+
+
+def gather_dot(high, low, matrix_ref, i):
+    width = matrix_ref.shape[2] // 2
+    both = dot(high, matrix_ref[i])
+    return both[:, :width] + (both[:, width:] + dot(low, matrix_ref[i, :, :width]))
 
 
 SIN_COEFFS = [(-1) ** k * math.pi ** (2 * k + 1) / math.factorial(2 * k + 1) for k in range(7)]
@@ -219,8 +229,8 @@
                 az_o[base : base + periods, :] = rows[2 * r + 1]
 
     def polar():
-        res_e[...] = dot3(az_e[...], spread_ref[0], spread_ref[1])
-        res_o[...] = dot3(az_o[...], spread_ref[2], spread_ref[3])
+        res_e[...] = spread_dot(az_e[...], spread_ref, 0)
+        res_o[...] = spread_dot(az_o[...], spread_ref, 1)
 
     def shift(block):
         for k in range(BLOCK):
@@ -264,7 +274,6 @@
 def dot2(exact, values):
     exact = exact.astype(bf16)
     high, low = split(values)
-    dot = functools.partial(jnp.dot, preferred_element_type=f32)
     return dot(exact, high) + dot(exact, low)
 
 
@@ -282,8 +291,8 @@
     a, b = TAPS_A, TAPS_B
     even = jnp.concatenate([b[0] * left, a[3] * right[0] + a[4] * right[1]], axis=0)
     odd = jnp.concatenate([a[0] * left, b[3] * right[0] + b[4] * right[1]], axis=0)
-    even = dot3(even, spread_ref[0], spread_ref[1])
-    odd = dot3(odd, spread_ref[2], spread_ref[3])
+    even = spread_dot(even, spread_ref, 0)
+    odd = spread_dot(odd, spread_ref, 1)
     first, last = slice(0, pairs), slice(pairs, 2 * pairs)
     low, high = slice(0, LANES), slice(LANES, 2 * LANES)
     refined = [
@@ -450,8 +459,8 @@
     join = functools.partial(jnp.concatenate, axis=1)
     even = jnp.concatenate([join([returned[2], returned[3]]), join([returned[4], returned[5]])], axis=0)
     odd = jnp.concatenate([join([returned[0], returned[1]]), join([returned[5], returned[6]])], axis=0)
-    even = dot3(even, gather_ref[0], gather_ref[1])
-    odd = dot3(odd, gather_ref[2], gather_ref[3])
+    even = gather_dot(*split(even), gather_ref, 0)
+    odd = gather_dot(*split(odd), gather_ref, 1)
     a, b = TAPS_A, TAPS_B
     prev_ref[...] = a[0] * odd[:pairs] + b[0] * even[:pairs]
     next_ref[0] = a[3] * even[pairs:] + b[3] * odd[pairs:]
@@ -483,13 +492,8 @@
 
     def polar():
         high, low = split(lhs[...])
-        dot = functools.partial(jnp.dot, preferred_element_type=f32)
-        for coarse, columns, i in ((coarse_e, slice(0, 2 * LANES), 0), (coarse_o, slice(LANES, 3 * LANES), 2)):
-            coarse[...] = (
-                dot(high[:, columns], gather_ref[i])
-                + dot(low[:, columns], gather_ref[i])
-                + dot(high[:, columns], gather_ref[i + 1])
-            )
+        coarse_e[...] = gather_dot(high[:, : 2 * LANES], low[:, : 2 * LANES], gather_ref, 0)
+        coarse_o[...] = gather_dot(high[:, LANES:], low[:, LANES:], gather_ref, 1)
 
     def azimuth(block):
         for j in range(2 * BLOCK):
@@ -597,7 +601,7 @@
 
     edges = len(edge_rows(periods))
     even, odd = polar_blocks()
-    blocks_np = np.stack([*split_np(even), *split_np(odd)])
+    blocks_np = np.stack([np.concatenate([h, h, l]) for h, l in (split_np(even), split_np(odd))])
     held, last, first, phases, edge_phases, spread = local_call(
         rows_kernel,
         [
@@ -616,7 +620,7 @@
     after = shifted(first, "dir", -1)
 
     odd_gather = np.concatenate([odd.T[LANES:], odd.T[:LANES]])
-    gather = np.stack([*split_np(even.T), *split_np(odd_gather)])
+    gather = np.stack([np.concatenate(split_np(m), axis=1) for m in (even.T, odd_gather)])
 
     frame = max(-(-((q * 2 * share) % 8 + 2 * share) // 8) * 8 for q in range(peers))
     view = trans_table.reshape(offsets, 2, flat_rows, LANES).transpose(0, 2, 1, 3).reshape(offsets, 2 * flat_rows, LANES)

time: 45.8 us -> 45.2 us (0.987)
  waiting for transfers between devices: 9.09 us -> 11.1 us
  Pallas kernels: 20.3 us -> 18.9 us
  starting transfers between devices: 16.1 us -> 14.8 us
    ppermute x6, waiting for transfers between devices: 7.18 us -> 8.53 us  [exchanged(): return lax.ppermute(values, axis, [(i, i ^ mask) for i in range(size)])]
    ppermute x4, starting transfers between devices: 8.97 us -> 7.69 us  [shifted(): lax.ppermute(values, axis, [(i, (i + by) % size) for i in range(size)])]
    pallas_call x1, Pallas kernels: 3.91 us -> 3.24 us  [on_device_exchange(): local_call(disaggregate_kernel, [array(pairs, azimuth_in, polar_in), arra...]
    ppermute x4, waiting for transfers between devices: 1.91 us -> 2.58 us  [shifted(): lax.ppermute(values, axis, [(i, (i + by) % size) for i in range(size)])]
    pallas_call x1, Pallas kernels: 3.09 us -> 2.5 us  [on_device_exchange(): local_call(functools.partial(main_kernel, peers), [array(2 * own * flat_r...]
  transfers between devices with their start and end apart: 10 -> 10, of which waited for: 5 -> 6; matrix products, arithmetic and copies ran while one was open for 0% -> 0% of each run, Pallas kernels for 31% -> 28%
where the time goes in v3:
time: 45.2 us; the launch traced here: 45 us
  Pallas kernels  18.9 us (42%)
  starting transfers between devices  14.8 us (33%)
  waiting for transfers between devices  11.1 us (25%)
    ppermute x6, waiting for transfers between devices, exchanged(): return lax.ppermute(values, axis, [(i, i ^ mask) for i in range(size)])  8.53 us
    ppermute x4, starting transfers between devices, shifted(): lax.ppermute(values, axis, [(i, (i + by) % size) for i in range(size)])  7.69 us
    ppermute x6, starting transfers between devices, exchanged(): return lax.ppermute(values, axis, [(i, i ^ mask) for i in range(size)])  7.1 us
    pallas_call x2, Pallas kernels, on_device_exchange(): local_call(functools.partial(gather_kernel, peers, frame, tuple(group)),...  4.9 us
    pallas_call x3, Pallas kernels, on_device_exchange(): local_call(functools.partial(translate_kernel, peers, frame, late, tuple(...  3.61 us
    pallas_call x1, Pallas kernels, on_device_exchange(): local_call(disaggregate_kernel, [array(pairs, azimuth_in, polar_in), arra...  3.24 us
    ppermute x4, waiting for transfers between devices, shifted(): lax.ppermute(values, axis, [(i, (i + by) % size) for i in range(size)])  2.58 us
    pallas_call x1, Pallas kernels, on_device_exchange(): local_call(functools.partial(main_kernel, peers), [array(2 * own * flat_r...  2.5 us
  transfers between devices with their start and end apart: 10, of which 6 were waited for; matrix products, arithmetic and copies ran while one was open for 0% of the time, Pallas kernels for 28%

profile of v3, /device:TPU:0, one launch (start us, length us, event | category | flops | bytes accessed | tf_op | source)
XLA Modules:
  0.0 45.0 jit_solution(13570513239401862409)
XLA Ops:
  0.0 1.6 %shard_map.91 = (f32[96,32,128]{2,1,0:T(8,128)S(1)}, f32[96,128]{1,0:T(8,128)S(1)}, f32[2,96,128]{2,1,0:T(8,128)S(1)}, f32[8,2,9,8,128]{4,3,2,1,0:T(8,128)S(1)},...) custom-call(s32[48]{0:T(128)} %octants_ref.3, f32[96,32,128]{2,1,0:T(8,128)} %bitcast.14, ...), custom_call_target="tpu_custom_call" | custom-call | flops 1000000 | bytes 1000000 | tf_op jit(solution)/shard_map/pallas_call | solution.py:605
  1.6 0.5 %collective-permute-start = (f32[96,128]{1,0:T(8,128)S(1)}, f32[96,128]{1,0:T(8,128)S(1)}, u32[]{:S(2)}, u32[]{:S(2)}) collective-permute-start(f32[96,128]{1,0:T(8,128)S(1)} %get-tuple-element.40), channel_id=1, source_target_pairs={{0,1},{1,2},{2,3},{3,4},{4,5},{5,6},{6,7},{7,0},{8,9},{9,10},{10,1... | collective-permute-start | bytes 147464 | tf_op jit(solution)/shard_map/ppermute | solution.py:556
  2.1 4.1 %collective-permute-start.1 = (f32[2,96,128]{2,1,0:T(8,128)S(1)}, f32[2,96,128]{2,1,0:T(8,128)S(1)}, u32[]{:S(2)}, u32[]{:S(2)}) collective-permute-start(f32[2,96,128]{2,1,0:T(8,128)S(1)} %get-tuple-element.41), channel_id=1, source_target_pairs={{0,7},{1,0},{2,1},{3,2},{4,3},{5,4},{6,5},{7,6},{8,15},{9,8},{10,9... | collective-permute-start | bytes 294920 | tf_op jit(solution)/shard_map/ppermute | solution.py:556
  6.2 0.0 copy-start.5
  6.2 2.5 %shard_map.92 = (f32[1152,128]{1,0:T(8,128)S(1)}, bf16[316,40,128]{2,1,0:T(8,128)(2,1)S(1)}) custom-call(s32[48]{0:T(128)S(1)} %bitcast.10, s32[48]{0:T(128)S(1)} %copy-done.4, f32[3072,128]{1,0:T(8,128)S(1)} %bitcast.13, bf16[316,144,128]{2,1,0:T(8,128)(2,1)} %bitcast.15, f32[8,2,9,8,128]{4,3,2,1,0:T(8,128)S(1)} %get-tuple-element.35.phase_ref, ...), custom_call_target="tpu_custom_call" | custom-call | flops 4000000000 | bytes 12000000 | tf_op jit(solution)/shard_map/pallas_call | solution.py:629
  8.7 0.0 collective-permute-done.before_ref
  8.7 0.0 collective-permute-done.1.after_ref
  8.8 0.5 %shard_map.94 = (f32[288,128]{1,0:T(8,128)S(1)}, f32[288,128]{1,0:T(8,128)S(1)}, f32[288,128]{1,0:T(8,128)S(1)}, f32[288,128]{1,0:T(8,128)S(1)}) custom-call(s32[1,48]{1,0:T(1,128)S(1)} %copy-done.3, f32[96,128]{1,0:T(8,128)S(1)} %collective-permute-done.before_ref, f32[2,96,128]{2,1,0:T(8,128)S(1)} %collective-permute-done.1.after_ref, ...), custom_call_target="tpu_custom_call" | custom-call | flops 1000000 | bytes 1000000 | tf_op jit(solution)/shard_map/pallas_call | solution.py:648
  9.3 2.0 %collective-permute-start.2 = (f32[288,128]{1,0:T(8,128)S(1)}, f32[288,128]{1,0:T(8,128)S(1)}, u32[]{:S(2)}, u32[]{:S(2)}) collective-permute-start(f32[288,128]{1,0:T(8,128)S(1)} %get-tuple-element.43), channel_id=1, source_target_pairs={{0,8},{8,0},{16,24},{24,16},{1,9},{9,1},{17,25},{25,17},{2,10},{10... | collective-permute-start | bytes 442376 | tf_op jit(solution)/shard_map/ppermute | solution.py:561
  11.2 1.5 %collective-permute-start.3 = (f32[288,128]{1,0:T(8,128)S(1)}, f32[288,128]{1,0:T(8,128)S(1)}, u32[]{:S(2)}, u32[]{:S(2)}) collective-permute-start(f32[288,128]{1,0:T(8,128)S(1)} %get-tuple-element.44), channel_id=1, source_target_pairs={{0,16},{8,24},{16,0},{24,8},{1,17},{9,25},{17,1},{25,9},{2,18},{10... | collective-permute-start | bytes 442376 | tf_op jit(solution)/shard_map/ppermute | solution.py:561
  12.8 0.0 collective-permute-start.4
  12.8 1.1 %shard_map.93 = (f32[12680,128]{1,0:T(8,128)S(1)}, s32[32,32]{1,0:T(8,128)S(1)}) custom-call(s32[32,31]{1,0:T(8,128)S(1)} %copy-done.1, s32[32,31]{1,0:T(8,128)S(1)} %copy-done.2, s32[1,32]{1,0:T(1,128)S(1)} %bitcast.12, bf16[316,40,128]{2,1,0:T(8,128)(2,1)S(1)} %get-tuple-element.37.table_ref), custom_call_target="tpu_custom_call" | custom-call | flops 50000000 | bytes 8000000 | tf_op jit(solution)/shard_map/pallas_call | solution.py:659
  13.9 1.8 %shard_map.95 = (f32[1280,128]{1,0:T(8,128)S(1)}, f32[1280,128]{1,0:T(8,128)S(1)}) custom-call(s32[32,32]{1,0:T(8,128)S(1)} %get-tuple-element.38.operator_ref, f32[12680,128]{1,0:T(8,128)S(1)} %get-tuple-element.39.wide_ref, f32[288,128]{1,0:T(8,128)S(1)} %get-tuple-element.45.rest_0_), custom_call_target="tpu_custom_call" | custom-call | flops 40000000 | bytes 4000000 | tf_op jit(solution)/shard_map/pallas_call | solution.py:671
  15.7 0.2 collective-permute-done.2.rest_0_
  15.9 4.1 %collective-permute-done.3.rest_1_ = f32[288,128]{1,0:T(8,128)S(1)} collective-permute-done((f32[288,128]{1,0:T(8,128)S(1)}, f32[288,128]{1,0:T(8,128)S(1)}, u32[]{:S(2)}, u32[]{:S(2)}) %collective-permute-start.3) | collective-permute-done | bytes 147488 | tf_op jit(solution)/shard_map/ppermute | solution.py:561
  20.0 3.1 %shard_map.96 = (f32[1280,128]{1,0:T(8,128)S(1)}, f32[1280,128]{1,0:T(8,128)S(1)}) custom-call(s32[32,32]{1,0:T(8,128)S(1)} %get-tuple-element.38.operator_ref, f32[12680,128]{1,0:T(8,128)S(1)} %get-tuple-element.39.wide_ref, f32[288,128]{1,0:T(8,128)S(1)} %collective-permute-done.2.rest_0_, f32[288,128]{1,0:T(8,128)S(1)} %collective-permute-done.3.rest_1_, ...), custom_call_target="tpu_custom_call" | custom-call | flops 80000000 | bytes 8000000 | tf_op jit(solution)/shard_map/pallas_call | solution.py:671
  23.1 1.1 %shard_map.97 = (f32[320,128]{1,0:T(8,128)S(1)}, f32[320,128]{1,0:T(8,128)S(1)}, f32[288,128]{1,0:T(8,128)S(1)}) custom-call(s32[32,32]{1,0:T(8,128)S(1)} %get-tuple-element.38.operator_ref, f32[12680,128]{1,0:T(8,128)S(1)} %get-tuple-element.39.wide_ref, f32[1280,128]{1,0:T(8,128)S(1)} %get-tuple-element.48.real_sum, ...), custom_call_target="tpu_custom_call" | custom-call | flops 10000000 | bytes 2000000 | tf_op jit(solution)/shard_map/pallas_call | solution.py:685
  24.2 1.4 %shard_map.99 = (f32[288,128]{1,0:T(8,128)S(1)}, f32[288,128]{1,0:T(8,128)S(1)}) custom-call(s32[32,32]{1,0:T(8,128)S(1)} %get-tuple-element.38.operator_ref, f32[12680,128]{1,0:T(8,128)S(1)} %get-tuple-element.39.wide_ref, f32[1280,128]{1,0:T(8,128)S(1)} %get-tuple-element.48.real_sum, f32[1280,128]{1,0:T(8,128)S(1)} %get-tuple-element.49.imag_sum, ...), custom_call_target="tpu_custom_call" | custom-call | flops 20000000 | bytes 4000000 | tf_op jit(solution)/shard_map/pallas_call | solution.py:685
  25.6 0.1 collective-permute-start.5
  25.7 2.0 %collective-permute-start.6 = (f32[288,128]{1,0:T(8,128)S(1)}, f32[288,128]{1,0:T(8,128)S(1)}, u32[]{:S(2)}, u32[]{:S(2)}) collective-permute-start(f32[288,128]{1,0:T(8,128)S(1)} %get-tuple-element.54), channel_id=1, source_target_pairs={{0,16},{8,24},{16,0},{24,8},{1,17},{9,25},{17,1},{25,9},{2,18},{10... | collective-permute-start | bytes 442376 | tf_op jit(solution)/shard_map/ppermute | solution.py:561
  27.7 1.4 %collective-permute-start.7 = (f32[288,128]{1,0:T(8,128)S(1)}, f32[288,128]{1,0:T(8,128)S(1)}, u32[]{:S(2)}, u32[]{:S(2)}) collective-permute-start(f32[288,128]{1,0:T(8,128)S(1)} %get-tuple-element.55), channel_id=1, source_target_pairs={{0,24},{8,16},{16,8},{24,0},{1,25},{9,17},{17,9},{25,1},{2,26},{10... | collective-permute-start | bytes 442376 | tf_op jit(solution)/shard_map/ppermute | solution.py:561
  29.1 1.1 %shard_map.98.rest_0_ = f32[288,128]{1,0:T(8,128)S(1)} custom-call(s32[32,32]{1,0:T(8,128)S(1)} %get-tuple-element.38.operator_ref, f32[12680,128]{1,0:T(8,128)S(1)} %get-tuple-element.39.wide_ref, f32[1280,128]{1,0:T(8,128)S(1)} %get-tuple-element.48.real_sum, f32[1280,128]{1,0:T(8,128)S(1)} %get-tuple-element.49.imag_sum, ...), custom_call_target="tpu_custom_call" | custom-call | flops 10000000 | bytes 2000000 | tf_op jit(solution)/shard_map/pallas_call | solution.py:685
  30.2 1.4 %collective-permute-done.5.rest_1_ = f32[288,128]{1,0:T(8,128)S(1)} collective-permute-done((f32[288,128]{1,0:T(8,128)S(1)}, f32[288,128]{1,0:T(8,128)S(1)}, u32[]{:S(2)}, u32[]{:S(2)}) %collective-permute-start.5) | collective-permute-done | bytes 147488 | tf_op jit(solution)/shard_map/ppermute | solution.py:561
  31.6 1.1 %collective-permute-done.6.rest_2_ = f32[288,128]{1,0:T(8,128)S(1)} collective-permute-done((f32[288,128]{1,0:T(8,128)S(1)}, f32[288,128]{1,0:T(8,128)S(1)}, u32[]{:S(2)}, u32[]{:S(2)}) %collective-permute-start.6) | collective-permute-done | bytes 147488 | tf_op jit(solution)/shard_map/ppermute | solution.py:561
  32.7 1.8 %collective-permute-done.7.rest_3_ = f32[288,128]{1,0:T(8,128)S(1)} collective-permute-done((f32[288,128]{1,0:T(8,128)S(1)}, f32[288,128]{1,0:T(8,128)S(1)}, u32[]{:S(2)}, u32[]{:S(2)}) %collective-permute-start.7) | collective-permute-done | bytes 147488 | tf_op jit(solution)/shard_map/ppermute | solution.py:561
  34.5 0.6 %shard_map.100 = (f32[16,9,8,128]{3,2,1,0:T(8,128)S(1)}, f32[2,96,128]{2,1,0:T(8,128)S(1)}, f32[96,128]{1,0:T(8,128)S(1)}) custom-call(s32[1,48]{1,0:T(1,128)S(1)} %copy-done.3, f32[7,2,48,128]{3,2,1,0:T(8,128)S(1)} %get-tuple-element.33.edge_phase_ref, bf16[2,256,256]{2,1,0:T(8,128)(2,1)S(1)} %copy-done, f32[288,128]{1,0:T(8,128)S(1)} %shard_map.98.rest_0_, ...), custom_call_target="tpu_custom_call" | custom-call | flops 1000000 | bytes 1000000 | tf_op jit(solution)/shard_map/pallas_call | solution.py:699
  35.1 3.1 %collective-permute-start.9 = (f32[96,128]{1,0:T(8,128)S(1)}, f32[96,128]{1,0:T(8,128)S(1)}, u32[]{:S(2)}, u32[]{:S(2)}) collective-permute-start(f32[96,128]{1,0:T(8,128)S(1)} %get-tuple-element.59), channel_id=1, source_target_pairs={{0,7},{1,0},{2,1},{3,2},{4,3},{5,4},{6,5},{7,6},{8,15},{9,8},{10,9... | collective-permute-start | bytes 147464 | tf_op jit(solution)/shard_map/ppermute | solution.py:556
  38.1 0.0 collective-permute-start.8
  38.1 3.2 %shard_map.101 = (f32[96,32,128]{2,1,0:T(8,128)}, f32[2,96,8,128]{3,2,1,0:T(8,128)S(1)}) custom-call(s32[48]{0:T(128)S(1)} %bitcast.11, s32[48]{0:T(128)S(1)} %copy-done.4, f32[16,9,8,128]{3,2,1,0:T(8,128)S(1)} %get-tuple-element.56.incoming_ref, f32[8,2,9,8,128]{4,3,2,1,0:T(8,128)S(1)} %get-tuple-element.35.phase_ref, bf16[2,256,256]{2,1,0:T(8,128)(2,1)S(1)} %copy-done), custom_call_target="tpu_custom_call" | custom-call | flops 4000000000 | bytes 12000000 | tf_op jit(solution)/shard_map/pallas_call | solution.py:710
  41.4 0.0 collective-permute-done.9.after_ref
  41.4 2.6 %collective-permute-done.8.before_ref = f32[2,96,128]{2,1,0:T(8,128)S(1)} collective-permute-done((f32[2,96,128]{2,1,0:T(8,128)S(1)}, f32[2,96,128]{2,1,0:T(8,128)S(1)}, u32[]{:S(2)}, u32[]{:S(2)}) %collective-permute-start.8) | collective-permute-done | bytes 98336 | tf_op jit(solution)/shard_map/ppermute | solution.py:556
  44.0 1.0 %shard_map.102 = f32[96,32,128]{2,1,0:T(8,128)} custom-call(f32[2,96,8,128]{3,2,1,0:T(8,128)S(1)} %get-tuple-element.57.edge_ref, f32[2,96,128]{2,1,0:T(8,128)S(1)} %collective-permute-done.8.before_ref, f32[96,128]{1,0:T(8,128)S(1)} %collective-permute-done.9.after_ref, f32[96,32,128]{2,1,0:T(8,128)} %get-tuple-element.60.part_ref), custom_call_target="tpu_custom_call", output_to_operand_aliasing={{}: (3, {})} | custom-call | flops 1000000 | bytes 1000000 | tf_op jit(solution)/shard_map/pallas_call | solution.py:727
  (12 shorter events, 0.0 us)
Async XLA Ops:
  0.0 6.2 %copy-start.4 = (s32[48]{0:T(128)S(1)}, s32[48]{0:T(128)}, u32[]{:S(2)}) copy-start(s32[48]{0:T(128)} %octants_ref.3) | copy-start | bytes 580
  0.0 6.2 %copy-start.3 = (s32[1,48]{1,0:T(1,128)S(1)}, s32[1,48]{1,0:T(1,128)}, u32[]{:S(2)}) copy-start(s32[1,48]{1,0:T(1,128)} %parents_ref.3) | copy-start | bytes 580
  1.6 7.2 %collective-permute-start = (f32[96,128]{1,0:T(8,128)S(1)}, f32[96,128]{1,0:T(8,128)S(1)}, u32[]{:S(2)}, u32[]{:S(2)}) collective-permute-start(f32[96,128]{1,0:T(8,128)S(1)} %get-tuple-element.40), channel_id=1, source_target_pairs={{0,1},{1,2},{2,3},{3,4},{4,5},{5,6},{6,7},{7,0},{8,9},{9,10},{10,1... | collective-permute-start | bytes 147464 | tf_op jit(solution)/shard_map/ppermute | solution.py:556
  2.1 6.6 %collective-permute-start.1 = (f32[2,96,128]{2,1,0:T(8,128)S(1)}, f32[2,96,128]{2,1,0:T(8,128)S(1)}, u32[]{:S(2)}, u32[]{:S(2)}) collective-permute-start(f32[2,96,128]{2,1,0:T(8,128)S(1)} %get-tuple-element.41), channel_id=1, source_target_pairs={{0,7},{1,0},{2,1},{3,2},{4,3},{5,4},{6,5},{7,6},{8,15},{9,8},{10,9... | collective-permute-start | bytes 294920 | tf_op jit(solution)/shard_map/ppermute | solution.py:556
  6.2 6.6 %copy-start.1 = (s32[32,31]{1,0:T(8,128)S(1)}, s32[32,31]{1,0:T(8,128)}, u32[]{:S(2)}) copy-start(s32[32,31]{1,0:T(8,128)} %source_ref.1) | copy-start | bytes 11908
  6.2 6.6 %copy-start.2 = (s32[32,31]{1,0:T(8,128)S(1)}, s32[32,31]{1,0:T(8,128)}, u32[]{:S(2)}) copy-start(s32[32,31]{1,0:T(8,128)} %offset_ref.1) | copy-start | bytes 11908
  6.2 6.6 %copy-start.5 = (s32[32]{0:T(128)S(1)}, s32[32]{0:T(128)}, u32[]{:S(2)}) copy-start(s32[32]{0:T(128)} %param.15) | copy-start | bytes 388
  9.3 6.6 %collective-permute-start.2 = (f32[288,128]{1,0:T(8,128)S(1)}, f32[288,128]{1,0:T(8,128)S(1)}, u32[]{:S(2)}, u32[]{:S(2)}) collective-permute-start(f32[288,128]{1,0:T(8,128)S(1)} %get-tuple-element.43), channel_id=1, source_target_pairs={{0,8},{8,0},{16,24},{24,16},{1,9},{9,1},{17,25},{25,17},{2,10},{10... | collective-permute-start | bytes 442376 | tf_op jit(solution)/shard_map/ppermute | solution.py:561
  11.2 8.7 %collective-permute-start.3 = (f32[288,128]{1,0:T(8,128)S(1)}, f32[288,128]{1,0:T(8,128)S(1)}, u32[]{:S(2)}, u32[]{:S(2)}) collective-permute-start(f32[288,128]{1,0:T(8,128)S(1)} %get-tuple-element.44), channel_id=1, source_target_pairs={{0,16},{8,24},{16,0},{24,8},{1,17},{9,25},{17,1},{25,9},{2,18},{10... | collective-permute-start | bytes 442376 | tf_op jit(solution)/shard_map/ppermute | solution.py:561
  12.8 10.3 %collective-permute-start.4 = (f32[288,128]{1,0:T(8,128)S(1)}, f32[288,128]{1,0:T(8,128)S(1)}, u32[]{:S(2)}, u32[]{:S(2)}) collective-permute-start(f32[288,128]{1,0:T(8,128)S(1)} %get-tuple-element.50), channel_id=1, source_target_pairs={{0,24},{8,16},{16,8},{24,0},{1,25},{9,17},{17,9},{25,1},{2,26},{10... | collective-permute-start | bytes 442376 | tf_op jit(solution)/shard_map/ppermute | solution.py:561
  25.6 6.1 %collective-permute-start.5 = (f32[288,128]{1,0:T(8,128)S(1)}, f32[288,128]{1,0:T(8,128)S(1)}, u32[]{:S(2)}, u32[]{:S(2)}) collective-permute-start(f32[288,128]{1,0:T(8,128)S(1)} %get-tuple-element.53), channel_id=1, source_target_pairs={{0,8},{8,0},{16,24},{24,16},{1,9},{9,1},{17,25},{25,17},{2,10},{10... | collective-permute-start | bytes 442376 | tf_op jit(solution)/shard_map/ppermute | solution.py:561
  25.7 7.0 %collective-permute-start.6 = (f32[288,128]{1,0:T(8,128)S(1)}, f32[288,128]{1,0:T(8,128)S(1)}, u32[]{:S(2)}, u32[]{:S(2)}) collective-permute-start(f32[288,128]{1,0:T(8,128)S(1)} %get-tuple-element.54), channel_id=1, source_target_pairs={{0,16},{8,24},{16,0},{24,8},{1,17},{9,25},{17,1},{25,9},{2,18},{10... | collective-permute-start | bytes 442376 | tf_op jit(solution)/shard_map/ppermute | solution.py:561
  27.7 6.8 %copy-start = (bf16[2,256,256]{2,1,0:T(8,128)(2,1)S(1)}, bf16[2,256,256]{2,1,0:T(8,128)(2,1)}, u32[]{:S(2)}) copy-start(bf16[2,256,256]{2,1,0:T(8,128)(2,1)} %constant.5.clone.gather_ref) | copy-start | bytes 786436
  27.7 6.8 %collective-permute-start.7 = (f32[288,128]{1,0:T(8,128)S(1)}, f32[288,128]{1,0:T(8,128)S(1)}, u32[]{:S(2)}, u32[]{:S(2)}) collective-permute-start(f32[288,128]{1,0:T(8,128)S(1)} %get-tuple-element.55), channel_id=1, source_target_pairs={{0,24},{8,16},{16,8},{24,0},{1,25},{9,17},{17,9},{25,1},{2,26},{10... | collective-permute-start | bytes 442376 | tf_op jit(solution)/shard_map/ppermute | solution.py:561
  35.1 6.3 %collective-permute-start.9 = (f32[96,128]{1,0:T(8,128)S(1)}, f32[96,128]{1,0:T(8,128)S(1)}, u32[]{:S(2)}, u32[]{:S(2)}) collective-permute-start(f32[96,128]{1,0:T(8,128)S(1)} %get-tuple-element.59), channel_id=1, source_target_pairs={{0,7},{1,0},{2,1},{3,2},{4,3},{5,4},{6,5},{7,6},{8,15},{9,8},{10,9... | collective-permute-start | bytes 147464 | tf_op jit(solution)/shard_map/ppermute | solution.py:556
  38.1 5.8 %collective-permute-start.8 = (f32[2,96,128]{2,1,0:T(8,128)S(1)}, f32[2,96,128]{2,1,0:T(8,128)S(1)}, u32[]{:S(2)}, u32[]{:S(2)}) collective-permute-start(f32[2,96,128]{2,1,0:T(8,128)S(1)} %get-tuple-element.58), channel_id=1, source_target_pairs={{0,1},{1,2},{2,3},{3,4},{4,5},{5,6},{6,7},{7,0},{8,9},{9,10},{10,1... | collective-permute-start | bytes 294920 | tf_op jit(solution)/shard_map/ppermute | solution.py:556

commit v4 on v3

--- a/solution.py
+++ b/solution.py
@@ -151,19 +151,35 @@
     return [(w, 0) for w in (1, 2, 3, 4)] + [(w, periods - 1) for w in (6, 7, 8)]
 
 
-def rows_kernel(
-    octants_hbm, x_ref, blocks_ref, held_ref, last_ref, first_ref, phase_ref, edge_phase_ref, blocks_out, octants_ref, sem, blocks_sem, octants_sem
-):
+def rows_kernel(x_ref, last_ref, first_ref, low, high, sems):
     pairs, azimuth_in, _ = x_ref.shape
+    low_copy = pltpu.make_async_copy(x_ref.at[:, pl.ds(0, TILE), :], low, sems.at[0])
+    high_copy = pltpu.make_async_copy(x_ref.at[:, pl.ds(azimuth_in - TILE, TILE), :], high, sems.at[1])
+    low_copy.start()
+    high_copy.start()
+    low_copy.wait()
+    high_copy.wait()
+    low_rows, high_rows = (ref.reshape(pairs * TILE, LANES) for ref in (low, high))
+    for part in range(2):
+        for k in range(0, pairs // 2, 8):
+            target = slice(part * (pairs // 2) + k, part * (pairs // 2) + k + 8)
+            base = (2 * k + part) * TILE
+            for i in range(2):
+                first_ref[i, target] = low_rows[pl.ds(base + i, 8, stride=2 * TILE), :]
+            last_ref[target] = high_rows[pl.ds(base + TILE - 1, 8, stride=2 * TILE), :]
+
+
+def phase_kernel(*refs):
+    octants_hbm, sources = refs[0], refs[1:5]
+    (phase_ref, edge_phase_ref), targets = refs[5:7], refs[7:11]
+    octants_ref, octants_sem, sems = refs[11:]
     periods = phase_ref.shape[3]
-    copy = pltpu.make_async_copy(x_ref, held_ref, sem)
-    copy.start()
-    blocks_copy = pltpu.make_async_copy(blocks_ref, blocks_out, blocks_sem)
-    blocks_copy.start()
     octants_copy = pltpu.make_async_copy(octants_hbm, octants_ref, octants_sem)
     octants_copy.start()
+    copies = [pltpu.make_async_copy(a, b, sems.at[i]) for i, (a, b) in enumerate(zip(sources, targets))]
+    for copy in copies:
+        copy.start()
     fill_phases(lax.axis_index("dir"), phase_ref)
-
     octants_copy.wait()
 
     def edges_of(step, carry):
@@ -175,15 +191,9 @@
                     edge_phase_ref[e, i, pl.ds(k, 1), :] = phase_ref[octant, i, w, m : m + 1, :]
         return carry
 
-    lax.fori_loop(0, pairs // 2 // GROUP, edges_of, 0)
-    copy.wait()
-    for part in range(2):
-        source = pl.ds(part, pairs // 2, stride=2)
-        target = slice(part * (pairs // 2), (part + 1) * (pairs // 2))
-        last_ref[target] = held_ref[source, azimuth_in - 1, :]
-        for i in range(2):
-            first_ref[i, target] = held_ref[source, i, :]
-    blocks_copy.wait()
+    lax.fori_loop(0, octants_ref.shape[0] // GROUP, edges_of, 0)
+    for copy in copies:
+        copy.wait()
 
 
 def both_taps(rows):
@@ -396,20 +406,17 @@
     lax.fori_loop(0, targets // TOGETHER, some_targets, 0)
 
 
-def translate_kernel(peers, frame, mask, targets, operator_ref, wide_ref, real_sum, imag_sum, *rest):
-    if len(rest) == 5 + len(targets):
-        chunk, real_twice, imag_twice = rest[:3]
-        prepare = True
-    else:
-        real_twice, imag_twice = rest[:2]
-        prepare = False
+def translate_kernel(peers, frame, masks, targets, operator_ref, wide_ref, real_sum, imag_sum, *rest):
+    prepare = len(rest) == len(masks) + len(targets) + 4
+    chunks, rest = (rest[: len(masks)], rest[len(masks) :]) if prepare else ((), rest)
+    real_twice, imag_twice = rest[:2]
     outs, (total_real, total_imag) = rest[-2 - len(targets) : -2], rest[-2:]
     me = lax.axis_index("clus")
     own = operator_ref.shape[0] // peers
     share = outs[0].shape[0] // (2 * own)
     skip = lax.rem(me * (2 * share), 8)
-    if prepare:
-        doubled(chunk, real_twice, imag_twice, 0, own, share, frame, skip)
+    for number, chunk in enumerate(chunks):
+        doubled(chunk, real_twice, imag_twice, number * own, own, share, frame, skip)
     even, odd = pl.ds(skip, share, stride=2), pl.ds(skip + 1, share, stride=2)
     for out, d in zip(outs, targets):
         first = (me ^ d) * own
@@ -419,7 +426,7 @@
             some = [first + g for g in places]
             rows = [pl.ds(pl.multiple_of(target * frame, 8), frame) for target in some]
             sums = [(real_sum[r, :], imag_sum[r, :]) for r in rows]
-            sums = add_sources(sums, some, [me ^ mask], own, frame, operator_ref, wide_ref, real_twice, imag_twice)
+            sums = add_sources(sums, some, [me ^ d for d in masks], own, frame, operator_ref, wide_ref, real_twice, imag_twice)
             for j, (g, (by_real, by_imag)) in enumerate(zip(places, sums)):
                 total_real[j] = by_real
                 total_imag[j] = by_imag
@@ -597,27 +604,29 @@
     offsets = trans_table.shape[0]
     array = lambda *shape: jax.ShapeDtypeStruct(shape, f32)
     buffer = lambda *shape: pltpu.VMEM(shape, f32)
-    parents = child_parent[0]
-
     edges = len(edge_rows(periods))
     even, odd = polar_blocks()
-    blocks_np = np.stack([np.concatenate([h, h, l]) for h, l in (split_np(even), split_np(odd))])
-    held, last, first, phases, edge_phases, spread = local_call(
+    spread = jnp.asarray(np.stack([np.concatenate([h, h, l]) for h, l in (split_np(even), split_np(odd))]))
+    last, first = local_call(
         rows_kernel,
-        [
-            array(pairs, azimuth_in, polar_in),
-            array(pairs, polar_in),
-            array(2, pairs, polar_in),
-            array(8, 2, ROWS_PER_PERIOD, periods, LANES),
-            array(edges, 2, children, LANES),
-            jax.ShapeDtypeStruct(blocks_np.shape, bf16),
-        ],
-        [HBM, HBM, HBM],
-        [pltpu.SMEM((children,), jnp.int32)] + [pltpu.SemaphoreType.DMA] * 3,
+        [array(pairs, polar_in), array(2, pairs, polar_in)],
+        [HBM],
+        [buffer(pairs, TILE, polar_in)] * 2 + [pltpu.SemaphoreType.DMA((2,))],
+        8,
+    )(in_hbm(child_patterns.reshape(pairs, azimuth_in, polar_in)))
+    after = shifted(first, "dir", -1)
+    before = shifted(last, "dir", 1)
+    copied = (child_patterns.reshape(pairs * azimuth_in, polar_in), spread, child_parent, child_octant.reshape(1, children))
+    phases, edge_phases, held, spread, parents, octants = local_call(
+        phase_kernel,
+        [array(8, 2, ROWS_PER_PERIOD, periods, LANES), array(edges, 2, children, LANES)]
+        + [jax.ShapeDtypeStruct(a.shape, a.dtype) for a in copied],
+        [HBM] * 5,
+        [pltpu.SMEM((children,), jnp.int32), pltpu.SemaphoreType.DMA, pltpu.SemaphoreType.DMA((len(copied),))],
         12,
-    )(in_hbm(child_octant), in_hbm(child_patterns.reshape(pairs, azimuth_in, polar_in)), in_hbm(jnp.asarray(blocks_np)))
-    before = shifted(last, "dir", 1)
-    after = shifted(first, "dir", -1)
+        flops=50_000_000,
+    )(in_hbm(child_octant), *[in_hbm(a) for a in copied])
+    parents, octants = parents[0], octants[0]
 
     odd_gather = np.concatenate([odd.T[LANES:], odd.T[:LANES]])
     gather = np.stack([np.concatenate(split_np(m), axis=1) for m in (even.T, odd_gather)])
@@ -642,7 +651,7 @@
         24,
         flops=4_000_000_000,
         bytes_accessed=12_000_000,
-    )(parents, child_octant, held.reshape(pairs * azimuth_in, polar_in), in_hbm(view), phases, spread)
+    )(parents, octants, held, in_hbm(view), phases, spread)
 
     chunk = array(2 * own * share, LANES)
     sent = local_call(
@@ -650,11 +659,12 @@
     )(child_parent, before, after, flat, edge_phases, spread)
 
     masks = sorted(range(1, peers), key=lambda d: bin(d).count("1"))
-    middle, late = masks[:-1], masks[-1]
+    early, late = masks[:1], masks[1:]
     received = {0: sent[0]}
-    for d in middle:
+    for d in early:
         received[d] = exchanged(sent[d], "clus", d)
-    received[late] = exchanged(sent[late], "clus", late)
+    for d in late:
+        received[d] = exchanged(sent[d], "clus", d)
 
     wide, operator = local_call(
         widen_kernel,
@@ -667,7 +677,7 @@
     )(partner_src, partner_off, partner_count.reshape(1, parent_total), table)
 
     sums = []
-    for group in ([0], middle):
+    for group in ([0], early):
         sums = local_call(
             functools.partial(gather_kernel, peers, frame, tuple(group)),
             [array(parent_total * frame, LANES)] * 2,
@@ -679,12 +689,12 @@
         )(operator, wide, *[received[d] for d in group], *sums)
 
     back = {}
-    last_sources = [received[late]]
-    for targets in ([late], middle, [0]):
-        prepare = len(last_sources) == 1
+    last_sources = [received[d] for d in late]
+    for number, targets in enumerate((masks[-1:], masks[:-1], [0])):
+        prepare = number == 0
         results = local_call(
-            functools.partial(translate_kernel, peers, frame, late, tuple(targets)),
-            ([array(own * frame, LANES)] * 2 if prepare else []) + [chunk] * len(targets),
+            functools.partial(translate_kernel, peers, frame, tuple(late), tuple(targets)),
+            ([array(len(late) * own * frame, LANES)] * 2 if prepare else []) + [chunk] * len(targets),
             [SMEM] + [VMEM] * (3 + len(last_sources)),
             [buffer(TOGETHER, frame, LANES)] * 2,
             20,
@@ -722,7 +732,7 @@
         flops=4_000_000_000,
         bytes_accessed=12_000_000,
         out_specs=[HBM, VMEM],
-    )(parents, child_octant, incoming, phases, gather)
+    )(parents, octants, incoming, phases, gather)
 
     out = local_call(
         finish_kernel,

time: 45.2 us -> 40.7 us (0.900)
  waiting for transfers between devices: 11.1 us -> 7.27 us
  starting transfers between devices: 14.8 us -> 13.2 us
  Pallas kernels: 18.9 us -> 19.8 us
    ppermute x6, waiting for transfers between devices: 8.53 us -> 4.71 us  [exchanged(): return lax.ppermute(values, axis, [(i, i ^ mask) for i in range(size)])]
    pallas_call x4 -> x5, Pallas kernels: 5.17 us -> 7.17 us  [the longest x3 4.47 us: on_device_exchange(): local_call(functools.partial(translate_kernel, peers, frame, tuple(late),...]
    ppermute x4, starting transfers between devices: 7.69 us -> 6.12 us  [shifted(): lax.ppermute(values, axis, [(i, (i + by) % size) for i in range(size)])]
    pallas_call x2, Pallas kernels: 4.9 us -> 3.75 us  [on_device_exchange(): local_call(functools.partial(gather_kernel, peers, frame, tuple(group)),...]
  transfers between devices with their start and end apart: 10 -> 10, of which waited for: 6 -> 5; matrix products, arithmetic and copies ran while one was open for 0% -> 0% of each run, Pallas kernels for 28% -> 33%
where the time goes in v4:
time: 40.7 us; the launch traced here: 40.5 us
  Pallas kernels  19.8 us (49%)
  starting transfers between devices  13.2 us (32%)
  waiting for transfers between devices  7.27 us (18%)
    ppermute x6, starting transfers between devices, exchanged(): return lax.ppermute(values, axis, [(i, i ^ mask) for i in range(size)])  7.11 us
    ppermute x4, starting transfers between devices, shifted(): lax.ppermute(values, axis, [(i, (i + by) % size) for i in range(size)])  6.12 us
    ppermute x6, waiting for transfers between devices, exchanged(): return lax.ppermute(values, axis, [(i, i ^ mask) for i in range(size)])  4.71 us
    pallas_call x3, Pallas kernels, on_device_exchange(): local_call(functools.partial(translate_kernel, peers, frame, tuple(late),...  4.47 us
    pallas_call x2, Pallas kernels, on_device_exchange(): local_call(functools.partial(gather_kernel, peers, frame, tuple(group)),...  3.75 us
    pallas_call x1, Pallas kernels, on_device_exchange(): local_call(disaggregate_kernel, [array(pairs, azimuth_in, polar_in), arra...  3.26 us
    ppermute x4, waiting for transfers between devices, shifted(): lax.ppermute(values, axis, [(i, (i + by) % size) for i in range(size)])  2.56 us
    pallas_call x1, Pallas kernels, on_device_exchange(): local_call(functools.partial(main_kernel, peers), [array(2 * own * flat_r...  2.53 us
  transfers between devices with their start and end apart: 10, of which 5 were waited for; matrix products, arithmetic and copies ran while one was open for 0% of the time, Pallas kernels for 33%

profile of v4, /device:TPU:0, one launch (start us, length us, event | category | flops | bytes accessed | tf_op | source)
XLA Modules:
  0.0 40.5 jit_solution(7546573284198019017)
XLA Ops:
  0.0 1.2 %shard_map.94 = (f32[96,128]{1,0:T(8,128)S(1)}, f32[2,96,128]{2,1,0:T(8,128)S(1)}) custom-call(f32[96,32,128]{2,1,0:T(8,128)} %bitcast.17), custom_call_target="tpu_custom_call" | custom-call | flops 1000000 | bytes 1000000 | tf_op jit(solution)/shard_map/pallas_call | solution.py:610
  1.2 0.5 %collective-permute-start = (f32[96,128]{1,0:T(8,128)S(1)}, f32[96,128]{1,0:T(8,128)S(1)}, u32[]{:S(2)}, u32[]{:S(2)}) collective-permute-start(f32[96,128]{1,0:T(8,128)S(1)} %get-tuple-element.44), channel_id=1, source_target_pairs={{0,1},{1,2},{2,3},{3,4},{4,5},{5,6},{6,7},{7,0},{8,9},{9,10},{10,1... | collective-permute-start | bytes 147464 | tf_op jit(solution)/shard_map/ppermute | solution.py:563
  1.7 4.1 %collective-permute-start.1 = (f32[2,96,128]{2,1,0:T(8,128)S(1)}, f32[2,96,128]{2,1,0:T(8,128)S(1)}, u32[]{:S(2)}, u32[]{:S(2)}) collective-permute-start(f32[2,96,128]{2,1,0:T(8,128)S(1)} %get-tuple-element.45), channel_id=1, source_target_pairs={{0,7},{1,0},{2,1},{3,2},{4,3},{5,4},{6,5},{7,6},{8,15},{9,8},{10,9... | collective-permute-start | bytes 294920 | tf_op jit(solution)/shard_map/ppermute | solution.py:563
  5.8 1.5 %shard_map.91 = (f32[8,2,9,8,128]{4,3,2,1,0:T(8,128)S(1)}, f32[7,2,48,128]{3,2,1,0:T(8,128)S(1)}, f32[3072,128]{1,0:T(8,128)S(1)}, bf16[2,384,256]{2,1,0:T(8,128...) custom-call(s32[48]{0:T(128)} %refs_0_.1, f32[3072,128]{1,0:T(8,128)} %bitcast.18, ...), custom_call_target="tpu_custom_call" | custom-call | flops 50000000 | bytes 1000000 | tf_op jit(solution)/shard_map/pallas_call | solution.py:620
  7.4 0.0 copy-start.3
  7.4 0.0 copy-start.1
  7.4 0.0 copy-start.2
  7.4 0.0 copy-start.4
  7.4 2.5 %shard_map.92 = (f32[1152,128]{1,0:T(8,128)S(1)}, bf16[316,40,128]{2,1,0:T(8,128)(2,1)S(1)}) custom-call(s32[48]{0:T(128)S(1)} %bitcast.13, s32[48]{0:T(128)S(1)} %bitcast.15, f32[3072,128]{1,0:T(8,128)S(1)} %get-tuple-element.38.x_ref, bf16[316,144,128]{2,1,0:T(8,128)(2,1)} %bitcast.20, f32[8,2,9,8,128]{4,3,2,1,0:T(8,128)S(1)} %get-tuple-element.39.phase_ref, ...), custom_call_target="tpu_custom_call" | custom-call | flops 4000000000 | bytes 12000000 | tf_op jit(solution)/shard_map/pallas_call | solution.py:638
  9.9 0.0 collective-permute-done.before_ref
  10.0 0.5 %shard_map.95 = (f32[288,128]{1,0:T(8,128)S(1)}, f32[288,128]{1,0:T(8,128)S(1)}, f32[288,128]{1,0:T(8,128)S(1)}, f32[288,128]{1,0:T(8,128)S(1)}) custom-call(s32[1,48]{1,0:T(1,128)S(1)} %copy-done.3, f32[96,128]{1,0:T(8,128)S(1)} %collective-permute-done.before_ref, f32[2,96,128]{2,1,0:T(8,128)S(1)} %collective-permute-done.1.after_ref, ...), custom_call_target="tpu_custom_call" | custom-call | flops 1000000 | bytes 1000000 | tf_op jit(solution)/shard_map/pallas_call | solution.py:657
  10.5 2.0 %collective-permute-start.2 = (f32[288,128]{1,0:T(8,128)S(1)}, f32[288,128]{1,0:T(8,128)S(1)}, u32[]{:S(2)}, u32[]{:S(2)}) collective-permute-start(f32[288,128]{1,0:T(8,128)S(1)} %get-tuple-element.47), channel_id=1, source_target_pairs={{0,8},{8,0},{16,24},{24,16},{1,9},{9,1},{17,25},{25,17},{2,10},{10... | collective-permute-start | bytes 442376 | tf_op jit(solution)/shard_map/ppermute | solution.py:568
  12.5 1.5 %collective-permute-start.3 = (f32[288,128]{1,0:T(8,128)S(1)}, f32[288,128]{1,0:T(8,128)S(1)}, u32[]{:S(2)}, u32[]{:S(2)}) collective-permute-start(f32[288,128]{1,0:T(8,128)S(1)} %get-tuple-element.53), channel_id=1, source_target_pairs={{0,16},{8,24},{16,0},{24,8},{1,17},{9,25},{17,1},{25,9},{2,18},{10... | collective-permute-start | bytes 442376 | tf_op jit(solution)/shard_map/ppermute | solution.py:568
  14.0 0.0 collective-permute-start.4
  14.0 1.1 %shard_map.93 = (f32[12680,128]{1,0:T(8,128)S(1)}, s32[32,32]{1,0:T(8,128)S(1)}) custom-call(s32[32,31]{1,0:T(8,128)S(1)} %copy-done.1, s32[32,31]{1,0:T(8,128)S(1)} %copy-done.2, s32[1,32]{1,0:T(1,128)S(1)} %bitcast.12, bf16[316,40,128]{2,1,0:T(8,128)(2,1)S(1)} %get-tuple-element.41.table_ref), custom_call_target="tpu_custom_call" | custom-call | flops 50000000 | bytes 8000000 | tf_op jit(solution)/shard_map/pallas_call | solution.py:669
  15.1 1.8 %shard_map.96 = (f32[1280,128]{1,0:T(8,128)S(1)}, f32[1280,128]{1,0:T(8,128)S(1)}) custom-call(s32[32,32]{1,0:T(8,128)S(1)} %get-tuple-element.42.operator_ref, f32[12680,128]{1,0:T(8,128)S(1)} %get-tuple-element.43.wide_ref, f32[288,128]{1,0:T(8,128)S(1)} %get-tuple-element.48.rest_0_), custom_call_target="tpu_custom_call" | custom-call | flops 40000000 | bytes 4000000 | tf_op jit(solution)/shard_map/pallas_call | solution.py:681
  16.9 1.9 %shard_map.97 = (f32[1280,128]{1,0:T(8,128)S(1)}, f32[1280,128]{1,0:T(8,128)S(1)}) custom-call(s32[32,32]{1,0:T(8,128)S(1)} %get-tuple-element.42.operator_ref, f32[12680,128]{1,0:T(8,128)S(1)} %get-tuple-element.43.wide_ref, f32[288,128]{1,0:T(8,128)S(1)} %collective-permute-done.2.rest_0_, f32[1280,128]{1,0:T(8,128)S(1)} %get-tuple-element.49.rest_1_, ...), custom_call_target="tpu_custom_call" | custom-call | flops 40000000 | bytes 4000000 | tf_op jit(solution)/shard_map/pallas_call | solution.py:681
  18.9 1.5 %collective-permute-done.3.rest_0_ = f32[288,128]{1,0:T(8,128)S(1)} collective-permute-done((f32[288,128]{1,0:T(8,128)S(1)}, f32[288,128]{1,0:T(8,128)S(1)}, u32[]{:S(2)}, u32[]{:S(2)}) %collective-permute-start.3) | collective-permute-done | bytes 147488 | tf_op jit(solution)/shard_map/ppermute | solution.py:568
  20.4 1.4 %shard_map.98 = (f32[640,128]{1,0:T(8,128)S(1)}, f32[640,128]{1,0:T(8,128)S(1)}, f32[288,128]{1,0:T(8,128)S(1)}) custom-call(s32[32,32]{1,0:T(8,128)S(1)} %get-tuple-element.42.operator_ref, f32[12680,128]{1,0:T(8,128)S(1)} %get-tuple-element.43.wide_ref, f32[1280,128]{1,0:T(8,128)S(1)} %get-tuple-element.51.real_sum, ...), custom_call_target="tpu_custom_call" | custom-call | flops 10000000 | bytes 2000000 | tf_op jit(solution)/shard_map/pallas_call | solution.py:695
  21.8 1.8 %shard_map.100 = (f32[288,128]{1,0:T(8,128)S(1)}, f32[288,128]{1,0:T(8,128)S(1)}) custom-call(s32[32,32]{1,0:T(8,128)S(1)} %get-tuple-element.42.operator_ref, f32[12680,128]{1,0:T(8,128)S(1)} %get-tuple-element.43.wide_ref, f32[1280,128]{1,0:T(8,128)S(1)} %get-tuple-element.51.real_sum, f32[1280,128]{1,0:T(8,128)S(1)} %get-tuple-element.52.imag_sum, ...), custom_call_target="tpu_custom_call" | custom-call | flops 20000000 | bytes 4000000 | tf_op jit(solution)/shard_map/pallas_call | solution.py:695
  23.6 0.5 %collective-permute-start.5 = (f32[288,128]{1,0:T(8,128)S(1)}, f32[288,128]{1,0:T(8,128)S(1)}, u32[]{:S(2)}, u32[]{:S(2)}) collective-permute-start(f32[288,128]{1,0:T(8,128)S(1)} %get-tuple-element.57), channel_id=1, source_target_pairs={{0,8},{8,0},{16,24},{24,16},{1,9},{9,1},{17,25},{25,17},{2,10},{10... | collective-permute-start | bytes 442376 | tf_op jit(solution)/shard_map/ppermute | solution.py:568
  24.0 1.5 %collective-permute-start.6 = (f32[288,128]{1,0:T(8,128)S(1)}, f32[288,128]{1,0:T(8,128)S(1)}, u32[]{:S(2)}, u32[]{:S(2)}) collective-permute-start(f32[288,128]{1,0:T(8,128)S(1)} %get-tuple-element.58), channel_id=1, source_target_pairs={{0,16},{8,24},{16,0},{24,8},{1,17},{9,25},{17,1},{25,9},{2,18},{10... | collective-permute-start | bytes 442376 | tf_op jit(solution)/shard_map/ppermute | solution.py:568
  25.6 1.6 %collective-permute-start.7 = (f32[288,128]{1,0:T(8,128)S(1)}, f32[288,128]{1,0:T(8,128)S(1)}, u32[]{:S(2)}, u32[]{:S(2)}) collective-permute-start(f32[288,128]{1,0:T(8,128)S(1)} %get-tuple-element.59), channel_id=1, source_target_pairs={{0,24},{8,16},{16,8},{24,0},{1,25},{9,17},{17,9},{25,1},{2,26},{10... | collective-permute-start | bytes 442376 | tf_op jit(solution)/shard_map/ppermute | solution.py:568
  27.1 1.3 %shard_map.99.rest_0_ = f32[288,128]{1,0:T(8,128)S(1)} custom-call(s32[32,32]{1,0:T(8,128)S(1)} %get-tuple-element.42.operator_ref, f32[12680,128]{1,0:T(8,128)S(1)} %get-tuple-element.43.wide_ref, f32[1280,128]{1,0:T(8,128)S(1)} %get-tuple-element.51.real_sum, f32[1280,128]{1,0:T(8,128)S(1)} %get-tuple-element.52.imag_sum, ...), custom_call_target="tpu_custom_call" | custom-call | flops 10000000 | bytes 2000000 | tf_op jit(solution)/shard_map/pallas_call | solution.py:695
  28.5 0.4 %collective-permute-done.5.rest_1_ = f32[288,128]{1,0:T(8,128)S(1)} collective-permute-done((f32[288,128]{1,0:T(8,128)S(1)}, f32[288,128]{1,0:T(8,128)S(1)}, u32[]{:S(2)}, u32[]{:S(2)}) %collective-permute-start.5) | collective-permute-done | bytes 147488 | tf_op jit(solution)/shard_map/ppermute | solution.py:568
  28.9 0.5 %collective-permute-done.6.rest_2_ = f32[288,128]{1,0:T(8,128)S(1)} collective-permute-done((f32[288,128]{1,0:T(8,128)S(1)}, f32[288,128]{1,0:T(8,128)S(1)}, u32[]{:S(2)}, u32[]{:S(2)}) %collective-permute-start.6) | collective-permute-done | bytes 147488 | tf_op jit(solution)/shard_map/ppermute | solution.py:568
  29.3 2.3 %collective-permute-done.7.rest_3_ = f32[288,128]{1,0:T(8,128)S(1)} collective-permute-done((f32[288,128]{1,0:T(8,128)S(1)}, f32[288,128]{1,0:T(8,128)S(1)}, u32[]{:S(2)}, u32[]{:S(2)}) %collective-permute-start.7) | collective-permute-done | bytes 147488 | tf_op jit(solution)/shard_map/ppermute | solution.py:568
  31.6 0.6 %shard_map.101 = (f32[16,9,8,128]{3,2,1,0:T(8,128)S(1)}, f32[2,96,128]{2,1,0:T(8,128)S(1)}, f32[96,128]{1,0:T(8,128)S(1)}) custom-call(s32[1,48]{1,0:T(1,128)S(1)} %copy-done.3, f32[7,2,48,128]{3,2,1,0:T(8,128)S(1)} %get-tuple-element.37.edge_phase_ref, bf16[2,256,256]{2,1,0:T(8,128)(2,1)S(1)} %copy-done, f32[288,128]{1,0:T(8,128)S(1)} %shard_map.99.rest_0_, ...), custom_call_target="tpu_custom_call" | custom-call | flops 1000000 | bytes 1000000 | tf_op jit(solution)/shard_map/pallas_call | solution.py:709
  32.2 1.5 %collective-permute-start.9 = (f32[96,128]{1,0:T(8,128)S(1)}, f32[96,128]{1,0:T(8,128)S(1)}, u32[]{:S(2)}, u32[]{:S(2)}) collective-permute-start(f32[96,128]{1,0:T(8,128)S(1)} %get-tuple-element.63), channel_id=1, source_target_pairs={{0,7},{1,0},{2,1},{3,2},{4,3},{5,4},{6,5},{7,6},{8,15},{9,8},{10,9... | collective-permute-start | bytes 147464 | tf_op jit(solution)/shard_map/ppermute | solution.py:563
  33.7 3.3 %shard_map.102 = (f32[96,32,128]{2,1,0:T(8,128)}, f32[2,96,8,128]{3,2,1,0:T(8,128)S(1)}) custom-call(s32[48]{0:T(128)S(1)} %bitcast.14, s32[48]{0:T(128)S(1)} %bitcast.16, f32[16,9,8,128]{3,2,1,0:T(8,128)S(1)} %get-tuple-element.60.incoming_ref, f32[8,2,9,8,128]{4,3,2,1,0:T(8,128)S(1)} %get-tuple-element.39.phase_ref, bf16[2,256,256]{2,1,0:T(8,128)(2,1)S(1)} %copy-done), custom_call_target="tpu_custom_call" | custom-call | flops 4000000000 | bytes 12000000 | tf_op jit(solution)/shard_map/pallas_call | solution.py:720
  37.0 2.6 %collective-permute-done.8.before_ref = f32[2,96,128]{2,1,0:T(8,128)S(1)} collective-permute-done((f32[2,96,128]{2,1,0:T(8,128)S(1)}, f32[2,96,128]{2,1,0:T(8,128)S(1)}, u32[]{:S(2)}, u32[]{:S(2)}) %collective-permute-start.8) | collective-permute-done | bytes 98336 | tf_op jit(solution)/shard_map/ppermute | solution.py:563
  39.5 1.0 %shard_map.103 = f32[96,32,128]{2,1,0:T(8,128)} custom-call(f32[2,96,8,128]{3,2,1,0:T(8,128)S(1)} %get-tuple-element.61.edge_ref, f32[2,96,128]{2,1,0:T(8,128)S(1)} %collective-permute-done.8.before_ref, f32[96,128]{1,0:T(8,128)S(1)} %collective-permute-done.9.after_ref, f32[96,32,128]{2,1,0:T(8,128)} %get-tuple-element.64.part_ref), custom_call_target="tpu_custom_call", output_to_operand_aliasing={{}: (3, {})} | custom-call | flops 1000000 | bytes 1000000 | tf_op jit(solution)/shard_map/pallas_call | solution.py:737
  (11 shorter events, 0.0 us)
Async XLA Ops:
  1.2 8.8 %collective-permute-start = (f32[96,128]{1,0:T(8,128)S(1)}, f32[96,128]{1,0:T(8,128)S(1)}, u32[]{:S(2)}, u32[]{:S(2)}) collective-permute-start(f32[96,128]{1,0:T(8,128)S(1)} %get-tuple-element.44), channel_id=1, source_target_pairs={{0,1},{1,2},{2,3},{3,4},{4,5},{5,6},{6,7},{7,0},{8,9},{9,10},{10,1... | collective-permute-start | bytes 147464 | tf_op jit(solution)/shard_map/ppermute | solution.py:563
  1.7 8.2 %collective-permute-start.1 = (f32[2,96,128]{2,1,0:T(8,128)S(1)}, f32[2,96,128]{2,1,0:T(8,128)S(1)}, u32[]{:S(2)}, u32[]{:S(2)}) collective-permute-start(f32[2,96,128]{2,1,0:T(8,128)S(1)} %get-tuple-element.45), channel_id=1, source_target_pairs={{0,7},{1,0},{2,1},{3,2},{4,3},{5,4},{6,5},{7,6},{8,15},{9,8},{10,9... | collective-permute-start | bytes 294920 | tf_op jit(solution)/shard_map/ppermute | solution.py:563
  7.4 2.6 %copy-start.3 = (s32[1,48]{1,0:T(1,128)S(1)}, s32[1,48]{1,0:T(1,128)}, u32[]{:S(2)}) copy-start(s32[1,48]{1,0:T(1,128)} %parents_ref.3) | copy-start | bytes 580
  7.4 6.7 %copy-start.1 = (s32[32,31]{1,0:T(8,128)S(1)}, s32[32,31]{1,0:T(8,128)}, u32[]{:S(2)}) copy-start(s32[32,31]{1,0:T(8,128)} %source_ref.1) | copy-start | bytes 11908
  7.4 6.7 %copy-start.2 = (s32[32,31]{1,0:T(8,128)S(1)}, s32[32,31]{1,0:T(8,128)}, u32[]{:S(2)}) copy-start(s32[32,31]{1,0:T(8,128)} %offset_ref.1) | copy-start | bytes 11908
  7.4 6.6 %copy-start.4 = (s32[32]{0:T(128)S(1)}, s32[32]{0:T(128)}, u32[]{:S(2)}) copy-start(s32[32]{0:T(128)} %param.15) | copy-start | bytes 388
  10.5 6.5 %collective-permute-start.2 = (f32[288,128]{1,0:T(8,128)S(1)}, f32[288,128]{1,0:T(8,128)S(1)}, u32[]{:S(2)}, u32[]{:S(2)}) collective-permute-start(f32[288,128]{1,0:T(8,128)S(1)} %get-tuple-element.47), channel_id=1, source_target_pairs={{0,8},{8,0},{16,24},{24,16},{1,9},{9,1},{17,25},{25,17},{2,10},{10... | collective-permute-start | bytes 442376 | tf_op jit(solution)/shard_map/ppermute | solution.py:568
  12.5 8.0 %collective-permute-start.3 = (f32[288,128]{1,0:T(8,128)S(1)}, f32[288,128]{1,0:T(8,128)S(1)}, u32[]{:S(2)}, u32[]{:S(2)}) collective-permute-start(f32[288,128]{1,0:T(8,128)S(1)} %get-tuple-element.53), channel_id=1, source_target_pairs={{0,16},{8,24},{16,0},{24,8},{1,17},{9,25},{17,1},{25,9},{2,18},{10... | collective-permute-start | bytes 442376 | tf_op jit(solution)/shard_map/ppermute | solution.py:568
  14.0 6.4 %collective-permute-start.4 = (f32[288,128]{1,0:T(8,128)S(1)}, f32[288,128]{1,0:T(8,128)S(1)}, u32[]{:S(2)}, u32[]{:S(2)}) collective-permute-start(f32[288,128]{1,0:T(8,128)S(1)} %get-tuple-element.54), channel_id=1, source_target_pairs={{0,24},{8,16},{16,8},{24,0},{1,25},{9,17},{17,9},{25,1},{2,26},{10... | collective-permute-start | bytes 442376 | tf_op jit(solution)/shard_map/ppermute | solution.py:568
  23.6 5.3 %collective-permute-start.5 = (f32[288,128]{1,0:T(8,128)S(1)}, f32[288,128]{1,0:T(8,128)S(1)}, u32[]{:S(2)}, u32[]{:S(2)}) collective-permute-start(f32[288,128]{1,0:T(8,128)S(1)} %get-tuple-element.57), channel_id=1, source_target_pairs={{0,8},{8,0},{16,24},{24,16},{1,9},{9,1},{17,25},{25,17},{2,10},{10... | collective-permute-start | bytes 442376 | tf_op jit(solution)/shard_map/ppermute | solution.py:568
  24.0 5.3 %collective-permute-start.6 = (f32[288,128]{1,0:T(8,128)S(1)}, f32[288,128]{1,0:T(8,128)S(1)}, u32[]{:S(2)}, u32[]{:S(2)}) collective-permute-start(f32[288,128]{1,0:T(8,128)S(1)} %get-tuple-element.58), channel_id=1, source_target_pairs={{0,16},{8,24},{16,0},{24,8},{1,17},{9,25},{17,1},{25,9},{2,18},{10... | collective-permute-start | bytes 442376 | tf_op jit(solution)/shard_map/ppermute | solution.py:568
  25.6 6.0 %copy-start = (bf16[2,256,256]{2,1,0:T(8,128)(2,1)S(1)}, bf16[2,256,256]{2,1,0:T(8,128)(2,1)}, u32[]{:S(2)}) copy-start(bf16[2,256,256]{2,1,0:T(8,128)(2,1)} %constant.5.clone.gather_ref) | copy-start | bytes 786436
  25.6 6.0 %collective-permute-start.7 = (f32[288,128]{1,0:T(8,128)S(1)}, f32[288,128]{1,0:T(8,128)S(1)}, u32[]{:S(2)}, u32[]{:S(2)}) collective-permute-start(f32[288,128]{1,0:T(8,128)S(1)} %get-tuple-element.59), channel_id=1, source_target_pairs={{0,24},{8,16},{16,8},{24,0},{1,25},{9,17},{17,9},{25,1},{2,26},{10... | collective-permute-start | bytes 442376 | tf_op jit(solution)/shard_map/ppermute | solution.py:568
  32.2 4.8 %collective-permute-start.9 = (f32[96,128]{1,0:T(8,128)S(1)}, f32[96,128]{1,0:T(8,128)S(1)}, u32[]{:S(2)}, u32[]{:S(2)}) collective-permute-start(f32[96,128]{1,0:T(8,128)S(1)} %get-tuple-element.63), channel_id=1, source_target_pairs={{0,7},{1,0},{2,1},{3,2},{4,3},{5,4},{6,5},{7,6},{8,15},{9,8},{10,9... | collective-permute-start | bytes 147464 | tf_op jit(solution)/shard_map/ppermute | solution.py:563
  33.7 5.8 %collective-permute-start.8 = (f32[2,96,128]{2,1,0:T(8,128)S(1)}, f32[2,96,128]{2,1,0:T(8,128)S(1)}, u32[]{:S(2)}, u32[]{:S(2)}) collective-permute-start(f32[2,96,128]{2,1,0:T(8,128)S(1)} %get-tuple-element.62), channel_id=1, source_target_pairs={{0,1},{1,2},{2,3},{3,4},{4,5},{5,6},{6,7},{7,0},{8,9},{9,10},{10,1... | collective-permute-start | bytes 294920 | tf_op jit(solution)/shard_map/ppermute | solution.py:563

commit v5 on v4

--- a/solution.py
+++ b/solution.py
@@ -151,7 +151,19 @@
     return [(w, 0) for w in (1, 2, 3, 4)] + [(w, periods - 1) for w in (6, 7, 8)]
 
 
-def rows_kernel(x_ref, last_ref, first_ref, low, high, sems):
+def by_parity(even, odd):
+    parity = lax.rem(lax.axis_index("dir"), 2)
+    pl.when(parity == 0)(even)
+    pl.when(parity == 1)(odd)
+
+
+def from_sides(far_ref, near_ref):
+    is_even = lax.rem(lax.axis_index("dir"), 2) == 0
+    far, near = far_ref[...], near_ref[...]
+    return jnp.where(is_even, far, near), jnp.where(is_even, near, far)
+
+
+def rows_kernel(x_ref, far_ref, near_ref, low, high, sems):
     pairs, azimuth_in, _ = x_ref.shape
     low_copy = pltpu.make_async_copy(x_ref.at[:, pl.ds(0, TILE), :], low, sems.at[0])
     high_copy = pltpu.make_async_copy(x_ref.at[:, pl.ds(azimuth_in - TILE, TILE), :], high, sems.at[1])
@@ -160,13 +172,19 @@
     low_copy.wait()
     high_copy.wait()
     low_rows, high_rows = (ref.reshape(pairs * TILE, LANES) for ref in (low, high))
-    for part in range(2):
-        for k in range(0, pairs // 2, 8):
-            target = slice(part * (pairs // 2) + k, part * (pairs // 2) + k + 8)
-            base = (2 * k + part) * TILE
-            for i in range(2):
-                first_ref[i, target] = low_rows[pl.ds(base + i, 8, stride=2 * TILE), :]
-            last_ref[target] = high_rows[pl.ds(base + TILE - 1, 8, stride=2 * TILE), :]
+
+    def fill(first_ref, last_ref):
+        for part in range(2):
+            for k in range(0, pairs // 2, 8):
+                target = slice(part * (pairs // 2) + k, part * (pairs // 2) + k + 8)
+                base = (2 * k + part) * TILE
+                for i in range(2):
+                    first_ref[i, target] = low_rows[pl.ds(base + i, 8, stride=2 * TILE), :]
+                last = high_rows[pl.ds(base + TILE - 1, 8, stride=2 * TILE), :]
+                for i in range(2):
+                    last_ref[i, target] = last
+
+    by_parity(lambda: fill(far_ref, near_ref), lambda: fill(near_ref, far_ref))
 
 
 def phase_kernel(*refs):
@@ -288,16 +306,17 @@
 
 
 def fix_kernel(
-    peers, own, parents_ref, before_ref, after_ref, flat_ref, edge_phase_ref, spread_ref, *rest
+    peers, own, parents_ref, far_ref, near_ref, flat_ref, edge_phase_ref, spread_ref, *rest
 ):
     outs, (fixed,) = rest[:peers], rest[peers:]
-    pairs = before_ref.shape[0]
+    pairs = far_ref.shape[1]
     children = pairs // 2
     chunk_rows = outs[0].shape[0]
     share = chunk_rows // (2 * own)
     periods = share * peers // ROWS_PER_PERIOD
     fixed[...] = flat_ref[...]
-    left, right = before_ref[...], [after_ref[0], after_ref[1]]
+    before, right = from_sides(far_ref, near_ref)
+    left = before[0]
     a, b = TAPS_A, TAPS_B
     even = jnp.concatenate([b[0] * left, a[3] * right[0] + a[4] * right[1]], axis=0)
     odd = jnp.concatenate([a[0] * left, b[3] * right[0] + b[4] * right[1]], axis=0)
@@ -440,10 +459,10 @@
 
 def edge_kernel(peers, parents_ref, edge_phase_ref, gather_ref, *rest):
     chunks = rest[:peers]
-    incoming_ref, next_ref, prev_ref, flat = rest[peers:]
+    incoming_ref, far_ref, near_ref, flat = rest[peers:]
     own2, _, periods, _ = incoming_ref.shape
     own = own2 // 2
-    pairs = prev_ref.shape[0]
+    pairs = far_ref.shape[1]
     flat_rows = ROWS_PER_PERIOD * periods
     share = flat_rows // peers
     me = lax.axis_index("clus")
@@ -469,9 +488,14 @@
     even = gather_dot(*split(even), gather_ref, 0)
     odd = gather_dot(*split(odd), gather_ref, 1)
     a, b = TAPS_A, TAPS_B
-    prev_ref[...] = a[0] * odd[:pairs] + b[0] * even[:pairs]
-    next_ref[0] = a[3] * even[pairs:] + b[3] * odd[pairs:]
-    next_ref[1] = a[4] * even[pairs:] + b[4] * odd[pairs:]
+
+    def fill(prev_ref, next_ref):
+        below = a[0] * odd[:pairs] + b[0] * even[:pairs]
+        for i in range(2):
+            prev_ref[i] = below
+            next_ref[i] = a[3 + i] * even[pairs:] + b[3 + i] * odd[pairs:]
+
+    by_parity(lambda: fill(far_ref, near_ref), lambda: fill(near_ref, far_ref))
     for gp in range(own2):
         for w in range(ROWS_PER_PERIOD):
             incoming_ref[gp, w] = flat[pl.ds(gp * flat_rows + w, periods, stride=ROWS_PER_PERIOD), :]
@@ -537,20 +561,21 @@
         written(block).wait()
 
 
-def finish_kernel(edge_ref, before_ref, after_ref, part_ref, out_ref, tiles, sems):
+def finish_kernel(edge_ref, far_ref, near_ref, part_ref, out_ref, tiles, sems):
     pairs, azimuth_in, _ = out_ref.shape
     tiles[...] = edge_ref[...]
     flat = tiles.reshape(2 * pairs * TILE, LANES)
-    ends = ((0, 0, before_ref.at[0]), (0, 1, before_ref.at[1]), (1, TILE - 1, after_ref))
+    before, after = from_sides(far_ref, near_ref)
+    ends = ((0, 0, before[0]), (0, 1, before[1]), (1, TILE - 1, after[0]))
     copies = []
     for i, start in enumerate((0, azimuth_in - TILE)):
-        for end, row, values_ref in ends:
+        for end, row, values in ends:
             if end == i:
                 for part in range(2):
                     for k in range(0, pairs // 2, 8):
                         source = slice(part * (pairs // 2) + k, part * (pairs // 2) + k + 8)
                         rows = pl.ds((i * pairs + 2 * k + part) * TILE + row, 8, stride=2 * TILE)
-                        flat[rows, :] = flat[rows, :] + values_ref[source, :]
+                        flat[rows, :] = flat[rows, :] + values[source]
         copy = pltpu.make_async_copy(tiles.at[i], out_ref.at[:, pl.ds(start, TILE), :], sems.at[i])
         copy.start()
         copies.append(copy)
@@ -558,9 +583,9 @@
         copy.wait()
 
 
-def shifted(values, axis, by):
+def swapped(values, axis, first):
     size = lax.axis_size(axis)
-    return lax.ppermute(values, axis, [(i, (i + by) % size) for i in range(size)])
+    return lax.ppermute(values, axis, [(i, (((i - first) ^ 1) + first) % size) for i in range(size)])
 
 
 def exchanged(values, axis, mask):
@@ -607,15 +632,12 @@
     edges = len(edge_rows(periods))
     even, odd = polar_blocks()
     spread = jnp.asarray(np.stack([np.concatenate([h, h, l]) for h, l in (split_np(even), split_np(odd))]))
-    last, first = local_call(
-        rows_kernel,
-        [array(pairs, polar_in), array(2, pairs, polar_in)],
-        [HBM],
-        [buffer(pairs, TILE, polar_in)] * 2 + [pltpu.SemaphoreType.DMA((2,))],
-        8,
+    edge = array(2, pairs, polar_in)
+    to_far, to_near = local_call(
+        rows_kernel, [edge, edge], [HBM], [buffer(pairs, TILE, polar_in)] * 2 + [pltpu.SemaphoreType.DMA((2,))], 8
     )(in_hbm(child_patterns.reshape(pairs, azimuth_in, polar_in)))
-    after = shifted(first, "dir", -1)
-    before = shifted(last, "dir", 1)
+    from_far = swapped(to_far, "dir", 1)
+    from_near = swapped(to_near, "dir", 0)
     copied = (child_patterns.reshape(pairs * azimuth_in, polar_in), spread, child_parent, child_octant.reshape(1, children))
     phases, edge_phases, held, spread, parents, octants = local_call(
         phase_kernel,
@@ -656,7 +678,7 @@
     chunk = array(2 * own * share, LANES)
     sent = local_call(
         functools.partial(fix_kernel, peers, own), [chunk] * peers, [VMEM] * 6, [buffer(2 * own * flat_rows, LANES)], 8
-    )(child_parent, before, after, flat, edge_phases, spread)
+    )(child_parent, from_far, from_near, flat, edge_phases, spread)
 
     masks = sorted(range(1, peers), key=lambda d: bin(d).count("1"))
     early, late = masks[:1], masks[1:]
@@ -706,16 +728,16 @@
         for d, result in zip(targets, results):
             back[d] = exchanged(result, "clus", d) if d else result
 
-    incoming, to_next, to_prev = local_call(
+    incoming, to_far, to_near = local_call(
         functools.partial(edge_kernel, peers),
-        [array(2 * own, ROWS_PER_PERIOD, periods, LANES), array(2, pairs, polar_in), array(pairs, polar_in)],
+        [array(2 * own, ROWS_PER_PERIOD, periods, LANES), edge, edge],
         [VMEM] * (3 + peers),
         [buffer(2 * own * flat_rows, LANES)],
         8,
     )(child_parent, edge_phases, gather, *[back[d] for d in range(peers)])
 
-    from_before = shifted(to_next, "dir", 1)
-    from_after = shifted(to_prev, "dir", -1)
+    from_far = swapped(to_far, "dir", 1)
+    from_near = swapped(to_near, "dir", 0)
 
     inner, edge_tiles = local_call(
         disaggregate_kernel,
@@ -742,7 +764,7 @@
         8,
         out_specs=HBM,
         aliases={3: 0},
-    )(edge_tiles, from_before, from_after, in_hbm(inner))
+    )(edge_tiles, from_far, from_near, in_hbm(inner))
     return out.reshape(child_patterns.shape)
 
 
@@ -902,6 +924,7 @@
             and flat_rows % peers == 0
             and peers & (peers - 1) == 0
             and peers > 2
+            and lax.axis_size("dir") % 2 == 0
             and children % BLOCK == 0
         )
         plan = on_device_exchange if fits else on_device_gather

time: 40.7 us -> 41.5 us (1.020)
  waiting for transfers between devices: 7.27 us -> 8.66 us
  starting transfers between devices: 13.2 us -> 12.6 us
    ppermute x6, waiting for transfers between devices: 4.71 us -> 6.96 us  [exchanged(): return lax.ppermute(values, axis, [(i, i ^ mask) for i in range(size)])]
    ppermute x4, waiting for transfers between devices: 2.56 us -> 1.7 us  [swapped(): lax.ppermute(values, axis, [(i, ((i - first ^ 1) + first) % size) for i i...]
    ppermute x4, starting transfers between devices: 6.12 us -> 5.52 us  [swapped(): lax.ppermute(values, axis, [(i, ((i - first ^ 1) + first) % size) for i i...]
where the time goes in v5:
time: 41.5 us; the launch traced here: 41.3 us
  Pallas kernels  19.9 us (48%)
  starting transfers between devices  12.6 us (30%)
  waiting for transfers between devices  8.66 us (21%)
    ppermute x6, starting transfers between devices, exchanged(): return lax.ppermute(values, axis, [(i, i ^ mask) for i in range(size)])  7.11 us
    ppermute x6, waiting for transfers between devices, exchanged(): return lax.ppermute(values, axis, [(i, i ^ mask) for i in range(size)])  6.96 us
    ppermute x4, starting transfers between devices, swapped(): lax.ppermute(values, axis, [(i, ((i - first ^ 1) + first) % size) for i i...  5.52 us
    pallas_call x3, Pallas kernels, on_device_exchange(): local_call(functools.partial(translate_kernel, peers, frame, tuple(late),...  4.47 us
    pallas_call x2, Pallas kernels, on_device_exchange(): local_call(functools.partial(gather_kernel, peers, frame, tuple(group)),...  3.75 us
    pallas_call x1, Pallas kernels, on_device_exchange(): local_call(disaggregate_kernel, [array(pairs, azimuth_in, polar_in), arra...  3.27 us
    pallas_call x1, Pallas kernels, on_device_exchange(): local_call(functools.partial(main_kernel, peers), [array(2 * own * flat_r...  2.55 us
    ppermute x4, waiting for transfers between devices, swapped(): lax.ppermute(values, axis, [(i, ((i - first ^ 1) + first) % size) for i i...  1.7 us
  transfers between devices with their start and end apart: 10, of which 5 were waited for; matrix products, arithmetic and copies ran while one was open for 0% of the time, Pallas kernels for 33%

profile of v5, /device:TPU:0, one launch (start us, length us, event | category | flops | bytes accessed | tf_op | source)
XLA Modules:
  0.0 41.3 jit_solution(16237647595211874193)
XLA Ops:
  0.0 1.2 %shard_map.94 = (f32[2,96,128]{2,1,0:T(8,128)S(1)}, f32[2,96,128]{2,1,0:T(8,128)S(1)}) custom-call(f32[96,32,128]{2,1,0:T(8,128)} %bitcast.17), custom_call_target="tpu_custom_call" | custom-call | flops 1000000 | bytes 1000000 | tf_op jit(solution)/shard_map/pallas_call | solution.py:636
  1.2 4.6 %collective-permute-start = (f32[2,96,128]{2,1,0:T(8,128)S(1)}, f32[2,96,128]{2,1,0:T(8,128)S(1)}, u32[]{:S(2)}, u32[]{:S(2)}) collective-permute-start(f32[2,96,128]{2,1,0:T(8,128)S(1)} %get-tuple-element.44), channel_id=1, source_target_pairs={{0,7},{1,2},{2,1},{3,4},{4,3},{5,6},{6,5},{7,0},{8,15},{9,10},{10,... | collective-permute-start | bytes 294920 | tf_op jit(solution)/shard_map/ppermute | solution.py:588
  5.8 0.0 collective-permute-start.1
  5.8 1.5 %shard_map.91 = (f32[8,2,9,8,128]{4,3,2,1,0:T(8,128)S(1)}, f32[7,2,48,128]{3,2,1,0:T(8,128)S(1)}, f32[3072,128]{1,0:T(8,128)S(1)}, bf16[2,384,256]{2,1,0:T(8,128...) custom-call(s32[48]{0:T(128)} %refs_0_.1, f32[3072,128]{1,0:T(8,128)} %bitcast.18, ...), custom_call_target="tpu_custom_call" | custom-call | flops 50000000 | bytes 1000000 | tf_op jit(solution)/shard_map/pallas_call | solution.py:642
  7.3 0.0 copy-start.3
  7.3 0.0 copy-start.1
  7.3 0.0 copy-start.2
  7.3 0.0 copy-start.4
  7.4 2.5 %shard_map.92 = (f32[1152,128]{1,0:T(8,128)S(1)}, bf16[316,40,128]{2,1,0:T(8,128)(2,1)S(1)}) custom-call(s32[48]{0:T(128)S(1)} %bitcast.13, s32[48]{0:T(128)S(1)} %bitcast.15, f32[3072,128]{1,0:T(8,128)S(1)} %get-tuple-element.38.x_ref, bf16[316,144,128]{2,1,0:T(8,128)(2,1)} %bitcast.20, f32[8,2,9,8,128]{4,3,2,1,0:T(8,128)S(1)} %get-tuple-element.39.phase_ref, ...), custom_call_target="tpu_custom_call" | custom-call | flops 4000000000 | bytes 12000000 | tf_op jit(solution)/shard_map/pallas_call | solution.py:660
  9.9 0.0 collective-permute-done.far_ref
  9.9 0.5 %shard_map.95 = (f32[288,128]{1,0:T(8,128)S(1)}, f32[288,128]{1,0:T(8,128)S(1)}, f32[288,128]{1,0:T(8,128)S(1)}, f32[288,128]{1,0:T(8,128)S(1)}) custom-call(s32[1,48]{1,0:T(1,128)S(1)} %copy-done.3, f32[2,96,128]{2,1,0:T(8,128)S(1)} %collective-permute-done.far_ref, f32[2,96,128]{2,1,0:T(8,128)S(1)} %collective-permute-done.1.near_ref, ...), custom_call_target="tpu_custom_call" | custom-call | flops 1000000 | bytes 1000000 | tf_op jit(solution)/shard_map/pallas_call | solution.py:679
  10.4 1.5 %collective-permute-start.2 = (f32[288,128]{1,0:T(8,128)S(1)}, f32[288,128]{1,0:T(8,128)S(1)}, u32[]{:S(2)}, u32[]{:S(2)}) collective-permute-start(f32[288,128]{1,0:T(8,128)S(1)} %get-tuple-element.47), channel_id=1, source_target_pairs={{0,8},{8,0},{16,24},{24,16},{1,9},{9,1},{17,25},{25,17},{2,10},{10... | collective-permute-start | bytes 442376 | tf_op jit(solution)/shard_map/ppermute | solution.py:593
  12.0 1.5 %collective-permute-start.3 = (f32[288,128]{1,0:T(8,128)S(1)}, f32[288,128]{1,0:T(8,128)S(1)}, u32[]{:S(2)}, u32[]{:S(2)}) collective-permute-start(f32[288,128]{1,0:T(8,128)S(1)} %get-tuple-element.53), channel_id=1, source_target_pairs={{0,16},{8,24},{16,0},{24,8},{1,17},{9,25},{17,1},{25,9},{2,18},{10... | collective-permute-start | bytes 442376 | tf_op jit(solution)/shard_map/ppermute | solution.py:593
  13.5 0.5 %collective-permute-start.4 = (f32[288,128]{1,0:T(8,128)S(1)}, f32[288,128]{1,0:T(8,128)S(1)}, u32[]{:S(2)}, u32[]{:S(2)}) collective-permute-start(f32[288,128]{1,0:T(8,128)S(1)} %get-tuple-element.54), channel_id=1, source_target_pairs={{0,24},{8,16},{16,8},{24,0},{1,25},{9,17},{17,9},{25,1},{2,26},{10... | collective-permute-start | bytes 442376 | tf_op jit(solution)/shard_map/ppermute | solution.py:593
  14.0 1.1 %shard_map.93 = (f32[12680,128]{1,0:T(8,128)S(1)}, s32[32,32]{1,0:T(8,128)S(1)}) custom-call(s32[32,31]{1,0:T(8,128)S(1)} %copy-done.1, s32[32,31]{1,0:T(8,128)S(1)} %copy-done.2, s32[1,32]{1,0:T(1,128)S(1)} %bitcast.12, bf16[316,40,128]{2,1,0:T(8,128)(2,1)S(1)} %get-tuple-element.41.table_ref), custom_call_target="tpu_custom_call" | custom-call | flops 50000000 | bytes 8000000 | tf_op jit(solution)/shard_map/pallas_call | solution.py:691
  15.1 1.8 %shard_map.96 = (f32[1280,128]{1,0:T(8,128)S(1)}, f32[1280,128]{1,0:T(8,128)S(1)}) custom-call(s32[32,32]{1,0:T(8,128)S(1)} %get-tuple-element.42.operator_ref, f32[12680,128]{1,0:T(8,128)S(1)} %get-tuple-element.43.wide_ref, f32[288,128]{1,0:T(8,128)S(1)} %get-tuple-element.48.rest_0_), custom_call_target="tpu_custom_call" | custom-call | flops 40000000 | bytes 4000000 | tf_op jit(solution)/shard_map/pallas_call | solution.py:703
  16.9 0.3 collective-permute-done.2.rest_0_
  17.2 1.9 %shard_map.97 = (f32[1280,128]{1,0:T(8,128)S(1)}, f32[1280,128]{1,0:T(8,128)S(1)}) custom-call(s32[32,32]{1,0:T(8,128)S(1)} %get-tuple-element.42.operator_ref, f32[12680,128]{1,0:T(8,128)S(1)} %get-tuple-element.43.wide_ref, f32[288,128]{1,0:T(8,128)S(1)} %collective-permute-done.2.rest_0_, f32[1280,128]{1,0:T(8,128)S(1)} %get-tuple-element.49.rest_1_, ...), custom_call_target="tpu_custom_call" | custom-call | flops 40000000 | bytes 4000000 | tf_op jit(solution)/shard_map/pallas_call | solution.py:703
  19.2 2.0 %collective-permute-done.3.rest_0_ = f32[288,128]{1,0:T(8,128)S(1)} collective-permute-done((f32[288,128]{1,0:T(8,128)S(1)}, f32[288,128]{1,0:T(8,128)S(1)}, u32[]{:S(2)}, u32[]{:S(2)}) %collective-permute-start.3) | collective-permute-done | bytes 147488 | tf_op jit(solution)/shard_map/ppermute | solution.py:593
  21.1 1.4 %shard_map.98 = (f32[640,128]{1,0:T(8,128)S(1)}, f32[640,128]{1,0:T(8,128)S(1)}, f32[288,128]{1,0:T(8,128)S(1)}) custom-call(s32[32,32]{1,0:T(8,128)S(1)} %get-tuple-element.42.operator_ref, f32[12680,128]{1,0:T(8,128)S(1)} %get-tuple-element.43.wide_ref, f32[1280,128]{1,0:T(8,128)S(1)} %get-tuple-element.51.real_sum, ...), custom_call_target="tpu_custom_call" | custom-call | flops 10000000 | bytes 2000000 | tf_op jit(solution)/shard_map/pallas_call | solution.py:717
  22.5 1.8 %shard_map.100 = (f32[288,128]{1,0:T(8,128)S(1)}, f32[288,128]{1,0:T(8,128)S(1)}) custom-call(s32[32,32]{1,0:T(8,128)S(1)} %get-tuple-element.42.operator_ref, f32[12680,128]{1,0:T(8,128)S(1)} %get-tuple-element.43.wide_ref, f32[1280,128]{1,0:T(8,128)S(1)} %get-tuple-element.51.real_sum, f32[1280,128]{1,0:T(8,128)S(1)} %get-tuple-element.52.imag_sum, ...), custom_call_target="tpu_custom_call" | custom-call | flops 20000000 | bytes 4000000 | tf_op jit(solution)/shard_map/pallas_call | solution.py:717
  24.3 1.3 %collective-permute-start.5 = (f32[288,128]{1,0:T(8,128)S(1)}, f32[288,128]{1,0:T(8,128)S(1)}, u32[]{:S(2)}, u32[]{:S(2)}) collective-permute-start(f32[288,128]{1,0:T(8,128)S(1)} %get-tuple-element.57), channel_id=1, source_target_pairs={{0,8},{8,0},{16,24},{24,16},{1,9},{9,1},{17,25},{25,17},{2,10},{10... | collective-permute-start | bytes 442376 | tf_op jit(solution)/shard_map/ppermute | solution.py:593
  25.6 0.8 %collective-permute-start.6 = (f32[288,128]{1,0:T(8,128)S(1)}, f32[288,128]{1,0:T(8,128)S(1)}, u32[]{:S(2)}, u32[]{:S(2)}) collective-permute-start(f32[288,128]{1,0:T(8,128)S(1)} %get-tuple-element.58), channel_id=1, source_target_pairs={{0,16},{8,24},{16,0},{24,8},{1,17},{9,25},{17,1},{25,9},{2,18},{10... | collective-permute-start | bytes 442376 | tf_op jit(solution)/shard_map/ppermute | solution.py:593
  26.4 1.4 %collective-permute-start.7 = (f32[288,128]{1,0:T(8,128)S(1)}, f32[288,128]{1,0:T(8,128)S(1)}, u32[]{:S(2)}, u32[]{:S(2)}) collective-permute-start(f32[288,128]{1,0:T(8,128)S(1)} %get-tuple-element.59), channel_id=1, source_target_pairs={{0,24},{8,16},{16,8},{24,0},{1,25},{9,17},{17,9},{25,1},{2,26},{10... | collective-permute-start | bytes 442376 | tf_op jit(solution)/shard_map/ppermute | solution.py:593
  27.8 1.3 %shard_map.99.rest_0_ = f32[288,128]{1,0:T(8,128)S(1)} custom-call(s32[32,32]{1,0:T(8,128)S(1)} %get-tuple-element.42.operator_ref, f32[12680,128]{1,0:T(8,128)S(1)} %get-tuple-element.43.wide_ref, f32[1280,128]{1,0:T(8,128)S(1)} %get-tuple-element.51.real_sum, f32[1280,128]{1,0:T(8,128)S(1)} %get-tuple-element.52.imag_sum, ...), custom_call_target="tpu_custom_call" | custom-call | flops 10000000 | bytes 2000000 | tf_op jit(solution)/shard_map/pallas_call | solution.py:717
  29.1 1.2 %collective-permute-done.5.rest_1_ = f32[288,128]{1,0:T(8,128)S(1)} collective-permute-done((f32[288,128]{1,0:T(8,128)S(1)}, f32[288,128]{1,0:T(8,128)S(1)}, u32[]{:S(2)}, u32[]{:S(2)}) %collective-permute-start.5) | collective-permute-done | bytes 147488 | tf_op jit(solution)/shard_map/ppermute | solution.py:593
  30.4 3.4 %collective-permute-done.6.rest_2_ = f32[288,128]{1,0:T(8,128)S(1)} collective-permute-done((f32[288,128]{1,0:T(8,128)S(1)}, f32[288,128]{1,0:T(8,128)S(1)}, u32[]{:S(2)}, u32[]{:S(2)}) %collective-permute-start.6) | collective-permute-done | bytes 147488 | tf_op jit(solution)/shard_map/ppermute | solution.py:593
  33.8 0.6 %shard_map.101 = (f32[16,9,8,128]{3,2,1,0:T(8,128)S(1)}, f32[2,96,128]{2,1,0:T(8,128)S(1)}, f32[2,96,128]{2,1,0:T(8,128)S(1)}) custom-call(s32[1,48]{1,0:T(1,128)S(1)} %copy-done.3, f32[7,2,48,128]{3,2,1,0:T(8,128)S(1)} %get-tuple-element.37.edge_phase_ref, bf16[2,256,256]{2,1,0:T(8,128)(2,1)S(1)} %copy-done, f32[288,128]{1,0:T(8,128)S(1)} %shard_map.99.rest_0_, ...), custom_call_target="tpu_custom_call" | custom-call | flops 1000000 | bytes 1000000 | tf_op jit(solution)/shard_map/pallas_call | solution.py:731
  34.4 0.9 %collective-permute-start.8 = (f32[2,96,128]{2,1,0:T(8,128)S(1)}, f32[2,96,128]{2,1,0:T(8,128)S(1)}, u32[]{:S(2)}, u32[]{:S(2)}) collective-permute-start(f32[2,96,128]{2,1,0:T(8,128)S(1)} %get-tuple-element.62), channel_id=1, source_target_pairs={{0,7},{1,2},{2,1},{3,4},{4,3},{5,6},{6,5},{7,0},{8,15},{9,10},{10,... | collective-permute-start | bytes 294920 | tf_op jit(solution)/shard_map/ppermute | solution.py:588
  35.4 3.3 %shard_map.102 = (f32[96,32,128]{2,1,0:T(8,128)}, f32[2,96,8,128]{3,2,1,0:T(8,128)S(1)}) custom-call(s32[48]{0:T(128)S(1)} %bitcast.14, s32[48]{0:T(128)S(1)} %bitcast.16, f32[16,9,8,128]{3,2,1,0:T(8,128)S(1)} %get-tuple-element.60.incoming_ref, f32[8,2,9,8,128]{4,3,2,1,0:T(8,128)S(1)} %get-tuple-element.39.phase_ref, bf16[2,256,256]{2,1,0:T(8,128)(2,1)S(1)} %copy-done), custom_call_target="tpu_custom_call" | custom-call | flops 4000000000 | bytes 12000000 | tf_op jit(solution)/shard_map/pallas_call | solution.py:742
  38.6 1.7 %collective-permute-done.8.far_ref = f32[2,96,128]{2,1,0:T(8,128)S(1)} collective-permute-done((f32[2,96,128]{2,1,0:T(8,128)S(1)}, f32[2,96,128]{2,1,0:T(8,128)S(1)}, u32[]{:S(2)}, u32[]{:S(2)}) %collective-permute-start.8) | collective-permute-done | bytes 98336 | tf_op jit(solution)/shard_map/ppermute | solution.py:588
  40.3 1.0 %shard_map.103 = f32[96,32,128]{2,1,0:T(8,128)} custom-call(f32[2,96,8,128]{3,2,1,0:T(8,128)S(1)} %get-tuple-element.61.edge_ref, f32[2,96,128]{2,1,0:T(8,128)S(1)} %collective-permute-done.8.far_ref, f32[2,96,128]{2,1,0:T(8,128)S(1)} %collective-permute-done.9.near_ref, f32[96,32,128]{2,1,0:T(8,128)} %get-tuple-element.64.part_ref), custom_call_target="tpu_custom_call", output_to_operand_aliasing={{}: (3, {})} | custom-call | flops 1000000 | bytes 1000000 | tf_op jit(solution)/shard_map/pallas_call | solution.py:759
  (11 shorter events, 0.0 us)
Async XLA Ops:
  1.2 8.7 %collective-permute-start = (f32[2,96,128]{2,1,0:T(8,128)S(1)}, f32[2,96,128]{2,1,0:T(8,128)S(1)}, u32[]{:S(2)}, u32[]{:S(2)}) collective-permute-start(f32[2,96,128]{2,1,0:T(8,128)S(1)} %get-tuple-element.44), channel_id=1, source_target_pairs={{0,7},{1,2},{2,1},{3,4},{4,3},{5,6},{6,5},{7,0},{8,15},{9,10},{10,... | collective-permute-start | bytes 294920 | tf_op jit(solution)/shard_map/ppermute | solution.py:588
  5.8 4.1 %collective-permute-start.1 = (f32[2,96,128]{2,1,0:T(8,128)S(1)}, f32[2,96,128]{2,1,0:T(8,128)S(1)}, u32[]{:S(2)}, u32[]{:S(2)}) collective-permute-start(f32[2,96,128]{2,1,0:T(8,128)S(1)} %get-tuple-element.45), channel_id=1, source_target_pairs={{0,1},{1,0},{2,3},{3,2},{4,5},{5,4},{6,7},{7,6},{8,9},{9,8},{10,11... | collective-permute-start | bytes 294920 | tf_op jit(solution)/shard_map/ppermute | solution.py:588
  7.3 2.6 %copy-start.3 = (s32[1,48]{1,0:T(1,128)S(1)}, s32[1,48]{1,0:T(1,128)}, u32[]{:S(2)}) copy-start(s32[1,48]{1,0:T(1,128)} %parents_ref.3) | copy-start | bytes 580
  7.3 6.7 %copy-start.1 = (s32[32,31]{1,0:T(8,128)S(1)}, s32[32,31]{1,0:T(8,128)}, u32[]{:S(2)}) copy-start(s32[32,31]{1,0:T(8,128)} %source_ref.1) | copy-start | bytes 11908
  7.3 6.7 %copy-start.2 = (s32[32,31]{1,0:T(8,128)S(1)}, s32[32,31]{1,0:T(8,128)}, u32[]{:S(2)}) copy-start(s32[32,31]{1,0:T(8,128)} %offset_ref.1) | copy-start | bytes 11908
  7.3 6.7 %copy-start.4 = (s32[32]{0:T(128)S(1)}, s32[32]{0:T(128)}, u32[]{:S(2)}) copy-start(s32[32]{0:T(128)} %param.15) | copy-start | bytes 388
  10.4 6.8 %collective-permute-start.2 = (f32[288,128]{1,0:T(8,128)S(1)}, f32[288,128]{1,0:T(8,128)S(1)}, u32[]{:S(2)}, u32[]{:S(2)}) collective-permute-start(f32[288,128]{1,0:T(8,128)S(1)} %get-tuple-element.47), channel_id=1, source_target_pairs={{0,8},{8,0},{16,24},{24,16},{1,9},{9,1},{17,25},{25,17},{2,10},{10... | collective-permute-start | bytes 442376 | tf_op jit(solution)/shard_map/ppermute | solution.py:593
  12.0 9.1 %collective-permute-start.3 = (f32[288,128]{1,0:T(8,128)S(1)}, f32[288,128]{1,0:T(8,128)S(1)}, u32[]{:S(2)}, u32[]{:S(2)}) collective-permute-start(f32[288,128]{1,0:T(8,128)S(1)} %get-tuple-element.53), channel_id=1, source_target_pairs={{0,16},{8,24},{16,0},{24,8},{1,17},{9,25},{17,1},{25,9},{2,18},{10... | collective-permute-start | bytes 442376 | tf_op jit(solution)/shard_map/ppermute | solution.py:593
  13.5 7.6 %collective-permute-start.4 = (f32[288,128]{1,0:T(8,128)S(1)}, f32[288,128]{1,0:T(8,128)S(1)}, u32[]{:S(2)}, u32[]{:S(2)}) collective-permute-start(f32[288,128]{1,0:T(8,128)S(1)} %get-tuple-element.54), channel_id=1, source_target_pairs={{0,24},{8,16},{16,8},{24,0},{1,25},{9,17},{17,9},{25,1},{2,26},{10... | collective-permute-start | bytes 442376 | tf_op jit(solution)/shard_map/ppermute | solution.py:593
  24.3 6.1 %collective-permute-start.5 = (f32[288,128]{1,0:T(8,128)S(1)}, f32[288,128]{1,0:T(8,128)S(1)}, u32[]{:S(2)}, u32[]{:S(2)}) collective-permute-start(f32[288,128]{1,0:T(8,128)S(1)} %get-tuple-element.57), channel_id=1, source_target_pairs={{0,8},{8,0},{16,24},{24,16},{1,9},{9,1},{17,25},{25,17},{2,10},{10... | collective-permute-start | bytes 442376 | tf_op jit(solution)/shard_map/ppermute | solution.py:593
  25.6 8.3 %collective-permute-start.6 = (f32[288,128]{1,0:T(8,128)S(1)}, f32[288,128]{1,0:T(8,128)S(1)}, u32[]{:S(2)}, u32[]{:S(2)}) collective-permute-start(f32[288,128]{1,0:T(8,128)S(1)} %get-tuple-element.58), channel_id=1, source_target_pairs={{0,16},{8,24},{16,0},{24,8},{1,17},{9,25},{17,1},{25,9},{2,18},{10... | collective-permute-start | bytes 442376 | tf_op jit(solution)/shard_map/ppermute | solution.py:593
  26.4 7.4 %copy-start = (bf16[2,256,256]{2,1,0:T(8,128)(2,1)S(1)}, bf16[2,256,256]{2,1,0:T(8,128)(2,1)}, u32[]{:S(2)}) copy-start(bf16[2,256,256]{2,1,0:T(8,128)(2,1)} %constant.5.clone.gather_ref) | copy-start | bytes 786436
  26.4 7.4 %collective-permute-start.7 = (f32[288,128]{1,0:T(8,128)S(1)}, f32[288,128]{1,0:T(8,128)S(1)}, u32[]{:S(2)}, u32[]{:S(2)}) collective-permute-start(f32[288,128]{1,0:T(8,128)S(1)} %get-tuple-element.59), channel_id=1, source_target_pairs={{0,24},{8,16},{16,8},{24,0},{1,25},{9,17},{17,9},{25,1},{2,26},{10... | collective-permute-start | bytes 442376 | tf_op jit(solution)/shard_map/ppermute | solution.py:593
  34.4 5.9 %collective-permute-start.8 = (f32[2,96,128]{2,1,0:T(8,128)S(1)}, f32[2,96,128]{2,1,0:T(8,128)S(1)}, u32[]{:S(2)}, u32[]{:S(2)}) collective-permute-start(f32[2,96,128]{2,1,0:T(8,128)S(1)} %get-tuple-element.62), channel_id=1, source_target_pairs={{0,7},{1,2},{2,1},{3,4},{4,3},{5,6},{6,5},{7,0},{8,15},{9,10},{10,... | collective-permute-start | bytes 294920 | tf_op jit(solution)/shard_map/ppermute | solution.py:588
  35.4 5.0 %collective-permute-start.9 = (f32[2,96,128]{2,1,0:T(8,128)S(1)}, f32[2,96,128]{2,1,0:T(8,128)S(1)}, u32[]{:S(2)}, u32[]{:S(2)}) collective-permute-start(f32[2,96,128]{2,1,0:T(8,128)S(1)} %get-tuple-element.63), channel_id=1, source_target_pairs={{0,1},{1,0},{2,3},{3,2},{4,5},{5,4},{6,7},{7,6},{8,9},{9,8},{10,11... | collective-permute-start | bytes 294920 | tf_op jit(solution)/shard_map/ppermute | solution.py:588

commit v6 on v5

--- a/solution.py
+++ b/solution.py
@@ -187,18 +187,45 @@
     by_parity(lambda: fill(far_ref, near_ref), lambda: fill(near_ref, far_ref))
 
 
-def phase_kernel(*refs):
-    octants_hbm, sources = refs[0], refs[1:5]
-    (phase_ref, edge_phase_ref), targets = refs[5:7], refs[7:11]
-    octants_ref, octants_sem, sems = refs[11:]
+def both_taps(rows):
+    even = SUMS[0] * (rows[0] + rows[4]) + SUMS[1] * (rows[1] + rows[3]) + CENTRE * rows[2]
+    odd = DIFFS[0] * (rows[0] - rows[4]) + DIFFS[1] * (rows[1] - rows[3])
+    return even + odd, even - odd
+
+
+def both_taps_transposed(first, second):
+    total, difference = first + second, first - second
+    outer = [SUMS[i] * total for i in range(2)]
+    inner = [DIFFS[i] * difference for i in range(2)]
+    return [outer[0] + inner[0], outer[1] + inner[1], CENTRE * total, outer[1] - inner[1], outer[0] - inner[0]]
+
+
+def main_kernel(peers, parents_hbm, octants_hbm, x_hbm, table_ref, spread_hbm, *rest):
+    phase_ref, edge_phase_ref, flat_ref, slice_ref = rest[:4]
+    parents_ref, octants_ref, x_ref, spread_ref, az_e, az_o, res_e, res_o, acc, flat, sems = rest[4:]
+    children = octants_ref.shape[0]
     periods = phase_ref.shape[3]
-    octants_copy = pltpu.make_async_copy(octants_hbm, octants_ref, octants_sem)
-    octants_copy.start()
-    copies = [pltpu.make_async_copy(a, b, sems.at[i]) for i, (a, b) in enumerate(zip(sources, targets))]
+    azimuth_in = periods * PERIOD_C
+    own = acc.shape[0]
+    me = lax.axis_index("clus")
+    share = ROWS_PER_PERIOD * periods // peers
+    first_tile = me * (2 * share) // 8
+    table_rows = pl.ds(pl.multiple_of(first_tile * 8, 8), slice_ref.shape[1])
+    ends = (
+        (octants_hbm, octants_ref),
+        (parents_hbm, parents_ref),
+        (x_hbm, x_ref),
+        (spread_hbm, spread_ref),
+        (table_ref.at[:, table_rows, :], slice_ref),
+    )
+    copies = [pltpu.make_async_copy(source, target, sems.at[i]) for i, (source, target) in enumerate(ends)]
     for copy in copies:
         copy.start()
     fill_phases(lax.axis_index("dir"), phase_ref)
-    octants_copy.wait()
+    acc[...] = jnp.zeros_like(acc)
+    sublane = lax.broadcasted_iota(jnp.int32, (periods, LANES), 0)
+    for copy in copies[:-1]:
+        copy.wait()
 
     def edges_of(step, carry):
         for j in range(GROUP):
@@ -209,38 +236,7 @@
                     edge_phase_ref[e, i, pl.ds(k, 1), :] = phase_ref[octant, i, w, m : m + 1, :]
         return carry
 
-    lax.fori_loop(0, octants_ref.shape[0] // GROUP, edges_of, 0)
-    for copy in copies:
-        copy.wait()
-
-
-def both_taps(rows):
-    even = SUMS[0] * (rows[0] + rows[4]) + SUMS[1] * (rows[1] + rows[3]) + CENTRE * rows[2]
-    odd = DIFFS[0] * (rows[0] - rows[4]) + DIFFS[1] * (rows[1] - rows[3])
-    return even + odd, even - odd
-
-
-def both_taps_transposed(first, second):
-    total, difference = first + second, first - second
-    outer = [SUMS[i] * total for i in range(2)]
-    inner = [DIFFS[i] * difference for i in range(2)]
-    return [outer[0] + inner[0], outer[1] + inner[1], CENTRE * total, outer[1] - inner[1], outer[0] - inner[0]]
-
-
-def main_kernel(peers, parents_ref, octants_ref, x_ref, table_ref, phase_ref, spread_ref, *rest):
-    flat_ref, slice_ref, az_e, az_o, res_e, res_o, acc, flat, table_sem = rest
-    children = octants_ref.shape[0]
-    periods = phase_ref.shape[3]
-    azimuth_in = periods * PERIOD_C
-    own = acc.shape[0]
-    me = lax.axis_index("clus")
-    share = ROWS_PER_PERIOD * periods // peers
-    first_tile = me * (2 * share) // 8
-    table_rows = pl.ds(pl.multiple_of(first_tile * 8, 8), slice_ref.shape[1])
-    table_copy = pltpu.make_async_copy(table_ref.at[:, table_rows, :], slice_ref, table_sem)
-    table_copy.start()
-    acc[...] = jnp.zeros_like(acc)
-    sublane = lax.broadcasted_iota(jnp.int32, (periods, LANES), 0)
+    lax.fori_loop(0, children // GROUP, edges_of, 0)
 
     def azimuth(block):
         for kp in range(2 * BLOCK):
@@ -291,7 +287,7 @@
             source = gp * ROWS_PER_PERIOD * periods + q * share
             target = (q * 2 * own + gp) * share
             flat_ref[target : target + share, :] = flat[source : source + share, :]
-    table_copy.wait()
+    copies[-1].wait()
 
 
 def one_hot(parents, own):
@@ -352,21 +348,10 @@
         outs[d][...] = fixed[pl.ds(start, chunk_rows), :]
 
 
-def widen_kernel(source_ref, offset_ref, count_ref, table_ref, wide_ref, operator_ref):
+def widen_kernel(peers, source_ref, offset_ref, count_ref, table_ref, chunk, wide_ref, operator_ref, real_sum, imag_sum, *rest):
+    listed, real_twice, imag_twice, sem = rest
     targets, partners = source_ref.shape
     offsets, frame, _ = table_ref.shape
-
-    def some_offsets(i, carry):
-        for j in range(4):
-            wide_ref[pl.ds(pl.multiple_of((i * 4 + j) * frame, 8), frame), :] = table_ref[i * 4 + j].astype(f32)
-        return carry
-
-    whole_steps = offsets // 4
-    lax.fori_loop(0, whole_steps, some_offsets, 0)
-    for offset in range(whole_steps * 4, offsets):
-        wide_ref[offset * frame : (offset + 1) * frame, :] = table_ref[offset].astype(f32)
-    wide_ref[offsets * frame :, :] = jnp.zeros((frame, LANES), f32)
-
     shape = (targets, targets)
     row, lane = (lax.broadcasted_iota(jnp.int32, shape, d) for d in range(2))
     count = jnp.sum(jnp.where(row == lane, count_ref[...], 0), axis=1, keepdims=True)
@@ -375,6 +360,21 @@
         here = (lane == source_ref[:, p : p + 1]) & (p < count)
         operator = jnp.where(here, offset_ref[:, p : p + 1], operator)
     operator_ref[...] = operator * frame
+    copy = pltpu.make_async_copy(operator_ref, listed, sem)
+    copy.start()
+
+    def some_offsets(i, carry):
+        for j in range(4):
+            wide_ref[pl.ds(pl.multiple_of((i * 4 + j) * frame, 8), frame), :] = table_ref[i * 4 + j].astype(f32)
+        return carry
+
+    whole_steps = offsets // 4
+    lax.fori_loop(0, whole_steps, some_offsets, 0)
+    for offset in range(whole_steps * 4, offsets):
+        wide_ref[offset * frame : (offset + 1) * frame, :] = table_ref[offset].astype(f32)
+    wide_ref[offsets * frame :, :] = jnp.zeros((frame, LANES), f32)
+    copy.wait()
+    gather_kernel(peers, frame, (0,), (), listed, wide_ref, chunk, real_sum, imag_sum, real_twice, imag_twice)
 
 
 def doubled(chunk, real_twice, imag_twice, first, own, share, frame, skip):
@@ -386,20 +386,19 @@
             twice[pl.ds(base + 1, share, stride=2), :] = rows
 
 
-def add_sources(sums, targets, devices, own, frame, operator_ref, wide_ref, real_twice, imag_twice):
-    for number, device in enumerate(devices):
-        for g in range(own):
-            source = slice((number * own + g) * frame, (number * own + g + 1) * frame)
-            real, imaginary = real_twice[source, :], imag_twice[source, :]
-            for i, target in enumerate(targets):
-                first = pl.multiple_of(operator_ref[target, device * own + g], 8)
-                operator = wide_ref[pl.ds(first, frame), :]
-                sums[i] = (sums[i][0] + operator * real, sums[i][1] + operator * imaginary)
+def add_sources(sums, sources, frame, operators, real_twice, imag_twice):
+    for source in range(sources):
+        place = slice(source * frame, (source + 1) * frame)
+        real, imaginary = real_twice[place, :], imag_twice[place, :]
+        for i in range(len(sums)):
+            operator = operators(i, source)
+            sums[i] = (sums[i][0] + operator * real, sums[i][1] + operator * imaginary)
     return sums
 
 
-def gather_kernel(peers, frame, masks, operator_ref, wide_ref, *rest):
+def gather_kernel(peers, frame, masks, late, operator_ref, wide_ref, *rest):
     chunks, rest = rest[: len(masks)], rest[len(masks) :]
+    late_ref, rest = (rest[-3], rest[:-3] + rest[-2:]) if late else (None, rest)
     before, (real_sum, imag_sum, real_twice, imag_twice) = rest[:-4], rest[-4:]
     me = lax.axis_index("clus")
     targets = operator_ref.shape[0]
@@ -409,6 +408,10 @@
     for number, chunk in enumerate(chunks):
         doubled(chunk, real_twice, imag_twice, number * own, own, share, frame, skip)
 
+    def operator_of(target, devices, source):
+        first = operator_ref[target, (me ^ devices[source // own]) * own + source % own]
+        return wide_ref[pl.ds(pl.multiple_of(first, 8), frame), :]
+
     def some_targets(i, carry):
         some = [i * TOGETHER + j for j in range(TOGETHER)]
         places = [pl.ds(pl.multiple_of(target * frame, 8), frame) for target in some]
@@ -416,7 +419,8 @@
             sums = [tuple(ref[place, :] for ref in before) for place in places]
         else:
             sums = [(jnp.zeros((frame, LANES), f32),) * 2 for _ in some]
-        sums = add_sources(sums, some, [me ^ d for d in masks], own, frame, operator_ref, wide_ref, real_twice, imag_twice)
+        operators = lambda j, source: operator_of(some[j], masks, source)
+        sums = add_sources(sums, len(masks) * own, frame, operators, real_twice, imag_twice)
         for place, (by_real, by_imag) in zip(places, sums):
             real_sum[place, :] = by_real
             imag_sum[place, :] = by_imag
@@ -424,14 +428,24 @@
 
     lax.fori_loop(0, targets // TOGETHER, some_targets, 0)
 
-
-def translate_kernel(peers, frame, masks, targets, operator_ref, wide_ref, real_sum, imag_sum, *rest):
+    def late_operators(target, carry):
+        for source in range(len(late) * own):
+            place = pl.multiple_of((target * (len(late) * own) + source) * frame, 8)
+            late_ref[pl.ds(place, frame), :] = operator_of(target, late, source)
+        return carry
+
+    if late:
+        lax.fori_loop(0, targets, late_operators, 0)
+
+
+def translate_kernel(frame, masks, targets, late_ref, real_sum, imag_sum, *rest):
     prepare = len(rest) == len(masks) + len(targets) + 4
     chunks, rest = (rest[: len(masks)], rest[len(masks) :]) if prepare else ((), rest)
     real_twice, imag_twice = rest[:2]
     outs, (total_real, total_imag) = rest[-2 - len(targets) : -2], rest[-2:]
     me = lax.axis_index("clus")
-    own = operator_ref.shape[0] // peers
+    sources = real_twice.shape[0] // frame
+    own = sources // len(masks)
     share = outs[0].shape[0] // (2 * own)
     skip = lax.rem(me * (2 * share), 8)
     for number, chunk in enumerate(chunks):
@@ -445,7 +459,12 @@
             some = [first + g for g in places]
             rows = [pl.ds(pl.multiple_of(target * frame, 8), frame) for target in some]
             sums = [(real_sum[r, :], imag_sum[r, :]) for r in rows]
-            sums = add_sources(sums, some, [me ^ d for d in masks], own, frame, operator_ref, wide_ref, real_twice, imag_twice)
+
+            def operators(j, source):
+                place = pl.multiple_of((some[j] * sources + source) * frame, 8)
+                return late_ref[pl.ds(place, frame), :]
+
+            sums = add_sources(sums, sources, frame, operators, real_twice, imag_twice)
             for j, (g, (by_real, by_imag)) in enumerate(zip(places, sums)):
                 total_real[j] = by_real
                 total_imag[j] = by_imag
@@ -457,14 +476,14 @@
         lax.fori_loop(0, own // TOGETHER, some_targets, 0)
 
 
-def edge_kernel(peers, parents_ref, edge_phase_ref, gather_ref, *rest):
+def edge_kernel(peers, own2, parents_ref, edge_phase_ref, gather_ref, *rest):
     chunks = rest[:peers]
-    incoming_ref, far_ref, near_ref, flat = rest[peers:]
-    own2, _, periods, _ = incoming_ref.shape
+    flat, far_ref, near_ref = rest[peers:]
+    share = chunks[0].shape[0] // own2
+    periods = share * peers // ROWS_PER_PERIOD
     own = own2 // 2
     pairs = far_ref.shape[1]
     flat_rows = ROWS_PER_PERIOD * periods
-    share = flat_rows // peers
     me = lax.axis_index("clus")
     for gp in range(own2):
         for d in range(peers):
@@ -496,21 +515,27 @@
             next_ref[i] = a[3 + i] * even[pairs:] + b[3 + i] * odd[pairs:]
 
     by_parity(lambda: fill(far_ref, near_ref), lambda: fill(near_ref, far_ref))
-    for gp in range(own2):
+
+
+def disaggregate_kernel(
+    parents_ref, octants_ref, flat_ref, phase_ref, gather_ref, out_ref, edge_ref, listed, incoming_ref, lhs, coarse_e, coarse_o, whole_out, sems
+):
+    periods = incoming_ref.shape[2]
+    packed = parents_ref[...] * 8 + octants_ref[...]
+    for k in range(listed.shape[0]):
+        listed[k] = packed[0, k]
+    for gp in range(incoming_ref.shape[0]):
         for w in range(ROWS_PER_PERIOD):
-            incoming_ref[gp, w] = flat[pl.ds(gp * flat_rows + w, periods, stride=ROWS_PER_PERIOD), :]
-
-
-def disaggregate_kernel(parents_ref, octants_ref, incoming_ref, phase_ref, gather_ref, out_ref, edge_ref, lhs, coarse_e, coarse_o, whole_out, sems):
-    periods = incoming_ref.shape[2]
+            first = gp * ROWS_PER_PERIOD * periods + w
+            incoming_ref[gp, w] = flat_ref[pl.ds(first, periods, stride=ROWS_PER_PERIOD), :]
     azimuth_in = periods * PERIOD_C
     sublane = lax.broadcasted_iota(jnp.int32, (periods, LANES), 0)
     inner = pl.ds(TILE, azimuth_in - 2 * TILE)
 
     def shift(block):
         for k in range(BLOCK):
-            octant = octants_ref[block * BLOCK + k]
-            parent = parents_ref[block * BLOCK + k]
+            code = listed[block * BLOCK + k]
+            octant, parent = code & 7, code >> 3
             for r in range(3):
                 for i in range(3):
                     w = 3 * r + i
@@ -555,7 +580,7 @@
         written(block).start()
         return carry
 
-    blocks = octants_ref.shape[0] // BLOCK
+    blocks = listed.shape[0] // BLOCK
     lax.fori_loop(0, blocks, one_block, 0)
     for block in range(blocks):
         written(block).wait()
@@ -638,18 +663,6 @@
     )(in_hbm(child_patterns.reshape(pairs, azimuth_in, polar_in)))
     from_far = swapped(to_far, "dir", 1)
     from_near = swapped(to_near, "dir", 0)
-    copied = (child_patterns.reshape(pairs * azimuth_in, polar_in), spread, child_parent, child_octant.reshape(1, children))
-    phases, edge_phases, held, spread, parents, octants = local_call(
-        phase_kernel,
-        [array(8, 2, ROWS_PER_PERIOD, periods, LANES), array(edges, 2, children, LANES)]
-        + [jax.ShapeDtypeStruct(a.shape, a.dtype) for a in copied],
-        [HBM] * 5,
-        [pltpu.SMEM((children,), jnp.int32), pltpu.SemaphoreType.DMA, pltpu.SemaphoreType.DMA((len(copied),))],
-        12,
-        flops=50_000_000,
-    )(in_hbm(child_octant), *[in_hbm(a) for a in copied])
-    parents, octants = parents[0], octants[0]
-
     odd_gather = np.concatenate([odd.T[LANES:], odd.T[:LANES]])
     gather = np.stack([np.concatenate(split_np(m), axis=1) for m in (even.T, odd_gather)])
 
@@ -657,23 +670,38 @@
     view = trans_table.reshape(offsets, 2, flat_rows, LANES).transpose(0, 2, 1, 3).reshape(offsets, 2 * flat_rows, LANES)
     blocks = children // BLOCK
     rows = 2 * BLOCK * 3 * periods
-    flat, table = local_call(
+    phases, edge_phases, flat, table = local_call(
         functools.partial(main_kernel, peers),
-        [array(2 * own * flat_rows, LANES), jax.ShapeDtypeStruct((offsets, frame, LANES), bf16)],
-        [SMEM] * 2 + [VMEM, HBM, VMEM, VMEM],
         [
+            array(8, 2, ROWS_PER_PERIOD, periods, LANES),
+            array(edges, 2, children, LANES),
+            array(2 * own * flat_rows, LANES),
+            jax.ShapeDtypeStruct((offsets, frame, LANES), bf16),
+        ],
+        [HBM] * 5,
+        [
+            pltpu.SMEM((children,), jnp.int32),
+            pltpu.SMEM((children,), jnp.int32),
+            buffer(pairs * azimuth_in, polar_in),
+            pltpu.VMEM(spread.shape, bf16),
             buffer(rows, LANES),
             buffer(rows, LANES),
             buffer(rows, 2 * LANES),
             buffer(rows, 2 * LANES),
             buffer(own, 2, ROWS_PER_PERIOD, periods, LANES),
             buffer(2 * own * flat_rows, LANES),
-            pltpu.SemaphoreType.DMA,
+            pltpu.SemaphoreType.DMA((5,)),
         ],
         24,
         flops=4_000_000_000,
         bytes_accessed=12_000_000,
-    )(parents, octants, held, in_hbm(view), phases, spread)
+    )(
+        in_hbm(child_parent[0]),
+        in_hbm(child_octant),
+        in_hbm(child_patterns.reshape(pairs * azimuth_in, polar_in)),
+        in_hbm(view),
+        in_hbm(spread),
+    )
 
     chunk = array(2 * own * share, LANES)
     sent = local_call(
@@ -688,51 +716,53 @@
     for d in late:
         received[d] = exchanged(sent[d], "clus", d)
 
-    wide, operator = local_call(
-        widen_kernel,
-        [array((offsets + 1) * frame, LANES), jax.ShapeDtypeStruct((parent_total, parent_total), jnp.int32)],
-        [VMEM] * 4,
-        [],
+    sum_pair = [array(parent_total * frame, LANES)] * 2
+    wide, operator, *sums = local_call(
+        functools.partial(widen_kernel, peers),
+        [array((offsets + 1) * frame, LANES), jax.ShapeDtypeStruct((parent_total, parent_total), jnp.int32)] + sum_pair,
+        [VMEM] * 5,
+        [pltpu.SMEM((parent_total, parent_total), jnp.int32)]
+        + [buffer(own * frame, LANES)] * 2
+        + [pltpu.SemaphoreType.DMA],
         20,
-        flops=50_000_000,
-        bytes_accessed=8_000_000,
-    )(partner_src, partner_off, partner_count.reshape(1, parent_total), table)
-
-    sums = []
-    for group in ([0], early):
-        sums = local_call(
-            functools.partial(gather_kernel, peers, frame, tuple(group)),
-            [array(parent_total * frame, LANES)] * 2,
-            [SMEM] + [VMEM] * (1 + len(group) + len(sums)),
-            [buffer(len(group) * own * frame, LANES)] * 2,
-            20,
-            flops=40_000_000 * len(group),
-            bytes_accessed=4_000_000 * len(group),
-        )(operator, wide, *[received[d] for d in group], *sums)
+        flops=90_000_000,
+        bytes_accessed=12_000_000,
+    )(partner_src, partner_off, partner_count.reshape(1, parent_total), table, received[0])
+
+    late_sources = len(late) * own
+    *sums, late_operators = local_call(
+        functools.partial(gather_kernel, peers, frame, tuple(early), tuple(late)),
+        sum_pair + [array(parent_total * late_sources * frame, LANES)],
+        [SMEM] + [VMEM] * (3 + len(early)),
+        [buffer(len(early) * own * frame, LANES)] * 2,
+        28,
+        flops=60_000_000,
+        bytes_accessed=12_000_000,
+    )(operator, wide, *[received[d] for d in early], *sums)
 
     back = {}
     last_sources = [received[d] for d in late]
     for number, targets in enumerate((masks[-1:], masks[:-1], [0])):
         prepare = number == 0
         results = local_call(
-            functools.partial(translate_kernel, peers, frame, tuple(late), tuple(targets)),
-            ([array(len(late) * own * frame, LANES)] * 2 if prepare else []) + [chunk] * len(targets),
-            [SMEM] + [VMEM] * (3 + len(last_sources)),
+            functools.partial(translate_kernel, frame, tuple(late), tuple(targets)),
+            ([array(late_sources * frame, LANES)] * 2 if prepare else []) + [chunk] * len(targets),
+            [VMEM] * (3 + len(last_sources)),
             [buffer(TOGETHER, frame, LANES)] * 2,
             20,
             flops=10_000_000 * len(targets),
             bytes_accessed=2_000_000 * len(targets),
-        )(operator, wide, *sums, *last_sources)
+        )(late_operators, *sums, *last_sources)
         if prepare:
             last_sources, results = results[:2], results[2:]
         for d, result in zip(targets, results):
             back[d] = exchanged(result, "clus", d) if d else result
 
     incoming, to_far, to_near = local_call(
-        functools.partial(edge_kernel, peers),
-        [array(2 * own, ROWS_PER_PERIOD, periods, LANES), edge, edge],
+        functools.partial(edge_kernel, peers, 2 * own),
+        [array(2 * own * flat_rows, LANES), edge, edge],
         [VMEM] * (3 + peers),
-        [buffer(2 * own * flat_rows, LANES)],
+        [],
         8,
     )(child_parent, edge_phases, gather, *[back[d] for d in range(peers)])
 
@@ -742,8 +772,10 @@
     inner, edge_tiles = local_call(
         disaggregate_kernel,
         [array(pairs, azimuth_in, polar_in), array(2, pairs, TILE, polar_in)],
-        [SMEM] * 2 + [VMEM] * 3,
+        [VMEM] * 5,
         [
+            pltpu.SMEM((children,), jnp.int32),
+            buffer(2 * own, ROWS_PER_PERIOD, periods, LANES),
             buffer(rows, 3 * LANES),
             buffer(rows, LANES),
             buffer(rows, LANES),
@@ -754,7 +786,7 @@
         flops=4_000_000_000,
         bytes_accessed=12_000_000,
         out_specs=[HBM, VMEM],
-    )(parents, octants, incoming, phases, gather)
+    )(child_parent, child_octant.reshape(1, children), incoming, phases, gather)
 
     out = local_call(
         finish_kernel,

time: 41.5 us -> 39.8 us (0.959)
  Pallas kernels: 19.9 us -> 17.7 us
  waiting for transfers between devices: 8.66 us -> 9.11 us
    pallas_call x9 -> x7, Pallas kernels: 13.9 us -> 12.1 us  [the longest x1 3.94 us: on_device_exchange(): local_call(functools.partial(main_kernel, peers), [array(8, 2, ROWS_PER_P...]
where the time goes in v6:
time: 39.8 us; the launch traced here: 39.6 us
  Pallas kernels  17.7 us (44%)
  starting transfers between devices  12.6 us (32%)
  waiting for transfers between devices  9.11 us (23%)
    ppermute x6, starting transfers between devices, exchanged(): return lax.ppermute(values, axis, [(i, i ^ mask) for i in range(size)])  7.11 us
    ppermute x6, waiting for transfers between devices, exchanged(): return lax.ppermute(values, axis, [(i, i ^ mask) for i in range(size)])  7.04 us
    ppermute x4, starting transfers between devices, swapped(): lax.ppermute(values, axis, [(i, ((i - first ^ 1) + first) % size) for i i...  5.54 us
    pallas_call x1, Pallas kernels, on_device_exchange(): local_call(functools.partial(main_kernel, peers), [array(8, 2, ROWS_PER_P...  3.94 us
    pallas_call x1, Pallas kernels, on_device_exchange(): local_call(functools.partial(gather_kernel, peers, frame, tuple(early), t...  3.33 us
    pallas_call x1, Pallas kernels, on_device_exchange(): local_call(disaggregate_kernel, [array(pairs, azimuth_in, polar_in), arra...  2.88 us
    pallas_call x1, Pallas kernels, on_device_exchange(): local_call(functools.partial(widen_kernel, peers), [array((offsets + 1) *...  2.28 us
    ppermute x4, waiting for transfers between devices, swapped(): lax.ppermute(values, axis, [(i, ((i - first ^ 1) + first) % size) for i i...  2.07 us
  transfers between devices with their start and end apart: 10, of which 5 were waited for; matrix products, arithmetic and copies ran while one was open for 0% of the time, Pallas kernels for 33%

profile of v6, /device:TPU:0, one launch (start us, length us, event | category | flops | bytes accessed | tf_op | source)
XLA Modules:
  0.0 39.6 jit_solution(7939380451726831707)
XLA Ops:
  0.0 1.2 %shard_map.92 = (f32[2,96,128]{2,1,0:T(8,128)S(1)}, f32[2,96,128]{2,1,0:T(8,128)S(1)}) custom-call(f32[96,32,128]{2,1,0:T(8,128)} %bitcast.14), custom_call_target="tpu_custom_call" | custom-call | flops 1000000 | bytes 1000000 | tf_op jit(solution)/shard_map/pallas_call | solution.py:661
  1.2 4.6 %collective-permute-start = (f32[2,96,128]{2,1,0:T(8,128)S(1)}, f32[2,96,128]{2,1,0:T(8,128)S(1)}, u32[]{:S(2)}, u32[]{:S(2)}) collective-permute-start(f32[2,96,128]{2,1,0:T(8,128)S(1)} %get-tuple-element.34), channel_id=1, source_target_pairs={{0,7},{1,2},{2,1},{3,4},{4,3},{5,6},{6,5},{7,0},{8,15},{9,10},{10,... | collective-permute-start | bytes 294920 | tf_op jit(solution)/shard_map/ppermute | solution.py:613
  5.8 0.0 collective-permute-start.1
  5.8 0.0 copy-start.3
  5.8 0.0 copy-start.5
  5.8 3.9 %shard_map.91 = (f32[8,2,9,8,128]{4,3,2,1,0:T(8,128)S(1)}, f32[7,2,48,128]{3,2,1,0:T(8,128)S(1)}, f32[1152,128]{1,0:T(8,128)S(1)}, bf16[316,40,128]{2,1,0:T(8,128)(2,1)S(1)}) custom-call(s32[48]{0:T(128)} %bitcast.11, s32[48]{0:T(128)} %octants_hbm.1, f32[3072,128]{1,0:T(8,128)} %bitcast.15, bf16[316,144,128]{2,1,0:T(8,128)(2,1)} %bitcast.16, ...), custom_call_target="tpu_custom_call" | custom-call | flops 4000000000 | bytes 12000000 | tf_op jit(solution)/shard_map/pallas_call | solution.py:673
  9.8 0.0 collective-permute-done.far_ref
  9.8 0.5 %shard_map.93 = (f32[288,128]{1,0:T(8,128)S(1)}, f32[288,128]{1,0:T(8,128)S(1)}, f32[288,128]{1,0:T(8,128)S(1)}, f32[288,128]{1,0:T(8,128)S(1)}) custom-call(s32[1,48]{1,0:T(1,128)S(1)} %copy-done.4, f32[2,96,128]{2,1,0:T(8,128)S(1)} %collective-permute-done.far_ref, f32[2,96,128]{2,1,0:T(8,128)S(1)} %collective-permute-done.1.near_ref, ...), custom_call_target="tpu_custom_call" | custom-call | flops 1000000 | bytes 1000000 | tf_op jit(solution)/shard_map/pallas_call | solution.py:707
  10.3 1.5 %collective-permute-start.2 = (f32[288,128]{1,0:T(8,128)S(1)}, f32[288,128]{1,0:T(8,128)S(1)}, u32[]{:S(2)}, u32[]{:S(2)}) collective-permute-start(f32[288,128]{1,0:T(8,128)S(1)} %get-tuple-element.40), channel_id=1, source_target_pairs={{0,8},{8,0},{16,24},{24,16},{1,9},{9,1},{17,25},{25,17},{2,10},{10... | collective-permute-start | bytes 442376 | tf_op jit(solution)/shard_map/ppermute | solution.py:618
  11.9 1.5 %collective-permute-start.3 = (f32[288,128]{1,0:T(8,128)S(1)}, f32[288,128]{1,0:T(8,128)S(1)}, u32[]{:S(2)}, u32[]{:S(2)}) collective-permute-start(f32[288,128]{1,0:T(8,128)S(1)} %get-tuple-element.46), channel_id=1, source_target_pairs={{0,16},{8,24},{16,0},{24,8},{1,17},{9,25},{17,1},{25,9},{2,18},{10... | collective-permute-start | bytes 442376 | tf_op jit(solution)/shard_map/ppermute | solution.py:618
  13.4 0.5 %collective-permute-start.4 = (f32[288,128]{1,0:T(8,128)S(1)}, f32[288,128]{1,0:T(8,128)S(1)}, u32[]{:S(2)}, u32[]{:S(2)}) collective-permute-start(f32[288,128]{1,0:T(8,128)S(1)} %get-tuple-element.47), channel_id=1, source_target_pairs={{0,24},{8,16},{16,8},{24,0},{1,25},{9,17},{17,9},{25,1},{2,26},{10... | collective-permute-start | bytes 442376 | tf_op jit(solution)/shard_map/ppermute | solution.py:618
  13.9 2.3 %shard_map.94 = (f32[12680,128]{1,0:T(8,128)S(1)}, s32[32,32]{1,0:T(8,128)S(1)}, f32[1280,128]{1,0:T(8,128)S(1)}, f32[1280,128]{1,0:T(8,128)S(1)}) custom-call(s32[32,31]{1,0:T(8,128)S(1)} %copy-done.2, s32[32,31]{1,0:T(8,128)S(1)} %copy-done.3, s32[1,32]{1,0:T(1,128)S(1)} %bitcast.12, bf16[316,40,128]{2,1,0:T(8,128)(2,1)S(1)} %get-tuple-element.33.table_ref, ...), custom_call_target="tpu_custom_call" | custom-call | flops 90000000 | bytes 12000000 | tf_op jit(solution)/shard_map/pallas_call | solution.py:720
  16.2 0.9 %collective-permute-done.2.rest_0_ = f32[288,128]{1,0:T(8,128)S(1)} collective-permute-done((f32[288,128]{1,0:T(8,128)S(1)}, f32[288,128]{1,0:T(8,128)S(1)}, u32[]{:S(2)}, u32[]{:S(2)}) %collective-permute-start.2) | collective-permute-done | bytes 147488 | tf_op jit(solution)/shard_map/ppermute | solution.py:618
  17.1 3.3 %shard_map.95 = (f32[1280,128]{1,0:T(8,128)S(1)}, f32[1280,128]{1,0:T(8,128)S(1)}, f32[20480,128]{1,0:T(8,128)S(1)}) custom-call(s32[32,32]{1,0:T(8,128)S(1)} %get-tuple-element.38.operator_ref, f32[12680,128]{1,0:T(8,128)S(1)} %get-tuple-element.39.wide_ref, f32[288,128]{1,0:T(8,128)S(1)} %collective-permute-done.2.rest_0_, ...), custom_call_target="tpu_custom_call" | custom-call | flops 60000000 | bytes 12000000 | tf_op jit(solution)/shard_map/pallas_call | solution.py:733
  20.4 0.6 %collective-permute-done.3.rest_0_ = f32[288,128]{1,0:T(8,128)S(1)} collective-permute-done((f32[288,128]{1,0:T(8,128)S(1)}, f32[288,128]{1,0:T(8,128)S(1)}, u32[]{:S(2)}, u32[]{:S(2)}) %collective-permute-start.3) | collective-permute-done | bytes 147488 | tf_op jit(solution)/shard_map/ppermute | solution.py:618
  21.0 0.0 collective-permute-done.4.rest_1_
  21.0 0.6 %shard_map.96 = (f32[640,128]{1,0:T(8,128)S(1)}, f32[640,128]{1,0:T(8,128)S(1)}, f32[288,128]{1,0:T(8,128)S(1)}) custom-call(f32[20480,128]{1,0:T(8,128)S(1)} %get-tuple-element.43.late_ref, f32[1280,128]{1,0:T(8,128)S(1)} %get-tuple-element.44.real_sum, f32[1280,128]{1,0:T(8,128)S(1)} %get-tuple-element.45.imag_sum, ...), custom_call_target="tpu_custom_call" | custom-call | flops 10000000 | bytes 2000000 | tf_op jit(solution)/shard_map/pallas_call | solution.py:747
  21.5 1.0 %shard_map.98 = (f32[288,128]{1,0:T(8,128)S(1)}, f32[288,128]{1,0:T(8,128)S(1)}) custom-call(f32[20480,128]{1,0:T(8,128)S(1)} %get-tuple-element.43.late_ref, f32[1280,128]{1,0:T(8,128)S(1)} %get-tuple-element.44.real_sum, f32[1280,128]{1,0:T(8,128)S(1)} %get-tuple-element.45.imag_sum, f32[640,128]{1,0:T(8,128)S(1)} %get-tuple-element.48.rest_0_, ...), custom_call_target="tpu_custom_call" | custom-call | flops 20000000 | bytes 4000000 | tf_op jit(solution)/shard_map/pallas_call | solution.py:747
  22.5 1.3 %collective-permute-start.5 = (f32[288,128]{1,0:T(8,128)S(1)}, f32[288,128]{1,0:T(8,128)S(1)}, u32[]{:S(2)}, u32[]{:S(2)}) collective-permute-start(f32[288,128]{1,0:T(8,128)S(1)} %get-tuple-element.50), channel_id=1, source_target_pairs={{0,8},{8,0},{16,24},{24,16},{1,9},{9,1},{17,25},{25,17},{2,10},{10... | collective-permute-start | bytes 442376 | tf_op jit(solution)/shard_map/ppermute | solution.py:618
  23.8 1.2 %collective-permute-start.6 = (f32[288,128]{1,0:T(8,128)S(1)}, f32[288,128]{1,0:T(8,128)S(1)}, u32[]{:S(2)}, u32[]{:S(2)}) collective-permute-start(f32[288,128]{1,0:T(8,128)S(1)} %get-tuple-element.51), channel_id=1, source_target_pairs={{0,16},{8,24},{16,0},{24,8},{1,17},{9,25},{17,1},{25,9},{2,18},{10... | collective-permute-start | bytes 442376 | tf_op jit(solution)/shard_map/ppermute | solution.py:618
  25.1 1.0 %collective-permute-start.7 = (f32[288,128]{1,0:T(8,128)S(1)}, f32[288,128]{1,0:T(8,128)S(1)}, u32[]{:S(2)}, u32[]{:S(2)}) collective-permute-start(f32[288,128]{1,0:T(8,128)S(1)} %get-tuple-element.52), channel_id=1, source_target_pairs={{0,24},{8,16},{16,8},{24,0},{1,25},{9,17},{17,9},{25,1},{2,26},{10... | collective-permute-start | bytes 442376 | tf_op jit(solution)/shard_map/ppermute | solution.py:618
  26.1 0.5 %shard_map.97.rest_0_ = f32[288,128]{1,0:T(8,128)S(1)} custom-call(f32[20480,128]{1,0:T(8,128)S(1)} %get-tuple-element.43.late_ref, f32[1280,128]{1,0:T(8,128)S(1)} %get-tuple-element.44.real_sum, f32[1280,128]{1,0:T(8,128)S(1)} %get-tuple-element.45.imag_sum, f32[640,128]{1,0:T(8,128)S(1)} %get-tuple-element.48.rest_0_, ...), custom_call_target="tpu_custom_call" | custom-call | flops 10000000 | bytes 2000000 | tf_op jit(solution)/shard_map/pallas_call | solution.py:747
  26.6 2.0 %collective-permute-done.5.rest_1_ = f32[288,128]{1,0:T(8,128)S(1)} collective-permute-done((f32[288,128]{1,0:T(8,128)S(1)}, f32[288,128]{1,0:T(8,128)S(1)}, u32[]{:S(2)}, u32[]{:S(2)}) %collective-permute-start.5) | collective-permute-done | bytes 147488 | tf_op jit(solution)/shard_map/ppermute | solution.py:618
  28.6 3.6 %collective-permute-done.6.rest_2_ = f32[288,128]{1,0:T(8,128)S(1)} collective-permute-done((f32[288,128]{1,0:T(8,128)S(1)}, f32[288,128]{1,0:T(8,128)S(1)}, u32[]{:S(2)}, u32[]{:S(2)}) %collective-permute-start.6) | collective-permute-done | bytes 147488 | tf_op jit(solution)/shard_map/ppermute | solution.py:618
  32.1 0.0 collective-permute-done.7.rest_3_
  32.1 0.6 %shard_map.99 = (f32[1152,128]{1,0:T(8,128)S(1)}, f32[2,96,128]{2,1,0:T(8,128)S(1)}, f32[2,96,128]{2,1,0:T(8,128)S(1)}) custom-call(s32[1,48]{1,0:T(1,128)S(1)} %copy-done.4, f32[7,2,48,128]{3,2,1,0:T(8,128)S(1)} %get-tuple-element.32.edge_phase_ref, bf16[2,256,256]{2,1,0:T(8,128)(2,1)S(1)} %copy-done.1, f32[288,128]{1,0:T(8,128)S(1)} %shard_map.97.rest_0_, ...), custom_call_target="tpu_custom_call" | custom-call | flops 1000000 | bytes 1000000 | tf_op jit(solution)/shard_map/pallas_call | solution.py:761
  32.7 0.9 %collective-permute-start.8 = (f32[2,96,128]{2,1,0:T(8,128)S(1)}, f32[2,96,128]{2,1,0:T(8,128)S(1)}, u32[]{:S(2)}, u32[]{:S(2)}) collective-permute-start(f32[2,96,128]{2,1,0:T(8,128)S(1)} %get-tuple-element.56), channel_id=1, source_target_pairs={{0,7},{1,2},{2,1},{3,4},{4,3},{5,6},{6,5},{7,0},{8,15},{9,10},{10,... | collective-permute-start | bytes 294920 | tf_op jit(solution)/shard_map/ppermute | solution.py:613
  33.6 0.0 collective-permute-start.9
  33.6 2.9 %shard_map.100 = (f32[96,32,128]{2,1,0:T(8,128)}, f32[2,96,8,128]{3,2,1,0:T(8,128)S(1)}) custom-call(s32[1,48]{1,0:T(1,128)S(1)} %copy-done.4, s32[1,48]{1,0:T(1,128)S(1)} %bitcast.13, f32[1152,128]{1,0:T(8,128)S(1)} %get-tuple-element.53.flat_ref, f32[8,2,9,8,128]{4,3,2,1,0:T(8,128)S(1)} %get-tuple-element.54.phase_ref, bf16[2,256,256]{2,1,0:T(8,128)(2,1)S(1)} %copy-done.1), custom_call_target="tpu_custom_call" | custom-call | flops 4000000000 | bytes 12000000 | tf_op jit(solution)/shard_map/pallas_call | solution.py:772
  36.5 2.1 %collective-permute-done.8.far_ref = f32[2,96,128]{2,1,0:T(8,128)S(1)} collective-permute-done((f32[2,96,128]{2,1,0:T(8,128)S(1)}, f32[2,96,128]{2,1,0:T(8,128)S(1)}, u32[]{:S(2)}, u32[]{:S(2)}) %collective-permute-start.8) | collective-permute-done | bytes 98336 | tf_op jit(solution)/shard_map/ppermute | solution.py:613
  38.6 0.0 collective-permute-done.9.near_ref
  38.6 1.0 %shard_map.101 = f32[96,32,128]{2,1,0:T(8,128)} custom-call(f32[2,96,8,128]{3,2,1,0:T(8,128)S(1)} %get-tuple-element.55.edge_ref, f32[2,96,128]{2,1,0:T(8,128)S(1)} %collective-permute-done.8.far_ref, f32[2,96,128]{2,1,0:T(8,128)S(1)} %collective-permute-done.9.near_ref, f32[96,32,128]{2,1,0:T(8,128)} %get-tuple-element.58.part_ref), custom_call_target="tpu_custom_call", output_to_operand_aliasing={{}: (3, {})} | custom-call | flops 1000000 | bytes 1000000 | tf_op jit(solution)/shard_map/pallas_call | solution.py:791
  (13 shorter events, 0.0 us)
Async XLA Ops:
  1.2 8.6 %collective-permute-start = (f32[2,96,128]{2,1,0:T(8,128)S(1)}, f32[2,96,128]{2,1,0:T(8,128)S(1)}, u32[]{:S(2)}, u32[]{:S(2)}) collective-permute-start(f32[2,96,128]{2,1,0:T(8,128)S(1)} %get-tuple-element.34), channel_id=1, source_target_pairs={{0,7},{1,2},{2,1},{3,4},{4,3},{5,6},{6,5},{7,0},{8,15},{9,10},{10,... | collective-permute-start | bytes 294920 | tf_op jit(solution)/shard_map/ppermute | solution.py:613
  5.8 4.0 %collective-permute-start.1 = (f32[2,96,128]{2,1,0:T(8,128)S(1)}, f32[2,96,128]{2,1,0:T(8,128)S(1)}, u32[]{:S(2)}, u32[]{:S(2)}) collective-permute-start(f32[2,96,128]{2,1,0:T(8,128)S(1)} %get-tuple-element.35), channel_id=1, source_target_pairs={{0,1},{1,0},{2,3},{3,2},{4,5},{5,4},{6,7},{7,6},{8,9},{9,8},{10,11... | collective-permute-start | bytes 294920 | tf_op jit(solution)/shard_map/ppermute | solution.py:613
  5.8 4.0 %copy-start = (bf16[2,384,256]{2,1,0:T(8,128)(2,1)S(1)}, bf16[2,384,256]{2,1,0:T(8,128)(2,1)}, u32[]{:S(2)}) copy-start(bf16[2,384,256]{2,1,0:T(8,128)(2,1)} %constant.4.clone.spread_hbm.spread_ref) | copy-start | bytes 1179652
  5.8 4.0 %copy-start.4 = (s32[1,48]{1,0:T(1,128)S(1)}, s32[1,48]{1,0:T(1,128)}, u32[]{:S(2)}) copy-start(s32[1,48]{1,0:T(1,128)} %parents_ref.5) | copy-start | bytes 580
  5.8 8.1 %copy-start.2 = (s32[32,31]{1,0:T(8,128)S(1)}, s32[32,31]{1,0:T(8,128)}, u32[]{:S(2)}) copy-start(s32[32,31]{1,0:T(8,128)} %source_ref.1) | copy-start | bytes 11908
  5.8 8.1 %copy-start.3 = (s32[32,31]{1,0:T(8,128)S(1)}, s32[32,31]{1,0:T(8,128)}, u32[]{:S(2)}) copy-start(s32[32,31]{1,0:T(8,128)} %offset_ref.1) | copy-start | bytes 11908
  5.8 8.1 %copy-start.5 = (s32[32]{0:T(128)S(1)}, s32[32]{0:T(128)}, u32[]{:S(2)}) copy-start(s32[32]{0:T(128)} %param.15) | copy-start | bytes 388
  10.3 6.8 %collective-permute-start.2 = (f32[288,128]{1,0:T(8,128)S(1)}, f32[288,128]{1,0:T(8,128)S(1)}, u32[]{:S(2)}, u32[]{:S(2)}) collective-permute-start(f32[288,128]{1,0:T(8,128)S(1)} %get-tuple-element.40), channel_id=1, source_target_pairs={{0,8},{8,0},{16,24},{24,16},{1,9},{9,1},{17,25},{25,17},{2,10},{10... | collective-permute-start | bytes 442376 | tf_op jit(solution)/shard_map/ppermute | solution.py:618
  11.9 9.1 %collective-permute-start.3 = (f32[288,128]{1,0:T(8,128)S(1)}, f32[288,128]{1,0:T(8,128)S(1)}, u32[]{:S(2)}, u32[]{:S(2)}) collective-permute-start(f32[288,128]{1,0:T(8,128)S(1)} %get-tuple-element.46), channel_id=1, source_target_pairs={{0,16},{8,24},{16,0},{24,8},{1,17},{9,25},{17,1},{25,9},{2,18},{10... | collective-permute-start | bytes 442376 | tf_op jit(solution)/shard_map/ppermute | solution.py:618
  13.4 7.6 %collective-permute-start.4 = (f32[288,128]{1,0:T(8,128)S(1)}, f32[288,128]{1,0:T(8,128)S(1)}, u32[]{:S(2)}, u32[]{:S(2)}) collective-permute-start(f32[288,128]{1,0:T(8,128)S(1)} %get-tuple-element.47), channel_id=1, source_target_pairs={{0,24},{8,16},{16,8},{24,0},{1,25},{9,17},{17,9},{25,1},{2,26},{10... | collective-permute-start | bytes 442376 | tf_op jit(solution)/shard_map/ppermute | solution.py:618
  22.5 6.0 %collective-permute-start.5 = (f32[288,128]{1,0:T(8,128)S(1)}, f32[288,128]{1,0:T(8,128)S(1)}, u32[]{:S(2)}, u32[]{:S(2)}) collective-permute-start(f32[288,128]{1,0:T(8,128)S(1)} %get-tuple-element.50), channel_id=1, source_target_pairs={{0,8},{8,0},{16,24},{24,16},{1,9},{9,1},{17,25},{25,17},{2,10},{10... | collective-permute-start | bytes 442376 | tf_op jit(solution)/shard_map/ppermute | solution.py:618
  23.8 8.3 %collective-permute-start.6 = (f32[288,128]{1,0:T(8,128)S(1)}, f32[288,128]{1,0:T(8,128)S(1)}, u32[]{:S(2)}, u32[]{:S(2)}) collective-permute-start(f32[288,128]{1,0:T(8,128)S(1)} %get-tuple-element.51), channel_id=1, source_target_pairs={{0,16},{8,24},{16,0},{24,8},{1,17},{9,25},{17,1},{25,9},{2,18},{10... | collective-permute-start | bytes 442376 | tf_op jit(solution)/shard_map/ppermute | solution.py:618
  25.1 7.0 %copy-start.1 = (bf16[2,256,256]{2,1,0:T(8,128)(2,1)S(1)}, bf16[2,256,256]{2,1,0:T(8,128)(2,1)}, u32[]{:S(2)}) copy-start(bf16[2,256,256]{2,1,0:T(8,128)(2,1)} %constant.5.clone.gather_ref) | copy-start | bytes 786436
  25.1 8.6 %copy-start.6 = (s32[48]{0:T(128)S(1)}, s32[48]{0:T(128)}, u32[]{:S(2)}) copy-start(s32[48]{0:T(128)} %octants_hbm.1) | copy-start | bytes 580
  25.1 7.0 %collective-permute-start.7 = (f32[288,128]{1,0:T(8,128)S(1)}, f32[288,128]{1,0:T(8,128)S(1)}, u32[]{:S(2)}, u32[]{:S(2)}) collective-permute-start(f32[288,128]{1,0:T(8,128)S(1)} %get-tuple-element.52), channel_id=1, source_target_pairs={{0,24},{8,16},{16,8},{24,0},{1,25},{9,17},{17,9},{25,1},{2,26},{10... | collective-permute-start | bytes 442376 | tf_op jit(solution)/shard_map/ppermute | solution.py:618
  32.7 5.9 %collective-permute-start.8 = (f32[2,96,128]{2,1,0:T(8,128)S(1)}, f32[2,96,128]{2,1,0:T(8,128)S(1)}, u32[]{:S(2)}, u32[]{:S(2)}) collective-permute-start(f32[2,96,128]{2,1,0:T(8,128)S(1)} %get-tuple-element.56), channel_id=1, source_target_pairs={{0,7},{1,2},{2,1},{3,4},{4,3},{5,6},{6,5},{7,0},{8,15},{9,10},{10,... | collective-permute-start | bytes 294920 | tf_op jit(solution)/shard_map/ppermute | solution.py:613
  33.6 5.0 %collective-permute-start.9 = (f32[2,96,128]{2,1,0:T(8,128)S(1)}, f32[2,96,128]{2,1,0:T(8,128)S(1)}, u32[]{:S(2)}, u32[]{:S(2)}) collective-permute-start(f32[2,96,128]{2,1,0:T(8,128)S(1)} %get-tuple-element.57), channel_id=1, source_target_pairs={{0,1},{1,0},{2,3},{3,2},{4,5},{5,4},{6,7},{7,6},{8,9},{9,8},{10,11... | collective-permute-start | bytes 294920 | tf_op jit(solution)/shard_map/ppermute | solution.py:613

commit v7 on v6

--- a/solution.py
+++ b/solution.py
@@ -219,13 +219,12 @@
         (table_ref.at[:, table_rows, :], slice_ref),
     )
     copies = [pltpu.make_async_copy(source, target, sems.at[i]) for i, (source, target) in enumerate(ends)]
-    for copy in copies:
+    for copy in copies[:-1]:
         copy.start()
     fill_phases(lax.axis_index("dir"), phase_ref)
     acc[...] = jnp.zeros_like(acc)
     sublane = lax.broadcasted_iota(jnp.int32, (periods, LANES), 0)
-    for copy in copies[:-1]:
-        copy.wait()
+    copies[0].wait()
 
     def edges_of(step, carry):
         for j in range(GROUP):
@@ -237,6 +236,9 @@
         return carry
 
     lax.fori_loop(0, children // GROUP, edges_of, 0)
+    for copy in copies[1:-1]:
+        copy.wait()
+    copies[-1].start()
 
     def azimuth(block):
         for kp in range(2 * BLOCK):
@@ -348,19 +350,22 @@
         outs[d][...] = fixed[pl.ds(start, chunk_rows), :]
 
 
-def widen_kernel(peers, source_ref, offset_ref, count_ref, table_ref, chunk, wide_ref, operator_ref, real_sum, imag_sum, *rest):
-    listed, real_twice, imag_twice, sem = rest
+def widen_kernel(peers, others, source_ref, offset_ref, count_ref, table_ref, chunk, placed_ref, real_sum, imag_sum, *rest):
+    wide_ref, numbers_ref, listed, real_twice, imag_twice, sem = rest
     targets, partners = source_ref.shape
     offsets, frame, _ = table_ref.shape
+    own = targets // peers
+    share = chunk.shape[0] // (2 * own)
+    me = lax.axis_index("clus")
     shape = (targets, targets)
     row, lane = (lax.broadcasted_iota(jnp.int32, shape, d) for d in range(2))
     count = jnp.sum(jnp.where(row == lane, count_ref[...], 0), axis=1, keepdims=True)
-    operator = jnp.full(shape, offsets, jnp.int32)
+    number = jnp.full(shape, offsets, jnp.int32)
     for p in range(partners):
         here = (lane == source_ref[:, p : p + 1]) & (p < count)
-        operator = jnp.where(here, offset_ref[:, p : p + 1], operator)
-    operator_ref[...] = operator * frame
-    copy = pltpu.make_async_copy(operator_ref, listed, sem)
+        number = jnp.where(here, offset_ref[:, p : p + 1], number)
+    numbers_ref[...] = number * frame
+    copy = pltpu.make_async_copy(numbers_ref, listed, sem)
     copy.start()
 
     def some_offsets(i, carry):
@@ -373,8 +378,26 @@
     for offset in range(whole_steps * 4, offsets):
         wide_ref[offset * frame : (offset + 1) * frame, :] = table_ref[offset].astype(f32)
     wide_ref[offsets * frame :, :] = jnp.zeros((frame, LANES), f32)
+    doubled(chunk, real_twice, imag_twice, 0, own, share, frame, lax.rem(me * (2 * share), 8))
     copy.wait()
-    gather_kernel(peers, frame, (0,), (), listed, wide_ref, chunk, real_sum, imag_sum, real_twice, imag_twice)
+
+    def operator_of(target, device, g):
+        first = listed[target, device * own + g]
+        return wide_ref[pl.ds(pl.multiple_of(first, 8), frame), :]
+
+    def own_sources(some, sums):
+        return add_sources(sums, own, frame, lambda j, source: operator_of(some[j], me, source), real_twice, imag_twice)
+
+    for_some_targets(targets, frame, own_sources, None, (real_sum, imag_sum))
+
+    def other_sources(target, carry):
+        for i, d in enumerate(others):
+            for g in range(own):
+                place = pl.multiple_of(((target * len(others) + i) * own + g) * frame, 8)
+                placed_ref[pl.ds(place, frame), :] = operator_of(target, me ^ d, g)
+        return carry
+
+    lax.fori_loop(0, targets, other_sources, 0)
 
 
 def doubled(chunk, real_twice, imag_twice, first, own, share, frame, skip):
@@ -396,49 +419,51 @@
     return sums
 
 
-def gather_kernel(peers, frame, masks, late, operator_ref, wide_ref, *rest):
-    chunks, rest = rest[: len(masks)], rest[len(masks) :]
-    late_ref, rest = (rest[-3], rest[:-3] + rest[-2:]) if late else (None, rest)
-    before, (real_sum, imag_sum, real_twice, imag_twice) = rest[:-4], rest[-4:]
+def for_some_targets(targets, frame, add, before, after):
+    def some_targets(i, carry):
+        some = [i * TOGETHER + j for j in range(TOGETHER)]
+        places = [pl.ds(pl.multiple_of(target * frame, 8), frame) for target in some]
+        if before is None:
+            sums = [(jnp.zeros((frame, LANES), f32),) * 2 for _ in some]
+        else:
+            sums = [tuple(ref[place, :] for ref in before) for place in places]
+        for place, values in zip(places, add(some, sums)):
+            for ref, value in zip(after, values):
+                ref[place, :] = value
+        return carry
+
+    lax.fori_loop(0, targets // TOGETHER, some_targets, 0)
+
+
+def placed(placed_ref, frame, others, own, masks):
+    firsts = [others.index(d) * own for d in masks]
+
+    def operator_of(target, source):
+        place = target * (len(others) * own) + firsts[source // own] + source % own
+        return placed_ref[pl.ds(pl.multiple_of(place * frame, 8), frame), :]
+
+    return operator_of
+
+
+def gather_kernel(peers, frame, others, masks, placed_ref, *rest):
+    chunks, (real_before, imag_before, real_sum, imag_sum, real_twice, imag_twice) = rest[:-6], rest[-6:]
     me = lax.axis_index("clus")
-    targets = operator_ref.shape[0]
+    targets = real_sum.shape[0] // frame
     own = targets // peers
     share = chunks[0].shape[0] // (2 * own)
     skip = lax.rem(me * (2 * share), 8)
     for number, chunk in enumerate(chunks):
         doubled(chunk, real_twice, imag_twice, number * own, own, share, frame, skip)
-
-    def operator_of(target, devices, source):
-        first = operator_ref[target, (me ^ devices[source // own]) * own + source % own]
-        return wide_ref[pl.ds(pl.multiple_of(first, 8), frame), :]
-
-    def some_targets(i, carry):
-        some = [i * TOGETHER + j for j in range(TOGETHER)]
-        places = [pl.ds(pl.multiple_of(target * frame, 8), frame) for target in some]
-        if before:
-            sums = [tuple(ref[place, :] for ref in before) for place in places]
-        else:
-            sums = [(jnp.zeros((frame, LANES), f32),) * 2 for _ in some]
-        operators = lambda j, source: operator_of(some[j], masks, source)
-        sums = add_sources(sums, len(masks) * own, frame, operators, real_twice, imag_twice)
-        for place, (by_real, by_imag) in zip(places, sums):
-            real_sum[place, :] = by_real
-            imag_sum[place, :] = by_imag
-        return carry
-
-    lax.fori_loop(0, targets // TOGETHER, some_targets, 0)
-
-    def late_operators(target, carry):
-        for source in range(len(late) * own):
-            place = pl.multiple_of((target * (len(late) * own) + source) * frame, 8)
-            late_ref[pl.ds(place, frame), :] = operator_of(target, late, source)
-        return carry
-
-    if late:
-        lax.fori_loop(0, targets, late_operators, 0)
-
-
-def translate_kernel(frame, masks, targets, late_ref, real_sum, imag_sum, *rest):
+    operator_of = placed(placed_ref, frame, others, own, masks)
+
+    def add(some, sums):
+        operators = lambda j, source: operator_of(some[j], source)
+        return add_sources(sums, len(masks) * own, frame, operators, real_twice, imag_twice)
+
+    for_some_targets(targets, frame, add, (real_before, imag_before), (real_sum, imag_sum))
+
+
+def translate_kernel(frame, others, masks, targets, placed_ref, real_sum, imag_sum, *rest):
     prepare = len(rest) == len(masks) + len(targets) + 4
     chunks, rest = (rest[: len(masks)], rest[len(masks) :]) if prepare else ((), rest)
     real_twice, imag_twice = rest[:2]
@@ -450,6 +475,7 @@
     skip = lax.rem(me * (2 * share), 8)
     for number, chunk in enumerate(chunks):
         doubled(chunk, real_twice, imag_twice, number * own, own, share, frame, skip)
+    operator_of = placed(placed_ref, frame, others, own, masks)
     even, odd = pl.ds(skip, share, stride=2), pl.ds(skip + 1, share, stride=2)
     for out, d in zip(outs, targets):
         first = (me ^ d) * own
@@ -459,11 +485,7 @@
             some = [first + g for g in places]
             rows = [pl.ds(pl.multiple_of(target * frame, 8), frame) for target in some]
             sums = [(real_sum[r, :], imag_sum[r, :]) for r in rows]
-
-            def operators(j, source):
-                place = pl.multiple_of((some[j] * sources + source) * frame, 8)
-                return late_ref[pl.ds(place, frame), :]
-
+            operators = lambda j, source: operator_of(some[j], source)
             sums = add_sources(sums, sources, frame, operators, real_twice, imag_twice)
             for j, (g, (by_real, by_imag)) in enumerate(zip(places, sums)):
                 total_real[j] = by_real
@@ -717,42 +739,47 @@
         received[d] = exchanged(sent[d], "clus", d)
 
     sum_pair = [array(parent_total * frame, LANES)] * 2
-    wide, operator, *sums = local_call(
-        functools.partial(widen_kernel, peers),
-        [array((offsets + 1) * frame, LANES), jax.ShapeDtypeStruct((parent_total, parent_total), jnp.int32)] + sum_pair,
+    others = tuple(early + late)
+    operators, *sums = local_call(
+        functools.partial(widen_kernel, peers, others),
+        [array(parent_total * len(others) * own * frame, LANES)] + sum_pair,
         [VMEM] * 5,
-        [pltpu.SMEM((parent_total, parent_total), jnp.int32)]
-        + [buffer(own * frame, LANES)] * 2
-        + [pltpu.SemaphoreType.DMA],
+        [
+            buffer((offsets + 1) * frame, LANES),
+            pltpu.VMEM((parent_total, parent_total), jnp.int32),
+            pltpu.SMEM((parent_total, parent_total), jnp.int32),
+            buffer(own * frame, LANES),
+            buffer(own * frame, LANES),
+            pltpu.SemaphoreType.DMA,
+        ],
         20,
         flops=90_000_000,
         bytes_accessed=12_000_000,
     )(partner_src, partner_off, partner_count.reshape(1, parent_total), table, received[0])
 
-    late_sources = len(late) * own
-    *sums, late_operators = local_call(
-        functools.partial(gather_kernel, peers, frame, tuple(early), tuple(late)),
-        sum_pair + [array(parent_total * late_sources * frame, LANES)],
-        [SMEM] + [VMEM] * (3 + len(early)),
+    sums = local_call(
+        functools.partial(gather_kernel, peers, frame, others, tuple(early)),
+        sum_pair,
+        [VMEM] * (3 + len(early)),
         [buffer(len(early) * own * frame, LANES)] * 2,
-        28,
+        12,
         flops=60_000_000,
         bytes_accessed=12_000_000,
-    )(operator, wide, *[received[d] for d in early], *sums)
+    )(operators, *[received[d] for d in early], *sums)
 
     back = {}
     last_sources = [received[d] for d in late]
-    for number, targets in enumerate((masks[-1:], masks[:-1], [0])):
+    for number, targets in enumerate((masks[:-1], masks[-1:], [0])):
         prepare = number == 0
         results = local_call(
-            functools.partial(translate_kernel, frame, tuple(late), tuple(targets)),
-            ([array(late_sources * frame, LANES)] * 2 if prepare else []) + [chunk] * len(targets),
+            functools.partial(translate_kernel, frame, others, tuple(late), tuple(targets)),
+            ([array(len(late) * own * frame, LANES)] * 2 if prepare else []) + [chunk] * len(targets),
             [VMEM] * (3 + len(last_sources)),
             [buffer(TOGETHER, frame, LANES)] * 2,
             20,
             flops=10_000_000 * len(targets),
             bytes_accessed=2_000_000 * len(targets),
-        )(late_operators, *sums, *last_sources)
+        )(operators, *sums, *last_sources)
         if prepare:
             last_sources, results = results[:2], results[2:]
         for d, result in zip(targets, results):

time: 39.8 us -> 39.2 us (0.985)
  starting transfers between devices: 12.6 us -> 13.4 us
  Pallas kernels: 17.7 us -> 17 us
  waiting for transfers between devices: 9.11 us -> 8.45 us
    ppermute x4, starting transfers between devices: 5.54 us -> 6.33 us  [swapped(): lax.ppermute(values, axis, [(i, ((i - first ^ 1) + first) % size) for i i...]
    ppermute x4, waiting for transfers between devices: 2.07 us -> 1.4 us  [swapped(): lax.ppermute(values, axis, [(i, ((i - first ^ 1) + first) % size) for i i...]
    pallas_call x1, Pallas kernels: 3.94 us -> 3.48 us  [on_device_exchange(): local_call(functools.partial(main_kernel, peers), [array(8, 2, ROWS_PER_P...]
  transfers between devices with their start and end apart: 10 -> 10, of which waited for: 5 -> 4; matrix products, arithmetic and copies ran while one was open for 0% -> 0% of each run, Pallas kernels for 33% -> 31%
where the time goes in v7:
time: 39.2 us; the launch traced here: 39 us
  Pallas kernels  17 us (43%)
  starting transfers between devices  13.4 us (34%)
  waiting for transfers between devices  8.45 us (22%)
    ppermute x6, starting transfers between devices, exchanged(): return lax.ppermute(values, axis, [(i, i ^ mask) for i in range(size)])  7.11 us
    ppermute x6, waiting for transfers between devices, exchanged(): return lax.ppermute(values, axis, [(i, i ^ mask) for i in range(size)])  7.05 us
    ppermute x4, starting transfers between devices, swapped(): lax.ppermute(values, axis, [(i, ((i - first ^ 1) + first) % size) for i i...  6.33 us
    pallas_call x1, Pallas kernels, on_device_exchange(): local_call(functools.partial(widen_kernel, peers, others), [array(parent_...  4.06 us
    pallas_call x1, Pallas kernels, on_device_exchange(): local_call(functools.partial(main_kernel, peers), [array(8, 2, ROWS_PER_P...  3.48 us
    pallas_call x1, Pallas kernels, on_device_exchange(): local_call(disaggregate_kernel, [array(pairs, azimuth_in, polar_in), arra...  2.86 us
    pallas_call x3, Pallas kernels, on_device_exchange(): local_call(functools.partial(translate_kernel, frame, others, tuple(late)...  2.09 us
    ppermute x4, waiting for transfers between devices, swapped(): lax.ppermute(values, axis, [(i, ((i - first ^ 1) + first) % size) for i i...  1.4 us
  transfers between devices with their start and end apart: 10, of which 4 were waited for; matrix products, arithmetic and copies ran while one was open for 0% of the time, Pallas kernels for 31%

profile of v7, /device:TPU:0, one launch (start us, length us, event | category | flops | bytes accessed | tf_op | source)
XLA Modules:
  0.0 39.0 jit_solution(4391820317898515090)
XLA Ops:
  0.0 1.2 %shard_map.92 = (f32[2,96,128]{2,1,0:T(8,128)S(1)}, f32[2,96,128]{2,1,0:T(8,128)S(1)}) custom-call(f32[96,32,128]{2,1,0:T(8,128)} %bitcast.14), custom_call_target="tpu_custom_call" | custom-call | flops 1000000 | bytes 1000000 | tf_op jit(solution)/shard_map/pallas_call | solution.py:683
  1.2 4.6 %collective-permute-start = (f32[2,96,128]{2,1,0:T(8,128)S(1)}, f32[2,96,128]{2,1,0:T(8,128)S(1)}, u32[]{:S(2)}, u32[]{:S(2)}) collective-permute-start(f32[2,96,128]{2,1,0:T(8,128)S(1)} %get-tuple-element.31), channel_id=1, source_target_pairs={{0,7},{1,2},{2,1},{3,4},{4,3},{5,6},{6,5},{7,0},{8,15},{9,10},{10,... | collective-permute-start | bytes 294920 | tf_op jit(solution)/shard_map/ppermute | solution.py:635
  5.8 0.0 collective-permute-start.1
  5.8 0.0 copy-start.3
  5.8 0.0 copy-start.5
  5.8 3.5 %shard_map.91 = (f32[8,2,9,8,128]{4,3,2,1,0:T(8,128)S(1)}, f32[7,2,48,128]{3,2,1,0:T(8,128)S(1)}, f32[1152,128]{1,0:T(8,128)S(1)}, bf16[316,40,128]{2,1,0:T(8,128)(2,1)S(1)}) custom-call(s32[48]{0:T(128)} %bitcast.11, s32[48]{0:T(128)} %octants_hbm.1, f32[3072,128]{1,0:T(8,128)} %bitcast.15, bf16[316,144,128]{2,1,0:T(8,128)(2,1)} %bitcast.16, ...), custom_call_target="tpu_custom_call" | custom-call | flops 4000000000 | bytes 12000000 | tf_op jit(solution)/shard_map/pallas_call | solution.py:695
  9.3 0.0 collective-permute-done.far_ref
  9.3 0.0 collective-permute-done.1.near_ref
  9.3 0.5 %shard_map.93 = (f32[288,128]{1,0:T(8,128)S(1)}, f32[288,128]{1,0:T(8,128)S(1)}, f32[288,128]{1,0:T(8,128)S(1)}, f32[288,128]{1,0:T(8,128)S(1)}) custom-call(s32[1,48]{1,0:T(1,128)S(1)} %copy-done.4, f32[2,96,128]{2,1,0:T(8,128)S(1)} %collective-permute-done.far_ref, f32[2,96,128]{2,1,0:T(8,128)S(1)} %collective-permute-done.1.near_ref, ...), custom_call_target="tpu_custom_call" | custom-call | flops 1000000 | bytes 1000000 | tf_op jit(solution)/shard_map/pallas_call | solution.py:729
  9.8 1.6 %collective-permute-start.2 = (f32[288,128]{1,0:T(8,128)S(1)}, f32[288,128]{1,0:T(8,128)S(1)}, u32[]{:S(2)}, u32[]{:S(2)}) collective-permute-start(f32[288,128]{1,0:T(8,128)S(1)} %get-tuple-element.36), channel_id=1, source_target_pairs={{0,8},{8,0},{16,24},{24,16},{1,9},{9,1},{17,25},{25,17},{2,10},{10... | collective-permute-start | bytes 442376 | tf_op jit(solution)/shard_map/ppermute | solution.py:640
  11.4 1.5 %collective-permute-start.3 = (f32[288,128]{1,0:T(8,128)S(1)}, f32[288,128]{1,0:T(8,128)S(1)}, u32[]{:S(2)}, u32[]{:S(2)}) collective-permute-start(f32[288,128]{1,0:T(8,128)S(1)} %get-tuple-element.41), channel_id=1, source_target_pairs={{0,16},{8,24},{16,0},{24,8},{1,17},{9,25},{17,1},{25,9},{2,18},{10... | collective-permute-start | bytes 442376 | tf_op jit(solution)/shard_map/ppermute | solution.py:640
  12.9 0.5 %collective-permute-start.4 = (f32[288,128]{1,0:T(8,128)S(1)}, f32[288,128]{1,0:T(8,128)S(1)}, u32[]{:S(2)}, u32[]{:S(2)}) collective-permute-start(f32[288,128]{1,0:T(8,128)S(1)} %get-tuple-element.42), channel_id=1, source_target_pairs={{0,24},{8,16},{16,8},{24,0},{1,25},{9,17},{17,9},{25,1},{2,26},{10... | collective-permute-start | bytes 442376 | tf_op jit(solution)/shard_map/ppermute | solution.py:640
  13.4 4.1 %shard_map.94 = (f32[30720,128]{1,0:T(8,128)S(1)}, f32[1280,128]{1,0:T(8,128)S(1)}, f32[1280,128]{1,0:T(8,128)S(1)}) custom-call(s32[32,31]{1,0:T(8,128)S(1)} %copy-done.2, s32[32,31]{1,0:T(8,128)S(1)} %copy-done.3, s32[1,32]{1,0:T(1,128)S(1)} %bitcast.12, bf16[316,40,128]{2,1,0:T(8,128)(2,1)S(1)} %get-tuple-element.30.table_ref, ...), custom_call_target="tpu_custom_call" | custom-call | flops 90000000 | bytes 12000000 | tf_op jit(solution)/shard_map/pallas_call | solution.py:743
  17.5 0.0 collective-permute-done.2.rest_0_
  17.5 1.2 %shard_map.95 = (f32[1280,128]{1,0:T(8,128)S(1)}, f32[1280,128]{1,0:T(8,128)S(1)}) custom-call(f32[30720,128]{1,0:T(8,128)S(1)} %get-tuple-element.35.placed_ref, f32[288,128]{1,0:T(8,128)S(1)} %collective-permute-done.2.rest_0_, f32[1280,128]{1,0:T(8,128)S(1)} %get-tuple-element.37.rest_1_, f32[1280,128]{1,0:T(8,128)S(1)} %get-tuple-element.38.rest_2_), custom_call_target="tpu_custom_call" | custom-call | flops 60000000 | bytes 12000000 | tf_op jit(solution)/shard_map/pallas_call | solution.py:760
  18.7 1.8 %collective-permute-done.3.rest_0_ = f32[288,128]{1,0:T(8,128)S(1)} collective-permute-done((f32[288,128]{1,0:T(8,128)S(1)}, f32[288,128]{1,0:T(8,128)S(1)}, u32[]{:S(2)}, u32[]{:S(2)}) %collective-permute-start.3) | collective-permute-done | bytes 147488 | tf_op jit(solution)/shard_map/ppermute | solution.py:640
  20.5 0.0 collective-permute-done.4.rest_1_
  20.5 1.1 %shard_map.96 = (f32[640,128]{1,0:T(8,128)S(1)}, f32[640,128]{1,0:T(8,128)S(1)}, f32[288,128]{1,0:T(8,128)S(1)}, f32[288,128]{1,0:T(8,128)S(1)}) custom-call(f32[30720,128]{1,0:T(8,128)S(1)} %get-tuple-element.35.placed_ref, f32[1280,128]{1,0:T(8,128)S(1)} %get-tuple-element.39.real_sum, f32[1280,128]{1,0:T(8,128)S(1)} %get-tuple-element.40.imag_sum, ...), custom_call_target="tpu_custom_call" | custom-call | flops 20000000 | bytes 4000000 | tf_op jit(solution)/shard_map/pallas_call | solution.py:774
  21.6 0.5 %shard_map.98 = f32[288,128]{1,0:T(8,128)S(1)} custom-call(f32[30720,128]{1,0:T(8,128)S(1)} %get-tuple-element.35.placed_ref, f32[1280,128]{1,0:T(8,128)S(1)} %get-tuple-element.39.real_sum, f32[1280,128]{1,0:T(8,128)S(1)} %get-tuple-element.40.imag_sum, f32[640,128]{1,0:T(8,128)S(1)} %get-tuple-element.43.rest_0_, f32[640,128]{1,0:T(8,128)S(1)} %get-tuple-element.44.rest_1_), custom_call_target="tpu_custom_call" | custom-call | flops 10000000 | bytes 2000000 | tf_op jit(solution)/shard_map/pallas_call | solution.py:774
  22.1 1.6 %collective-permute-start.7 = (f32[288,128]{1,0:T(8,128)S(1)}, f32[288,128]{1,0:T(8,128)S(1)}, u32[]{:S(2)}, u32[]{:S(2)}) collective-permute-start(f32[288,128]{1,0:T(8,128)S(1)} %shard_map.98), channel_id=1, source_target_pairs={{0,24},{8,16},{16,8},{24,0},{1,25},{9,17},{17,9},{25,1},{2,26},{10... | collective-permute-start | bytes 442376 | tf_op jit(solution)/shard_map/ppermute | solution.py:640
  23.7 1.5 %collective-permute-start.5 = (f32[288,128]{1,0:T(8,128)S(1)}, f32[288,128]{1,0:T(8,128)S(1)}, u32[]{:S(2)}, u32[]{:S(2)}) collective-permute-start(f32[288,128]{1,0:T(8,128)S(1)} %get-tuple-element.45), channel_id=1, source_target_pairs={{0,8},{8,0},{16,24},{24,16},{1,9},{9,1},{17,25},{25,17},{2,10},{10... | collective-permute-start | bytes 442376 | tf_op jit(solution)/shard_map/ppermute | solution.py:640
  25.2 0.5 %collective-permute-start.6 = (f32[288,128]{1,0:T(8,128)S(1)}, f32[288,128]{1,0:T(8,128)S(1)}, u32[]{:S(2)}, u32[]{:S(2)}) collective-permute-start(f32[288,128]{1,0:T(8,128)S(1)} %get-tuple-element.46), channel_id=1, source_target_pairs={{0,16},{8,24},{16,0},{24,8},{1,17},{9,25},{17,1},{25,9},{2,18},{10... | collective-permute-start | bytes 442376 | tf_op jit(solution)/shard_map/ppermute | solution.py:640
  25.7 0.5 %shard_map.97.rest_0_ = f32[288,128]{1,0:T(8,128)S(1)} custom-call(f32[30720,128]{1,0:T(8,128)S(1)} %get-tuple-element.35.placed_ref, f32[1280,128]{1,0:T(8,128)S(1)} %get-tuple-element.39.real_sum, f32[1280,128]{1,0:T(8,128)S(1)} %get-tuple-element.40.imag_sum, f32[640,128]{1,0:T(8,128)S(1)} %get-tuple-element.43.rest_0_, ...), custom_call_target="tpu_custom_call" | custom-call | flops 10000000 | bytes 2000000 | tf_op jit(solution)/shard_map/pallas_call | solution.py:774
  26.2 3.6 %collective-permute-done.7.rest_3_ = f32[288,128]{1,0:T(8,128)S(1)} collective-permute-done((f32[288,128]{1,0:T(8,128)S(1)}, f32[288,128]{1,0:T(8,128)S(1)}, u32[]{:S(2)}, u32[]{:S(2)}) %collective-permute-start.7) | collective-permute-done | bytes 147488 | tf_op jit(solution)/shard_map/ppermute | solution.py:640
  29.8 1.6 %collective-permute-done.5.rest_1_ = f32[288,128]{1,0:T(8,128)S(1)} collective-permute-done((f32[288,128]{1,0:T(8,128)S(1)}, f32[288,128]{1,0:T(8,128)S(1)}, u32[]{:S(2)}, u32[]{:S(2)}) %collective-permute-start.5) | collective-permute-done | bytes 147488 | tf_op jit(solution)/shard_map/ppermute | solution.py:640
  31.4 0.0 collective-permute-done.6.rest_2_
  31.4 0.6 %shard_map.99 = (f32[1152,128]{1,0:T(8,128)S(1)}, f32[2,96,128]{2,1,0:T(8,128)S(1)}, f32[2,96,128]{2,1,0:T(8,128)S(1)}) custom-call(s32[1,48]{1,0:T(1,128)S(1)} %copy-done.4, f32[7,2,48,128]{3,2,1,0:T(8,128)S(1)} %get-tuple-element.29.edge_phase_ref, bf16[2,256,256]{2,1,0:T(8,128)(2,1)S(1)} %copy-done.1, f32[288,128]{1,0:T(8,128)S(1)} %shard_map.97.rest_0_, ...), custom_call_target="tpu_custom_call" | custom-call | flops 1000000 | bytes 1000000 | tf_op jit(solution)/shard_map/pallas_call | solution.py:788
  32.0 1.7 %collective-permute-start.8 = (f32[2,96,128]{2,1,0:T(8,128)S(1)}, f32[2,96,128]{2,1,0:T(8,128)S(1)}, u32[]{:S(2)}, u32[]{:S(2)}) collective-permute-start(f32[2,96,128]{2,1,0:T(8,128)S(1)} %get-tuple-element.50), channel_id=1, source_target_pairs={{0,7},{1,2},{2,1},{3,4},{4,3},{5,6},{6,5},{7,0},{8,15},{9,10},{10,... | collective-permute-start | bytes 294920 | tf_op jit(solution)/shard_map/ppermute | solution.py:635
  33.7 0.0 collective-permute-start.9
  33.7 2.9 %shard_map.100 = (f32[96,32,128]{2,1,0:T(8,128)}, f32[2,96,8,128]{3,2,1,0:T(8,128)S(1)}) custom-call(s32[1,48]{1,0:T(1,128)S(1)} %copy-done.4, s32[1,48]{1,0:T(1,128)S(1)} %bitcast.13, f32[1152,128]{1,0:T(8,128)S(1)} %get-tuple-element.47.flat_ref, f32[8,2,9,8,128]{4,3,2,1,0:T(8,128)S(1)} %get-tuple-element.48.phase_ref, bf16[2,256,256]{2,1,0:T(8,128)(2,1)S(1)} %copy-done.1), custom_call_target="tpu_custom_call" | custom-call | flops 4000000000 | bytes 12000000 | tf_op jit(solution)/shard_map/pallas_call | solution.py:799
  36.6 1.4 %collective-permute-done.8.far_ref = f32[2,96,128]{2,1,0:T(8,128)S(1)} collective-permute-done((f32[2,96,128]{2,1,0:T(8,128)S(1)}, f32[2,96,128]{2,1,0:T(8,128)S(1)}, u32[]{:S(2)}, u32[]{:S(2)}) %collective-permute-start.8) | collective-permute-done | bytes 98336 | tf_op jit(solution)/shard_map/ppermute | solution.py:635
  38.0 1.0 %shard_map.101 = f32[96,32,128]{2,1,0:T(8,128)} custom-call(f32[2,96,8,128]{3,2,1,0:T(8,128)S(1)} %get-tuple-element.49.edge_ref, f32[2,96,128]{2,1,0:T(8,128)S(1)} %collective-permute-done.8.far_ref, f32[2,96,128]{2,1,0:T(8,128)S(1)} %collective-permute-done.9.near_ref, f32[96,32,128]{2,1,0:T(8,128)} %get-tuple-element.52.part_ref), custom_call_target="tpu_custom_call", output_to_operand_aliasing={{}: (3, {})} | custom-call | flops 1000000 | bytes 1000000 | tf_op jit(solution)/shard_map/pallas_call | solution.py:818
  (13 shorter events, 0.0 us)
Async XLA Ops:
  1.2 8.1 %collective-permute-start = (f32[2,96,128]{2,1,0:T(8,128)S(1)}, f32[2,96,128]{2,1,0:T(8,128)S(1)}, u32[]{:S(2)}, u32[]{:S(2)}) collective-permute-start(f32[2,96,128]{2,1,0:T(8,128)S(1)} %get-tuple-element.31), channel_id=1, source_target_pairs={{0,7},{1,2},{2,1},{3,4},{4,3},{5,6},{6,5},{7,0},{8,15},{9,10},{10,... | collective-permute-start | bytes 294920 | tf_op jit(solution)/shard_map/ppermute | solution.py:635
  5.8 3.5 %collective-permute-start.1 = (f32[2,96,128]{2,1,0:T(8,128)S(1)}, f32[2,96,128]{2,1,0:T(8,128)S(1)}, u32[]{:S(2)}, u32[]{:S(2)}) collective-permute-start(f32[2,96,128]{2,1,0:T(8,128)S(1)} %get-tuple-element.32), channel_id=1, source_target_pairs={{0,1},{1,0},{2,3},{3,2},{4,5},{5,4},{6,7},{7,6},{8,9},{9,8},{10,11... | collective-permute-start | bytes 294920 | tf_op jit(solution)/shard_map/ppermute | solution.py:635
  5.8 3.5 %copy-start = (bf16[2,384,256]{2,1,0:T(8,128)(2,1)S(1)}, bf16[2,384,256]{2,1,0:T(8,128)(2,1)}, u32[]{:S(2)}) copy-start(bf16[2,384,256]{2,1,0:T(8,128)(2,1)} %constant.4.clone.spread_hbm.spread_ref) | copy-start | bytes 1179652
  5.8 3.6 %copy-start.4 = (s32[1,48]{1,0:T(1,128)S(1)}, s32[1,48]{1,0:T(1,128)}, u32[]{:S(2)}) copy-start(s32[1,48]{1,0:T(1,128)} %parents_ref.5) | copy-start | bytes 580
  5.8 7.6 %copy-start.2 = (s32[32,31]{1,0:T(8,128)S(1)}, s32[32,31]{1,0:T(8,128)}, u32[]{:S(2)}) copy-start(s32[32,31]{1,0:T(8,128)} %source_ref.1) | copy-start | bytes 11908
  5.8 7.6 %copy-start.3 = (s32[32,31]{1,0:T(8,128)S(1)}, s32[32,31]{1,0:T(8,128)}, u32[]{:S(2)}) copy-start(s32[32,31]{1,0:T(8,128)} %offset_ref.1) | copy-start | bytes 11908
  5.8 7.6 %copy-start.5 = (s32[32]{0:T(128)S(1)}, s32[32]{0:T(128)}, u32[]{:S(2)}) copy-start(s32[32]{0:T(128)} %param.15) | copy-start | bytes 388
  9.8 7.6 %collective-permute-start.2 = (f32[288,128]{1,0:T(8,128)S(1)}, f32[288,128]{1,0:T(8,128)S(1)}, u32[]{:S(2)}, u32[]{:S(2)}) collective-permute-start(f32[288,128]{1,0:T(8,128)S(1)} %get-tuple-element.36), channel_id=1, source_target_pairs={{0,8},{8,0},{16,24},{24,16},{1,9},{9,1},{17,25},{25,17},{2,10},{10... | collective-permute-start | bytes 442376 | tf_op jit(solution)/shard_map/ppermute | solution.py:640
  11.4 9.1 %collective-permute-start.3 = (f32[288,128]{1,0:T(8,128)S(1)}, f32[288,128]{1,0:T(8,128)S(1)}, u32[]{:S(2)}, u32[]{:S(2)}) collective-permute-start(f32[288,128]{1,0:T(8,128)S(1)} %get-tuple-element.41), channel_id=1, source_target_pairs={{0,16},{8,24},{16,0},{24,8},{1,17},{9,25},{17,1},{25,9},{2,18},{10... | collective-permute-start | bytes 442376 | tf_op jit(solution)/shard_map/ppermute | solution.py:640
  12.9 7.6 %collective-permute-start.4 = (f32[288,128]{1,0:T(8,128)S(1)}, f32[288,128]{1,0:T(8,128)S(1)}, u32[]{:S(2)}, u32[]{:S(2)}) collective-permute-start(f32[288,128]{1,0:T(8,128)S(1)} %get-tuple-element.42), channel_id=1, source_target_pairs={{0,24},{8,16},{16,8},{24,0},{1,25},{9,17},{17,9},{25,1},{2,26},{10... | collective-permute-start | bytes 442376 | tf_op jit(solution)/shard_map/ppermute | solution.py:640
  22.1 7.7 %collective-permute-start.7 = (f32[288,128]{1,0:T(8,128)S(1)}, f32[288,128]{1,0:T(8,128)S(1)}, u32[]{:S(2)}, u32[]{:S(2)}) collective-permute-start(f32[288,128]{1,0:T(8,128)S(1)} %shard_map.98), channel_id=1, source_target_pairs={{0,24},{8,16},{16,8},{24,0},{1,25},{9,17},{17,9},{25,1},{2,26},{10... | collective-permute-start | bytes 442376 | tf_op jit(solution)/shard_map/ppermute | solution.py:640
  23.7 7.7 %collective-permute-start.5 = (f32[288,128]{1,0:T(8,128)S(1)}, f32[288,128]{1,0:T(8,128)S(1)}, u32[]{:S(2)}, u32[]{:S(2)}) collective-permute-start(f32[288,128]{1,0:T(8,128)S(1)} %get-tuple-element.45), channel_id=1, source_target_pairs={{0,8},{8,0},{16,24},{24,16},{1,9},{9,1},{17,25},{25,17},{2,10},{10... | collective-permute-start | bytes 442376 | tf_op jit(solution)/shard_map/ppermute | solution.py:640
  25.2 6.3 %copy-start.1 = (bf16[2,256,256]{2,1,0:T(8,128)(2,1)S(1)}, bf16[2,256,256]{2,1,0:T(8,128)(2,1)}, u32[]{:S(2)}) copy-start(bf16[2,256,256]{2,1,0:T(8,128)(2,1)} %constant.5.clone.gather_ref) | copy-start | bytes 786436
  25.2 8.6 %copy-start.6 = (s32[48]{0:T(128)S(1)}, s32[48]{0:T(128)}, u32[]{:S(2)}) copy-start(s32[48]{0:T(128)} %octants_hbm.1) | copy-start | bytes 580
  25.2 6.2 %collective-permute-start.6 = (f32[288,128]{1,0:T(8,128)S(1)}, f32[288,128]{1,0:T(8,128)S(1)}, u32[]{:S(2)}, u32[]{:S(2)}) collective-permute-start(f32[288,128]{1,0:T(8,128)S(1)} %get-tuple-element.46), channel_id=1, source_target_pairs={{0,16},{8,24},{16,0},{24,8},{1,17},{9,25},{17,1},{25,9},{2,18},{10... | collective-permute-start | bytes 442376 | tf_op jit(solution)/shard_map/ppermute | solution.py:640
  32.0 6.0 %collective-permute-start.8 = (f32[2,96,128]{2,1,0:T(8,128)S(1)}, f32[2,96,128]{2,1,0:T(8,128)S(1)}, u32[]{:S(2)}, u32[]{:S(2)}) collective-permute-start(f32[2,96,128]{2,1,0:T(8,128)S(1)} %get-tuple-element.50), channel_id=1, source_target_pairs={{0,7},{1,2},{2,1},{3,4},{4,3},{5,6},{6,5},{7,0},{8,15},{9,10},{10,... | collective-permute-start | bytes 294920 | tf_op jit(solution)/shard_map/ppermute | solution.py:635
  33.7 4.3 %collective-permute-start.9 = (f32[2,96,128]{2,1,0:T(8,128)S(1)}, f32[2,96,128]{2,1,0:T(8,128)S(1)}, u32[]{:S(2)}, u32[]{:S(2)}) collective-permute-start(f32[2,96,128]{2,1,0:T(8,128)S(1)} %get-tuple-element.51), channel_id=1, source_target_pairs={{0,1},{1,0},{2,3},{3,2},{4,5},{5,4},{6,7},{7,6},{8,9},{9,8},{10,11... | collective-permute-start | bytes 294920 | tf_op jit(solution)/shard_map/ppermute | solution.py:635

commit v8 on v7

--- a/solution.py
+++ b/solution.py
@@ -498,28 +498,75 @@
         lax.fori_loop(0, own // TOGETHER, some_targets, 0)
 
 
-def edge_kernel(peers, own2, parents_ref, edge_phase_ref, gather_ref, *rest):
+def extract_kernel(peers, own2, *rest):
     chunks = rest[:peers]
     flat, far_ref, near_ref = rest[peers:]
     share = chunks[0].shape[0] // own2
     periods = share * peers // ROWS_PER_PERIOD
     own = own2 // 2
-    pairs = far_ref.shape[1]
     flat_rows = ROWS_PER_PERIOD * periods
     me = lax.axis_index("clus")
     for gp in range(own2):
         for d in range(peers):
             flat[pl.ds(gp * flat_rows + (me ^ d) * share, share), :] = chunks[d][gp * share : (gp + 1) * share, :]
-    edges = []
-    for w, m in edge_rows(periods):
-        for part in range(2):
-            edges.append(flat[pl.ds(part * flat_rows + ROWS_PER_PERIOD * m + w, own, stride=2 * flat_rows), :])
-    per_child = dot2(one_hot(parents_ref[...], own).T, jnp.concatenate(edges, axis=1))
+
+    def fill(prev_ref, next_ref):
+        for ref in (prev_ref, next_ref):
+            ref[...] = jnp.zeros_like(ref)
+        places = [(prev_ref, e) for e in range(4)] + [(next_ref, e) for e in range(3)]
+        for (ref, e), (w, m) in zip(places, edge_rows(periods)):
+            for part in range(2):
+                first = part * flat_rows + ROWS_PER_PERIOD * m + w
+                row = (2 * e + part) * own
+                ref[row : row + own, :] = flat[pl.ds(first, own, stride=2 * flat_rows), :]
+
+    by_parity(lambda: fill(far_ref, near_ref), lambda: fill(near_ref, far_ref))
+
+
+def neighbour_kernel(periods, octants_hbm, out_ref, by_octant, octants_ref, sem):
+    copy = pltpu.make_async_copy(octants_hbm, octants_ref, sem)
+    copy.start()
+    here = lax.axis_index("dir")
+    octant = lax.broadcasted_iota(jnp.int32, (8, LANES), 0)
+    lane = lax.broadcasted_iota(jnp.int32, (8, LANES), 1)
+    signs = [(1 - 2 * ((octant >> bit) & 1)).astype(f32) for bit in range(3)]
+    for e, (w, m) in enumerate(edge_rows(periods)):
+        place = here + 1 if m == 0 else here - 1
+        position = lane + w * LANES
+        row = w * LANES // NTHETA_P
+        row = jnp.where(position >= (row + 1) * NTHETA_P, row + 1, row)
+        polar_index = position - row * NTHETA_P
+        azimuth_index = (place * periods + m) * PERIOD_P + row
+        sin_polar, cos_polar = sincos_turns((polar_index.astype(f32) + 0.5) / (2 * NTHETA_P))
+        sin_azimuth, cos_azimuth = sincos_turns(azimuth_index.astype(f32) / NPHI_P)
+        along = (sin_polar * cos_azimuth, sin_polar * sin_azimuth, cos_polar)
+        sine, cosine = sincos_turns(4.0 * (signs[0] * along[0] + signs[1] * along[1] + signs[2] * along[2]))
+        by_octant[e, 0] = cosine
+        by_octant[e, 1] = sine
+    copy.wait()
+
+    def some_children(step, carry):
+        for j in range(GROUP):
+            k = step * GROUP + j
+            for e in range(by_octant.shape[0]):
+                for i in range(2):
+                    out_ref[e, i, pl.ds(k, 1), :] = by_octant[e, i, pl.ds(octants_ref[k], 1), :]
+        return carry
+
+    lax.fori_loop(0, octants_ref.shape[0] // GROUP, some_children, 0)
+
+
+def edge_contributions(parents, phase_ref, gather_ref, above, below):
+    children = parents.shape[1]
+    own = below.shape[0] // 8
+    rows = [above[2 * e * own : 2 * (e + 1) * own] for e in range(4)] + [below[2 * e * own : 2 * (e + 1) * own] for e in range(3)]
+    edges = jnp.concatenate([r[part * own : (part + 1) * own] for r in rows for part in range(2)], axis=1)
+    per_child = dot2(one_hot(parents, own).T, edges)
     returned = []
-    for e in range(len(edges) // 2):
+    for e in range(len(rows)):
         real = per_child[:, 2 * e * LANES : (2 * e + 1) * LANES]
         imaginary = per_child[:, (2 * e + 1) * LANES : (2 * e + 2) * LANES]
-        cosine, sine = edge_phase_ref[e, 0], edge_phase_ref[e, 1]
+        cosine, sine = phase_ref[e, 0], phase_ref[e, 1]
         returned.append(
             jnp.concatenate([real * cosine + imaginary * sine, imaginary * cosine - real * sine], axis=0)
         )
@@ -529,14 +576,10 @@
     even = gather_dot(*split(even), gather_ref, 0)
     odd = gather_dot(*split(odd), gather_ref, 1)
     a, b = TAPS_A, TAPS_B
-
-    def fill(prev_ref, next_ref):
-        below = a[0] * odd[:pairs] + b[0] * even[:pairs]
-        for i in range(2):
-            prev_ref[i] = below
-            next_ref[i] = a[3 + i] * even[pairs:] + b[3 + i] * odd[pairs:]
-
-    by_parity(lambda: fill(far_ref, near_ref), lambda: fill(near_ref, far_ref))
+    pairs = 2 * children
+    last = a[0] * odd[:pairs] + b[0] * even[:pairs]
+    first = [a[3 + i] * even[pairs:] + b[3 + i] * odd[pairs:] for i in range(2)]
+    return first, last
 
 
 def disaggregate_kernel(
@@ -608,12 +651,13 @@
         written(block).wait()
 
 
-def finish_kernel(edge_ref, far_ref, near_ref, part_ref, out_ref, tiles, sems):
+def finish_kernel(parents_ref, phase_ref, gather_ref, edge_ref, far_ref, near_ref, part_ref, out_ref, tiles, sems):
     pairs, azimuth_in, _ = out_ref.shape
     tiles[...] = edge_ref[...]
     flat = tiles.reshape(2 * pairs * TILE, LANES)
-    before, after = from_sides(far_ref, near_ref)
-    ends = ((0, 0, before[0]), (0, 1, before[1]), (1, TILE - 1, after[0]))
+    below, above = from_sides(far_ref, near_ref)
+    heads, tail = edge_contributions(parents_ref[...], phase_ref, gather_ref, above, below)
+    ends = ((0, 0, heads[0]), (0, 1, heads[1]), (1, TILE - 1, tail))
     copies = []
     for i, start in enumerate((0, azimuth_in - TILE)):
         for end, row, values in ends:
@@ -769,7 +813,7 @@
 
     back = {}
     last_sources = [received[d] for d in late]
-    for number, targets in enumerate((masks[:-1], masks[-1:], [0])):
+    for number, targets in enumerate((masks[-1:], masks[:-1], [0])):
         prepare = number == 0
         results = local_call(
             functools.partial(translate_kernel, frame, others, tuple(late), tuple(targets)),
@@ -785,13 +829,23 @@
         for d, result in zip(targets, results):
             back[d] = exchanged(result, "clus", d) if d else result
 
+    neighbour_phases = local_call(
+        functools.partial(neighbour_kernel, periods),
+        array(edges, 2, children, LANES),
+        [HBM],
+        [buffer(edges, 2, 8, LANES), pltpu.SMEM((children,), jnp.int32), pltpu.SemaphoreType.DMA],
+        8,
+        flops=20_000_000,
+    )(in_hbm(child_octant))
+
+    side = array(8 * own, LANES)
     incoming, to_far, to_near = local_call(
-        functools.partial(edge_kernel, peers, 2 * own),
-        [array(2 * own * flat_rows, LANES), edge, edge],
-        [VMEM] * (3 + peers),
+        functools.partial(extract_kernel, peers, 2 * own),
+        [array(2 * own * flat_rows, LANES), side, side],
+        [VMEM] * peers,
         [],
         8,
-    )(child_parent, edge_phases, gather, *[back[d] for d in range(peers)])
+    )(*[back[d] for d in range(peers)])
 
     from_far = swapped(to_far, "dir", 1)
     from_near = swapped(to_near, "dir", 0)
@@ -818,12 +872,12 @@
     out = local_call(
         finish_kernel,
         array(pairs, azimuth_in, polar_in),
-        [VMEM] * 3 + [HBM],
+        [VMEM] * 6 + [HBM],
         [buffer(2, pairs, TILE, polar_in), pltpu.SemaphoreType.DMA((2,))],
         8,
         out_specs=HBM,
-        aliases={3: 0},
-    )(edge_tiles, from_far, from_near, in_hbm(inner))
+        aliases={6: 0},
+    )(child_parent, neighbour_phases, gather, edge_tiles, from_far, from_near, in_hbm(inner))
     return out.reshape(child_patterns.shape)
 
 

time: 39.2 us -> 38.7 us (0.987)
  Pallas kernels: 17 us -> 18.1 us
  waiting for transfers between devices: 8.45 us -> 7.53 us
  starting transfers between devices: 13.4 us -> 12.7 us
    pallas_call x2 -> x3, Pallas kernels: 1.57 us -> 2.64 us  [the longest x1 1.47 us: on_device_exchange(): local_call(finish_kernel, array(pairs, azimuth_in, polar_in), [VMEM] * 6...]
    ppermute x6, waiting for transfers between devices: 7.05 us -> 6.21 us  [exchanged(): return lax.ppermute(values, axis, [(i, i ^ mask) for i in range(size)])]
    ppermute x4, starting transfers between devices: 6.33 us -> 5.58 us  [swapped(): lax.ppermute(values, axis, [(i, ((i - first ^ 1) + first) % size) for i i...]
  transfers between devices with their start and end apart: 10 -> 10, of which waited for: 4 -> 4; matrix products, arithmetic and copies ran while one was open for 0% -> 0% of each run, Pallas kernels for 31% -> 34%
where the time goes in v8:
time: 38.7 us; the launch traced here: 38.5 us
  Pallas kernels  18.1 us (47%)
  starting transfers between devices  12.7 us (33%)
  waiting for transfers between devices  7.53 us (19%)
    ppermute x6, starting transfers between devices, exchanged(): return lax.ppermute(values, axis, [(i, i ^ mask) for i in range(size)])  7.11 us
    ppermute x6, waiting for transfers between devices, exchanged(): return lax.ppermute(values, axis, [(i, i ^ mask) for i in range(size)])  6.21 us
    ppermute x4, starting transfers between devices, swapped(): lax.ppermute(values, axis, [(i, ((i - first ^ 1) + first) % size) for i i...  5.58 us
    pallas_call x1, Pallas kernels, on_device_exchange(): local_call(functools.partial(widen_kernel, peers, others), [array(parent_...  4.06 us
    pallas_call x1, Pallas kernels, on_device_exchange(): local_call(functools.partial(main_kernel, peers), [array(8, 2, ROWS_PER_P...  3.48 us
    pallas_call x1, Pallas kernels, on_device_exchange(): local_call(disaggregate_kernel, [array(pairs, azimuth_in, polar_in), arra...  2.88 us
    pallas_call x3, Pallas kernels, on_device_exchange(): local_call(functools.partial(translate_kernel, frame, others, tuple(late)...  2.1 us
    pallas_call x1, Pallas kernels, on_device_exchange(): local_call(finish_kernel, array(pairs, azimuth_in, polar_in), [VMEM] * 6...  1.47 us
  transfers between devices with their start and end apart: 10, of which 4 were waited for; matrix products, arithmetic and copies ran while one was open for 0% of the time, Pallas kernels for 34%

profile of v8, /device:TPU:0, one launch (start us, length us, event | category | flops | bytes accessed | tf_op | source)
XLA Modules:
  0.0 38.5 jit_solution(9790321024022810360)
XLA Ops:
  0.0 1.2 %shard_map.93 = (f32[2,96,128]{2,1,0:T(8,128)S(1)}, f32[2,96,128]{2,1,0:T(8,128)S(1)}) custom-call(f32[96,32,128]{2,1,0:T(8,128)} %bitcast.14), custom_call_target="tpu_custom_call" | custom-call | flops 1000000 | bytes 1000000 | tf_op jit(solution)/shard_map/pallas_call | solution.py:727
  1.2 4.6 %collective-permute-start = (f32[2,96,128]{2,1,0:T(8,128)S(1)}, f32[2,96,128]{2,1,0:T(8,128)S(1)}, u32[]{:S(2)}, u32[]{:S(2)}) collective-permute-start(f32[2,96,128]{2,1,0:T(8,128)S(1)} %get-tuple-element.31), channel_id=1, source_target_pairs={{0,7},{1,2},{2,1},{3,4},{4,3},{5,6},{6,5},{7,0},{8,15},{9,10},{10,... | collective-permute-start | bytes 294920 | tf_op jit(solution)/shard_map/ppermute | solution.py:679
  5.8 0.0 collective-permute-start.1
  5.8 0.0 copy-start.3
  5.8 0.0 copy-start.5
  5.8 3.5 %shard_map.92 = (f32[8,2,9,8,128]{4,3,2,1,0:T(8,128)S(1)}, f32[7,2,48,128]{3,2,1,0:T(8,128)S(1)}, f32[1152,128]{1,0:T(8,128)S(1)}, bf16[316,40,128]{2,1,0:T(8,128)(2,1)S(1)}) custom-call(s32[48]{0:T(128)} %bitcast.11, s32[48]{0:T(128)} %octants_hbm.3, f32[3072,128]{1,0:T(8,128)} %bitcast.15, bf16[316,144,128]{2,1,0:T(8,128)(2,1)} %bitcast.16, ...), custom_call_target="tpu_custom_call" | custom-call | flops 4000000000 | bytes 12000000 | tf_op jit(solution)/shard_map/pallas_call | solution.py:739
  9.3 0.0 collective-permute-done.1.near_ref
  9.3 0.5 %shard_map.94 = (f32[288,128]{1,0:T(8,128)S(1)}, f32[288,128]{1,0:T(8,128)S(1)}, f32[288,128]{1,0:T(8,128)S(1)}, f32[288,128]{1,0:T(8,128)S(1)}) custom-call(s32[1,48]{1,0:T(1,128)S(1)} %copy-done.4, f32[2,96,128]{2,1,0:T(8,128)S(1)} %collective-permute-done.far_ref, f32[2,96,128]{2,1,0:T(8,128)S(1)} %collective-permute-done.1.near_ref, ...), custom_call_target="tpu_custom_call" | custom-call | flops 1000000 | bytes 1000000 | tf_op jit(solution)/shard_map/pallas_call | solution.py:773
  9.8 1.6 %collective-permute-start.2 = (f32[288,128]{1,0:T(8,128)S(1)}, f32[288,128]{1,0:T(8,128)S(1)}, u32[]{:S(2)}, u32[]{:S(2)}) collective-permute-start(f32[288,128]{1,0:T(8,128)S(1)} %get-tuple-element.37), channel_id=1, source_target_pairs={{0,8},{8,0},{16,24},{24,16},{1,9},{9,1},{17,25},{25,17},{2,10},{10... | collective-permute-start | bytes 442376 | tf_op jit(solution)/shard_map/ppermute | solution.py:684
  11.4 1.5 %collective-permute-start.3 = (f32[288,128]{1,0:T(8,128)S(1)}, f32[288,128]{1,0:T(8,128)S(1)}, u32[]{:S(2)}, u32[]{:S(2)}) collective-permute-start(f32[288,128]{1,0:T(8,128)S(1)} %get-tuple-element.42), channel_id=1, source_target_pairs={{0,16},{8,24},{16,0},{24,8},{1,17},{9,25},{17,1},{25,9},{2,18},{10... | collective-permute-start | bytes 442376 | tf_op jit(solution)/shard_map/ppermute | solution.py:684
  12.9 0.5 %collective-permute-start.4 = (f32[288,128]{1,0:T(8,128)S(1)}, f32[288,128]{1,0:T(8,128)S(1)}, u32[]{:S(2)}, u32[]{:S(2)}) collective-permute-start(f32[288,128]{1,0:T(8,128)S(1)} %get-tuple-element.43), channel_id=1, source_target_pairs={{0,24},{8,16},{16,8},{24,0},{1,25},{9,17},{17,9},{25,1},{2,26},{10... | collective-permute-start | bytes 442376 | tf_op jit(solution)/shard_map/ppermute | solution.py:684
  13.4 4.1 %shard_map.95 = (f32[30720,128]{1,0:T(8,128)S(1)}, f32[1280,128]{1,0:T(8,128)S(1)}, f32[1280,128]{1,0:T(8,128)S(1)}) custom-call(s32[32,31]{1,0:T(8,128)S(1)} %copy-done.2, s32[32,31]{1,0:T(8,128)S(1)} %copy-done.3, s32[1,32]{1,0:T(1,128)S(1)} %bitcast.12, bf16[316,40,128]{2,1,0:T(8,128)(2,1)S(1)} %get-tuple-element.30.table_ref, ...), custom_call_target="tpu_custom_call" | custom-call | flops 90000000 | bytes 12000000 | tf_op jit(solution)/shard_map/pallas_call | solution.py:787
  17.5 0.0 collective-permute-done.2.rest_0_
  17.5 1.2 %shard_map.96 = (f32[1280,128]{1,0:T(8,128)S(1)}, f32[1280,128]{1,0:T(8,128)S(1)}) custom-call(f32[30720,128]{1,0:T(8,128)S(1)} %get-tuple-element.36.placed_ref, f32[288,128]{1,0:T(8,128)S(1)} %collective-permute-done.2.rest_0_, f32[1280,128]{1,0:T(8,128)S(1)} %get-tuple-element.38.rest_1_, f32[1280,128]{1,0:T(8,128)S(1)} %get-tuple-element.39.rest_2_), custom_call_target="tpu_custom_call" | custom-call | flops 60000000 | bytes 12000000 | tf_op jit(solution)/shard_map/pallas_call | solution.py:804
  18.7 1.8 %collective-permute-done.3.rest_0_ = f32[288,128]{1,0:T(8,128)S(1)} collective-permute-done((f32[288,128]{1,0:T(8,128)S(1)}, f32[288,128]{1,0:T(8,128)S(1)}, u32[]{:S(2)}, u32[]{:S(2)}) %collective-permute-start.3) | collective-permute-done | bytes 147488 | tf_op jit(solution)/shard_map/ppermute | solution.py:684
  20.5 0.0 collective-permute-done.4.rest_1_
  20.5 0.6 %shard_map.97 = (f32[640,128]{1,0:T(8,128)S(1)}, f32[640,128]{1,0:T(8,128)S(1)}, f32[288,128]{1,0:T(8,128)S(1)}) custom-call(f32[30720,128]{1,0:T(8,128)S(1)} %get-tuple-element.36.placed_ref, f32[1280,128]{1,0:T(8,128)S(1)} %get-tuple-element.40.real_sum, f32[1280,128]{1,0:T(8,128)S(1)} %get-tuple-element.41.imag_sum, ...), custom_call_target="tpu_custom_call" | custom-call | flops 10000000 | bytes 2000000 | tf_op jit(solution)/shard_map/pallas_call | solution.py:818
  21.1 1.0 %shard_map.99 = (f32[288,128]{1,0:T(8,128)S(1)}, f32[288,128]{1,0:T(8,128)S(1)}) custom-call(f32[30720,128]{1,0:T(8,128)S(1)} %get-tuple-element.36.placed_ref, f32[1280,128]{1,0:T(8,128)S(1)} %get-tuple-element.40.real_sum, f32[1280,128]{1,0:T(8,128)S(1)} %get-tuple-element.41.imag_sum, f32[640,128]{1,0:T(8,128)S(1)} %get-tuple-element.44.rest_0_, ...), custom_call_target="tpu_custom_call" | custom-call | flops 20000000 | bytes 4000000 | tf_op jit(solution)/shard_map/pallas_call | solution.py:818
  22.1 1.3 %collective-permute-start.5 = (f32[288,128]{1,0:T(8,128)S(1)}, f32[288,128]{1,0:T(8,128)S(1)}, u32[]{:S(2)}, u32[]{:S(2)}) collective-permute-start(f32[288,128]{1,0:T(8,128)S(1)} %get-tuple-element.46), channel_id=1, source_target_pairs={{0,8},{8,0},{16,24},{24,16},{1,9},{9,1},{17,25},{25,17},{2,10},{10... | collective-permute-start | bytes 442376 | tf_op jit(solution)/shard_map/ppermute | solution.py:684
  23.4 0.8 %collective-permute-start.6 = (f32[288,128]{1,0:T(8,128)S(1)}, f32[288,128]{1,0:T(8,128)S(1)}, u32[]{:S(2)}, u32[]{:S(2)}) collective-permute-start(f32[288,128]{1,0:T(8,128)S(1)} %get-tuple-element.47), channel_id=1, source_target_pairs={{0,16},{8,24},{16,0},{24,8},{1,17},{9,25},{17,1},{25,9},{2,18},{10... | collective-permute-start | bytes 442376 | tf_op jit(solution)/shard_map/ppermute | solution.py:684
  24.2 1.4 %collective-permute-start.7 = (f32[288,128]{1,0:T(8,128)S(1)}, f32[288,128]{1,0:T(8,128)S(1)}, u32[]{:S(2)}, u32[]{:S(2)}) collective-permute-start(f32[288,128]{1,0:T(8,128)S(1)} %get-tuple-element.48), channel_id=1, source_target_pairs={{0,24},{8,16},{16,8},{24,0},{1,25},{9,17},{17,9},{25,1},{2,26},{10... | collective-permute-start | bytes 442376 | tf_op jit(solution)/shard_map/ppermute | solution.py:684
  25.7 1.1 %shard_map.91.phase_ref = f32[7,2,48,128]{3,2,1,0:T(8,128)S(1)} custom-call(s32[48]{0:T(128)} %octants_hbm.3), custom_call_target="tpu_custom_call" | custom-call | flops 20000000 | bytes 1000000 | tf_op jit(solution)/shard_map/pallas_call | solution.py:832
  26.8 0.0 copy-start.1
  26.8 0.0 copy-start.6
  26.8 0.5 %shard_map.98.rest_0_ = f32[288,128]{1,0:T(8,128)S(1)} custom-call(f32[30720,128]{1,0:T(8,128)S(1)} %get-tuple-element.36.placed_ref, f32[1280,128]{1,0:T(8,128)S(1)} %get-tuple-element.40.real_sum, f32[1280,128]{1,0:T(8,128)S(1)} %get-tuple-element.41.imag_sum, f32[640,128]{1,0:T(8,128)S(1)} %get-tuple-element.44.rest_0_, ...), custom_call_target="tpu_custom_call" | custom-call | flops 10000000 | bytes 2000000 | tf_op jit(solution)/shard_map/pallas_call | solution.py:818
  27.3 0.9 %collective-permute-done.5.rest_1_ = f32[288,128]{1,0:T(8,128)S(1)} collective-permute-done((f32[288,128]{1,0:T(8,128)S(1)}, f32[288,128]{1,0:T(8,128)S(1)}, u32[]{:S(2)}, u32[]{:S(2)}) %collective-permute-start.5) | collective-permute-done | bytes 147488 | tf_op jit(solution)/shard_map/ppermute | solution.py:684
  28.2 3.5 %collective-permute-done.6.rest_2_ = f32[288,128]{1,0:T(8,128)S(1)} collective-permute-done((f32[288,128]{1,0:T(8,128)S(1)}, f32[288,128]{1,0:T(8,128)S(1)}, u32[]{:S(2)}, u32[]{:S(2)}) %collective-permute-start.6) | collective-permute-done | bytes 147488 | tf_op jit(solution)/shard_map/ppermute | solution.py:684
  31.7 0.1 shard_map.100
  31.8 1.0 %collective-permute-start.8 = (f32[64,128]{1,0:T(8,128)S(1)}, f32[64,128]{1,0:T(8,128)S(1)}, u32[]{:S(2)}, u32[]{:S(2)}) collective-permute-start(f32[64,128]{1,0:T(8,128)S(1)} %get-tuple-element.52), channel_id=1, source_target_pairs={{0,7},{1,2},{2,1},{3,4},{4,3},{5,6},{6,5},{7,0},{8,15},{9,10},{10,... | collective-permute-start | bytes 98312 | tf_op jit(solution)/shard_map/ppermute | solution.py:679
  32.8 2.9 %shard_map.101 = (f32[96,32,128]{2,1,0:T(8,128)}, f32[2,96,8,128]{3,2,1,0:T(8,128)S(1)}) custom-call(s32[1,48]{1,0:T(1,128)S(1)} %copy-done.4, s32[1,48]{1,0:T(1,128)S(1)} %bitcast.13, f32[1152,128]{1,0:T(8,128)S(1)} %get-tuple-element.49.flat_ref, f32[8,2,9,8,128]{4,3,2,1,0:T(8,128)S(1)} %get-tuple-element.50.phase_ref, bf16[2,256,256]{2,1,0:T(8,128)(2,1)S(1)} %copy-done.1), custom_call_target="tpu_custom_call" | custom-call | flops 4000000000 | bytes 12000000 | tf_op jit(solution)/shard_map/pallas_call | solution.py:853
  35.7 1.3 %collective-permute-done.8.far_ref = f32[64,128]{1,0:T(8,128)S(1)} collective-permute-done((f32[64,128]{1,0:T(8,128)S(1)}, f32[64,128]{1,0:T(8,128)S(1)}, u32[]{:S(2)}, u32[]{:S(2)}) %collective-permute-start.8) | collective-permute-done | bytes 32800 | tf_op jit(solution)/shard_map/ppermute | solution.py:679
  37.0 1.5 %shard_map.102 = f32[96,32,128]{2,1,0:T(8,128)} custom-call(s32[1,48]{1,0:T(1,128)S(1)} %copy-done.4, f32[7,2,48,128]{3,2,1,0:T(8,128)S(1)} %shard_map.91.phase_ref, bf16[2,256,256]{2,1,0:T(8,128)(2,1)S(1)} %copy-done.1, f32[2,96,8,128]{3,2,1,0:T(8,128)S(1)} %get-tuple-element.51.edge_ref, ...), custom_call_target="tpu_custom_call", output_to_operand_aliasing={{}: (6, {})} | custom-call | flops 1000000 | bytes 1000000 | tf_op jit(solution)/shard_map/pallas_call | solution.py:872
  (14 shorter events, 0.0 us)
Async XLA Ops:
  1.2 8.1 %collective-permute-start = (f32[2,96,128]{2,1,0:T(8,128)S(1)}, f32[2,96,128]{2,1,0:T(8,128)S(1)}, u32[]{:S(2)}, u32[]{:S(2)}) collective-permute-start(f32[2,96,128]{2,1,0:T(8,128)S(1)} %get-tuple-element.31), channel_id=1, source_target_pairs={{0,7},{1,2},{2,1},{3,4},{4,3},{5,6},{6,5},{7,0},{8,15},{9,10},{10,... | collective-permute-start | bytes 294920 | tf_op jit(solution)/shard_map/ppermute | solution.py:679
  5.8 3.5 %collective-permute-start.1 = (f32[2,96,128]{2,1,0:T(8,128)S(1)}, f32[2,96,128]{2,1,0:T(8,128)S(1)}, u32[]{:S(2)}, u32[]{:S(2)}) collective-permute-start(f32[2,96,128]{2,1,0:T(8,128)S(1)} %get-tuple-element.32), channel_id=1, source_target_pairs={{0,1},{1,0},{2,3},{3,2},{4,5},{5,4},{6,7},{7,6},{8,9},{9,8},{10,11... | collective-permute-start | bytes 294920 | tf_op jit(solution)/shard_map/ppermute | solution.py:679
  5.8 3.5 %copy-start = (bf16[2,384,256]{2,1,0:T(8,128)(2,1)S(1)}, bf16[2,384,256]{2,1,0:T(8,128)(2,1)}, u32[]{:S(2)}) copy-start(bf16[2,384,256]{2,1,0:T(8,128)(2,1)} %constant.4.clone.spread_hbm.spread_ref) | copy-start | bytes 1179652
  5.8 3.6 %copy-start.4 = (s32[1,48]{1,0:T(1,128)S(1)}, s32[1,48]{1,0:T(1,128)}, u32[]{:S(2)}) copy-start(s32[1,48]{1,0:T(1,128)} %parents_ref.5) | copy-start | bytes 580
  5.8 7.6 %copy-start.2 = (s32[32,31]{1,0:T(8,128)S(1)}, s32[32,31]{1,0:T(8,128)}, u32[]{:S(2)}) copy-start(s32[32,31]{1,0:T(8,128)} %source_ref.1) | copy-start | bytes 11908
  5.8 7.6 %copy-start.3 = (s32[32,31]{1,0:T(8,128)S(1)}, s32[32,31]{1,0:T(8,128)}, u32[]{:S(2)}) copy-start(s32[32,31]{1,0:T(8,128)} %offset_ref.1) | copy-start | bytes 11908
  5.8 7.6 %copy-start.5 = (s32[32]{0:T(128)S(1)}, s32[32]{0:T(128)}, u32[]{:S(2)}) copy-start(s32[32]{0:T(128)} %param.15) | copy-start | bytes 388
  9.8 7.6 %collective-permute-start.2 = (f32[288,128]{1,0:T(8,128)S(1)}, f32[288,128]{1,0:T(8,128)S(1)}, u32[]{:S(2)}, u32[]{:S(2)}) collective-permute-start(f32[288,128]{1,0:T(8,128)S(1)} %get-tuple-element.37), channel_id=1, source_target_pairs={{0,8},{8,0},{16,24},{24,16},{1,9},{9,1},{17,25},{25,17},{2,10},{10... | collective-permute-start | bytes 442376 | tf_op jit(solution)/shard_map/ppermute | solution.py:684
  11.4 9.1 %collective-permute-start.3 = (f32[288,128]{1,0:T(8,128)S(1)}, f32[288,128]{1,0:T(8,128)S(1)}, u32[]{:S(2)}, u32[]{:S(2)}) collective-permute-start(f32[288,128]{1,0:T(8,128)S(1)} %get-tuple-element.42), channel_id=1, source_target_pairs={{0,16},{8,24},{16,0},{24,8},{1,17},{9,25},{17,1},{25,9},{2,18},{10... | collective-permute-start | bytes 442376 | tf_op jit(solution)/shard_map/ppermute | solution.py:684
  12.9 7.6 %collective-permute-start.4 = (f32[288,128]{1,0:T(8,128)S(1)}, f32[288,128]{1,0:T(8,128)S(1)}, u32[]{:S(2)}, u32[]{:S(2)}) collective-permute-start(f32[288,128]{1,0:T(8,128)S(1)} %get-tuple-element.43), channel_id=1, source_target_pairs={{0,24},{8,16},{16,8},{24,0},{1,25},{9,17},{17,9},{25,1},{2,26},{10... | collective-permute-start | bytes 442376 | tf_op jit(solution)/shard_map/ppermute | solution.py:684
  22.1 6.0 %collective-permute-start.5 = (f32[288,128]{1,0:T(8,128)S(1)}, f32[288,128]{1,0:T(8,128)S(1)}, u32[]{:S(2)}, u32[]{:S(2)}) collective-permute-start(f32[288,128]{1,0:T(8,128)S(1)} %get-tuple-element.46), channel_id=1, source_target_pairs={{0,8},{8,0},{16,24},{24,16},{1,9},{9,1},{17,25},{25,17},{2,10},{10... | collective-permute-start | bytes 442376 | tf_op jit(solution)/shard_map/ppermute | solution.py:684
  23.4 8.3 %collective-permute-start.6 = (f32[288,128]{1,0:T(8,128)S(1)}, f32[288,128]{1,0:T(8,128)S(1)}, u32[]{:S(2)}, u32[]{:S(2)}) collective-permute-start(f32[288,128]{1,0:T(8,128)S(1)} %get-tuple-element.47), channel_id=1, source_target_pairs={{0,16},{8,24},{16,0},{24,8},{1,17},{9,25},{17,1},{25,9},{2,18},{10... | collective-permute-start | bytes 442376 | tf_op jit(solution)/shard_map/ppermute | solution.py:684
  24.2 7.5 %collective-permute-start.7 = (f32[288,128]{1,0:T(8,128)S(1)}, f32[288,128]{1,0:T(8,128)S(1)}, u32[]{:S(2)}, u32[]{:S(2)}) collective-permute-start(f32[288,128]{1,0:T(8,128)S(1)} %get-tuple-element.48), channel_id=1, source_target_pairs={{0,24},{8,16},{16,8},{24,0},{1,25},{9,17},{17,9},{25,1},{2,26},{10... | collective-permute-start | bytes 442376 | tf_op jit(solution)/shard_map/ppermute | solution.py:684
  26.8 6.0 %copy-start.1 = (bf16[2,256,256]{2,1,0:T(8,128)(2,1)S(1)}, bf16[2,256,256]{2,1,0:T(8,128)(2,1)}, u32[]{:S(2)}) copy-start(bf16[2,256,256]{2,1,0:T(8,128)(2,1)} %constant.5.clone.gather_ref) | copy-start | bytes 786436
  26.8 6.0 %copy-start.6 = (s32[48]{0:T(128)S(1)}, s32[48]{0:T(128)}, u32[]{:S(2)}) copy-start(s32[48]{0:T(128)} %octants_hbm.3) | copy-start | bytes 580
  31.8 5.2 %collective-permute-start.8 = (f32[64,128]{1,0:T(8,128)S(1)}, f32[64,128]{1,0:T(8,128)S(1)}, u32[]{:S(2)}, u32[]{:S(2)}) collective-permute-start(f32[64,128]{1,0:T(8,128)S(1)} %get-tuple-element.52), channel_id=1, source_target_pairs={{0,7},{1,2},{2,1},{3,4},{4,3},{5,6},{6,5},{7,0},{8,15},{9,10},{10,... | collective-permute-start | bytes 98312 | tf_op jit(solution)/shard_map/ppermute | solution.py:679
  32.8 4.2 %collective-permute-start.9 = (f32[64,128]{1,0:T(8,128)S(1)}, f32[64,128]{1,0:T(8,128)S(1)}, u32[]{:S(2)}, u32[]{:S(2)}) collective-permute-start(f32[64,128]{1,0:T(8,128)S(1)} %get-tuple-element.53), channel_id=1, source_target_pairs={{0,1},{1,0},{2,3},{3,2},{4,5},{5,4},{6,7},{7,6},{8,9},{9,8},{10,11... | collective-permute-start | bytes 98312 | tf_op jit(solution)/shard_map/ppermute | solution.py:679

commit v9 on v8

--- a/solution.py
+++ b/solution.py
@@ -445,24 +445,6 @@
     return operator_of
 
 
-def gather_kernel(peers, frame, others, masks, placed_ref, *rest):
-    chunks, (real_before, imag_before, real_sum, imag_sum, real_twice, imag_twice) = rest[:-6], rest[-6:]
-    me = lax.axis_index("clus")
-    targets = real_sum.shape[0] // frame
-    own = targets // peers
-    share = chunks[0].shape[0] // (2 * own)
-    skip = lax.rem(me * (2 * share), 8)
-    for number, chunk in enumerate(chunks):
-        doubled(chunk, real_twice, imag_twice, number * own, own, share, frame, skip)
-    operator_of = placed(placed_ref, frame, others, own, masks)
-
-    def add(some, sums):
-        operators = lambda j, source: operator_of(some[j], source)
-        return add_sources(sums, len(masks) * own, frame, operators, real_twice, imag_twice)
-
-    for_some_targets(targets, frame, add, (real_before, imag_before), (real_sum, imag_sum))
-
-
 def translate_kernel(frame, others, masks, targets, placed_ref, real_sum, imag_sum, *rest):
     prepare = len(rest) == len(masks) + len(targets) + 4
     chunks, rest = (rest[: len(masks)], rest[len(masks) :]) if prepare else ((), rest)
@@ -556,30 +538,23 @@
     lax.fori_loop(0, octants_ref.shape[0] // GROUP, some_children, 0)
 
 
-def edge_contributions(parents, phase_ref, gather_ref, above, below):
-    children = parents.shape[1]
-    own = below.shape[0] // 8
-    rows = [above[2 * e * own : 2 * (e + 1) * own] for e in range(4)] + [below[2 * e * own : 2 * (e + 1) * own] for e in range(3)]
-    edges = jnp.concatenate([r[part * own : (part + 1) * own] for r in rows for part in range(2)], axis=1)
-    per_child = dot2(one_hot(parents, own).T, edges)
+def returned_rows(parents, phase_ref, edges, rows_ref):
+    own = rows_ref.shape[0] // 8
+    columns = [rows_ref[row * own : (row + 1) * own, :] for row in range(2 * len(edges))]
+    per_child = dot2(one_hot(parents, own).T, jnp.concatenate(columns, axis=1))
     returned = []
-    for e in range(len(rows)):
-        real = per_child[:, 2 * e * LANES : (2 * e + 1) * LANES]
-        imaginary = per_child[:, (2 * e + 1) * LANES : (2 * e + 2) * LANES]
+    for i, e in enumerate(edges):
+        real = per_child[:, 2 * i * LANES : (2 * i + 1) * LANES]
+        imaginary = per_child[:, (2 * i + 1) * LANES : (2 * i + 2) * LANES]
         cosine, sine = phase_ref[e, 0], phase_ref[e, 1]
         returned.append(
             jnp.concatenate([real * cosine + imaginary * sine, imaginary * cosine - real * sine], axis=0)
         )
-    join = functools.partial(jnp.concatenate, axis=1)
-    even = jnp.concatenate([join([returned[2], returned[3]]), join([returned[4], returned[5]])], axis=0)
-    odd = jnp.concatenate([join([returned[0], returned[1]]), join([returned[5], returned[6]])], axis=0)
-    even = gather_dot(*split(even), gather_ref, 0)
-    odd = gather_dot(*split(odd), gather_ref, 1)
-    a, b = TAPS_A, TAPS_B
-    pairs = 2 * children
-    last = a[0] * odd[:pairs] + b[0] * even[:pairs]
-    first = [a[3 + i] * even[pairs:] + b[3 + i] * odd[pairs:] for i in range(2)]
-    return first, last
+    return returned
+
+
+def side_by_side(left, right):
+    return split(jnp.concatenate([left, right], axis=1))
 
 
 def disaggregate_kernel(
@@ -651,27 +626,36 @@
         written(block).wait()
 
 
-def finish_kernel(parents_ref, phase_ref, gather_ref, edge_ref, far_ref, near_ref, part_ref, out_ref, tiles, sems):
+def finish_kernel(is_far, parents_ref, phase_ref, gather_ref, edge_ref, side_ref, part_ref, out_ref, tiles, sem):
     pairs, azimuth_in, _ = out_ref.shape
-    tiles[...] = edge_ref[...]
-    flat = tiles.reshape(2 * pairs * TILE, LANES)
-    below, above = from_sides(far_ref, near_ref)
-    heads, tail = edge_contributions(parents_ref[...], phase_ref, gather_ref, above, below)
-    ends = ((0, 0, heads[0]), (0, 1, heads[1]), (1, TILE - 1, tail))
-    copies = []
-    for i, start in enumerate((0, azimuth_in - TILE)):
-        for end, row, values in ends:
-            if end == i:
-                for part in range(2):
-                    for k in range(0, pairs // 2, 8):
-                        source = slice(part * (pairs // 2) + k, part * (pairs // 2) + k + 8)
-                        rows = pl.ds((i * pairs + 2 * k + part) * TILE + row, 8, stride=2 * TILE)
-                        flat[rows, :] = flat[rows, :] + values[source]
-        copy = pltpu.make_async_copy(tiles.at[i], out_ref.at[:, pl.ds(start, TILE), :], sems.at[i])
+    a, b = TAPS_A, TAPS_B
+
+    def write(end, start, additions):
+        tiles[...] = edge_ref[end]
+        flat = tiles.reshape(pairs * TILE, LANES)
+        for row, values in additions:
+            for part in range(2):
+                for k in range(0, pairs // 2, 8):
+                    source = slice(part * (pairs // 2) + k, part * (pairs // 2) + k + 8)
+                    rows = pl.ds((2 * k + part) * TILE + row, 8, stride=2 * TILE)
+                    flat[rows, :] = flat[rows, :] + values[source]
+        copy = pltpu.make_async_copy(tiles, out_ref.at[:, pl.ds(start, TILE), :], sem)
         copy.start()
-        copies.append(copy)
-    for copy in copies:
         copy.wait()
+
+    def from_below():
+        returned = returned_rows(parents_ref[...], phase_ref, (4, 5, 6), side_ref)
+        even = gather_dot(*side_by_side(returned[0], returned[1]), gather_ref, 0)
+        odd = gather_dot(*side_by_side(returned[1], returned[2]), gather_ref, 1)
+        write(0, 0, [(i, a[3 + i] * even + b[3 + i] * odd) for i in range(2)])
+
+    def from_above():
+        returned = returned_rows(parents_ref[...], phase_ref, (0, 1, 2, 3), side_ref)
+        even = gather_dot(*side_by_side(returned[2], returned[3]), gather_ref, 0)
+        odd = gather_dot(*side_by_side(returned[0], returned[1]), gather_ref, 1)
+        write(1, azimuth_in - TILE, [(TILE - 1, a[0] * odd + b[0] * even)])
+
+    by_parity(*((from_below, from_above) if is_far else (from_above, from_below)))
 
 
 def swapped(values, axis, first):
@@ -774,16 +758,13 @@
         functools.partial(fix_kernel, peers, own), [chunk] * peers, [VMEM] * 6, [buffer(2 * own * flat_rows, LANES)], 8
     )(child_parent, from_far, from_near, flat, edge_phases, spread)
 
-    masks = sorted(range(1, peers), key=lambda d: bin(d).count("1"))
-    early, late = masks[:1], masks[1:]
+    masks = sorted(range(1, peers), key=lambda d: -bin(d).count("1"))
     received = {0: sent[0]}
-    for d in early:
+    for d in masks:
         received[d] = exchanged(sent[d], "clus", d)
-    for d in late:
-        received[d] = exchanged(sent[d], "clus", d)
 
     sum_pair = [array(parent_total * frame, LANES)] * 2
-    others = tuple(early + late)
+    others = tuple(masks)
     operators, *sums = local_call(
         functools.partial(widen_kernel, peers, others),
         [array(parent_total * len(others) * own * frame, LANES)] + sum_pair,
@@ -801,23 +782,13 @@
         bytes_accessed=12_000_000,
     )(partner_src, partner_off, partner_count.reshape(1, parent_total), table, received[0])
 
-    sums = local_call(
-        functools.partial(gather_kernel, peers, frame, others, tuple(early)),
-        sum_pair,
-        [VMEM] * (3 + len(early)),
-        [buffer(len(early) * own * frame, LANES)] * 2,
-        12,
-        flops=60_000_000,
-        bytes_accessed=12_000_000,
-    )(operators, *[received[d] for d in early], *sums)
-
     back = {}
-    last_sources = [received[d] for d in late]
-    for number, targets in enumerate((masks[-1:], masks[:-1], [0])):
+    last_sources = [received[d] for d in masks]
+    for number, targets in enumerate((masks[:1], masks[1:], [0])):
         prepare = number == 0
         results = local_call(
-            functools.partial(translate_kernel, frame, others, tuple(late), tuple(targets)),
-            ([array(len(late) * own * frame, LANES)] * 2 if prepare else []) + [chunk] * len(targets),
+            functools.partial(translate_kernel, frame, others, others, tuple(targets)),
+            ([array(len(others) * own * frame, LANES)] * 2 if prepare else []) + [chunk] * len(targets),
             [VMEM] * (3 + len(last_sources)),
             [buffer(TOGETHER, frame, LANES)] * 2,
             20,
@@ -869,15 +840,17 @@
         out_specs=[HBM, VMEM],
     )(child_parent, child_octant.reshape(1, children), incoming, phases, gather)
 
-    out = local_call(
-        finish_kernel,
-        array(pairs, azimuth_in, polar_in),
-        [VMEM] * 6 + [HBM],
-        [buffer(2, pairs, TILE, polar_in), pltpu.SemaphoreType.DMA((2,))],
-        8,
-        out_specs=HBM,
-        aliases={6: 0},
-    )(child_parent, neighbour_phases, gather, edge_tiles, from_far, from_near, in_hbm(inner))
+    out = inner
+    for is_far, side in ((False, from_near), (True, from_far)):
+        out = local_call(
+            functools.partial(finish_kernel, is_far),
+            array(pairs, azimuth_in, polar_in),
+            [VMEM] * 5 + [HBM],
+            [buffer(pairs, TILE, polar_in), pltpu.SemaphoreType.DMA],
+            8,
+            out_specs=HBM,
+            aliases={5: 0},
+        )(child_parent, neighbour_phases, gather, edge_tiles, side, in_hbm(out))
     return out.reshape(child_patterns.shape)
 
 

time: 38.7 us -> 40.2 us (1.039)
  starting transfers between devices: 12.7 us -> 13.5 us
  Pallas kernels: 18.1 us -> 18.7 us
    ppermute x6, waiting for transfers between devices: 6.21 us -> 7.56 us  [exchanged(): return lax.ppermute(values, axis, [(i, i ^ mask) for i in range(size)])]
    ppermute x4, waiting for transfers between devices: 1.33 us -> 0.01 us  [swapped(): lax.ppermute(values, axis, [(i, ((i - first ^ 1) + first) % size) for i i...]
    ppermute x4, starting transfers between devices: 5.58 us -> 6.38 us  [swapped(): lax.ppermute(values, axis, [(i, ((i - first ^ 1) + first) % size) for i i...]
    pallas_call x5, Pallas kernels: 4.81 us -> 5.42 us  [the longest x3 2.97 us: on_device_exchange(): local_call(functools.partial(translate_kernel, frame, others, others, tup...]
where the time goes in v9:
time: 40.2 us; the launch traced here: 40 us
  Pallas kernels  18.7 us (47%)
  starting transfers between devices  13.5 us (34%)
  waiting for transfers between devices  7.57 us (19%)
    ppermute x6, waiting for transfers between devices, exchanged(): return lax.ppermute(values, axis, [(i, i ^ mask) for i in range(size)])  7.56 us
    ppermute x6, starting transfers between devices, exchanged(): return lax.ppermute(values, axis, [(i, i ^ mask) for i in range(size)])  7.11 us
    ppermute x4, starting transfers between devices, swapped(): lax.ppermute(values, axis, [(i, ((i - first ^ 1) + first) % size) for i i...  6.38 us
    pallas_call x1, Pallas kernels, on_device_exchange(): local_call(functools.partial(widen_kernel, peers, others), [array(parent_...  4.06 us
    pallas_call x1, Pallas kernels, on_device_exchange(): local_call(functools.partial(main_kernel, peers), [array(8, 2, ROWS_PER_P...  3.48 us
    pallas_call x3, Pallas kernels, on_device_exchange(): local_call(functools.partial(translate_kernel, frame, others, others, tup...  2.97 us
    pallas_call x1, Pallas kernels, on_device_exchange(): local_call(disaggregate_kernel, [array(pairs, azimuth_in, polar_in), arra...  2.87 us
    pallas_call x2, Pallas kernels, on_device_exchange(): local_call(functools.partial(finish_kernel, is_far), array(pairs, azimuth...  2.45 us
  transfers between devices with their start and end apart: 10, of which 4 were waited for; matrix products, arithmetic and copies ran while one was open for 0% of the time, Pallas kernels for 34%

profile of v9, /device:TPU:0, one launch (start us, length us, event | category | flops | bytes accessed | tf_op | source)
XLA Modules:
  0.0 40.0 jit_solution(1547344106641130231)
XLA Ops:
  0.0 1.2 %shard_map.93 = (f32[2,96,128]{2,1,0:T(8,128)S(1)}, f32[2,96,128]{2,1,0:T(8,128)S(1)}) custom-call(f32[96,32,128]{2,1,0:T(8,128)} %bitcast.14), custom_call_target="tpu_custom_call" | custom-call | flops 1000000 | bytes 1000000 | tf_op jit(solution)/shard_map/pallas_call | solution.py:711
  1.2 4.6 %collective-permute-start = (f32[2,96,128]{2,1,0:T(8,128)S(1)}, f32[2,96,128]{2,1,0:T(8,128)S(1)}, u32[]{:S(2)}, u32[]{:S(2)}) collective-permute-start(f32[2,96,128]{2,1,0:T(8,128)S(1)} %get-tuple-element.29), channel_id=1, source_target_pairs={{0,7},{1,2},{2,1},{3,4},{4,3},{5,6},{6,5},{7,0},{8,15},{9,10},{10,... | collective-permute-start | bytes 294920 | tf_op jit(solution)/shard_map/ppermute | solution.py:663
  5.8 0.0 collective-permute-start.1
  5.8 0.0 copy-start.3
  5.8 0.0 copy-start.5
  5.8 3.5 %shard_map.92 = (f32[8,2,9,8,128]{4,3,2,1,0:T(8,128)S(1)}, f32[7,2,48,128]{3,2,1,0:T(8,128)S(1)}, f32[1152,128]{1,0:T(8,128)S(1)}, bf16[316,40,128]{2,1,0:T(8,128)(2,1)S(1)}) custom-call(s32[48]{0:T(128)} %bitcast.11, s32[48]{0:T(128)} %octants_hbm.3, f32[3072,128]{1,0:T(8,128)} %bitcast.15, bf16[316,144,128]{2,1,0:T(8,128)(2,1)} %bitcast.16, ...), custom_call_target="tpu_custom_call" | custom-call | flops 4000000000 | bytes 12000000 | tf_op jit(solution)/shard_map/pallas_call | solution.py:723
  9.3 0.0 collective-permute-done.1.near_ref
  9.3 0.5 %shard_map.94 = (f32[288,128]{1,0:T(8,128)S(1)}, f32[288,128]{1,0:T(8,128)S(1)}, f32[288,128]{1,0:T(8,128)S(1)}, f32[288,128]{1,0:T(8,128)S(1)}) custom-call(s32[1,48]{1,0:T(1,128)S(1)} %copy-done.4, f32[2,96,128]{2,1,0:T(8,128)S(1)} %collective-permute-done.far_ref, f32[2,96,128]{2,1,0:T(8,128)S(1)} %collective-permute-done.1.near_ref, ...), custom_call_target="tpu_custom_call" | custom-call | flops 1000000 | bytes 1000000 | tf_op jit(solution)/shard_map/pallas_call | solution.py:757
  9.8 2.5 %collective-permute-start.2 = (f32[288,128]{1,0:T(8,128)S(1)}, f32[288,128]{1,0:T(8,128)S(1)}, u32[]{:S(2)}, u32[]{:S(2)}) collective-permute-start(f32[288,128]{1,0:T(8,128)S(1)} %get-tuple-element.37), channel_id=1, source_target_pairs={{0,24},{8,16},{16,8},{24,0},{1,25},{9,17},{17,9},{25,1},{2,26},{10... | collective-permute-start | bytes 442376 | tf_op jit(solution)/shard_map/ppermute | solution.py:668
  12.3 0.5 %collective-permute-start.3 = (f32[288,128]{1,0:T(8,128)S(1)}, f32[288,128]{1,0:T(8,128)S(1)}, u32[]{:S(2)}, u32[]{:S(2)}) collective-permute-start(f32[288,128]{1,0:T(8,128)S(1)} %get-tuple-element.38), channel_id=1, source_target_pairs={{0,8},{8,0},{16,24},{24,16},{1,9},{9,1},{17,25},{25,17},{2,10},{10... | collective-permute-start | bytes 442376 | tf_op jit(solution)/shard_map/ppermute | solution.py:668
  12.9 0.5 %collective-permute-start.4 = (f32[288,128]{1,0:T(8,128)S(1)}, f32[288,128]{1,0:T(8,128)S(1)}, u32[]{:S(2)}, u32[]{:S(2)}) collective-permute-start(f32[288,128]{1,0:T(8,128)S(1)} %get-tuple-element.39), channel_id=1, source_target_pairs={{0,16},{8,24},{16,0},{24,8},{1,17},{9,25},{17,1},{25,9},{2,18},{10... | collective-permute-start | bytes 442376 | tf_op jit(solution)/shard_map/ppermute | solution.py:668
  13.4 4.1 %shard_map.95 = (f32[30720,128]{1,0:T(8,128)S(1)}, f32[1280,128]{1,0:T(8,128)S(1)}, f32[1280,128]{1,0:T(8,128)S(1)}) custom-call(s32[32,31]{1,0:T(8,128)S(1)} %copy-done.2, s32[32,31]{1,0:T(8,128)S(1)} %copy-done.3, s32[1,32]{1,0:T(1,128)S(1)} %bitcast.12, bf16[316,40,128]{2,1,0:T(8,128)(2,1)S(1)} %get-tuple-element.28.table_ref, ...), custom_call_target="tpu_custom_call" | custom-call | flops 90000000 | bytes 12000000 | tf_op jit(solution)/shard_map/pallas_call | solution.py:768
  17.5 0.1 collective-permute-done.2.rest_0_
  17.5 2.8 %collective-permute-done.3.rest_1_ = f32[288,128]{1,0:T(8,128)S(1)} collective-permute-done((f32[288,128]{1,0:T(8,128)S(1)}, f32[288,128]{1,0:T(8,128)S(1)}, u32[]{:S(2)}, u32[]{:S(2)}) %collective-permute-start.3) | collective-permute-done | bytes 147488 | tf_op jit(solution)/shard_map/ppermute | solution.py:668
  20.3 0.8 %shard_map.96 = (f32[960,128]{1,0:T(8,128)S(1)}, f32[960,128]{1,0:T(8,128)S(1)}, f32[288,128]{1,0:T(8,128)S(1)}) custom-call(f32[30720,128]{1,0:T(8,128)S(1)} %get-tuple-element.34.placed_ref, f32[1280,128]{1,0:T(8,128)S(1)} %get-tuple-element.35.real_sum, f32[1280,128]{1,0:T(8,128)S(1)} %get-tuple-element.36.imag_sum, ...), custom_call_target="tpu_custom_call" | custom-call | flops 10000000 | bytes 2000000 | tf_op jit(solution)/shard_map/pallas_call | solution.py:789
  21.1 1.4 %shard_map.98 = (f32[288,128]{1,0:T(8,128)S(1)}, f32[288,128]{1,0:T(8,128)S(1)}) custom-call(f32[30720,128]{1,0:T(8,128)S(1)} %get-tuple-element.34.placed_ref, f32[1280,128]{1,0:T(8,128)S(1)} %get-tuple-element.35.real_sum, f32[1280,128]{1,0:T(8,128)S(1)} %get-tuple-element.36.imag_sum, f32[960,128]{1,0:T(8,128)S(1)} %get-tuple-element.40.rest_0_, ...), custom_call_target="tpu_custom_call" | custom-call | flops 20000000 | bytes 4000000 | tf_op jit(solution)/shard_map/pallas_call | solution.py:789
  22.6 1.6 %collective-permute-start.5 = (f32[288,128]{1,0:T(8,128)S(1)}, f32[288,128]{1,0:T(8,128)S(1)}, u32[]{:S(2)}, u32[]{:S(2)}) collective-permute-start(f32[288,128]{1,0:T(8,128)S(1)} %get-tuple-element.42), channel_id=1, source_target_pairs={{0,8},{8,0},{16,24},{24,16},{1,9},{9,1},{17,25},{25,17},{2,10},{10... | collective-permute-start | bytes 442376 | tf_op jit(solution)/shard_map/ppermute | solution.py:668
  24.1 1.4 %collective-permute-start.6 = (f32[288,128]{1,0:T(8,128)S(1)}, f32[288,128]{1,0:T(8,128)S(1)}, u32[]{:S(2)}, u32[]{:S(2)}) collective-permute-start(f32[288,128]{1,0:T(8,128)S(1)} %get-tuple-element.43), channel_id=1, source_target_pairs={{0,16},{8,24},{16,0},{24,8},{1,17},{9,25},{17,1},{25,9},{2,18},{10... | collective-permute-start | bytes 442376 | tf_op jit(solution)/shard_map/ppermute | solution.py:668
  25.5 0.6 %collective-permute-start.7 = (f32[288,128]{1,0:T(8,128)S(1)}, f32[288,128]{1,0:T(8,128)S(1)}, u32[]{:S(2)}, u32[]{:S(2)}) collective-permute-start(f32[288,128]{1,0:T(8,128)S(1)} %get-tuple-element.44), channel_id=1, source_target_pairs={{0,24},{8,16},{16,8},{24,0},{1,25},{9,17},{17,9},{25,1},{2,26},{10... | collective-permute-start | bytes 442376 | tf_op jit(solution)/shard_map/ppermute | solution.py:668
  26.1 1.1 %shard_map.91.phase_ref = f32[7,2,48,128]{3,2,1,0:T(8,128)S(1)} custom-call(s32[48]{0:T(128)} %octants_hbm.3), custom_call_target="tpu_custom_call" | custom-call | flops 20000000 | bytes 1000000 | tf_op jit(solution)/shard_map/pallas_call | solution.py:803
  27.2 0.0 copy-start
  27.2 0.0 copy-start.6
  27.2 0.7 %shard_map.97.rest_0_ = f32[288,128]{1,0:T(8,128)S(1)} custom-call(f32[30720,128]{1,0:T(8,128)S(1)} %get-tuple-element.34.placed_ref, f32[1280,128]{1,0:T(8,128)S(1)} %get-tuple-element.35.real_sum, f32[1280,128]{1,0:T(8,128)S(1)} %get-tuple-element.36.imag_sum, f32[960,128]{1,0:T(8,128)S(1)} %get-tuple-element.40.rest_0_, ...), custom_call_target="tpu_custom_call" | custom-call | flops 10000000 | bytes 2000000 | tf_op jit(solution)/shard_map/pallas_call | solution.py:789
  28.0 1.1 %collective-permute-done.5.rest_1_ = f32[288,128]{1,0:T(8,128)S(1)} collective-permute-done((f32[288,128]{1,0:T(8,128)S(1)}, f32[288,128]{1,0:T(8,128)S(1)}, u32[]{:S(2)}, u32[]{:S(2)}) %collective-permute-start.5) | collective-permute-done | bytes 147488 | tf_op jit(solution)/shard_map/ppermute | solution.py:668
  29.1 3.6 %collective-permute-done.6.rest_2_ = f32[288,128]{1,0:T(8,128)S(1)} collective-permute-done((f32[288,128]{1,0:T(8,128)S(1)}, f32[288,128]{1,0:T(8,128)S(1)}, u32[]{:S(2)}, u32[]{:S(2)}) %collective-permute-start.6) | collective-permute-done | bytes 147488 | tf_op jit(solution)/shard_map/ppermute | solution.py:668
  32.7 0.1 shard_map.99
  32.8 0.1 collective-permute-start.9
  32.9 1.7 %collective-permute-start.8 = (f32[64,128]{1,0:T(8,128)S(1)}, f32[64,128]{1,0:T(8,128)S(1)}, u32[]{:S(2)}, u32[]{:S(2)}) collective-permute-start(f32[64,128]{1,0:T(8,128)S(1)} %get-tuple-element.48), channel_id=1, source_target_pairs={{0,7},{1,2},{2,1},{3,4},{4,3},{5,6},{6,5},{7,0},{8,15},{9,10},{10,... | collective-permute-start | bytes 98312 | tf_op jit(solution)/shard_map/ppermute | solution.py:663
  34.6 2.9 %shard_map.100 = (f32[96,32,128]{2,1,0:T(8,128)}, f32[2,96,8,128]{3,2,1,0:T(8,128)S(1)}) custom-call(s32[1,48]{1,0:T(1,128)S(1)} %copy-done.4, s32[1,48]{1,0:T(1,128)S(1)} %bitcast.13, f32[1152,128]{1,0:T(8,128)S(1)} %get-tuple-element.45.flat_ref, f32[8,2,9,8,128]{4,3,2,1,0:T(8,128)S(1)} %get-tuple-element.46.phase_ref, bf16[2,256,256]{2,1,0:T(8,128)(2,1)S(1)} %copy-done), custom_call_target="tpu_custom_call" | custom-call | flops 4000000000 | bytes 12000000 | tf_op jit(solution)/shard_map/pallas_call | solution.py:824
  37.5 0.0 collective-permute-done.9.side_ref
  37.5 1.2 %shard_map.101.part_ref = f32[96,32,128]{2,1,0:T(8,128)} custom-call(s32[1,48]{1,0:T(1,128)S(1)} %copy-done.4, f32[7,2,48,128]{3,2,1,0:T(8,128)S(1)} %shard_map.91.phase_ref, bf16[2,256,256]{2,1,0:T(8,128)(2,1)S(1)} %copy-done, f32[2,96,8,128]{3,2,1,0:T(8,128)S(1)} %get-tuple-element.47.edge_ref, ...), custom_call_target="tpu_custom_call", output_to_operand_aliasing={{}: (5, {})} | custom-call | flops 1000000 | bytes 1000000 | tf_op jit(solution)/shard_map/pallas_call | solution.py:845
  38.7 1.2 %shard_map.102 = f32[96,32,128]{2,1,0:T(8,128)} custom-call(s32[1,48]{1,0:T(1,128)S(1)} %copy-done.4, f32[7,2,48,128]{3,2,1,0:T(8,128)S(1)} %shard_map.91.phase_ref, bf16[2,256,256]{2,1,0:T(8,128)(2,1)S(1)} %copy-done, f32[2,96,8,128]{3,2,1,0:T(8,128)S(1)} %get-tuple-element.47.edge_ref, ...), custom_call_target="tpu_custom_call", output_to_operand_aliasing={{}: (5, {})} | custom-call | flops 1000000 | bytes 1000000 | tf_op jit(solution)/shard_map/pallas_call | solution.py:845
  (14 shorter events, 0.0 us)
Async XLA Ops:
  1.2 8.1 %collective-permute-start = (f32[2,96,128]{2,1,0:T(8,128)S(1)}, f32[2,96,128]{2,1,0:T(8,128)S(1)}, u32[]{:S(2)}, u32[]{:S(2)}) collective-permute-start(f32[2,96,128]{2,1,0:T(8,128)S(1)} %get-tuple-element.29), channel_id=1, source_target_pairs={{0,7},{1,2},{2,1},{3,4},{4,3},{5,6},{6,5},{7,0},{8,15},{9,10},{10,... | collective-permute-start | bytes 294920 | tf_op jit(solution)/shard_map/ppermute | solution.py:663
  5.8 3.5 %collective-permute-start.1 = (f32[2,96,128]{2,1,0:T(8,128)S(1)}, f32[2,96,128]{2,1,0:T(8,128)S(1)}, u32[]{:S(2)}, u32[]{:S(2)}) collective-permute-start(f32[2,96,128]{2,1,0:T(8,128)S(1)} %get-tuple-element.30), channel_id=1, source_target_pairs={{0,1},{1,0},{2,3},{3,2},{4,5},{5,4},{6,7},{7,6},{8,9},{9,8},{10,11... | collective-permute-start | bytes 294920 | tf_op jit(solution)/shard_map/ppermute | solution.py:663
  5.8 3.5 %copy-start.1 = (bf16[2,384,256]{2,1,0:T(8,128)(2,1)S(1)}, bf16[2,384,256]{2,1,0:T(8,128)(2,1)}, u32[]{:S(2)}) copy-start(bf16[2,384,256]{2,1,0:T(8,128)(2,1)} %constant.4.clone.spread_hbm.spread_ref) | copy-start | bytes 1179652
  5.8 3.6 %copy-start.4 = (s32[1,48]{1,0:T(1,128)S(1)}, s32[1,48]{1,0:T(1,128)}, u32[]{:S(2)}) copy-start(s32[1,48]{1,0:T(1,128)} %parents_ref.7) | copy-start | bytes 580
  5.8 7.6 %copy-start.2 = (s32[32,31]{1,0:T(8,128)S(1)}, s32[32,31]{1,0:T(8,128)}, u32[]{:S(2)}) copy-start(s32[32,31]{1,0:T(8,128)} %source_ref.1) | copy-start | bytes 11908
  5.8 7.6 %copy-start.3 = (s32[32,31]{1,0:T(8,128)S(1)}, s32[32,31]{1,0:T(8,128)}, u32[]{:S(2)}) copy-start(s32[32,31]{1,0:T(8,128)} %offset_ref.1) | copy-start | bytes 11908
  5.8 7.6 %copy-start.5 = (s32[32]{0:T(128)S(1)}, s32[32]{0:T(128)}, u32[]{:S(2)}) copy-start(s32[32]{0:T(128)} %param.15) | copy-start | bytes 388
  9.8 7.7 %collective-permute-start.2 = (f32[288,128]{1,0:T(8,128)S(1)}, f32[288,128]{1,0:T(8,128)S(1)}, u32[]{:S(2)}, u32[]{:S(2)}) collective-permute-start(f32[288,128]{1,0:T(8,128)S(1)} %get-tuple-element.37), channel_id=1, source_target_pairs={{0,24},{8,16},{16,8},{24,0},{1,25},{9,17},{17,9},{25,1},{2,26},{10... | collective-permute-start | bytes 442376 | tf_op jit(solution)/shard_map/ppermute | solution.py:668
  12.3 8.0 %collective-permute-start.3 = (f32[288,128]{1,0:T(8,128)S(1)}, f32[288,128]{1,0:T(8,128)S(1)}, u32[]{:S(2)}, u32[]{:S(2)}) collective-permute-start(f32[288,128]{1,0:T(8,128)S(1)} %get-tuple-element.38), channel_id=1, source_target_pairs={{0,8},{8,0},{16,24},{24,16},{1,9},{9,1},{17,25},{25,17},{2,10},{10... | collective-permute-start | bytes 442376 | tf_op jit(solution)/shard_map/ppermute | solution.py:668
  12.9 7.4 %collective-permute-start.4 = (f32[288,128]{1,0:T(8,128)S(1)}, f32[288,128]{1,0:T(8,128)S(1)}, u32[]{:S(2)}, u32[]{:S(2)}) collective-permute-start(f32[288,128]{1,0:T(8,128)S(1)} %get-tuple-element.39), channel_id=1, source_target_pairs={{0,16},{8,24},{16,0},{24,8},{1,17},{9,25},{17,1},{25,9},{2,18},{10... | collective-permute-start | bytes 442376 | tf_op jit(solution)/shard_map/ppermute | solution.py:668
  22.6 6.5 %collective-permute-start.5 = (f32[288,128]{1,0:T(8,128)S(1)}, f32[288,128]{1,0:T(8,128)S(1)}, u32[]{:S(2)}, u32[]{:S(2)}) collective-permute-start(f32[288,128]{1,0:T(8,128)S(1)} %get-tuple-element.42), channel_id=1, source_target_pairs={{0,8},{8,0},{16,24},{24,16},{1,9},{9,1},{17,25},{25,17},{2,10},{10... | collective-permute-start | bytes 442376 | tf_op jit(solution)/shard_map/ppermute | solution.py:668
  24.1 8.5 %collective-permute-start.6 = (f32[288,128]{1,0:T(8,128)S(1)}, f32[288,128]{1,0:T(8,128)S(1)}, u32[]{:S(2)}, u32[]{:S(2)}) collective-permute-start(f32[288,128]{1,0:T(8,128)S(1)} %get-tuple-element.43), channel_id=1, source_target_pairs={{0,16},{8,24},{16,0},{24,8},{1,17},{9,25},{17,1},{25,9},{2,18},{10... | collective-permute-start | bytes 442376 | tf_op jit(solution)/shard_map/ppermute | solution.py:668
  25.5 7.1 %collective-permute-start.7 = (f32[288,128]{1,0:T(8,128)S(1)}, f32[288,128]{1,0:T(8,128)S(1)}, u32[]{:S(2)}, u32[]{:S(2)}) collective-permute-start(f32[288,128]{1,0:T(8,128)S(1)} %get-tuple-element.44), channel_id=1, source_target_pairs={{0,24},{8,16},{16,8},{24,0},{1,25},{9,17},{17,9},{25,1},{2,26},{10... | collective-permute-start | bytes 442376 | tf_op jit(solution)/shard_map/ppermute | solution.py:668
  27.2 7.4 %copy-start = (bf16[2,256,256]{2,1,0:T(8,128)(2,1)S(1)}, bf16[2,256,256]{2,1,0:T(8,128)(2,1)}, u32[]{:S(2)}) copy-start(bf16[2,256,256]{2,1,0:T(8,128)(2,1)} %constant.5.clone.gather_ref) | copy-start | bytes 786436
  27.2 7.4 %copy-start.6 = (s32[48]{0:T(128)S(1)}, s32[48]{0:T(128)}, u32[]{:S(2)}) copy-start(s32[48]{0:T(128)} %octants_hbm.3) | copy-start | bytes 580
  32.8 4.7 %collective-permute-start.9 = (f32[64,128]{1,0:T(8,128)S(1)}, f32[64,128]{1,0:T(8,128)S(1)}, u32[]{:S(2)}, u32[]{:S(2)}) collective-permute-start(f32[64,128]{1,0:T(8,128)S(1)} %get-tuple-element.49), channel_id=1, source_target_pairs={{0,1},{1,0},{2,3},{3,2},{4,5},{5,4},{6,7},{7,6},{8,9},{9,8},{10,11... | collective-permute-start | bytes 98312 | tf_op jit(solution)/shard_map/ppermute | solution.py:663
  32.9 5.9 %collective-permute-start.8 = (f32[64,128]{1,0:T(8,128)S(1)}, f32[64,128]{1,0:T(8,128)S(1)}, u32[]{:S(2)}, u32[]{:S(2)}) collective-permute-start(f32[64,128]{1,0:T(8,128)S(1)} %get-tuple-element.48), channel_id=1, source_target_pairs={{0,7},{1,2},{2,1},{3,4},{4,3},{5,6},{6,5},{7,0},{8,15},{9,10},{10,... | collective-permute-start | bytes 98312 | tf_op jit(solution)/shard_map/ppermute | solution.py:663

commit v10 on v8

--- a/solution.py
+++ b/solution.py
@@ -163,26 +163,16 @@
     return jnp.where(is_even, far, near), jnp.where(is_even, near, far)
 
 
-def rows_kernel(x_ref, far_ref, near_ref, low, high, sems):
-    pairs, azimuth_in, _ = x_ref.shape
-    low_copy = pltpu.make_async_copy(x_ref.at[:, pl.ds(0, TILE), :], low, sems.at[0])
-    high_copy = pltpu.make_async_copy(x_ref.at[:, pl.ds(azimuth_in - TILE, TILE), :], high, sems.at[1])
-    low_copy.start()
-    high_copy.start()
-    low_copy.wait()
-    high_copy.wait()
-    low_rows, high_rows = (ref.reshape(pairs * TILE, LANES) for ref in (low, high))
+def rows_kernel(x_ref, far_ref, near_ref, sems):
+    azimuth_in = x_ref.shape[1]
 
     def fill(first_ref, last_ref):
-        for part in range(2):
-            for k in range(0, pairs // 2, 8):
-                target = slice(part * (pairs // 2) + k, part * (pairs // 2) + k + 8)
-                base = (2 * k + part) * TILE
-                for i in range(2):
-                    first_ref[i, target] = low_rows[pl.ds(base + i, 8, stride=2 * TILE), :]
-                last = high_rows[pl.ds(base + TILE - 1, 8, stride=2 * TILE), :]
-                for i in range(2):
-                    last_ref[i, target] = last
+        ends = [(0, first_ref.at[0]), (1, first_ref.at[1]), (azimuth_in - 1, last_ref.at[0]), (azimuth_in - 1, last_ref.at[1])]
+        copies = [pltpu.make_async_copy(x_ref.at[:, row, :], target, sems.at[i]) for i, (row, target) in enumerate(ends)]
+        for copy in copies:
+            copy.start()
+        for copy in copies:
+            copy.wait()
 
     by_parity(lambda: fill(far_ref, near_ref), lambda: fill(near_ref, far_ref))
 
@@ -224,19 +214,11 @@
     fill_phases(lax.axis_index("dir"), phase_ref)
     acc[...] = jnp.zeros_like(acc)
     sublane = lax.broadcasted_iota(jnp.int32, (periods, LANES), 0)
-    copies[0].wait()
-
-    def edges_of(step, carry):
-        for j in range(GROUP):
-            k = step * GROUP + j
-            octant = octants_ref[k]
-            for e, (w, m) in enumerate(edge_rows(periods)):
-                for i in range(2):
-                    edge_phase_ref[e, i, pl.ds(k, 1), :] = phase_ref[octant, i, w, m : m + 1, :]
-        return carry
-
-    lax.fori_loop(0, children // GROUP, edges_of, 0)
-    for copy in copies[1:-1]:
+    for e, (w, m) in enumerate(edge_rows(periods)):
+        for octant in range(8):
+            for i in range(2):
+                edge_phase_ref[e, i, octant : octant + 1, :] = phase_ref[octant, i, w, m : m + 1, :]
+    for copy in copies[:-1]:
         copy.wait()
     copies[-1].start()
 
@@ -304,7 +286,7 @@
 
 
 def fix_kernel(
-    peers, own, parents_ref, far_ref, near_ref, flat_ref, edge_phase_ref, spread_ref, *rest
+    peers, own, parents_ref, octants_ref, far_ref, near_ref, flat_ref, edge_phase_ref, spread_ref, *rest
 ):
     outs, (fixed,) = rest[:peers], rest[peers:]
     pairs = far_ref.shape[1]
@@ -313,8 +295,14 @@
     share = chunk_rows // (2 * own)
     periods = share * peers // ROWS_PER_PERIOD
     fixed[...] = flat_ref[...]
-    before, right = from_sides(far_ref, near_ref)
-    left = before[0]
+    is_even = lax.rem(lax.axis_index("dir"), 2) == 0
+
+    def by_part(ref, i):
+        return jnp.concatenate([ref[i, pl.ds(part, children, stride=2), :] for part in range(2)], axis=0)
+
+    far, near = ([by_part(ref, i) for i in range(2)] for ref in (far_ref, near_ref))
+    left = jnp.where(is_even, far[0], near[0])
+    right = [jnp.where(is_even, n, f) for f, n in zip(far, near)]
     a, b = TAPS_A, TAPS_B
     even = jnp.concatenate([b[0] * left, a[3] * right[0] + a[4] * right[1]], axis=0)
     odd = jnp.concatenate([a[0] * left, b[3] * right[0] + b[4] * right[1]], axis=0)
@@ -331,10 +319,12 @@
         even[last, high] + odd[last, high],
         odd[last, low],
     ]
+    by_octant = jnp.concatenate([edge_phase_ref[e, i] for e in range(len(refined)) for i in range(2)], axis=1)
+    phases = dot2(one_hot(octants_ref[...], 8).T, by_octant)
     shifted_rows = []
     for e, rows in enumerate(refined):
         real, imaginary = rows[:children], rows[children:]
-        cosine, sine = edge_phase_ref[e, 0], edge_phase_ref[e, 1]
+        cosine, sine = (phases[:, (2 * e + i) * LANES : (2 * e + i + 1) * LANES] for i in range(2))
         shifted_rows.append(real * cosine - imaginary * sine)
         shifted_rows.append(real * sine + imaginary * cosine)
     summed = dot2(one_hot(parents_ref[...], own), jnp.concatenate(shifted_rows, axis=1))
@@ -725,7 +715,7 @@
     spread = jnp.asarray(np.stack([np.concatenate([h, h, l]) for h, l in (split_np(even), split_np(odd))]))
     edge = array(2, pairs, polar_in)
     to_far, to_near = local_call(
-        rows_kernel, [edge, edge], [HBM], [buffer(pairs, TILE, polar_in)] * 2 + [pltpu.SemaphoreType.DMA((2,))], 8
+        rows_kernel, [edge, edge], [HBM], [pltpu.SemaphoreType.DMA((4,))], 8
     )(in_hbm(child_patterns.reshape(pairs, azimuth_in, polar_in)))
     from_far = swapped(to_far, "dir", 1)
     from_near = swapped(to_near, "dir", 0)
@@ -740,7 +730,7 @@
         functools.partial(main_kernel, peers),
         [
             array(8, 2, ROWS_PER_PERIOD, periods, LANES),
-            array(edges, 2, children, LANES),
+            array(edges, 2, 8, LANES),
             array(2 * own * flat_rows, LANES),
             jax.ShapeDtypeStruct((offsets, frame, LANES), bf16),
         ],
@@ -771,8 +761,8 @@
 
     chunk = array(2 * own * share, LANES)
     sent = local_call(
-        functools.partial(fix_kernel, peers, own), [chunk] * peers, [VMEM] * 6, [buffer(2 * own * flat_rows, LANES)], 8
-    )(child_parent, from_far, from_near, flat, edge_phases, spread)
+        functools.partial(fix_kernel, peers, own), [chunk] * peers, [VMEM] * 7, [buffer(2 * own * flat_rows, LANES)], 8
+    )(child_parent, child_octant.reshape(1, children), from_far, from_near, flat, edge_phases, spread)
 
     masks = sorted(range(1, peers), key=lambda d: bin(d).count("1"))
     early, late = masks[:1], masks[1:]

time: 38.7 us -> 38.5 us (level)
  transfers between devices with their start and end apart: 10 -> 10, of which waited for: 4 -> 4; matrix products, arithmetic and copies ran while one was open for 0% -> 0% of each run, Pallas kernels for 34% -> 35%
where the time goes in v10:
time: 38.5 us; the launch traced here: 38.3 us
  Pallas kernels  17.9 us (46%)
  starting transfers between devices  12.7 us (33%)
  waiting for transfers between devices  7.54 us (20%)
    ppermute x6, starting transfers between devices, exchanged(): return lax.ppermute(values, axis, [(i, i ^ mask) for i in range(size)])  7.11 us
    ppermute x6, waiting for transfers between devices, exchanged(): return lax.ppermute(values, axis, [(i, i ^ mask) for i in range(size)])  6.21 us
    ppermute x4, starting transfers between devices, swapped(): lax.ppermute(values, axis, [(i, ((i - first ^ 1) + first) % size) for i i...  5.57 us
    pallas_call x1, Pallas kernels, on_device_exchange(): local_call(functools.partial(widen_kernel, peers, others), [array(parent_...  4.06 us
    pallas_call x1, Pallas kernels, on_device_exchange(): local_call(functools.partial(main_kernel, peers), [array(8, 2, ROWS_PER_P...  3.48 us
    pallas_call x1, Pallas kernels, on_device_exchange(): local_call(disaggregate_kernel, [array(pairs, azimuth_in, polar_in), arra...  2.88 us
    pallas_call x3, Pallas kernels, on_device_exchange(): local_call(functools.partial(translate_kernel, frame, others, tuple(late)...  2.1 us
    pallas_call x1, Pallas kernels, on_device_exchange(): local_call(finish_kernel, array(pairs, azimuth_in, polar_in), [VMEM] * 6...  1.46 us
  transfers between devices with their start and end apart: 10, of which 4 were waited for; matrix products, arithmetic and copies ran while one was open for 0% of the time, Pallas kernels for 35%

profile of v10, /device:TPU:0, one launch (start us, length us, event | category | flops | bytes accessed | tf_op | source)
XLA Modules:
  0.0 38.3 jit_solution(174836420757650996)
XLA Ops:
  0.0 0.9 %shard_map.93 = (f32[2,96,128]{2,1,0:T(8,128)S(1)}, f32[2,96,128]{2,1,0:T(8,128)S(1)}) custom-call(f32[96,32,128]{2,1,0:T(8,128)} %bitcast.15), custom_call_target="tpu_custom_call" | custom-call | flops 1000000 | bytes 1000000 | tf_op jit(solution)/shard_map/pallas_call | solution.py:717
  0.9 4.6 %collective-permute-start = (f32[2,96,128]{2,1,0:T(8,128)S(1)}, f32[2,96,128]{2,1,0:T(8,128)S(1)}, u32[]{:S(2)}, u32[]{:S(2)}) collective-permute-start(f32[2,96,128]{2,1,0:T(8,128)S(1)} %get-tuple-element.31), channel_id=1, source_target_pairs={{0,7},{1,2},{2,1},{3,4},{4,3},{5,6},{6,5},{7,0},{8,15},{9,10},{10,... | collective-permute-start | bytes 294920 | tf_op jit(solution)/shard_map/ppermute | solution.py:669
  5.5 0.0 copy-start.2
  5.5 0.0 copy-start.3
  5.6 0.0 copy-start.7
  5.6 3.5 %shard_map.92 = (f32[8,2,9,8,128]{4,3,2,1,0:T(8,128)S(1)}, f32[7,2,8,128]{3,2,1,0:T(8,128)S(1)}, f32[1152,128]{1,0:T(8,128)S(1)}, bf16[316,40,128]{2,1,0:T(8,128)(2,1)S(1)}) custom-call(s32[48]{0:T(128)} %bitcast.13, s32[48]{0:T(128)} %octants_hbm.3, f32[3072,128]{1,0:T(8,128)} %bitcast.16, bf16[316,144,128]{2,1,0:T(8,128)(2,1)} %bitcast.17, ...), custom_call_target="tpu_custom_call" | custom-call | flops 4000000000 | bytes 12000000 | tf_op jit(solution)/shard_map/pallas_call | solution.py:729
  9.1 0.0 collective-permute-done.1.near_ref
  9.1 0.5 %shard_map.94 = (f32[288,128]{1,0:T(8,128)S(1)}, f32[288,128]{1,0:T(8,128)S(1)}, f32[288,128]{1,0:T(8,128)S(1)}, f32[288,128]{1,0:T(8,128)S(1)}) custom-call(s32[1,48]{1,0:T(1,128)S(1)} %copy-done.6, s32[1,48]{1,0:T(1,128)S(1)} %bitcast.11, f32[2,96,128]{2,1,0:T(8,128)S(1)} %collective-permute-done.far_ref, ...), custom_call_target="tpu_custom_call" | custom-call | flops 1000000 | bytes 1000000 | tf_op jit(solution)/shard_map/pallas_call | solution.py:763
  9.7 1.6 %collective-permute-start.2 = (f32[288,128]{1,0:T(8,128)S(1)}, f32[288,128]{1,0:T(8,128)S(1)}, u32[]{:S(2)}, u32[]{:S(2)}) collective-permute-start(f32[288,128]{1,0:T(8,128)S(1)} %get-tuple-element.37), channel_id=1, source_target_pairs={{0,8},{8,0},{16,24},{24,16},{1,9},{9,1},{17,25},{25,17},{2,10},{10... | collective-permute-start | bytes 442376 | tf_op jit(solution)/shard_map/ppermute | solution.py:674
  11.2 1.5 %collective-permute-start.3 = (f32[288,128]{1,0:T(8,128)S(1)}, f32[288,128]{1,0:T(8,128)S(1)}, u32[]{:S(2)}, u32[]{:S(2)}) collective-permute-start(f32[288,128]{1,0:T(8,128)S(1)} %get-tuple-element.42), channel_id=1, source_target_pairs={{0,16},{8,24},{16,0},{24,8},{1,17},{9,25},{17,1},{25,9},{2,18},{10... | collective-permute-start | bytes 442376 | tf_op jit(solution)/shard_map/ppermute | solution.py:674
  12.7 0.5 %collective-permute-start.4 = (f32[288,128]{1,0:T(8,128)S(1)}, f32[288,128]{1,0:T(8,128)S(1)}, u32[]{:S(2)}, u32[]{:S(2)}) collective-permute-start(f32[288,128]{1,0:T(8,128)S(1)} %get-tuple-element.43), channel_id=1, source_target_pairs={{0,24},{8,16},{16,8},{24,0},{1,25},{9,17},{17,9},{25,1},{2,26},{10... | collective-permute-start | bytes 442376 | tf_op jit(solution)/shard_map/ppermute | solution.py:674
  13.2 4.1 %shard_map.95 = (f32[30720,128]{1,0:T(8,128)S(1)}, f32[1280,128]{1,0:T(8,128)S(1)}, f32[1280,128]{1,0:T(8,128)S(1)}) custom-call(s32[32,31]{1,0:T(8,128)S(1)} %copy-done.2, s32[32,31]{1,0:T(8,128)S(1)} %copy-done.3, s32[1,32]{1,0:T(1,128)S(1)} %bitcast.14, bf16[316,40,128]{2,1,0:T(8,128)(2,1)S(1)} %get-tuple-element.30.table_ref, ...), custom_call_target="tpu_custom_call" | custom-call | flops 90000000 | bytes 12000000 | tf_op jit(solution)/shard_map/pallas_call | solution.py:777
  17.3 0.0 collective-permute-done.2.rest_0_
  17.3 1.2 %shard_map.96 = (f32[1280,128]{1,0:T(8,128)S(1)}, f32[1280,128]{1,0:T(8,128)S(1)}) custom-call(f32[30720,128]{1,0:T(8,128)S(1)} %get-tuple-element.36.placed_ref, f32[288,128]{1,0:T(8,128)S(1)} %collective-permute-done.2.rest_0_, f32[1280,128]{1,0:T(8,128)S(1)} %get-tuple-element.38.rest_1_, f32[1280,128]{1,0:T(8,128)S(1)} %get-tuple-element.39.rest_2_), custom_call_target="tpu_custom_call" | custom-call | flops 60000000 | bytes 12000000 | tf_op jit(solution)/shard_map/pallas_call | solution.py:794
  18.5 1.8 %collective-permute-done.3.rest_0_ = f32[288,128]{1,0:T(8,128)S(1)} collective-permute-done((f32[288,128]{1,0:T(8,128)S(1)}, f32[288,128]{1,0:T(8,128)S(1)}, u32[]{:S(2)}, u32[]{:S(2)}) %collective-permute-start.3) | collective-permute-done | bytes 147488 | tf_op jit(solution)/shard_map/ppermute | solution.py:674
  20.3 0.0 collective-permute-done.4.rest_1_
  20.3 0.6 %shard_map.97 = (f32[640,128]{1,0:T(8,128)S(1)}, f32[640,128]{1,0:T(8,128)S(1)}, f32[288,128]{1,0:T(8,128)S(1)}) custom-call(f32[30720,128]{1,0:T(8,128)S(1)} %get-tuple-element.36.placed_ref, f32[1280,128]{1,0:T(8,128)S(1)} %get-tuple-element.40.real_sum, f32[1280,128]{1,0:T(8,128)S(1)} %get-tuple-element.41.imag_sum, ...), custom_call_target="tpu_custom_call" | custom-call | flops 10000000 | bytes 2000000 | tf_op jit(solution)/shard_map/pallas_call | solution.py:808
  20.9 1.0 %shard_map.99 = (f32[288,128]{1,0:T(8,128)S(1)}, f32[288,128]{1,0:T(8,128)S(1)}) custom-call(f32[30720,128]{1,0:T(8,128)S(1)} %get-tuple-element.36.placed_ref, f32[1280,128]{1,0:T(8,128)S(1)} %get-tuple-element.40.real_sum, f32[1280,128]{1,0:T(8,128)S(1)} %get-tuple-element.41.imag_sum, f32[640,128]{1,0:T(8,128)S(1)} %get-tuple-element.44.rest_0_, ...), custom_call_target="tpu_custom_call" | custom-call | flops 20000000 | bytes 4000000 | tf_op jit(solution)/shard_map/pallas_call | solution.py:808
  21.9 1.3 %collective-permute-start.5 = (f32[288,128]{1,0:T(8,128)S(1)}, f32[288,128]{1,0:T(8,128)S(1)}, u32[]{:S(2)}, u32[]{:S(2)}) collective-permute-start(f32[288,128]{1,0:T(8,128)S(1)} %get-tuple-element.46), channel_id=1, source_target_pairs={{0,8},{8,0},{16,24},{24,16},{1,9},{9,1},{17,25},{25,17},{2,10},{10... | collective-permute-start | bytes 442376 | tf_op jit(solution)/shard_map/ppermute | solution.py:674
  23.3 0.8 %collective-permute-start.6 = (f32[288,128]{1,0:T(8,128)S(1)}, f32[288,128]{1,0:T(8,128)S(1)}, u32[]{:S(2)}, u32[]{:S(2)}) collective-permute-start(f32[288,128]{1,0:T(8,128)S(1)} %get-tuple-element.47), channel_id=1, source_target_pairs={{0,16},{8,24},{16,0},{24,8},{1,17},{9,25},{17,1},{25,9},{2,18},{10... | collective-permute-start | bytes 442376 | tf_op jit(solution)/shard_map/ppermute | solution.py:674
  24.1 1.4 %collective-permute-start.7 = (f32[288,128]{1,0:T(8,128)S(1)}, f32[288,128]{1,0:T(8,128)S(1)}, u32[]{:S(2)}, u32[]{:S(2)}) collective-permute-start(f32[288,128]{1,0:T(8,128)S(1)} %get-tuple-element.48), channel_id=1, source_target_pairs={{0,24},{8,16},{16,8},{24,0},{1,25},{9,17},{17,9},{25,1},{2,26},{10... | collective-permute-start | bytes 442376 | tf_op jit(solution)/shard_map/ppermute | solution.py:674
  25.5 1.1 %shard_map.91.phase_ref = f32[7,2,48,128]{3,2,1,0:T(8,128)S(1)} custom-call(s32[48]{0:T(128)} %octants_hbm.3), custom_call_target="tpu_custom_call" | custom-call | flops 20000000 | bytes 1000000 | tf_op jit(solution)/shard_map/pallas_call | solution.py:822
  26.6 0.0 copy-start.1
  26.6 0.0 copy-start.5
  26.6 0.5 %shard_map.98.rest_0_ = f32[288,128]{1,0:T(8,128)S(1)} custom-call(f32[30720,128]{1,0:T(8,128)S(1)} %get-tuple-element.36.placed_ref, f32[1280,128]{1,0:T(8,128)S(1)} %get-tuple-element.40.real_sum, f32[1280,128]{1,0:T(8,128)S(1)} %get-tuple-element.41.imag_sum, f32[640,128]{1,0:T(8,128)S(1)} %get-tuple-element.44.rest_0_, ...), custom_call_target="tpu_custom_call" | custom-call | flops 10000000 | bytes 2000000 | tf_op jit(solution)/shard_map/pallas_call | solution.py:808
  27.1 0.9 %collective-permute-done.5.rest_1_ = f32[288,128]{1,0:T(8,128)S(1)} collective-permute-done((f32[288,128]{1,0:T(8,128)S(1)}, f32[288,128]{1,0:T(8,128)S(1)}, u32[]{:S(2)}, u32[]{:S(2)}) %collective-permute-start.5) | collective-permute-done | bytes 147488 | tf_op jit(solution)/shard_map/ppermute | solution.py:674
  28.0 3.5 %collective-permute-done.6.rest_2_ = f32[288,128]{1,0:T(8,128)S(1)} collective-permute-done((f32[288,128]{1,0:T(8,128)S(1)}, f32[288,128]{1,0:T(8,128)S(1)}, u32[]{:S(2)}, u32[]{:S(2)}) %collective-permute-start.6) | collective-permute-done | bytes 147488 | tf_op jit(solution)/shard_map/ppermute | solution.py:674
  31.5 0.1 shard_map.100
  31.6 1.0 %collective-permute-start.8 = (f32[64,128]{1,0:T(8,128)S(1)}, f32[64,128]{1,0:T(8,128)S(1)}, u32[]{:S(2)}, u32[]{:S(2)}) collective-permute-start(f32[64,128]{1,0:T(8,128)S(1)} %get-tuple-element.52), channel_id=1, source_target_pairs={{0,7},{1,2},{2,1},{3,4},{4,3},{5,6},{6,5},{7,0},{8,15},{9,10},{10,... | collective-permute-start | bytes 98312 | tf_op jit(solution)/shard_map/ppermute | solution.py:669
  32.6 2.9 %shard_map.101 = (f32[96,32,128]{2,1,0:T(8,128)}, f32[2,96,8,128]{3,2,1,0:T(8,128)S(1)}) custom-call(s32[1,48]{1,0:T(1,128)S(1)} %copy-done.6, s32[1,48]{1,0:T(1,128)S(1)} %bitcast.12, f32[1152,128]{1,0:T(8,128)S(1)} %get-tuple-element.49.flat_ref, f32[8,2,9,8,128]{4,3,2,1,0:T(8,128)S(1)} %get-tuple-element.50.phase_ref, bf16[2,256,256]{2,1,0:T(8,128)(2,1)S(1)} %copy-done.1), custom_call_target="tpu_custom_call" | custom-call | flops 4000000000 | bytes 12000000 | tf_op jit(solution)/shard_map/pallas_call | solution.py:843
  35.5 1.3 %collective-permute-done.8.far_ref = f32[64,128]{1,0:T(8,128)S(1)} collective-permute-done((f32[64,128]{1,0:T(8,128)S(1)}, f32[64,128]{1,0:T(8,128)S(1)}, u32[]{:S(2)}, u32[]{:S(2)}) %collective-permute-start.8) | collective-permute-done | bytes 32800 | tf_op jit(solution)/shard_map/ppermute | solution.py:669
  36.8 1.5 %shard_map.102 = f32[96,32,128]{2,1,0:T(8,128)} custom-call(s32[1,48]{1,0:T(1,128)S(1)} %copy-done.6, f32[7,2,48,128]{3,2,1,0:T(8,128)S(1)} %shard_map.91.phase_ref, bf16[2,256,256]{2,1,0:T(8,128)(2,1)S(1)} %copy-done.1, f32[2,96,8,128]{3,2,1,0:T(8,128)S(1)} %get-tuple-element.51.edge_ref, ...), custom_call_target="tpu_custom_call", output_to_operand_aliasing={{}: (6, {})} | custom-call | flops 1000000 | bytes 1000000 | tf_op jit(solution)/shard_map/pallas_call | solution.py:862
  (16 shorter events, 0.0 us)
Async XLA Ops:
  0.9 8.1 %collective-permute-start = (f32[2,96,128]{2,1,0:T(8,128)S(1)}, f32[2,96,128]{2,1,0:T(8,128)S(1)}, u32[]{:S(2)}, u32[]{:S(2)}) collective-permute-start(f32[2,96,128]{2,1,0:T(8,128)S(1)} %get-tuple-element.31), channel_id=1, source_target_pairs={{0,7},{1,2},{2,1},{3,4},{4,3},{5,6},{6,5},{7,0},{8,15},{9,10},{10,... | collective-permute-start | bytes 294920 | tf_op jit(solution)/shard_map/ppermute | solution.py:669
  5.5 3.5 %collective-permute-start.1 = (f32[2,96,128]{2,1,0:T(8,128)S(1)}, f32[2,96,128]{2,1,0:T(8,128)S(1)}, u32[]{:S(2)}, u32[]{:S(2)}) collective-permute-start(f32[2,96,128]{2,1,0:T(8,128)S(1)} %get-tuple-element.32), channel_id=1, source_target_pairs={{0,1},{1,0},{2,3},{3,2},{4,5},{5,4},{6,7},{7,6},{8,9},{9,8},{10,11... | collective-permute-start | bytes 294920 | tf_op jit(solution)/shard_map/ppermute | solution.py:669
  5.5 3.6 %copy-start = (bf16[2,384,256]{2,1,0:T(8,128)(2,1)S(1)}, bf16[2,384,256]{2,1,0:T(8,128)(2,1)}, u32[]{:S(2)}) copy-start(bf16[2,384,256]{2,1,0:T(8,128)(2,1)} %constant.4.clone.spread_hbm.spread_ref) | copy-start | bytes 1179652
  5.5 3.6 %copy-start.4 = (s32[48]{0:T(128)S(1)}, s32[48]{0:T(128)}, u32[]{:S(2)}) copy-start(s32[48]{0:T(128)} %octants_hbm.3) | copy-start | bytes 580
  5.5 3.6 %copy-start.6 = (s32[1,48]{1,0:T(1,128)S(1)}, s32[1,48]{1,0:T(1,128)}, u32[]{:S(2)}) copy-start(s32[1,48]{1,0:T(1,128)} %parents_ref.5) | copy-start | bytes 580
  5.5 7.7 %copy-start.2 = (s32[32,31]{1,0:T(8,128)S(1)}, s32[32,31]{1,0:T(8,128)}, u32[]{:S(2)}) copy-start(s32[32,31]{1,0:T(8,128)} %source_ref.1) | copy-start | bytes 11908
  5.5 7.7 %copy-start.3 = (s32[32,31]{1,0:T(8,128)S(1)}, s32[32,31]{1,0:T(8,128)}, u32[]{:S(2)}) copy-start(s32[32,31]{1,0:T(8,128)} %offset_ref.1) | copy-start | bytes 11908
  5.6 7.7 %copy-start.7 = (s32[32]{0:T(128)S(1)}, s32[32]{0:T(128)}, u32[]{:S(2)}) copy-start(s32[32]{0:T(128)} %param.15) | copy-start | bytes 388
  9.7 7.6 %collective-permute-start.2 = (f32[288,128]{1,0:T(8,128)S(1)}, f32[288,128]{1,0:T(8,128)S(1)}, u32[]{:S(2)}, u32[]{:S(2)}) collective-permute-start(f32[288,128]{1,0:T(8,128)S(1)} %get-tuple-element.37), channel_id=1, source_target_pairs={{0,8},{8,0},{16,24},{24,16},{1,9},{9,1},{17,25},{25,17},{2,10},{10... | collective-permute-start | bytes 442376 | tf_op jit(solution)/shard_map/ppermute | solution.py:674
  11.2 9.1 %collective-permute-start.3 = (f32[288,128]{1,0:T(8,128)S(1)}, f32[288,128]{1,0:T(8,128)S(1)}, u32[]{:S(2)}, u32[]{:S(2)}) collective-permute-start(f32[288,128]{1,0:T(8,128)S(1)} %get-tuple-element.42), channel_id=1, source_target_pairs={{0,16},{8,24},{16,0},{24,8},{1,17},{9,25},{17,1},{25,9},{2,18},{10... | collective-permute-start | bytes 442376 | tf_op jit(solution)/shard_map/ppermute | solution.py:674
  12.7 7.6 %collective-permute-start.4 = (f32[288,128]{1,0:T(8,128)S(1)}, f32[288,128]{1,0:T(8,128)S(1)}, u32[]{:S(2)}, u32[]{:S(2)}) collective-permute-start(f32[288,128]{1,0:T(8,128)S(1)} %get-tuple-element.43), channel_id=1, source_target_pairs={{0,24},{8,16},{16,8},{24,0},{1,25},{9,17},{17,9},{25,1},{2,26},{10... | collective-permute-start | bytes 442376 | tf_op jit(solution)/shard_map/ppermute | solution.py:674
  21.9 6.0 %collective-permute-start.5 = (f32[288,128]{1,0:T(8,128)S(1)}, f32[288,128]{1,0:T(8,128)S(1)}, u32[]{:S(2)}, u32[]{:S(2)}) collective-permute-start(f32[288,128]{1,0:T(8,128)S(1)} %get-tuple-element.46), channel_id=1, source_target_pairs={{0,8},{8,0},{16,24},{24,16},{1,9},{9,1},{17,25},{25,17},{2,10},{10... | collective-permute-start | bytes 442376 | tf_op jit(solution)/shard_map/ppermute | solution.py:674
  23.3 8.3 %collective-permute-start.6 = (f32[288,128]{1,0:T(8,128)S(1)}, f32[288,128]{1,0:T(8,128)S(1)}, u32[]{:S(2)}, u32[]{:S(2)}) collective-permute-start(f32[288,128]{1,0:T(8,128)S(1)} %get-tuple-element.47), channel_id=1, source_target_pairs={{0,16},{8,24},{16,0},{24,8},{1,17},{9,25},{17,1},{25,9},{2,18},{10... | collective-permute-start | bytes 442376 | tf_op jit(solution)/shard_map/ppermute | solution.py:674
  24.1 7.5 %collective-permute-start.7 = (f32[288,128]{1,0:T(8,128)S(1)}, f32[288,128]{1,0:T(8,128)S(1)}, u32[]{:S(2)}, u32[]{:S(2)}) collective-permute-start(f32[288,128]{1,0:T(8,128)S(1)} %get-tuple-element.48), channel_id=1, source_target_pairs={{0,24},{8,16},{16,8},{24,0},{1,25},{9,17},{17,9},{25,1},{2,26},{10... | collective-permute-start | bytes 442376 | tf_op jit(solution)/shard_map/ppermute | solution.py:674
  26.6 6.0 %copy-start.1 = (bf16[2,256,256]{2,1,0:T(8,128)(2,1)S(1)}, bf16[2,256,256]{2,1,0:T(8,128)(2,1)}, u32[]{:S(2)}) copy-start(bf16[2,256,256]{2,1,0:T(8,128)(2,1)} %constant.5.clone.gather_ref) | copy-start | bytes 786436
  26.6 6.0 %copy-start.5 = (s32[48]{0:T(128)S(1)}, s32[48]{0:T(128)}, u32[]{:S(2)}) copy-start(s32[48]{0:T(128)} %octants_hbm.3) | copy-start | bytes 580
  31.6 5.2 %collective-permute-start.8 = (f32[64,128]{1,0:T(8,128)S(1)}, f32[64,128]{1,0:T(8,128)S(1)}, u32[]{:S(2)}, u32[]{:S(2)}) collective-permute-start(f32[64,128]{1,0:T(8,128)S(1)} %get-tuple-element.52), channel_id=1, source_target_pairs={{0,7},{1,2},{2,1},{3,4},{4,3},{5,6},{6,5},{7,0},{8,15},{9,10},{10,... | collective-permute-start | bytes 98312 | tf_op jit(solution)/shard_map/ppermute | solution.py:669
  32.6 4.2 %collective-permute-start.9 = (f32[64,128]{1,0:T(8,128)S(1)}, f32[64,128]{1,0:T(8,128)S(1)}, u32[]{:S(2)}, u32[]{:S(2)}) collective-permute-start(f32[64,128]{1,0:T(8,128)S(1)} %get-tuple-element.53), channel_id=1, source_target_pairs={{0,1},{1,0},{2,3},{3,2},{4,5},{5,4},{6,7},{7,6},{8,9},{9,8},{10,11... | collective-permute-start | bytes 98312 | tf_op jit(solution)/shard_map/ppermute | solution.py:669

commit v11 on v10

--- a/solution.py
+++ b/solution.py
@@ -190,27 +190,38 @@
     return [outer[0] + inner[0], outer[1] + inner[1], CENTRE * total, outer[1] - inner[1], outer[0] - inner[0]]
 
 
+def table_part(table_ref, first_row, first, target):
+    rows = pl.ds(pl.multiple_of(first_row // 8 * 8, 8), target.shape[1])
+    return table_ref.at[pl.ds(first, target.shape[0]), rows, :]
+
+
 def main_kernel(peers, parents_hbm, octants_hbm, x_hbm, table_ref, spread_hbm, *rest):
     phase_ref, edge_phase_ref, flat_ref, slice_ref = rest[:4]
-    parents_ref, octants_ref, x_ref, spread_ref, az_e, az_o, res_e, res_o, acc, flat, sems = rest[4:]
+    parents_ref, octants_ref, x_ref, spread_ref, az_e, az_o, res_e, res_o, acc, flat, sems, x_sems = rest[4:]
     children = octants_ref.shape[0]
     periods = phase_ref.shape[3]
     azimuth_in = periods * PERIOD_C
     own = acc.shape[0]
     me = lax.axis_index("clus")
     share = ROWS_PER_PERIOD * periods // peers
-    first_tile = me * (2 * share) // 8
-    table_rows = pl.ds(pl.multiple_of(first_tile * 8, 8), slice_ref.shape[1])
     ends = (
         (octants_hbm, octants_ref),
         (parents_hbm, parents_ref),
-        (x_hbm, x_ref),
         (spread_hbm, spread_ref),
-        (table_ref.at[:, table_rows, :], slice_ref),
+        (table_part(table_ref, me * (2 * share), 0, slice_ref), slice_ref),
     )
     copies = [pltpu.make_async_copy(source, target, sems.at[i]) for i, (source, target) in enumerate(ends)]
+    blocks = children // BLOCK
+    block_rows = 2 * BLOCK * azimuth_in
+
+    def x_copy(block):
+        some = pl.ds(pl.multiple_of(block * block_rows, 8), block_rows)
+        return pltpu.make_async_copy(x_hbm.at[some], x_ref.at[some], x_sems.at[block])
+
     for copy in copies[:-1]:
         copy.start()
+    for block in range(blocks):
+        x_copy(block).start()
     fill_phases(lax.axis_index("dir"), phase_ref)
     acc[...] = jnp.zeros_like(acc)
     sublane = lax.broadcasted_iota(jnp.int32, (periods, LANES), 0)
@@ -258,12 +269,13 @@
                     acc[parent, 1, w] += real * sine + imaginary * cosine
 
     def one_block(block, carry):
+        x_copy(block).wait()
         azimuth(block)
         polar()
         shift(block)
         return carry
 
-    lax.fori_loop(0, children // BLOCK, one_block, 0)
+    lax.fori_loop(0, blocks, one_block, 0)
     for gp in range(2 * own):
         for w in range(ROWS_PER_PERIOD):
             flat[pl.ds(gp * ROWS_PER_PERIOD * periods + w, periods, stride=ROWS_PER_PERIOD), :] = acc[gp // 2, gp % 2, w]
@@ -340,13 +352,16 @@
         outs[d][...] = fixed[pl.ds(start, chunk_rows), :]
 
 
-def widen_kernel(peers, others, source_ref, offset_ref, count_ref, table_ref, chunk, placed_ref, real_sum, imag_sum, *rest):
-    wide_ref, numbers_ref, listed, real_twice, imag_twice, sem = rest
+def widen_kernel(peers, others, source_ref, offset_ref, count_ref, head_ref, table_ref, chunk, placed_ref, real_sum, imag_sum, *rest):
+    tail_ref, wide_ref, numbers_ref, listed, real_twice, imag_twice, sem, tail_sem = rest
     targets, partners = source_ref.shape
-    offsets, frame, _ = table_ref.shape
+    half, frame, _ = head_ref.shape
+    offsets = half + tail_ref.shape[0]
     own = targets // peers
     share = chunk.shape[0] // (2 * own)
     me = lax.axis_index("clus")
+    tail_copy = pltpu.make_async_copy(table_part(table_ref, me * (2 * share), half, tail_ref), tail_ref, tail_sem)
+    tail_copy.start()
     shape = (targets, targets)
     row, lane = (lax.broadcasted_iota(jnp.int32, shape, d) for d in range(2))
     count = jnp.sum(jnp.where(row == lane, count_ref[...], 0), axis=1, keepdims=True)
@@ -358,18 +373,24 @@
     copy = pltpu.make_async_copy(numbers_ref, listed, sem)
     copy.start()
 
-    def some_offsets(i, carry):
-        for j in range(4):
-            wide_ref[pl.ds(pl.multiple_of((i * 4 + j) * frame, 8), frame), :] = table_ref[i * 4 + j].astype(f32)
-        return carry
-
-    whole_steps = offsets // 4
-    lax.fori_loop(0, whole_steps, some_offsets, 0)
-    for offset in range(whole_steps * 4, offsets):
-        wide_ref[offset * frame : (offset + 1) * frame, :] = table_ref[offset].astype(f32)
+    def widen(part_ref, first):
+        def some_offsets(i, carry):
+            for j in range(4):
+                place = pl.multiple_of((first + i * 4 + j) * frame, 8)
+                wide_ref[pl.ds(place, frame), :] = part_ref[i * 4 + j].astype(f32)
+            return carry
+
+        whole_steps = part_ref.shape[0] // 4
+        lax.fori_loop(0, whole_steps, some_offsets, 0)
+        for offset in range(whole_steps * 4, part_ref.shape[0]):
+            wide_ref[(first + offset) * frame : (first + offset + 1) * frame, :] = part_ref[offset].astype(f32)
+
+    widen(head_ref, 0)
     wide_ref[offsets * frame :, :] = jnp.zeros((frame, LANES), f32)
     doubled(chunk, real_twice, imag_twice, 0, own, share, frame, lax.rem(me * (2 * share), 8))
     copy.wait()
+    tail_copy.wait()
+    widen(tail_ref, half)
 
     def operator_of(target, device, g):
         first = listed[target, device * own + g]
@@ -725,6 +746,7 @@
     frame = max(-(-((q * 2 * share) % 8 + 2 * share) // 8) * 8 for q in range(peers))
     view = trans_table.reshape(offsets, 2, flat_rows, LANES).transpose(0, 2, 1, 3).reshape(offsets, 2 * flat_rows, LANES)
     blocks = children // BLOCK
+    half = offsets // 2
     rows = 2 * BLOCK * 3 * periods
     phases, edge_phases, flat, table = local_call(
         functools.partial(main_kernel, peers),
@@ -732,7 +754,7 @@
             array(8, 2, ROWS_PER_PERIOD, periods, LANES),
             array(edges, 2, 8, LANES),
             array(2 * own * flat_rows, LANES),
-            jax.ShapeDtypeStruct((offsets, frame, LANES), bf16),
+            jax.ShapeDtypeStruct((half, frame, LANES), bf16),
         ],
         [HBM] * 5,
         [
@@ -746,7 +768,8 @@
             buffer(rows, 2 * LANES),
             buffer(own, 2, ROWS_PER_PERIOD, periods, LANES),
             buffer(2 * own * flat_rows, LANES),
-            pltpu.SemaphoreType.DMA((5,)),
+            pltpu.SemaphoreType.DMA((4,)),
+            pltpu.SemaphoreType.DMA((blocks,)),
         ],
         24,
         flops=4_000_000_000,
@@ -777,19 +800,21 @@
     operators, *sums = local_call(
         functools.partial(widen_kernel, peers, others),
         [array(parent_total * len(others) * own * frame, LANES)] + sum_pair,
-        [VMEM] * 5,
+        [VMEM] * 4 + [HBM, VMEM],
         [
+            pltpu.VMEM((offsets - half, frame, LANES), bf16),
             buffer((offsets + 1) * frame, LANES),
             pltpu.VMEM((parent_total, parent_total), jnp.int32),
             pltpu.SMEM((parent_total, parent_total), jnp.int32),
             buffer(own * frame, LANES),
             buffer(own * frame, LANES),
             pltpu.SemaphoreType.DMA,
+            pltpu.SemaphoreType.DMA,
         ],
         20,
         flops=90_000_000,
         bytes_accessed=12_000_000,
-    )(partner_src, partner_off, partner_count.reshape(1, parent_total), table, received[0])
+    )(partner_src, partner_off, partner_count.reshape(1, parent_total), table, in_hbm(view), received[0])
 
     sums = local_call(
         functools.partial(gather_kernel, peers, frame, others, tuple(early)),

time: 38.5 us -> 38.5 us (level)
  waiting for transfers between devices: 7.54 us -> 6.62 us
  Pallas kernels: 17.9 us -> 18.6 us
    pallas_call x1, Pallas kernels: 4.06 us -> 4.97 us  [on_device_exchange(): local_call(functools.partial(widen_kernel, peers, others), [array(parent_...]
    ppermute x6, waiting for transfers between devices: 6.21 us -> 5.42 us  [exchanged(): return lax.ppermute(values, axis, [(i, i ^ mask) for i in range(size)])]
  transfers between devices with their start and end apart: 10 -> 10, of which waited for: 4 -> 4; matrix products, arithmetic and copies ran while one was open for 0% -> 0% of each run, Pallas kernels for 35% -> 36%
where the time goes in v11:
time: 38.5 us; the launch traced here: 38.2 us
  Pallas kernels  18.6 us (48%)
  starting transfers between devices  12.8 us (33%)
  waiting for transfers between devices  6.62 us (17%)
    ppermute x6, starting transfers between devices, exchanged(): return lax.ppermute(values, axis, [(i, i ^ mask) for i in range(size)])  7.11 us
    ppermute x4, starting transfers between devices, swapped(): lax.ppermute(values, axis, [(i, ((i - first ^ 1) + first) % size) for i i...  5.7 us
    ppermute x6, waiting for transfers between devices, exchanged(): return lax.ppermute(values, axis, [(i, i ^ mask) for i in range(size)])  5.42 us
    pallas_call x1, Pallas kernels, on_device_exchange(): local_call(functools.partial(widen_kernel, peers, others), [array(parent_...  4.97 us
    pallas_call x1, Pallas kernels, on_device_exchange(): local_call(functools.partial(main_kernel, peers), [array(8, 2, ROWS_PER_P...  3.34 us
    pallas_call x1, Pallas kernels, on_device_exchange(): local_call(disaggregate_kernel, [array(pairs, azimuth_in, polar_in), arra...  2.88 us
    pallas_call x3, Pallas kernels, on_device_exchange(): local_call(functools.partial(translate_kernel, frame, others, tuple(late)...  2.18 us
    pallas_call x1, Pallas kernels, on_device_exchange(): local_call(finish_kernel, array(pairs, azimuth_in, polar_in), [VMEM] * 6...  1.46 us
  transfers between devices with their start and end apart: 10, of which 4 were waited for; matrix products, arithmetic and copies ran while one was open for 0% of the time, Pallas kernels for 36%

profile of v11, /device:TPU:0, one launch (start us, length us, event | category | flops | bytes accessed | tf_op | source)
XLA Modules:
  0.0 38.2 jit_solution(6203170624717325384)
XLA Ops:
  0.0 0.9 %shard_map.93 = (f32[2,96,128]{2,1,0:T(8,128)S(1)}, f32[2,96,128]{2,1,0:T(8,128)S(1)}) custom-call(f32[96,32,128]{2,1,0:T(8,128)} %bitcast.17), custom_call_target="tpu_custom_call" | custom-call | flops 1000000 | bytes 1000000 | tf_op jit(solution)/shard_map/pallas_call | solution.py:738
  0.9 4.6 %collective-permute-start = (f32[2,96,128]{2,1,0:T(8,128)S(1)}, f32[2,96,128]{2,1,0:T(8,128)S(1)}, u32[]{:S(2)}, u32[]{:S(2)}) collective-permute-start(f32[2,96,128]{2,1,0:T(8,128)S(1)} %get-tuple-element.31), channel_id=1, source_target_pairs={{0,7},{1,2},{2,1},{3,4},{4,3},{5,6},{6,5},{7,0},{8,15},{9,10},{10,... | collective-permute-start | bytes 294920 | tf_op jit(solution)/shard_map/ppermute | solution.py:690
  5.5 0.0 copy-start.2
  5.5 0.0 copy-start.3
  5.6 0.0 copy-start.7
  5.6 3.3 %shard_map.92 = (f32[8,2,9,8,128]{4,3,2,1,0:T(8,128)S(1)}, f32[7,2,8,128]{3,2,1,0:T(8,128)S(1)}, f32[1152,128]{1,0:T(8,128)S(1)}, bf16[158,40,128]{2,1,0:T(8,128)(2,1)S(1)}) custom-call(s32[48]{0:T(128)} %bitcast.13, s32[48]{0:T(128)} %octants_hbm.3, f32[3072,128]{1,0:T(8,128)} %bitcast.18, bf16[316,144,128]{2,1,0:T(8,128)(2,1)} %bitcast.15, ...), custom_call_target="tpu_custom_call" | custom-call | flops 4000000000 | bytes 12000000 | tf_op jit(solution)/shard_map/pallas_call | solution.py:751
  8.9 0.0 collective-permute-done.far_ref
  9.0 0.6 %shard_map.94 = (f32[288,128]{1,0:T(8,128)S(1)}, f32[288,128]{1,0:T(8,128)S(1)}, f32[288,128]{1,0:T(8,128)S(1)}, f32[288,128]{1,0:T(8,128)S(1)}) custom-call(s32[1,48]{1,0:T(1,128)S(1)} %copy-done.6, s32[1,48]{1,0:T(1,128)S(1)} %bitcast.11, f32[2,96,128]{2,1,0:T(8,128)S(1)} %collective-permute-done.far_ref, ...), custom_call_target="tpu_custom_call" | custom-call | flops 1000000 | bytes 1000000 | tf_op jit(solution)/shard_map/pallas_call | solution.py:786
  9.5 1.6 %collective-permute-start.2 = (f32[288,128]{1,0:T(8,128)S(1)}, f32[288,128]{1,0:T(8,128)S(1)}, u32[]{:S(2)}, u32[]{:S(2)}) collective-permute-start(f32[288,128]{1,0:T(8,128)S(1)} %get-tuple-element.37), channel_id=1, source_target_pairs={{0,8},{8,0},{16,24},{24,16},{1,9},{9,1},{17,25},{25,17},{2,10},{10... | collective-permute-start | bytes 442376 | tf_op jit(solution)/shard_map/ppermute | solution.py:695
  11.1 1.5 %collective-permute-start.3 = (f32[288,128]{1,0:T(8,128)S(1)}, f32[288,128]{1,0:T(8,128)S(1)}, u32[]{:S(2)}, u32[]{:S(2)}) collective-permute-start(f32[288,128]{1,0:T(8,128)S(1)} %get-tuple-element.42), channel_id=1, source_target_pairs={{0,16},{8,24},{16,0},{24,8},{1,17},{9,25},{17,1},{25,9},{2,18},{10... | collective-permute-start | bytes 442376 | tf_op jit(solution)/shard_map/ppermute | solution.py:695
  12.7 0.4 %collective-permute-start.4 = (f32[288,128]{1,0:T(8,128)S(1)}, f32[288,128]{1,0:T(8,128)S(1)}, u32[]{:S(2)}, u32[]{:S(2)}) collective-permute-start(f32[288,128]{1,0:T(8,128)S(1)} %get-tuple-element.43), channel_id=1, source_target_pairs={{0,24},{8,16},{16,8},{24,0},{1,25},{9,17},{17,9},{25,1},{2,26},{10... | collective-permute-start | bytes 442376 | tf_op jit(solution)/shard_map/ppermute | solution.py:695
  13.1 5.0 %shard_map.95 = (f32[30720,128]{1,0:T(8,128)S(1)}, f32[1280,128]{1,0:T(8,128)S(1)}, f32[1280,128]{1,0:T(8,128)S(1)}) custom-call(s32[32,31]{1,0:T(8,128)S(1)} %copy-done.2, s32[32,31]{1,0:T(8,128)S(1)} %copy-done.3, s32[1,32]{1,0:T(1,128)S(1)} %bitcast.14, bf16[158,40,128]{2,1,0:T(8,128)(2,1)S(1)} %get-tuple-element.30.head_ref, ...), custom_call_target="tpu_custom_call" | custom-call | flops 90000000 | bytes 12000000 | tf_op jit(solution)/shard_map/pallas_call | solution.py:800
  18.1 1.1 %shard_map.96 = (f32[1280,128]{1,0:T(8,128)S(1)}, f32[1280,128]{1,0:T(8,128)S(1)}) custom-call(f32[30720,128]{1,0:T(8,128)S(1)} %get-tuple-element.36.placed_ref, f32[288,128]{1,0:T(8,128)S(1)} %collective-permute-done.2.rest_0_, f32[1280,128]{1,0:T(8,128)S(1)} %get-tuple-element.38.rest_1_, f32[1280,128]{1,0:T(8,128)S(1)} %get-tuple-element.39.rest_2_), custom_call_target="tpu_custom_call" | custom-call | flops 60000000 | bytes 12000000 | tf_op jit(solution)/shard_map/pallas_call | solution.py:819
  19.2 1.0 %collective-permute-done.3.rest_0_ = f32[288,128]{1,0:T(8,128)S(1)} collective-permute-done((f32[288,128]{1,0:T(8,128)S(1)}, f32[288,128]{1,0:T(8,128)S(1)}, u32[]{:S(2)}, u32[]{:S(2)}) %collective-permute-start.3) | collective-permute-done | bytes 147488 | tf_op jit(solution)/shard_map/ppermute | solution.py:695
  20.2 0.0 collective-permute-done.4.rest_1_
  20.2 0.6 %shard_map.97 = (f32[640,128]{1,0:T(8,128)S(1)}, f32[640,128]{1,0:T(8,128)S(1)}, f32[288,128]{1,0:T(8,128)S(1)}) custom-call(f32[30720,128]{1,0:T(8,128)S(1)} %get-tuple-element.36.placed_ref, f32[1280,128]{1,0:T(8,128)S(1)} %get-tuple-element.40.real_sum, f32[1280,128]{1,0:T(8,128)S(1)} %get-tuple-element.41.imag_sum, ...), custom_call_target="tpu_custom_call" | custom-call | flops 10000000 | bytes 2000000 | tf_op jit(solution)/shard_map/pallas_call | solution.py:833
  20.8 1.1 %shard_map.99 = (f32[288,128]{1,0:T(8,128)S(1)}, f32[288,128]{1,0:T(8,128)S(1)}) custom-call(f32[30720,128]{1,0:T(8,128)S(1)} %get-tuple-element.36.placed_ref, f32[1280,128]{1,0:T(8,128)S(1)} %get-tuple-element.40.real_sum, f32[1280,128]{1,0:T(8,128)S(1)} %get-tuple-element.41.imag_sum, f32[640,128]{1,0:T(8,128)S(1)} %get-tuple-element.44.rest_0_, ...), custom_call_target="tpu_custom_call" | custom-call | flops 20000000 | bytes 4000000 | tf_op jit(solution)/shard_map/pallas_call | solution.py:833
  21.9 1.3 %collective-permute-start.5 = (f32[288,128]{1,0:T(8,128)S(1)}, f32[288,128]{1,0:T(8,128)S(1)}, u32[]{:S(2)}, u32[]{:S(2)}) collective-permute-start(f32[288,128]{1,0:T(8,128)S(1)} %get-tuple-element.46), channel_id=1, source_target_pairs={{0,8},{8,0},{16,24},{24,16},{1,9},{9,1},{17,25},{25,17},{2,10},{10... | collective-permute-start | bytes 442376 | tf_op jit(solution)/shard_map/ppermute | solution.py:695
  23.2 0.8 %collective-permute-start.6 = (f32[288,128]{1,0:T(8,128)S(1)}, f32[288,128]{1,0:T(8,128)S(1)}, u32[]{:S(2)}, u32[]{:S(2)}) collective-permute-start(f32[288,128]{1,0:T(8,128)S(1)} %get-tuple-element.47), channel_id=1, source_target_pairs={{0,16},{8,24},{16,0},{24,8},{1,17},{9,25},{17,1},{25,9},{2,18},{10... | collective-permute-start | bytes 442376 | tf_op jit(solution)/shard_map/ppermute | solution.py:695
  24.0 1.4 %collective-permute-start.7 = (f32[288,128]{1,0:T(8,128)S(1)}, f32[288,128]{1,0:T(8,128)S(1)}, u32[]{:S(2)}, u32[]{:S(2)}) collective-permute-start(f32[288,128]{1,0:T(8,128)S(1)} %get-tuple-element.48), channel_id=1, source_target_pairs={{0,24},{8,16},{16,8},{24,0},{1,25},{9,17},{17,9},{25,1},{2,26},{10... | collective-permute-start | bytes 442376 | tf_op jit(solution)/shard_map/ppermute | solution.py:695
  25.4 1.1 %shard_map.91.phase_ref = f32[7,2,48,128]{3,2,1,0:T(8,128)S(1)} custom-call(s32[48]{0:T(128)} %octants_hbm.3), custom_call_target="tpu_custom_call" | custom-call | flops 20000000 | bytes 1000000 | tf_op jit(solution)/shard_map/pallas_call | solution.py:847
  26.5 0.0 copy-start.1
  26.5 0.0 copy-start.5
  26.5 0.5 %shard_map.98.rest_0_ = f32[288,128]{1,0:T(8,128)S(1)} custom-call(f32[30720,128]{1,0:T(8,128)S(1)} %get-tuple-element.36.placed_ref, f32[1280,128]{1,0:T(8,128)S(1)} %get-tuple-element.40.real_sum, f32[1280,128]{1,0:T(8,128)S(1)} %get-tuple-element.41.imag_sum, f32[640,128]{1,0:T(8,128)S(1)} %get-tuple-element.44.rest_0_, ...), custom_call_target="tpu_custom_call" | custom-call | flops 10000000 | bytes 2000000 | tf_op jit(solution)/shard_map/pallas_call | solution.py:833
  27.1 0.8 %collective-permute-done.5.rest_1_ = f32[288,128]{1,0:T(8,128)S(1)} collective-permute-done((f32[288,128]{1,0:T(8,128)S(1)}, f32[288,128]{1,0:T(8,128)S(1)}, u32[]{:S(2)}, u32[]{:S(2)}) %collective-permute-start.5) | collective-permute-done | bytes 147488 | tf_op jit(solution)/shard_map/ppermute | solution.py:695
  27.8 3.6 %collective-permute-done.6.rest_2_ = f32[288,128]{1,0:T(8,128)S(1)} collective-permute-done((f32[288,128]{1,0:T(8,128)S(1)}, f32[288,128]{1,0:T(8,128)S(1)}, u32[]{:S(2)}, u32[]{:S(2)}) %collective-permute-start.6) | collective-permute-done | bytes 147488 | tf_op jit(solution)/shard_map/ppermute | solution.py:695
  31.5 0.1 shard_map.100
  31.6 1.1 %collective-permute-start.8 = (f32[64,128]{1,0:T(8,128)S(1)}, f32[64,128]{1,0:T(8,128)S(1)}, u32[]{:S(2)}, u32[]{:S(2)}) collective-permute-start(f32[64,128]{1,0:T(8,128)S(1)} %get-tuple-element.52), channel_id=1, source_target_pairs={{0,7},{1,2},{2,1},{3,4},{4,3},{5,6},{6,5},{7,0},{8,15},{9,10},{10,... | collective-permute-start | bytes 98312 | tf_op jit(solution)/shard_map/ppermute | solution.py:690
  32.7 2.9 %shard_map.101 = (f32[96,32,128]{2,1,0:T(8,128)}, f32[2,96,8,128]{3,2,1,0:T(8,128)S(1)}) custom-call(s32[1,48]{1,0:T(1,128)S(1)} %copy-done.6, s32[1,48]{1,0:T(1,128)S(1)} %bitcast.12, f32[1152,128]{1,0:T(8,128)S(1)} %get-tuple-element.49.flat_ref, f32[8,2,9,8,128]{4,3,2,1,0:T(8,128)S(1)} %get-tuple-element.50.phase_ref, bf16[2,256,256]{2,1,0:T(8,128)(2,1)S(1)} %copy-done.1), custom_call_target="tpu_custom_call" | custom-call | flops 4000000000 | bytes 12000000 | tf_op jit(solution)/shard_map/pallas_call | solution.py:868
  35.6 1.2 %collective-permute-done.8.far_ref = f32[64,128]{1,0:T(8,128)S(1)} collective-permute-done((f32[64,128]{1,0:T(8,128)S(1)}, f32[64,128]{1,0:T(8,128)S(1)}, u32[]{:S(2)}, u32[]{:S(2)}) %collective-permute-start.8) | collective-permute-done | bytes 32800 | tf_op jit(solution)/shard_map/ppermute | solution.py:690
  36.8 0.0 collective-permute-done.9.near_ref
  36.8 1.5 %shard_map.102 = f32[96,32,128]{2,1,0:T(8,128)} custom-call(s32[1,48]{1,0:T(1,128)S(1)} %copy-done.6, f32[7,2,48,128]{3,2,1,0:T(8,128)S(1)} %shard_map.91.phase_ref, bf16[2,256,256]{2,1,0:T(8,128)(2,1)S(1)} %copy-done.1, f32[2,96,8,128]{3,2,1,0:T(8,128)S(1)} %get-tuple-element.51.edge_ref, ...), custom_call_target="tpu_custom_call", output_to_operand_aliasing={{}: (6, {})} | custom-call | flops 1000000 | bytes 1000000 | tf_op jit(solution)/shard_map/pallas_call | solution.py:887
  (16 shorter events, 0.0 us)
Async XLA Ops:
  0.9 8.0 %collective-permute-start = (f32[2,96,128]{2,1,0:T(8,128)S(1)}, f32[2,96,128]{2,1,0:T(8,128)S(1)}, u32[]{:S(2)}, u32[]{:S(2)}) collective-permute-start(f32[2,96,128]{2,1,0:T(8,128)S(1)} %get-tuple-element.31), channel_id=1, source_target_pairs={{0,7},{1,2},{2,1},{3,4},{4,3},{5,6},{6,5},{7,0},{8,15},{9,10},{10,... | collective-permute-start | bytes 294920 | tf_op jit(solution)/shard_map/ppermute | solution.py:690
  5.5 3.4 %collective-permute-start.1 = (f32[2,96,128]{2,1,0:T(8,128)S(1)}, f32[2,96,128]{2,1,0:T(8,128)S(1)}, u32[]{:S(2)}, u32[]{:S(2)}) collective-permute-start(f32[2,96,128]{2,1,0:T(8,128)S(1)} %get-tuple-element.32), channel_id=1, source_target_pairs={{0,1},{1,0},{2,3},{3,2},{4,5},{5,4},{6,7},{7,6},{8,9},{9,8},{10,11... | collective-permute-start | bytes 294920 | tf_op jit(solution)/shard_map/ppermute | solution.py:690
  5.5 3.4 %copy-start = (bf16[2,384,256]{2,1,0:T(8,128)(2,1)S(1)}, bf16[2,384,256]{2,1,0:T(8,128)(2,1)}, u32[]{:S(2)}) copy-start(bf16[2,384,256]{2,1,0:T(8,128)(2,1)} %constant.4.clone.spread_hbm.spread_ref) | copy-start | bytes 1179652
  5.5 3.4 %copy-start.4 = (s32[48]{0:T(128)S(1)}, s32[48]{0:T(128)}, u32[]{:S(2)}) copy-start(s32[48]{0:T(128)} %octants_hbm.3) | copy-start | bytes 580
  5.5 3.4 %copy-start.6 = (s32[1,48]{1,0:T(1,128)S(1)}, s32[1,48]{1,0:T(1,128)}, u32[]{:S(2)}) copy-start(s32[1,48]{1,0:T(1,128)} %parents_ref.5) | copy-start | bytes 580
  5.5 7.6 %copy-start.2 = (s32[32,31]{1,0:T(8,128)S(1)}, s32[32,31]{1,0:T(8,128)}, u32[]{:S(2)}) copy-start(s32[32,31]{1,0:T(8,128)} %source_ref.1) | copy-start | bytes 11908
  5.5 7.5 %copy-start.3 = (s32[32,31]{1,0:T(8,128)S(1)}, s32[32,31]{1,0:T(8,128)}, u32[]{:S(2)}) copy-start(s32[32,31]{1,0:T(8,128)} %offset_ref.1) | copy-start | bytes 11908
  5.6 7.5 %copy-start.7 = (s32[32]{0:T(128)S(1)}, s32[32]{0:T(128)}, u32[]{:S(2)}) copy-start(s32[32]{0:T(128)} %param.15) | copy-start | bytes 388
  9.5 8.5 %collective-permute-start.2 = (f32[288,128]{1,0:T(8,128)S(1)}, f32[288,128]{1,0:T(8,128)S(1)}, u32[]{:S(2)}, u32[]{:S(2)}) collective-permute-start(f32[288,128]{1,0:T(8,128)S(1)} %get-tuple-element.37), channel_id=1, source_target_pairs={{0,8},{8,0},{16,24},{24,16},{1,9},{9,1},{17,25},{25,17},{2,10},{10... | collective-permute-start | bytes 442376 | tf_op jit(solution)/shard_map/ppermute | solution.py:695
  11.1 9.1 %collective-permute-start.3 = (f32[288,128]{1,0:T(8,128)S(1)}, f32[288,128]{1,0:T(8,128)S(1)}, u32[]{:S(2)}, u32[]{:S(2)}) collective-permute-start(f32[288,128]{1,0:T(8,128)S(1)} %get-tuple-element.42), channel_id=1, source_target_pairs={{0,16},{8,24},{16,0},{24,8},{1,17},{9,25},{17,1},{25,9},{2,18},{10... | collective-permute-start | bytes 442376 | tf_op jit(solution)/shard_map/ppermute | solution.py:695
  12.7 7.5 %collective-permute-start.4 = (f32[288,128]{1,0:T(8,128)S(1)}, f32[288,128]{1,0:T(8,128)S(1)}, u32[]{:S(2)}, u32[]{:S(2)}) collective-permute-start(f32[288,128]{1,0:T(8,128)S(1)} %get-tuple-element.43), channel_id=1, source_target_pairs={{0,24},{8,16},{16,8},{24,0},{1,25},{9,17},{17,9},{25,1},{2,26},{10... | collective-permute-start | bytes 442376 | tf_op jit(solution)/shard_map/ppermute | solution.py:695
  21.9 6.0 %collective-permute-start.5 = (f32[288,128]{1,0:T(8,128)S(1)}, f32[288,128]{1,0:T(8,128)S(1)}, u32[]{:S(2)}, u32[]{:S(2)}) collective-permute-start(f32[288,128]{1,0:T(8,128)S(1)} %get-tuple-element.46), channel_id=1, source_target_pairs={{0,8},{8,0},{16,24},{24,16},{1,9},{9,1},{17,25},{25,17},{2,10},{10... | collective-permute-start | bytes 442376 | tf_op jit(solution)/shard_map/ppermute | solution.py:695
  23.2 8.2 %collective-permute-start.6 = (f32[288,128]{1,0:T(8,128)S(1)}, f32[288,128]{1,0:T(8,128)S(1)}, u32[]{:S(2)}, u32[]{:S(2)}) collective-permute-start(f32[288,128]{1,0:T(8,128)S(1)} %get-tuple-element.47), channel_id=1, source_target_pairs={{0,16},{8,24},{16,0},{24,8},{1,17},{9,25},{17,1},{25,9},{2,18},{10... | collective-permute-start | bytes 442376 | tf_op jit(solution)/shard_map/ppermute | solution.py:695
  24.0 7.4 %collective-permute-start.7 = (f32[288,128]{1,0:T(8,128)S(1)}, f32[288,128]{1,0:T(8,128)S(1)}, u32[]{:S(2)}, u32[]{:S(2)}) collective-permute-start(f32[288,128]{1,0:T(8,128)S(1)} %get-tuple-element.48), channel_id=1, source_target_pairs={{0,24},{8,16},{16,8},{24,0},{1,25},{9,17},{17,9},{25,1},{2,26},{10... | collective-permute-start | bytes 442376 | tf_op jit(solution)/shard_map/ppermute | solution.py:695
  26.5 6.2 %copy-start.1 = (bf16[2,256,256]{2,1,0:T(8,128)(2,1)S(1)}, bf16[2,256,256]{2,1,0:T(8,128)(2,1)}, u32[]{:S(2)}) copy-start(bf16[2,256,256]{2,1,0:T(8,128)(2,1)} %constant.5.clone.gather_ref) | copy-start | bytes 786436
  26.5 6.2 %copy-start.5 = (s32[48]{0:T(128)S(1)}, s32[48]{0:T(128)}, u32[]{:S(2)}) copy-start(s32[48]{0:T(128)} %octants_hbm.3) | copy-start | bytes 580
  31.6 5.2 %collective-permute-start.8 = (f32[64,128]{1,0:T(8,128)S(1)}, f32[64,128]{1,0:T(8,128)S(1)}, u32[]{:S(2)}, u32[]{:S(2)}) collective-permute-start(f32[64,128]{1,0:T(8,128)S(1)} %get-tuple-element.52), channel_id=1, source_target_pairs={{0,7},{1,2},{2,1},{3,4},{4,3},{5,6},{6,5},{7,0},{8,15},{9,10},{10,... | collective-permute-start | bytes 98312 | tf_op jit(solution)/shard_map/ppermute | solution.py:690
  32.7 4.1 %collective-permute-start.9 = (f32[64,128]{1,0:T(8,128)S(1)}, f32[64,128]{1,0:T(8,128)S(1)}, u32[]{:S(2)}, u32[]{:S(2)}) collective-permute-start(f32[64,128]{1,0:T(8,128)S(1)} %get-tuple-element.53), channel_id=1, source_target_pairs={{0,1},{1,0},{2,3},{3,2},{4,5},{5,4},{6,7},{7,6},{8,9},{9,8},{10,11... | collective-permute-start | bytes 98312 | tf_op jit(solution)/shard_map/ppermute | solution.py:690

commit v12 on v11

--- a/solution.py
+++ b/solution.py
@@ -20,7 +20,6 @@
 PERIOD_C = 4
 ROWS_PER_PERIOD = PERIOD_P * NTHETA_P // LANES
 GROUP = 8
-TILE = 8
 TOGETHER = 2
 BLOCK = 2 * GROUP
 
@@ -155,12 +154,6 @@
     parity = lax.rem(lax.axis_index("dir"), 2)
     pl.when(parity == 0)(even)
     pl.when(parity == 1)(odd)
-
-
-def from_sides(far_ref, near_ref):
-    is_even = lax.rem(lax.axis_index("dir"), 2) == 0
-    far, near = far_ref[...], near_ref[...]
-    return jnp.where(is_even, far, near), jnp.where(is_even, near, far)
 
 
 def rows_kernel(x_ref, far_ref, near_ref, sems):
@@ -567,30 +560,23 @@
     lax.fori_loop(0, octants_ref.shape[0] // GROUP, some_children, 0)
 
 
-def edge_contributions(parents, phase_ref, gather_ref, above, below):
-    children = parents.shape[1]
-    own = below.shape[0] // 8
-    rows = [above[2 * e * own : 2 * (e + 1) * own] for e in range(4)] + [below[2 * e * own : 2 * (e + 1) * own] for e in range(3)]
-    edges = jnp.concatenate([r[part * own : (part + 1) * own] for r in rows for part in range(2)], axis=1)
-    per_child = dot2(one_hot(parents, own).T, edges)
+def returned_rows(parents, phase_ref, edges, rows_ref):
+    own = rows_ref.shape[0] // 8
+    columns = [rows_ref[row * own : (row + 1) * own, :] for row in range(2 * len(edges))]
+    per_child = dot2(one_hot(parents, own).T, jnp.concatenate(columns, axis=1))
     returned = []
-    for e in range(len(rows)):
-        real = per_child[:, 2 * e * LANES : (2 * e + 1) * LANES]
-        imaginary = per_child[:, (2 * e + 1) * LANES : (2 * e + 2) * LANES]
+    for i, e in enumerate(edges):
+        real = per_child[:, 2 * i * LANES : (2 * i + 1) * LANES]
+        imaginary = per_child[:, (2 * i + 1) * LANES : (2 * i + 2) * LANES]
         cosine, sine = phase_ref[e, 0], phase_ref[e, 1]
         returned.append(
             jnp.concatenate([real * cosine + imaginary * sine, imaginary * cosine - real * sine], axis=0)
         )
-    join = functools.partial(jnp.concatenate, axis=1)
-    even = jnp.concatenate([join([returned[2], returned[3]]), join([returned[4], returned[5]])], axis=0)
-    odd = jnp.concatenate([join([returned[0], returned[1]]), join([returned[5], returned[6]])], axis=0)
-    even = gather_dot(*split(even), gather_ref, 0)
-    odd = gather_dot(*split(odd), gather_ref, 1)
-    a, b = TAPS_A, TAPS_B
-    pairs = 2 * children
-    last = a[0] * odd[:pairs] + b[0] * even[:pairs]
-    first = [a[3 + i] * even[pairs:] + b[3 + i] * odd[pairs:] for i in range(2)]
-    return first, last
+    return returned
+
+
+def side_by_side(left, right):
+    return split(jnp.concatenate([left, right], axis=1))
 
 
 def disaggregate_kernel(
@@ -604,9 +590,7 @@
         for w in range(ROWS_PER_PERIOD):
             first = gp * ROWS_PER_PERIOD * periods + w
             incoming_ref[gp, w] = flat_ref[pl.ds(first, periods, stride=ROWS_PER_PERIOD), :]
-    azimuth_in = periods * PERIOD_C
     sublane = lax.broadcasted_iota(jnp.int32, (periods, LANES), 0)
-    inner = pl.ds(TILE, azimuth_in - 2 * TILE)
 
     def shift(block):
         for k in range(BLOCK):
@@ -642,12 +626,12 @@
             kp = block * (2 * BLOCK) + j
             for u in range(PERIOD_C):
                 whole_out[kp, pl.ds(u, periods, stride=PERIOD_C), :] = rows[u]
-            edge_ref[0, kp] = whole_out[kp, :TILE, :]
-            edge_ref[1, kp] = whole_out[kp, azimuth_in - TILE :, :]
+            for i, (u, m) in enumerate(((0, 0), (1, 0), (PERIOD_C - 1, periods - 1))):
+                edge_ref[i, pl.ds(kp, 1), :] = rows[u][m : m + 1]
 
     def written(block):
         some = pl.ds(block * (2 * BLOCK), 2 * BLOCK)
-        return pltpu.make_async_copy(whole_out.at[some, inner, :], out_ref.at[some, inner, :], sems.at[block])
+        return pltpu.make_async_copy(whole_out.at[some], out_ref.at[some], sems.at[block])
 
     def one_block(block, carry):
         shift(block)
@@ -662,27 +646,36 @@
         written(block).wait()
 
 
-def finish_kernel(parents_ref, phase_ref, gather_ref, edge_ref, far_ref, near_ref, part_ref, out_ref, tiles, sems):
+def finish_kernel(is_far, parents_ref, phase_ref, gather_ref, edge_ref, side_ref, part_ref, out_ref, sums, sems):
     pairs, azimuth_in, _ = out_ref.shape
-    tiles[...] = edge_ref[...]
-    flat = tiles.reshape(2 * pairs * TILE, LANES)
-    below, above = from_sides(far_ref, near_ref)
-    heads, tail = edge_contributions(parents_ref[...], phase_ref, gather_ref, above, below)
-    ends = ((0, 0, heads[0]), (0, 1, heads[1]), (1, TILE - 1, tail))
-    copies = []
-    for i, start in enumerate((0, azimuth_in - TILE)):
-        for end, row, values in ends:
-            if end == i:
-                for part in range(2):
-                    for k in range(0, pairs // 2, 8):
-                        source = slice(part * (pairs // 2) + k, part * (pairs // 2) + k + 8)
-                        rows = pl.ds((i * pairs + 2 * k + part) * TILE + row, 8, stride=2 * TILE)
-                        flat[rows, :] = flat[rows, :] + values[source]
-        copy = pltpu.make_async_copy(tiles.at[i], out_ref.at[:, pl.ds(start, TILE), :], sems.at[i])
-        copy.start()
-        copies.append(copy)
-    for copy in copies:
-        copy.wait()
+    children = pairs // 2
+    a, b = TAPS_A, TAPS_B
+
+    def write(additions):
+        copies = []
+        for i, row, values in additions:
+            for part in range(2):
+                place = pl.ds(part, children, stride=2)
+                sums[i, place, :] = edge_ref[i, place, :] + values[part * children : (part + 1) * children]
+            copy = pltpu.make_async_copy(sums.at[i], out_ref.at[:, row, :], sems.at[i])
+            copy.start()
+            copies.append(copy)
+        for copy in copies:
+            copy.wait()
+
+    def from_below():
+        returned = returned_rows(parents_ref[...], phase_ref, (4, 5, 6), side_ref)
+        even = gather_dot(*side_by_side(returned[0], returned[1]), gather_ref, 0)
+        odd = gather_dot(*side_by_side(returned[1], returned[2]), gather_ref, 1)
+        write([(i, i, a[3 + i] * even + b[3 + i] * odd) for i in range(2)])
+
+    def from_above():
+        returned = returned_rows(parents_ref[...], phase_ref, (0, 1, 2, 3), side_ref)
+        even = gather_dot(*side_by_side(returned[2], returned[3]), gather_ref, 0)
+        odd = gather_dot(*side_by_side(returned[0], returned[1]), gather_ref, 1)
+        write([(2, azimuth_in - 1, a[0] * odd + b[0] * even)])
+
+    by_parity(*((from_below, from_above) if is_far else (from_above, from_below)))
 
 
 def swapped(values, axis, first):
@@ -865,9 +858,9 @@
     from_far = swapped(to_far, "dir", 1)
     from_near = swapped(to_near, "dir", 0)
 
-    inner, edge_tiles = local_call(
+    partial_out, edge_sums = local_call(
         disaggregate_kernel,
-        [array(pairs, azimuth_in, polar_in), array(2, pairs, TILE, polar_in)],
+        [array(pairs, azimuth_in, polar_in), array(3, pairs, polar_in)],
         [VMEM] * 5,
         [
             pltpu.SMEM((children,), jnp.int32),
@@ -884,15 +877,17 @@
         out_specs=[HBM, VMEM],
     )(child_parent, child_octant.reshape(1, children), incoming, phases, gather)
 
-    out = local_call(
-        finish_kernel,
-        array(pairs, azimuth_in, polar_in),
-        [VMEM] * 6 + [HBM],
-        [buffer(2, pairs, TILE, polar_in), pltpu.SemaphoreType.DMA((2,))],
-        8,
-        out_specs=HBM,
-        aliases={6: 0},
-    )(child_parent, neighbour_phases, gather, edge_tiles, from_far, from_near, in_hbm(inner))
+    out = partial_out
+    for is_far, side in ((False, from_near), (True, from_far)):
+        out = local_call(
+            functools.partial(finish_kernel, is_far),
+            array(pairs, azimuth_in, polar_in),
+            [VMEM] * 5 + [HBM],
+            [buffer(3, pairs, polar_in), pltpu.SemaphoreType.DMA((3,))],
+            8,
+            out_specs=HBM,
+            aliases={5: 0},
+        )(child_parent, neighbour_phases, gather, edge_sums, side, in_hbm(out))
     return out.reshape(child_patterns.shape)
 
 

time: 38.5 us -> 39.2 us (1.018)
  waiting for transfers between devices: 6.62 us -> 5.42 us
  starting transfers between devices: 12.8 us -> 14 us
  Pallas kernels: 18.6 us -> 19.3 us
    ppermute x4, waiting for transfers between devices: 1.2 us -> 0.01 us  [swapped(): lax.ppermute(values, axis, [(i, ((i - first ^ 1) + first) % size) for i i...]
    ppermute x4, starting transfers between devices: 5.7 us -> 6.88 us  [swapped(): lax.ppermute(values, axis, [(i, ((i - first ^ 1) + first) % size) for i i...]
    pallas_call x1 -> x2, Pallas kernels: 1.46 us -> 2.21 us  [on_device_exchange(): local_call(functools.partial(finish_kernel, is_far), array(pairs, azimuth...]
  transfers between devices with their start and end apart: 10 -> 10, of which waited for: 4 -> 3; matrix products, arithmetic and copies ran while one was open for 0% -> 0% of each run, Pallas kernels for 36% -> 38%
where the time goes in v12:
time: 39.2 us; the launch traced here: 38.9 us
  Pallas kernels  19.3 us (49%)
  starting transfers between devices  14 us (36%)
  waiting for transfers between devices  5.42 us (14%)
    ppermute x6, starting transfers between devices, exchanged(): return lax.ppermute(values, axis, [(i, i ^ mask) for i in range(size)])  7.11 us
    ppermute x4, starting transfers between devices, swapped(): lax.ppermute(values, axis, [(i, ((i - first ^ 1) + first) % size) for i i...  6.88 us
    ppermute x6, waiting for transfers between devices, exchanged(): return lax.ppermute(values, axis, [(i, i ^ mask) for i in range(size)])  5.41 us
    pallas_call x1, Pallas kernels, on_device_exchange(): local_call(functools.partial(widen_kernel, peers, others), [array(parent_...  4.97 us
    pallas_call x1, Pallas kernels, on_device_exchange(): local_call(functools.partial(main_kernel, peers), [array(8, 2, ROWS_PER_P...  3.34 us
    pallas_call x1, Pallas kernels, on_device_exchange(): local_call(disaggregate_kernel, [array(pairs, azimuth_in, polar_in), arra...  2.82 us
    pallas_call x2, Pallas kernels, on_device_exchange(): local_call(functools.partial(finish_kernel, is_far), array(pairs, azimuth...  2.21 us
    pallas_call x3, Pallas kernels, on_device_exchange(): local_call(functools.partial(translate_kernel, frame, others, tuple(late)...  2.18 us
  transfers between devices with their start and end apart: 10, of which 3 were waited for; matrix products, arithmetic and copies ran while one was open for 0% of the time, Pallas kernels for 38%

profile of v12, /device:TPU:0, one launch (start us, length us, event | category | flops | bytes accessed | tf_op | source)
XLA Modules:
  0.0 38.9 jit_solution(16281090181421104832)
XLA Ops:
  0.0 0.9 %shard_map.93 = (f32[2,96,128]{2,1,0:T(8,128)S(1)}, f32[2,96,128]{2,1,0:T(8,128)S(1)}) custom-call(f32[96,32,128]{2,1,0:T(8,128)} %bitcast.17), custom_call_target="tpu_custom_call" | custom-call | flops 1000000 | bytes 1000000 | tf_op jit(solution)/shard_map/pallas_call | solution.py:731
  0.9 4.6 %collective-permute-start = (f32[2,96,128]{2,1,0:T(8,128)S(1)}, f32[2,96,128]{2,1,0:T(8,128)S(1)}, u32[]{:S(2)}, u32[]{:S(2)}) collective-permute-start(f32[2,96,128]{2,1,0:T(8,128)S(1)} %get-tuple-element.31), channel_id=1, source_target_pairs={{0,7},{1,2},{2,1},{3,4},{4,3},{5,6},{6,5},{7,0},{8,15},{9,10},{10,... | collective-permute-start | bytes 294920 | tf_op jit(solution)/shard_map/ppermute | solution.py:683
  5.5 0.0 copy-start.2
  5.5 0.0 copy-start.3
  5.6 0.0 copy-start.7
  5.6 3.3 %shard_map.92 = (f32[8,2,9,8,128]{4,3,2,1,0:T(8,128)S(1)}, f32[7,2,8,128]{3,2,1,0:T(8,128)S(1)}, f32[1152,128]{1,0:T(8,128)S(1)}, bf16[158,40,128]{2,1,0:T(8,128)(2,1)S(1)}) custom-call(s32[48]{0:T(128)} %bitcast.11, s32[48]{0:T(128)} %octants_hbm.3, f32[3072,128]{1,0:T(8,128)} %bitcast.18, bf16[316,144,128]{2,1,0:T(8,128)(2,1)} %bitcast.15, ...), custom_call_target="tpu_custom_call" | custom-call | flops 4000000000 | bytes 12000000 | tf_op jit(solution)/shard_map/pallas_call | solution.py:744
  8.9 0.0 collective-permute-done.far_ref
  9.0 0.5 %shard_map.94 = (f32[288,128]{1,0:T(8,128)S(1)}, f32[288,128]{1,0:T(8,128)S(1)}, f32[288,128]{1,0:T(8,128)S(1)}, f32[288,128]{1,0:T(8,128)S(1)}) custom-call(s32[1,48]{1,0:T(1,128)S(1)} %copy-done.4, s32[1,48]{1,0:T(1,128)S(1)} %bitcast.12, f32[2,96,128]{2,1,0:T(8,128)S(1)} %collective-permute-done.far_ref, ...), custom_call_target="tpu_custom_call" | custom-call | flops 1000000 | bytes 1000000 | tf_op jit(solution)/shard_map/pallas_call | solution.py:779
  9.5 1.6 %collective-permute-start.2 = (f32[288,128]{1,0:T(8,128)S(1)}, f32[288,128]{1,0:T(8,128)S(1)}, u32[]{:S(2)}, u32[]{:S(2)}) collective-permute-start(f32[288,128]{1,0:T(8,128)S(1)} %get-tuple-element.37), channel_id=1, source_target_pairs={{0,8},{8,0},{16,24},{24,16},{1,9},{9,1},{17,25},{25,17},{2,10},{10... | collective-permute-start | bytes 442376 | tf_op jit(solution)/shard_map/ppermute | solution.py:688
  11.1 1.5 %collective-permute-start.3 = (f32[288,128]{1,0:T(8,128)S(1)}, f32[288,128]{1,0:T(8,128)S(1)}, u32[]{:S(2)}, u32[]{:S(2)}) collective-permute-start(f32[288,128]{1,0:T(8,128)S(1)} %get-tuple-element.42), channel_id=1, source_target_pairs={{0,16},{8,24},{16,0},{24,8},{1,17},{9,25},{17,1},{25,9},{2,18},{10... | collective-permute-start | bytes 442376 | tf_op jit(solution)/shard_map/ppermute | solution.py:688
  12.7 0.4 %collective-permute-start.4 = (f32[288,128]{1,0:T(8,128)S(1)}, f32[288,128]{1,0:T(8,128)S(1)}, u32[]{:S(2)}, u32[]{:S(2)}) collective-permute-start(f32[288,128]{1,0:T(8,128)S(1)} %get-tuple-element.43), channel_id=1, source_target_pairs={{0,24},{8,16},{16,8},{24,0},{1,25},{9,17},{17,9},{25,1},{2,26},{10... | collective-permute-start | bytes 442376 | tf_op jit(solution)/shard_map/ppermute | solution.py:688
  13.1 5.0 %shard_map.95 = (f32[30720,128]{1,0:T(8,128)S(1)}, f32[1280,128]{1,0:T(8,128)S(1)}, f32[1280,128]{1,0:T(8,128)S(1)}) custom-call(s32[32,31]{1,0:T(8,128)S(1)} %copy-done.2, s32[32,31]{1,0:T(8,128)S(1)} %copy-done.3, s32[1,32]{1,0:T(1,128)S(1)} %bitcast.14, bf16[158,40,128]{2,1,0:T(8,128)(2,1)S(1)} %get-tuple-element.30.head_ref, ...), custom_call_target="tpu_custom_call" | custom-call | flops 90000000 | bytes 12000000 | tf_op jit(solution)/shard_map/pallas_call | solution.py:793
  18.1 1.1 %shard_map.96 = (f32[1280,128]{1,0:T(8,128)S(1)}, f32[1280,128]{1,0:T(8,128)S(1)}) custom-call(f32[30720,128]{1,0:T(8,128)S(1)} %get-tuple-element.36.placed_ref, f32[288,128]{1,0:T(8,128)S(1)} %collective-permute-done.2.rest_0_, f32[1280,128]{1,0:T(8,128)S(1)} %get-tuple-element.38.rest_1_, f32[1280,128]{1,0:T(8,128)S(1)} %get-tuple-element.39.rest_2_), custom_call_target="tpu_custom_call" | custom-call | flops 60000000 | bytes 12000000 | tf_op jit(solution)/shard_map/pallas_call | solution.py:812
  19.2 1.0 %collective-permute-done.3.rest_0_ = f32[288,128]{1,0:T(8,128)S(1)} collective-permute-done((f32[288,128]{1,0:T(8,128)S(1)}, f32[288,128]{1,0:T(8,128)S(1)}, u32[]{:S(2)}, u32[]{:S(2)}) %collective-permute-start.3) | collective-permute-done | bytes 147488 | tf_op jit(solution)/shard_map/ppermute | solution.py:688
  20.2 0.0 collective-permute-done.4.rest_1_
  20.2 0.6 %shard_map.97 = (f32[640,128]{1,0:T(8,128)S(1)}, f32[640,128]{1,0:T(8,128)S(1)}, f32[288,128]{1,0:T(8,128)S(1)}) custom-call(f32[30720,128]{1,0:T(8,128)S(1)} %get-tuple-element.36.placed_ref, f32[1280,128]{1,0:T(8,128)S(1)} %get-tuple-element.40.real_sum, f32[1280,128]{1,0:T(8,128)S(1)} %get-tuple-element.41.imag_sum, ...), custom_call_target="tpu_custom_call" | custom-call | flops 10000000 | bytes 2000000 | tf_op jit(solution)/shard_map/pallas_call | solution.py:826
  20.8 1.1 %shard_map.99 = (f32[288,128]{1,0:T(8,128)S(1)}, f32[288,128]{1,0:T(8,128)S(1)}) custom-call(f32[30720,128]{1,0:T(8,128)S(1)} %get-tuple-element.36.placed_ref, f32[1280,128]{1,0:T(8,128)S(1)} %get-tuple-element.40.real_sum, f32[1280,128]{1,0:T(8,128)S(1)} %get-tuple-element.41.imag_sum, f32[640,128]{1,0:T(8,128)S(1)} %get-tuple-element.44.rest_0_, ...), custom_call_target="tpu_custom_call" | custom-call | flops 20000000 | bytes 4000000 | tf_op jit(solution)/shard_map/pallas_call | solution.py:826
  21.9 1.3 %collective-permute-start.5 = (f32[288,128]{1,0:T(8,128)S(1)}, f32[288,128]{1,0:T(8,128)S(1)}, u32[]{:S(2)}, u32[]{:S(2)}) collective-permute-start(f32[288,128]{1,0:T(8,128)S(1)} %get-tuple-element.46), channel_id=1, source_target_pairs={{0,8},{8,0},{16,24},{24,16},{1,9},{9,1},{17,25},{25,17},{2,10},{10... | collective-permute-start | bytes 442376 | tf_op jit(solution)/shard_map/ppermute | solution.py:688
  23.2 0.8 %collective-permute-start.6 = (f32[288,128]{1,0:T(8,128)S(1)}, f32[288,128]{1,0:T(8,128)S(1)}, u32[]{:S(2)}, u32[]{:S(2)}) collective-permute-start(f32[288,128]{1,0:T(8,128)S(1)} %get-tuple-element.47), channel_id=1, source_target_pairs={{0,16},{8,24},{16,0},{24,8},{1,17},{9,25},{17,1},{25,9},{2,18},{10... | collective-permute-start | bytes 442376 | tf_op jit(solution)/shard_map/ppermute | solution.py:688
  24.0 1.4 %collective-permute-start.7 = (f32[288,128]{1,0:T(8,128)S(1)}, f32[288,128]{1,0:T(8,128)S(1)}, u32[]{:S(2)}, u32[]{:S(2)}) collective-permute-start(f32[288,128]{1,0:T(8,128)S(1)} %get-tuple-element.48), channel_id=1, source_target_pairs={{0,24},{8,16},{16,8},{24,0},{1,25},{9,17},{17,9},{25,1},{2,26},{10... | collective-permute-start | bytes 442376 | tf_op jit(solution)/shard_map/ppermute | solution.py:688
  25.4 1.1 %shard_map.91.phase_ref = f32[7,2,48,128]{3,2,1,0:T(8,128)S(1)} custom-call(s32[48]{0:T(128)} %octants_hbm.3), custom_call_target="tpu_custom_call" | custom-call | flops 20000000 | bytes 1000000 | tf_op jit(solution)/shard_map/pallas_call | solution.py:840
  26.5 0.0 copy-start
  26.5 0.0 copy-start.6
  26.5 0.5 %shard_map.98.rest_0_ = f32[288,128]{1,0:T(8,128)S(1)} custom-call(f32[30720,128]{1,0:T(8,128)S(1)} %get-tuple-element.36.placed_ref, f32[1280,128]{1,0:T(8,128)S(1)} %get-tuple-element.40.real_sum, f32[1280,128]{1,0:T(8,128)S(1)} %get-tuple-element.41.imag_sum, f32[640,128]{1,0:T(8,128)S(1)} %get-tuple-element.44.rest_0_, ...), custom_call_target="tpu_custom_call" | custom-call | flops 10000000 | bytes 2000000 | tf_op jit(solution)/shard_map/pallas_call | solution.py:826
  27.1 0.8 %collective-permute-done.5.rest_1_ = f32[288,128]{1,0:T(8,128)S(1)} collective-permute-done((f32[288,128]{1,0:T(8,128)S(1)}, f32[288,128]{1,0:T(8,128)S(1)}, u32[]{:S(2)}, u32[]{:S(2)}) %collective-permute-start.5) | collective-permute-done | bytes 147488 | tf_op jit(solution)/shard_map/ppermute | solution.py:688
  27.8 3.6 %collective-permute-done.6.rest_2_ = f32[288,128]{1,0:T(8,128)S(1)} collective-permute-done((f32[288,128]{1,0:T(8,128)S(1)}, f32[288,128]{1,0:T(8,128)S(1)}, u32[]{:S(2)}, u32[]{:S(2)}) %collective-permute-start.6) | collective-permute-done | bytes 147488 | tf_op jit(solution)/shard_map/ppermute | solution.py:688
  31.4 0.1 shard_map.100
  31.5 0.1 collective-permute-start.9
  31.6 2.2 %collective-permute-start.8 = (f32[64,128]{1,0:T(8,128)S(1)}, f32[64,128]{1,0:T(8,128)S(1)}, u32[]{:S(2)}, u32[]{:S(2)}) collective-permute-start(f32[64,128]{1,0:T(8,128)S(1)} %get-tuple-element.52), channel_id=1, source_target_pairs={{0,7},{1,2},{2,1},{3,4},{4,3},{5,6},{6,5},{7,0},{8,15},{9,10},{10,... | collective-permute-start | bytes 98312 | tf_op jit(solution)/shard_map/ppermute | solution.py:683
  33.8 2.8 %shard_map.101 = (f32[96,32,128]{2,1,0:T(8,128)}, f32[3,96,128]{2,1,0:T(8,128)S(1)}) custom-call(s32[1,48]{1,0:T(1,128)S(1)} %copy-done.4, s32[1,48]{1,0:T(1,128)S(1)} %bitcast.13, f32[1152,128]{1,0:T(8,128)S(1)} %get-tuple-element.49.flat_ref, f32[8,2,9,8,128]{4,3,2,1,0:T(8,128)S(1)} %get-tuple-element.50.phase_ref, bf16[2,256,256]{2,1,0:T(8,128)(2,1)S(1)} %copy-done), custom_call_target="tpu_custom_call" | custom-call | flops 4000000000 | bytes 12000000 | tf_op jit(solution)/shard_map/pallas_call | solution.py:861
  36.7 1.1 %shard_map.102.part_ref = f32[96,32,128]{2,1,0:T(8,128)} custom-call(s32[1,48]{1,0:T(1,128)S(1)} %copy-done.4, f32[7,2,48,128]{3,2,1,0:T(8,128)S(1)} %shard_map.91.phase_ref, bf16[2,256,256]{2,1,0:T(8,128)(2,1)S(1)} %copy-done, f32[3,96,128]{2,1,0:T(8,128)S(1)} %get-tuple-element.51.edge_ref, ...), custom_call_target="tpu_custom_call", output_to_operand_aliasing={{}: (5, {})} | custom-call | flops 1000000 | bytes 1000000 | tf_op jit(solution)/shard_map/pallas_call | solution.py:882
  37.8 1.1 %shard_map.103 = f32[96,32,128]{2,1,0:T(8,128)} custom-call(s32[1,48]{1,0:T(1,128)S(1)} %copy-done.4, f32[7,2,48,128]{3,2,1,0:T(8,128)S(1)} %shard_map.91.phase_ref, bf16[2,256,256]{2,1,0:T(8,128)(2,1)S(1)} %copy-done, f32[3,96,128]{2,1,0:T(8,128)S(1)} %get-tuple-element.51.edge_ref, ...), custom_call_target="tpu_custom_call", output_to_operand_aliasing={{}: (5, {})} | custom-call | flops 1000000 | bytes 1000000 | tf_op jit(solution)/shard_map/pallas_call | solution.py:882
  (17 shorter events, 0.0 us)
Async XLA Ops:
  0.9 8.0 %collective-permute-start = (f32[2,96,128]{2,1,0:T(8,128)S(1)}, f32[2,96,128]{2,1,0:T(8,128)S(1)}, u32[]{:S(2)}, u32[]{:S(2)}) collective-permute-start(f32[2,96,128]{2,1,0:T(8,128)S(1)} %get-tuple-element.31), channel_id=1, source_target_pairs={{0,7},{1,2},{2,1},{3,4},{4,3},{5,6},{6,5},{7,0},{8,15},{9,10},{10,... | collective-permute-start | bytes 294920 | tf_op jit(solution)/shard_map/ppermute | solution.py:683
  5.5 3.4 %collective-permute-start.1 = (f32[2,96,128]{2,1,0:T(8,128)S(1)}, f32[2,96,128]{2,1,0:T(8,128)S(1)}, u32[]{:S(2)}, u32[]{:S(2)}) collective-permute-start(f32[2,96,128]{2,1,0:T(8,128)S(1)} %get-tuple-element.32), channel_id=1, source_target_pairs={{0,1},{1,0},{2,3},{3,2},{4,5},{5,4},{6,7},{7,6},{8,9},{9,8},{10,11... | collective-permute-start | bytes 294920 | tf_op jit(solution)/shard_map/ppermute | solution.py:683
  5.5 3.4 %copy-start.1 = (bf16[2,384,256]{2,1,0:T(8,128)(2,1)S(1)}, bf16[2,384,256]{2,1,0:T(8,128)(2,1)}, u32[]{:S(2)}) copy-start(bf16[2,384,256]{2,1,0:T(8,128)(2,1)} %constant.4.clone.spread_hbm.spread_ref) | copy-start | bytes 1179652
  5.5 3.4 %copy-start.4 = (s32[1,48]{1,0:T(1,128)S(1)}, s32[1,48]{1,0:T(1,128)}, u32[]{:S(2)}) copy-start(s32[1,48]{1,0:T(1,128)} %parents_ref.7) | copy-start | bytes 580
  5.5 3.4 %copy-start.5 = (s32[48]{0:T(128)S(1)}, s32[48]{0:T(128)}, u32[]{:S(2)}) copy-start(s32[48]{0:T(128)} %octants_hbm.3) | copy-start | bytes 580
  5.5 7.6 %copy-start.2 = (s32[32,31]{1,0:T(8,128)S(1)}, s32[32,31]{1,0:T(8,128)}, u32[]{:S(2)}) copy-start(s32[32,31]{1,0:T(8,128)} %source_ref.1) | copy-start | bytes 11908
  5.5 7.5 %copy-start.3 = (s32[32,31]{1,0:T(8,128)S(1)}, s32[32,31]{1,0:T(8,128)}, u32[]{:S(2)}) copy-start(s32[32,31]{1,0:T(8,128)} %offset_ref.1) | copy-start | bytes 11908
  5.6 7.5 %copy-start.7 = (s32[32]{0:T(128)S(1)}, s32[32]{0:T(128)}, u32[]{:S(2)}) copy-start(s32[32]{0:T(128)} %param.15) | copy-start | bytes 388
  9.5 8.5 %collective-permute-start.2 = (f32[288,128]{1,0:T(8,128)S(1)}, f32[288,128]{1,0:T(8,128)S(1)}, u32[]{:S(2)}, u32[]{:S(2)}) collective-permute-start(f32[288,128]{1,0:T(8,128)S(1)} %get-tuple-element.37), channel_id=1, source_target_pairs={{0,8},{8,0},{16,24},{24,16},{1,9},{9,1},{17,25},{25,17},{2,10},{10... | collective-permute-start | bytes 442376 | tf_op jit(solution)/shard_map/ppermute | solution.py:688
  11.1 9.1 %collective-permute-start.3 = (f32[288,128]{1,0:T(8,128)S(1)}, f32[288,128]{1,0:T(8,128)S(1)}, u32[]{:S(2)}, u32[]{:S(2)}) collective-permute-start(f32[288,128]{1,0:T(8,128)S(1)} %get-tuple-element.42), channel_id=1, source_target_pairs={{0,16},{8,24},{16,0},{24,8},{1,17},{9,25},{17,1},{25,9},{2,18},{10... | collective-permute-start | bytes 442376 | tf_op jit(solution)/shard_map/ppermute | solution.py:688
  12.7 7.5 %collective-permute-start.4 = (f32[288,128]{1,0:T(8,128)S(1)}, f32[288,128]{1,0:T(8,128)S(1)}, u32[]{:S(2)}, u32[]{:S(2)}) collective-permute-start(f32[288,128]{1,0:T(8,128)S(1)} %get-tuple-element.43), channel_id=1, source_target_pairs={{0,24},{8,16},{16,8},{24,0},{1,25},{9,17},{17,9},{25,1},{2,26},{10... | collective-permute-start | bytes 442376 | tf_op jit(solution)/shard_map/ppermute | solution.py:688
  21.9 6.0 %collective-permute-start.5 = (f32[288,128]{1,0:T(8,128)S(1)}, f32[288,128]{1,0:T(8,128)S(1)}, u32[]{:S(2)}, u32[]{:S(2)}) collective-permute-start(f32[288,128]{1,0:T(8,128)S(1)} %get-tuple-element.46), channel_id=1, source_target_pairs={{0,8},{8,0},{16,24},{24,16},{1,9},{9,1},{17,25},{25,17},{2,10},{10... | collective-permute-start | bytes 442376 | tf_op jit(solution)/shard_map/ppermute | solution.py:688
  23.2 8.2 %collective-permute-start.6 = (f32[288,128]{1,0:T(8,128)S(1)}, f32[288,128]{1,0:T(8,128)S(1)}, u32[]{:S(2)}, u32[]{:S(2)}) collective-permute-start(f32[288,128]{1,0:T(8,128)S(1)} %get-tuple-element.47), channel_id=1, source_target_pairs={{0,16},{8,24},{16,0},{24,8},{1,17},{9,25},{17,1},{25,9},{2,18},{10... | collective-permute-start | bytes 442376 | tf_op jit(solution)/shard_map/ppermute | solution.py:688
  24.0 7.4 %collective-permute-start.7 = (f32[288,128]{1,0:T(8,128)S(1)}, f32[288,128]{1,0:T(8,128)S(1)}, u32[]{:S(2)}, u32[]{:S(2)}) collective-permute-start(f32[288,128]{1,0:T(8,128)S(1)} %get-tuple-element.48), channel_id=1, source_target_pairs={{0,24},{8,16},{16,8},{24,0},{1,25},{9,17},{17,9},{25,1},{2,26},{10... | collective-permute-start | bytes 442376 | tf_op jit(solution)/shard_map/ppermute | solution.py:688
  26.5 7.3 %copy-start = (bf16[2,256,256]{2,1,0:T(8,128)(2,1)S(1)}, bf16[2,256,256]{2,1,0:T(8,128)(2,1)}, u32[]{:S(2)}) copy-start(bf16[2,256,256]{2,1,0:T(8,128)(2,1)} %constant.5.clone.gather_ref) | copy-start | bytes 786436
  26.5 7.3 %copy-start.6 = (s32[48]{0:T(128)S(1)}, s32[48]{0:T(128)}, u32[]{:S(2)}) copy-start(s32[48]{0:T(128)} %octants_hbm.3) | copy-start | bytes 580
  31.5 5.1 %collective-permute-start.9 = (f32[64,128]{1,0:T(8,128)S(1)}, f32[64,128]{1,0:T(8,128)S(1)}, u32[]{:S(2)}, u32[]{:S(2)}) collective-permute-start(f32[64,128]{1,0:T(8,128)S(1)} %get-tuple-element.53), channel_id=1, source_target_pairs={{0,1},{1,0},{2,3},{3,2},{4,5},{5,4},{6,7},{7,6},{8,9},{9,8},{10,11... | collective-permute-start | bytes 98312 | tf_op jit(solution)/shard_map/ppermute | solution.py:683
  31.6 6.2 %collective-permute-start.8 = (f32[64,128]{1,0:T(8,128)S(1)}, f32[64,128]{1,0:T(8,128)S(1)}, u32[]{:S(2)}, u32[]{:S(2)}) collective-permute-start(f32[64,128]{1,0:T(8,128)S(1)} %get-tuple-element.52), channel_id=1, source_target_pairs={{0,7},{1,2},{2,1},{3,4},{4,3},{5,6},{6,5},{7,0},{8,15},{9,10},{10,... | collective-permute-start | bytes 98312 | tf_op jit(solution)/shard_map/ppermute | solution.py:683

commit v13 on v11

--- a/solution.py
+++ b/solution.py
@@ -20,7 +20,6 @@
 PERIOD_C = 4
 ROWS_PER_PERIOD = PERIOD_P * NTHETA_P // LANES
 GROUP = 8
-TILE = 8
 TOGETHER = 2
 BLOCK = 2 * GROUP
 
@@ -604,9 +603,7 @@
         for w in range(ROWS_PER_PERIOD):
             first = gp * ROWS_PER_PERIOD * periods + w
             incoming_ref[gp, w] = flat_ref[pl.ds(first, periods, stride=ROWS_PER_PERIOD), :]
-    azimuth_in = periods * PERIOD_C
     sublane = lax.broadcasted_iota(jnp.int32, (periods, LANES), 0)
-    inner = pl.ds(TILE, azimuth_in - 2 * TILE)
 
     def shift(block):
         for k in range(BLOCK):
@@ -642,12 +639,12 @@
             kp = block * (2 * BLOCK) + j
             for u in range(PERIOD_C):
                 whole_out[kp, pl.ds(u, periods, stride=PERIOD_C), :] = rows[u]
-            edge_ref[0, kp] = whole_out[kp, :TILE, :]
-            edge_ref[1, kp] = whole_out[kp, azimuth_in - TILE :, :]
+            for i, (u, m) in enumerate(((0, 0), (1, 0), (PERIOD_C - 1, periods - 1))):
+                edge_ref[i, pl.ds(kp, 1), :] = rows[u][m : m + 1]
 
     def written(block):
         some = pl.ds(block * (2 * BLOCK), 2 * BLOCK)
-        return pltpu.make_async_copy(whole_out.at[some, inner, :], out_ref.at[some, inner, :], sems.at[block])
+        return pltpu.make_async_copy(whole_out.at[some], out_ref.at[some], sems.at[block])
 
     def one_block(block, carry):
         shift(block)
@@ -662,23 +659,17 @@
         written(block).wait()
 
 
-def finish_kernel(parents_ref, phase_ref, gather_ref, edge_ref, far_ref, near_ref, part_ref, out_ref, tiles, sems):
+def finish_kernel(parents_ref, phase_ref, gather_ref, edge_ref, far_ref, near_ref, part_ref, out_ref, sums, sems):
     pairs, azimuth_in, _ = out_ref.shape
-    tiles[...] = edge_ref[...]
-    flat = tiles.reshape(2 * pairs * TILE, LANES)
+    children = pairs // 2
     below, above = from_sides(far_ref, near_ref)
     heads, tail = edge_contributions(parents_ref[...], phase_ref, gather_ref, above, below)
-    ends = ((0, 0, heads[0]), (0, 1, heads[1]), (1, TILE - 1, tail))
     copies = []
-    for i, start in enumerate((0, azimuth_in - TILE)):
-        for end, row, values in ends:
-            if end == i:
-                for part in range(2):
-                    for k in range(0, pairs // 2, 8):
-                        source = slice(part * (pairs // 2) + k, part * (pairs // 2) + k + 8)
-                        rows = pl.ds((i * pairs + 2 * k + part) * TILE + row, 8, stride=2 * TILE)
-                        flat[rows, :] = flat[rows, :] + values[source]
-        copy = pltpu.make_async_copy(tiles.at[i], out_ref.at[:, pl.ds(start, TILE), :], sems.at[i])
+    for i, (row, values) in enumerate(((0, heads[0]), (1, heads[1]), (azimuth_in - 1, tail))):
+        for part in range(2):
+            place = pl.ds(part, children, stride=2)
+            sums[i, place, :] = edge_ref[i, place, :] + values[part * children : (part + 1) * children]
+        copy = pltpu.make_async_copy(sums.at[i], out_ref.at[:, row, :], sems.at[i])
         copy.start()
         copies.append(copy)
     for copy in copies:
@@ -746,7 +737,7 @@
     frame = max(-(-((q * 2 * share) % 8 + 2 * share) // 8) * 8 for q in range(peers))
     view = trans_table.reshape(offsets, 2, flat_rows, LANES).transpose(0, 2, 1, 3).reshape(offsets, 2 * flat_rows, LANES)
     blocks = children // BLOCK
-    half = offsets // 2
+    half = offsets * 3 // 4
     rows = 2 * BLOCK * 3 * periods
     phases, edge_phases, flat, table = local_call(
         functools.partial(main_kernel, peers),
@@ -865,9 +856,9 @@
     from_far = swapped(to_far, "dir", 1)
     from_near = swapped(to_near, "dir", 0)
 
-    inner, edge_tiles = local_call(
+    partial_out, edge_sums = local_call(
         disaggregate_kernel,
-        [array(pairs, azimuth_in, polar_in), array(2, pairs, TILE, polar_in)],
+        [array(pairs, azimuth_in, polar_in), array(3, pairs, polar_in)],
         [VMEM] * 5,
         [
             pltpu.SMEM((children,), jnp.int32),
@@ -888,11 +879,11 @@
         finish_kernel,
         array(pairs, azimuth_in, polar_in),
         [VMEM] * 6 + [HBM],
-        [buffer(2, pairs, TILE, polar_in), pltpu.SemaphoreType.DMA((2,))],
+        [buffer(3, pairs, polar_in), pltpu.SemaphoreType.DMA((3,))],
         8,
         out_specs=HBM,
         aliases={6: 0},
-    )(child_parent, neighbour_phases, gather, edge_tiles, from_far, from_near, in_hbm(inner))
+    )(child_parent, neighbour_phases, gather, edge_sums, from_far, from_near, in_hbm(partial_out))
     return out.reshape(child_patterns.shape)
 
 

time: 38.5 us -> 38.2 us (level)
  Pallas kernels: 18.6 us -> 17.9 us
    pallas_call x1, Pallas kernels: 4.97 us -> 4.5 us  [on_device_exchange(): local_call(functools.partial(widen_kernel, peers, others), [array(parent_...]
where the time goes in v13:
time: 38.2 us; the launch traced here: 38 us
  Pallas kernels  17.9 us (47%)
  starting transfers between devices  12.8 us (34%)
  waiting for transfers between devices  6.98 us (18%)
    ppermute x6, starting transfers between devices, exchanged(): return lax.ppermute(values, axis, [(i, i ^ mask) for i in range(size)])  7.11 us
    ppermute x6, waiting for transfers between devices, exchanged(): return lax.ppermute(values, axis, [(i, i ^ mask) for i in range(size)])  5.75 us
    ppermute x4, starting transfers between devices, swapped(): lax.ppermute(values, axis, [(i, ((i - first ^ 1) + first) % size) for i i...  5.72 us
    pallas_call x1, Pallas kernels, on_device_exchange(): local_call(functools.partial(widen_kernel, peers, others), [array(parent_...  4.5 us
    pallas_call x1, Pallas kernels, on_device_exchange(): local_call(functools.partial(main_kernel, peers), [array(8, 2, ROWS_PER_P...  3.34 us
    pallas_call x1, Pallas kernels, on_device_exchange(): local_call(disaggregate_kernel, [array(pairs, azimuth_in, polar_in), arra...  2.83 us
    pallas_call x3, Pallas kernels, on_device_exchange(): local_call(functools.partial(translate_kernel, frame, others, tuple(late)...  2.18 us
    ppermute x4, waiting for transfers between devices, swapped(): lax.ppermute(values, axis, [(i, ((i - first ^ 1) + first) % size) for i i...  1.23 us
  transfers between devices with their start and end apart: 10, of which 4 were waited for; matrix products, arithmetic and copies ran while one was open for 0% of the time, Pallas kernels for 36%

profile of v13, /device:TPU:0, one launch (start us, length us, event | category | flops | bytes accessed | tf_op | source)
XLA Modules:
  0.0 38.0 jit_solution(10345640377624901920)
XLA Ops:
  0.0 0.9 %shard_map.93 = (f32[2,96,128]{2,1,0:T(8,128)S(1)}, f32[2,96,128]{2,1,0:T(8,128)S(1)}) custom-call(f32[96,32,128]{2,1,0:T(8,128)} %bitcast.17), custom_call_target="tpu_custom_call" | custom-call | flops 1000000 | bytes 1000000 | tf_op jit(solution)/shard_map/pallas_call | solution.py:729
  0.9 4.6 %collective-permute-start = (f32[2,96,128]{2,1,0:T(8,128)S(1)}, f32[2,96,128]{2,1,0:T(8,128)S(1)}, u32[]{:S(2)}, u32[]{:S(2)}) collective-permute-start(f32[2,96,128]{2,1,0:T(8,128)S(1)} %get-tuple-element.31), channel_id=1, source_target_pairs={{0,7},{1,2},{2,1},{3,4},{4,3},{5,6},{6,5},{7,0},{8,15},{9,10},{10,... | collective-permute-start | bytes 294920 | tf_op jit(solution)/shard_map/ppermute | solution.py:681
  5.5 0.0 copy-start.2
  5.5 0.0 copy-start.3
  5.6 0.0 copy-start.7
  5.6 3.3 %shard_map.92 = (f32[8,2,9,8,128]{4,3,2,1,0:T(8,128)S(1)}, f32[7,2,8,128]{3,2,1,0:T(8,128)S(1)}, f32[1152,128]{1,0:T(8,128)S(1)}, bf16[237,40,128]{2,1,0:T(8,128)(2,1)S(1)}) custom-call(s32[48]{0:T(128)} %bitcast.13, s32[48]{0:T(128)} %octants_hbm.3, f32[3072,128]{1,0:T(8,128)} %bitcast.18, bf16[316,144,128]{2,1,0:T(8,128)(2,1)} %bitcast.15, ...), custom_call_target="tpu_custom_call" | custom-call | flops 4000000000 | bytes 12000000 | tf_op jit(solution)/shard_map/pallas_call | solution.py:742
  8.9 0.0 collective-permute-done.far_ref
  9.0 0.6 %shard_map.94 = (f32[288,128]{1,0:T(8,128)S(1)}, f32[288,128]{1,0:T(8,128)S(1)}, f32[288,128]{1,0:T(8,128)S(1)}, f32[288,128]{1,0:T(8,128)S(1)}) custom-call(s32[1,48]{1,0:T(1,128)S(1)} %copy-done.6, s32[1,48]{1,0:T(1,128)S(1)} %bitcast.11, f32[2,96,128]{2,1,0:T(8,128)S(1)} %collective-permute-done.far_ref, ...), custom_call_target="tpu_custom_call" | custom-call | flops 1000000 | bytes 1000000 | tf_op jit(solution)/shard_map/pallas_call | solution.py:777
  9.5 1.6 %collective-permute-start.2 = (f32[288,128]{1,0:T(8,128)S(1)}, f32[288,128]{1,0:T(8,128)S(1)}, u32[]{:S(2)}, u32[]{:S(2)}) collective-permute-start(f32[288,128]{1,0:T(8,128)S(1)} %get-tuple-element.37), channel_id=1, source_target_pairs={{0,8},{8,0},{16,24},{24,16},{1,9},{9,1},{17,25},{25,17},{2,10},{10... | collective-permute-start | bytes 442376 | tf_op jit(solution)/shard_map/ppermute | solution.py:686
  11.1 1.5 %collective-permute-start.3 = (f32[288,128]{1,0:T(8,128)S(1)}, f32[288,128]{1,0:T(8,128)S(1)}, u32[]{:S(2)}, u32[]{:S(2)}) collective-permute-start(f32[288,128]{1,0:T(8,128)S(1)} %get-tuple-element.42), channel_id=1, source_target_pairs={{0,16},{8,24},{16,0},{24,8},{1,17},{9,25},{17,1},{25,9},{2,18},{10... | collective-permute-start | bytes 442376 | tf_op jit(solution)/shard_map/ppermute | solution.py:686
  12.7 0.4 %collective-permute-start.4 = (f32[288,128]{1,0:T(8,128)S(1)}, f32[288,128]{1,0:T(8,128)S(1)}, u32[]{:S(2)}, u32[]{:S(2)}) collective-permute-start(f32[288,128]{1,0:T(8,128)S(1)} %get-tuple-element.43), channel_id=1, source_target_pairs={{0,24},{8,16},{16,8},{24,0},{1,25},{9,17},{17,9},{25,1},{2,26},{10... | collective-permute-start | bytes 442376 | tf_op jit(solution)/shard_map/ppermute | solution.py:686
  13.1 4.5 %shard_map.95 = (f32[30720,128]{1,0:T(8,128)S(1)}, f32[1280,128]{1,0:T(8,128)S(1)}, f32[1280,128]{1,0:T(8,128)S(1)}) custom-call(s32[32,31]{1,0:T(8,128)S(1)} %copy-done.2, s32[32,31]{1,0:T(8,128)S(1)} %copy-done.3, s32[1,32]{1,0:T(1,128)S(1)} %bitcast.14, bf16[237,40,128]{2,1,0:T(8,128)(2,1)S(1)} %get-tuple-element.30.head_ref, ...), custom_call_target="tpu_custom_call" | custom-call | flops 90000000 | bytes 12000000 | tf_op jit(solution)/shard_map/pallas_call | solution.py:791
  17.6 0.0 collective-permute-done.2.rest_0_
  17.6 1.2 %shard_map.96 = (f32[1280,128]{1,0:T(8,128)S(1)}, f32[1280,128]{1,0:T(8,128)S(1)}) custom-call(f32[30720,128]{1,0:T(8,128)S(1)} %get-tuple-element.36.placed_ref, f32[288,128]{1,0:T(8,128)S(1)} %collective-permute-done.2.rest_0_, f32[1280,128]{1,0:T(8,128)S(1)} %get-tuple-element.38.rest_1_, f32[1280,128]{1,0:T(8,128)S(1)} %get-tuple-element.39.rest_2_), custom_call_target="tpu_custom_call" | custom-call | flops 60000000 | bytes 12000000 | tf_op jit(solution)/shard_map/pallas_call | solution.py:810
  18.8 1.4 %collective-permute-done.3.rest_0_ = f32[288,128]{1,0:T(8,128)S(1)} collective-permute-done((f32[288,128]{1,0:T(8,128)S(1)}, f32[288,128]{1,0:T(8,128)S(1)}, u32[]{:S(2)}, u32[]{:S(2)}) %collective-permute-start.3) | collective-permute-done | bytes 147488 | tf_op jit(solution)/shard_map/ppermute | solution.py:686
  20.2 0.6 %shard_map.97 = (f32[640,128]{1,0:T(8,128)S(1)}, f32[640,128]{1,0:T(8,128)S(1)}, f32[288,128]{1,0:T(8,128)S(1)}) custom-call(f32[30720,128]{1,0:T(8,128)S(1)} %get-tuple-element.36.placed_ref, f32[1280,128]{1,0:T(8,128)S(1)} %get-tuple-element.40.real_sum, f32[1280,128]{1,0:T(8,128)S(1)} %get-tuple-element.41.imag_sum, ...), custom_call_target="tpu_custom_call" | custom-call | flops 10000000 | bytes 2000000 | tf_op jit(solution)/shard_map/pallas_call | solution.py:824
  20.8 1.1 %shard_map.99 = (f32[288,128]{1,0:T(8,128)S(1)}, f32[288,128]{1,0:T(8,128)S(1)}) custom-call(f32[30720,128]{1,0:T(8,128)S(1)} %get-tuple-element.36.placed_ref, f32[1280,128]{1,0:T(8,128)S(1)} %get-tuple-element.40.real_sum, f32[1280,128]{1,0:T(8,128)S(1)} %get-tuple-element.41.imag_sum, f32[640,128]{1,0:T(8,128)S(1)} %get-tuple-element.44.rest_0_, ...), custom_call_target="tpu_custom_call" | custom-call | flops 20000000 | bytes 4000000 | tf_op jit(solution)/shard_map/pallas_call | solution.py:824
  21.9 1.3 %collective-permute-start.5 = (f32[288,128]{1,0:T(8,128)S(1)}, f32[288,128]{1,0:T(8,128)S(1)}, u32[]{:S(2)}, u32[]{:S(2)}) collective-permute-start(f32[288,128]{1,0:T(8,128)S(1)} %get-tuple-element.46), channel_id=1, source_target_pairs={{0,8},{8,0},{16,24},{24,16},{1,9},{9,1},{17,25},{25,17},{2,10},{10... | collective-permute-start | bytes 442376 | tf_op jit(solution)/shard_map/ppermute | solution.py:686
  23.2 0.8 %collective-permute-start.6 = (f32[288,128]{1,0:T(8,128)S(1)}, f32[288,128]{1,0:T(8,128)S(1)}, u32[]{:S(2)}, u32[]{:S(2)}) collective-permute-start(f32[288,128]{1,0:T(8,128)S(1)} %get-tuple-element.47), channel_id=1, source_target_pairs={{0,16},{8,24},{16,0},{24,8},{1,17},{9,25},{17,1},{25,9},{2,18},{10... | collective-permute-start | bytes 442376 | tf_op jit(solution)/shard_map/ppermute | solution.py:686
  24.0 1.4 %collective-permute-start.7 = (f32[288,128]{1,0:T(8,128)S(1)}, f32[288,128]{1,0:T(8,128)S(1)}, u32[]{:S(2)}, u32[]{:S(2)}) collective-permute-start(f32[288,128]{1,0:T(8,128)S(1)} %get-tuple-element.48), channel_id=1, source_target_pairs={{0,24},{8,16},{16,8},{24,0},{1,25},{9,17},{17,9},{25,1},{2,26},{10... | collective-permute-start | bytes 442376 | tf_op jit(solution)/shard_map/ppermute | solution.py:686
  25.4 1.1 %shard_map.91.phase_ref = f32[7,2,48,128]{3,2,1,0:T(8,128)S(1)} custom-call(s32[48]{0:T(128)} %octants_hbm.3), custom_call_target="tpu_custom_call" | custom-call | flops 20000000 | bytes 1000000 | tf_op jit(solution)/shard_map/pallas_call | solution.py:838
  26.5 0.0 copy-start.1
  26.5 0.0 copy-start.5
  26.5 0.5 %shard_map.98.rest_0_ = f32[288,128]{1,0:T(8,128)S(1)} custom-call(f32[30720,128]{1,0:T(8,128)S(1)} %get-tuple-element.36.placed_ref, f32[1280,128]{1,0:T(8,128)S(1)} %get-tuple-element.40.real_sum, f32[1280,128]{1,0:T(8,128)S(1)} %get-tuple-element.41.imag_sum, f32[640,128]{1,0:T(8,128)S(1)} %get-tuple-element.44.rest_0_, ...), custom_call_target="tpu_custom_call" | custom-call | flops 10000000 | bytes 2000000 | tf_op jit(solution)/shard_map/pallas_call | solution.py:824
  27.1 0.8 %collective-permute-done.5.rest_1_ = f32[288,128]{1,0:T(8,128)S(1)} collective-permute-done((f32[288,128]{1,0:T(8,128)S(1)}, f32[288,128]{1,0:T(8,128)S(1)}, u32[]{:S(2)}, u32[]{:S(2)}) %collective-permute-start.5) | collective-permute-done | bytes 147488 | tf_op jit(solution)/shard_map/ppermute | solution.py:686
  27.9 3.6 %collective-permute-done.6.rest_2_ = f32[288,128]{1,0:T(8,128)S(1)} collective-permute-done((f32[288,128]{1,0:T(8,128)S(1)}, f32[288,128]{1,0:T(8,128)S(1)}, u32[]{:S(2)}, u32[]{:S(2)}) %collective-permute-start.6) | collective-permute-done | bytes 147488 | tf_op jit(solution)/shard_map/ppermute | solution.py:686
  31.4 0.0 collective-permute-done.7.rest_3_
  31.4 0.1 shard_map.100
  31.5 1.1 %collective-permute-start.8 = (f32[64,128]{1,0:T(8,128)S(1)}, f32[64,128]{1,0:T(8,128)S(1)}, u32[]{:S(2)}, u32[]{:S(2)}) collective-permute-start(f32[64,128]{1,0:T(8,128)S(1)} %get-tuple-element.52), channel_id=1, source_target_pairs={{0,7},{1,2},{2,1},{3,4},{4,3},{5,6},{6,5},{7,0},{8,15},{9,10},{10,... | collective-permute-start | bytes 98312 | tf_op jit(solution)/shard_map/ppermute | solution.py:681
  32.7 2.8 %shard_map.101 = (f32[96,32,128]{2,1,0:T(8,128)}, f32[3,96,128]{2,1,0:T(8,128)S(1)}) custom-call(s32[1,48]{1,0:T(1,128)S(1)} %copy-done.6, s32[1,48]{1,0:T(1,128)S(1)} %bitcast.12, f32[1152,128]{1,0:T(8,128)S(1)} %get-tuple-element.49.flat_ref, f32[8,2,9,8,128]{4,3,2,1,0:T(8,128)S(1)} %get-tuple-element.50.phase_ref, bf16[2,256,256]{2,1,0:T(8,128)(2,1)S(1)} %copy-done.1), custom_call_target="tpu_custom_call" | custom-call | flops 4000000000 | bytes 12000000 | tf_op jit(solution)/shard_map/pallas_call | solution.py:859
  35.5 1.2 %collective-permute-done.8.far_ref = f32[64,128]{1,0:T(8,128)S(1)} collective-permute-done((f32[64,128]{1,0:T(8,128)S(1)}, f32[64,128]{1,0:T(8,128)S(1)}, u32[]{:S(2)}, u32[]{:S(2)}) %collective-permute-start.8) | collective-permute-done | bytes 32800 | tf_op jit(solution)/shard_map/ppermute | solution.py:681
  36.8 1.2 %shard_map.102 = f32[96,32,128]{2,1,0:T(8,128)} custom-call(s32[1,48]{1,0:T(1,128)S(1)} %copy-done.6, f32[7,2,48,128]{3,2,1,0:T(8,128)S(1)} %shard_map.91.phase_ref, bf16[2,256,256]{2,1,0:T(8,128)(2,1)S(1)} %copy-done.1, f32[3,96,128]{2,1,0:T(8,128)S(1)} %get-tuple-element.51.edge_ref, ...), custom_call_target="tpu_custom_call", output_to_operand_aliasing={{}: (6, {})} | custom-call | flops 1000000 | bytes 1000000 | tf_op jit(solution)/shard_map/pallas_call | solution.py:878
  (16 shorter events, 0.0 us)
Async XLA Ops:
  0.9 8.0 %collective-permute-start = (f32[2,96,128]{2,1,0:T(8,128)S(1)}, f32[2,96,128]{2,1,0:T(8,128)S(1)}, u32[]{:S(2)}, u32[]{:S(2)}) collective-permute-start(f32[2,96,128]{2,1,0:T(8,128)S(1)} %get-tuple-element.31), channel_id=1, source_target_pairs={{0,7},{1,2},{2,1},{3,4},{4,3},{5,6},{6,5},{7,0},{8,15},{9,10},{10,... | collective-permute-start | bytes 294920 | tf_op jit(solution)/shard_map/ppermute | solution.py:681
  5.5 3.4 %collective-permute-start.1 = (f32[2,96,128]{2,1,0:T(8,128)S(1)}, f32[2,96,128]{2,1,0:T(8,128)S(1)}, u32[]{:S(2)}, u32[]{:S(2)}) collective-permute-start(f32[2,96,128]{2,1,0:T(8,128)S(1)} %get-tuple-element.32), channel_id=1, source_target_pairs={{0,1},{1,0},{2,3},{3,2},{4,5},{5,4},{6,7},{7,6},{8,9},{9,8},{10,11... | collective-permute-start | bytes 294920 | tf_op jit(solution)/shard_map/ppermute | solution.py:681
  5.5 3.4 %copy-start = (bf16[2,384,256]{2,1,0:T(8,128)(2,1)S(1)}, bf16[2,384,256]{2,1,0:T(8,128)(2,1)}, u32[]{:S(2)}) copy-start(bf16[2,384,256]{2,1,0:T(8,128)(2,1)} %constant.4.clone.spread_hbm.spread_ref) | copy-start | bytes 1179652
  5.5 3.4 %copy-start.4 = (s32[48]{0:T(128)S(1)}, s32[48]{0:T(128)}, u32[]{:S(2)}) copy-start(s32[48]{0:T(128)} %octants_hbm.3) | copy-start | bytes 580
  5.5 3.4 %copy-start.6 = (s32[1,48]{1,0:T(1,128)S(1)}, s32[1,48]{1,0:T(1,128)}, u32[]{:S(2)}) copy-start(s32[1,48]{1,0:T(1,128)} %parents_ref.5) | copy-start | bytes 580
  5.5 7.6 %copy-start.2 = (s32[32,31]{1,0:T(8,128)S(1)}, s32[32,31]{1,0:T(8,128)}, u32[]{:S(2)}) copy-start(s32[32,31]{1,0:T(8,128)} %source_ref.1) | copy-start | bytes 11908
  5.5 7.5 %copy-start.3 = (s32[32,31]{1,0:T(8,128)S(1)}, s32[32,31]{1,0:T(8,128)}, u32[]{:S(2)}) copy-start(s32[32,31]{1,0:T(8,128)} %offset_ref.1) | copy-start | bytes 11908
  5.6 7.5 %copy-start.7 = (s32[32]{0:T(128)S(1)}, s32[32]{0:T(128)}, u32[]{:S(2)}) copy-start(s32[32]{0:T(128)} %param.15) | copy-start | bytes 388
  9.5 8.1 %collective-permute-start.2 = (f32[288,128]{1,0:T(8,128)S(1)}, f32[288,128]{1,0:T(8,128)S(1)}, u32[]{:S(2)}, u32[]{:S(2)}) collective-permute-start(f32[288,128]{1,0:T(8,128)S(1)} %get-tuple-element.37), channel_id=1, source_target_pairs={{0,8},{8,0},{16,24},{24,16},{1,9},{9,1},{17,25},{25,17},{2,10},{10... | collective-permute-start | bytes 442376 | tf_op jit(solution)/shard_map/ppermute | solution.py:686
  11.1 9.1 %collective-permute-start.3 = (f32[288,128]{1,0:T(8,128)S(1)}, f32[288,128]{1,0:T(8,128)S(1)}, u32[]{:S(2)}, u32[]{:S(2)}) collective-permute-start(f32[288,128]{1,0:T(8,128)S(1)} %get-tuple-element.42), channel_id=1, source_target_pairs={{0,16},{8,24},{16,0},{24,8},{1,17},{9,25},{17,1},{25,9},{2,18},{10... | collective-permute-start | bytes 442376 | tf_op jit(solution)/shard_map/ppermute | solution.py:686
  12.7 7.5 %collective-permute-start.4 = (f32[288,128]{1,0:T(8,128)S(1)}, f32[288,128]{1,0:T(8,128)S(1)}, u32[]{:S(2)}, u32[]{:S(2)}) collective-permute-start(f32[288,128]{1,0:T(8,128)S(1)} %get-tuple-element.43), channel_id=1, source_target_pairs={{0,24},{8,16},{16,8},{24,0},{1,25},{9,17},{17,9},{25,1},{2,26},{10... | collective-permute-start | bytes 442376 | tf_op jit(solution)/shard_map/ppermute | solution.py:686
  21.9 6.0 %collective-permute-start.5 = (f32[288,128]{1,0:T(8,128)S(1)}, f32[288,128]{1,0:T(8,128)S(1)}, u32[]{:S(2)}, u32[]{:S(2)}) collective-permute-start(f32[288,128]{1,0:T(8,128)S(1)} %get-tuple-element.46), channel_id=1, source_target_pairs={{0,8},{8,0},{16,24},{24,16},{1,9},{9,1},{17,25},{25,17},{2,10},{10... | collective-permute-start | bytes 442376 | tf_op jit(solution)/shard_map/ppermute | solution.py:686
  23.2 8.2 %collective-permute-start.6 = (f32[288,128]{1,0:T(8,128)S(1)}, f32[288,128]{1,0:T(8,128)S(1)}, u32[]{:S(2)}, u32[]{:S(2)}) collective-permute-start(f32[288,128]{1,0:T(8,128)S(1)} %get-tuple-element.47), channel_id=1, source_target_pairs={{0,16},{8,24},{16,0},{24,8},{1,17},{9,25},{17,1},{25,9},{2,18},{10... | collective-permute-start | bytes 442376 | tf_op jit(solution)/shard_map/ppermute | solution.py:686
  24.0 7.4 %collective-permute-start.7 = (f32[288,128]{1,0:T(8,128)S(1)}, f32[288,128]{1,0:T(8,128)S(1)}, u32[]{:S(2)}, u32[]{:S(2)}) collective-permute-start(f32[288,128]{1,0:T(8,128)S(1)} %get-tuple-element.48), channel_id=1, source_target_pairs={{0,24},{8,16},{16,8},{24,0},{1,25},{9,17},{17,9},{25,1},{2,26},{10... | collective-permute-start | bytes 442376 | tf_op jit(solution)/shard_map/ppermute | solution.py:686
  26.5 6.2 %copy-start.1 = (bf16[2,256,256]{2,1,0:T(8,128)(2,1)S(1)}, bf16[2,256,256]{2,1,0:T(8,128)(2,1)}, u32[]{:S(2)}) copy-start(bf16[2,256,256]{2,1,0:T(8,128)(2,1)} %constant.5.clone.gather_ref) | copy-start | bytes 786436
  26.5 6.2 %copy-start.5 = (s32[48]{0:T(128)S(1)}, s32[48]{0:T(128)}, u32[]{:S(2)}) copy-start(s32[48]{0:T(128)} %octants_hbm.3) | copy-start | bytes 580
  31.5 5.2 %collective-permute-start.8 = (f32[64,128]{1,0:T(8,128)S(1)}, f32[64,128]{1,0:T(8,128)S(1)}, u32[]{:S(2)}, u32[]{:S(2)}) collective-permute-start(f32[64,128]{1,0:T(8,128)S(1)} %get-tuple-element.52), channel_id=1, source_target_pairs={{0,7},{1,2},{2,1},{3,4},{4,3},{5,6},{6,5},{7,0},{8,15},{9,10},{10,... | collective-permute-start | bytes 98312 | tf_op jit(solution)/shard_map/ppermute | solution.py:681
  32.7 4.1 %collective-permute-start.9 = (f32[64,128]{1,0:T(8,128)S(1)}, f32[64,128]{1,0:T(8,128)S(1)}, u32[]{:S(2)}, u32[]{:S(2)}) collective-permute-start(f32[64,128]{1,0:T(8,128)S(1)} %get-tuple-element.53), channel_id=1, source_target_pairs={{0,1},{1,0},{2,3},{3,2},{4,5},{5,4},{6,7},{7,6},{8,9},{9,8},{10,11... | collective-permute-start | bytes 98312 | tf_op jit(solution)/shard_map/ppermute | solution.py:681
